TPU v7x, 32 devices: a whole 2x2x4 slice. The times are simulated.
32 devices in a mesh: section: 2 (over core), dp: 4 (over z), tensor: 4 (over y, x).
Axes of the slice: x: 2, y: 2, z: 4, core: 2. Of those that a mesh axis runs over, the one named last changes fastest.
Arguments:
- x_in: bfloat16 [2, 1536, 4, 1536], P(None, 'tensor', 'dp'), may hold values from -6 to 6
- d_out: bfloat16 [2, 1536, 4, 1536], P(None, 'tensor', 'dp'), may hold values from -6 to 6
- doc_lengths: int32 [2, 4, 3], P(None, 'dp'), may hold values from 1 to 1024, 1536 in all within a row
- token_mask: int32 [2, 1536, 4], P(None, None, 'dp'), may hold values 0 or 1
- gain_in: float32 [2, 1536], P('section'), may hold values from 0.5 to 1.5
- w_zx: bfloat16 [2, 1536, 2, 3072], P('section', 'dp', None, 'tensor'), may hold values from -0.15625 to 0.15625
- w_bcdt: bfloat16 [2, 1536, 304], P('section', 'dp'), may hold values from -0.15625 to 0.15625
- conv_x: float32 [2, 5, 3072], P('section', None, 'tensor'), may hold values from -3 to 3
- conv_bc: float32 [2, 5, 256], P('section'), may hold values from -3 to 3
- dt_bias: float32 [2, 48], P('section', 'tensor'), may hold values from -4 to -1
- a_log: float32 [2, 48], P('section', 'tensor'), may hold values from -4.6 to 1
- d_skip: float32 [2, 48], P('section', 'tensor'), may hold values from 0.5 to 1.5
- gain_inner: float32 [2, 3072], P('section', 'tensor'), may hold values from 0.5 to 1.5
- w_out: bfloat16 [2, 3072, 1536], P('section', 'tensor', 'dp'), may hold values from -0.109375 to 0.109375
Outputs:
- out_act: float32 [2, 1536, 4, 1536], P(None, 'tensor', 'dp')
- grad_in: float32 [2, 1536, 4, 1536], P(None, 'tensor', 'dp', 'section')
- grad_gain_in: float32 [2, 1536], P('section')
- grad_w_zx: float32 [2, 1536, 2, 3072], P('section', 'dp', None, 'tensor')
- grad_w_bcdt: float32 [2, 1536, 304], P('section', 'dp')
- grad_conv_x: float32 [2, 5, 3072], P('section', None, 'tensor')
- grad_conv_bc: float32 [2, 5, 256], P('section')
- grad_dt_bias: float32 [2, 48], P('section', 'tensor')
- grad_a_log: float32 [2, 48], P('section', 'tensor')
- grad_d_skip: float32 [2, 48], P('section', 'tensor')
- grad_gain_inner: float32 [2, 3072], P('section', 'tensor')
- grad_w_out: float32 [2, 3072, 1536], P('section', 'tensor', 'dp')
Inputs may be any that keep to these rules, and one draw needn't show every extreme that they name: `doc_lengths`: in each slot the 3 lengths add up to 1536, and the longest is exactly 1024.
All inputs are finite; a program needn't handle non-finite values. No bound on the sum of `token_mask` on one device may be relied on, other than what follows from the above.
Results may differ from a plain program's by a relative error of at most 0.012.
The roundings to bfloat16 on the way count: a program that leaves them out, or rounds other values in their place, can miss the bound.
Values may be sent and summed in bfloat16 or wider, within the bound.
No kernel may reach another device: no remote copies, remote signals or barrier semaphores. Data moves between devices by JAX's collectives and lax.ppermute only.
A program may use at most 448 MiB of HBM per device.

v0:
```python
from functools import partial

import jax
import jax.numpy as jnp
from jax import lax
from jax.sharding import PartitionSpec as P

DI = 3072
SCAN_BLOCK = 256


EPS = 1e-05
PRECISE = lax.Precision.HIGHEST


def from_behind(value, axis, steps):
    count = lax.axis_size(axis)
    pairs = [(source, (source + steps) % count) for source in range(count)]
    return lax.ppermute(value, axis, pairs)


def conv_taps(signal, taps, doc_ids):
    reach = taps.shape[0] - 1
    length = signal.shape[0]
    summed = taps[reach] + taps[reach - 1] * signal
    for offset in range(1, reach):
        shifted = jnp.concatenate([jnp.zeros_like(signal[:offset]), signal[: length - offset]], 0)
        moved_ids = jnp.concatenate(
            [jnp.full_like(doc_ids[:offset], -1), doc_ids[: length - offset]], 0
        )
        same_doc = (moved_ids == doc_ids).astype(jnp.float32)[..., None]
        summed = summed + taps[reach - 1 - offset] * shifted * same_doc
    return summed


def settle(values):
    return lax.optimization_barrier(values.astype(jnp.bfloat16)).astype(jnp.float32)


def doc_index(lengths, length):
    doc_ends = jnp.cumsum(lengths, -1)
    places = jnp.arange(length, dtype=jnp.int32)
    return jnp.sum((places[:, None, None] >= doc_ends[None, :, :-1]).astype(jnp.int32), -1)


def conv_piece(proj_x, proj_bc, conv_x, conv_bc, live_mask, doc_ids):
    conv_out = jax.nn.silu(conv_taps(proj_x * live_mask, conv_x, doc_ids))
    bc_out = jax.nn.silu(conv_taps(proj_bc * live_mask, conv_bc, doc_ids))
    return (conv_out, bc_out)


def ssd_slot(heads_in, bc_out, steps_dt, log_decay, doc_ids, block_len):
    length, head_count, head_size = heads_in.shape
    state_count = bc_out.shape[1] // 2
    block_count = length // block_len
    in_blocks = heads_in.reshape(block_count, block_len, head_count, head_size)
    b_blocks = bc_out[:, :state_count].reshape(block_count, block_len, state_count)
    c_blocks = bc_out[:, state_count:].reshape(block_count, block_len, state_count)
    dt_blocks = steps_dt.reshape(block_count, block_len, head_count)
    id_blocks = doc_ids.reshape(block_count, block_len)
    cumulative = jnp.cumsum(log_decay.reshape(block_count, block_len, head_count), 1)
    places = jnp.arange(block_len)
    usable = (
        (places[:, None] >= places[None, :])[None]
        & (id_blocks[:, :, None] == id_blocks[:, None, :])
    )[..., None]
    spread = cumulative[:, :, None, :] - cumulative[:, None, :, :]
    decays = jnp.where(usable, jnp.exp(jnp.where(usable, spread, 0.0)), 0.0)
    scores = jnp.einsum("cte,cse->cts", c_blocks, b_blocks, precision=PRECISE)
    mixing = decays * scores[..., None] * dt_blocks[:, None, :, :]
    within = jnp.einsum("ctsh,cshp->cthp", mixing, in_blocks, precision=PRECISE)
    tail_same = (id_blocks == id_blocks[:, -1:]).astype(jnp.float32)[..., None]
    to_end = jnp.exp(cumulative[:, -1:, :] - cumulative) * tail_same * dt_blocks
    pieces = jnp.einsum("csh,cshp,csn->chpn", to_end, in_blocks, b_blocks, precision=PRECISE)
    carried = jnp.zeros((head_count, head_size, state_count), jnp.float32)
    entering = []
    for block_no in range(block_count):
        entering.append(carried)
        if block_no:
            linked = (id_blocks[block_no, -1] == id_blocks[block_no - 1, -1]).astype(jnp.float32)
        else:
            linked = jnp.zeros((), jnp.float32)
        carried = (
            pieces[block_no] + (jnp.exp(cumulative[block_no, -1]) * linked)[:, None, None] * carried
        )
    starting = jnp.stack(entering)
    prev_ids = jnp.concatenate([id_blocks[:1, :1] - 1, id_blocks[:-1, -1:]], 0)
    from_prev = jnp.exp(cumulative) * (id_blocks == prev_ids).astype(jnp.float32)[..., None]
    across = (
        jnp.einsum("ctn,chpn->cthp", c_blocks, starting, precision=PRECISE) * from_prev[..., None]
    )
    return (within + across).reshape(length, head_count, head_size)


def mixer_piece(
    conv_out, bc_out, dt_raw, gate_in, dt_bias, a_log, d_skip, live_mask, doc_ids, block_len
):
    length, slot_count, inner_width = conv_out.shape
    head_count = dt_bias.shape[0]
    steps_dt = jax.nn.softplus(dt_raw + dt_bias) * live_mask
    log_decay = -jnp.exp(a_log) * steps_dt
    heads_in = conv_out.reshape(length, slot_count, head_count, inner_width // head_count)
    per_slot = jax.vmap(partial(ssd_slot, block_len=block_len), in_axes=(1, 1, 1, 1, 1), out_axes=1)
    outputs = per_slot(heads_in, bc_out, steps_dt, log_decay, doc_ids) + d_skip[:, None] * heads_in
    return outputs.reshape(length, slot_count, inner_width) * jax.nn.silu(gate_in)


def inner_scale(gated):
    summed = lax.psum(jnp.sum(gated * gated, -1), "tensor")
    return lax.rsqrt(summed / DI + EPS)[..., None]


def gather_weights(w_zx, w_bcdt, w_out):
    return (
        lax.all_gather(w_zx[0], "dp", axis=0, tiled=True),
        lax.all_gather(w_bcdt[0], "dp", axis=0, tiled=True),
        lax.all_gather(w_out[0], "dp", axis=1, tiled=True),
    )


def layer_parts(residual, matrices, params, live_mask, doc_ids):
    gain_in, conv_x, conv_bc, dt_bias, a_log, d_skip, gain_inner = params
    row_scale = lax.rsqrt(jnp.mean(residual * residual, -1, keepdims=True) + EPS)
    normed = (residual * row_scale * gain_in).astype(jnp.bfloat16)
    gathered = lax.all_gather(normed, "tensor", axis=0, tiled=True)
    length, slot_count, model_width = gathered.shape
    flat_rows = gathered.reshape(length * slot_count, model_width)
    proj_zx = jnp.einsum(
        "rd,dkc->rkc", flat_rows, matrices[0], preferred_element_type=jnp.float32
    ).reshape(length, slot_count, 2, -1)
    proj_bcd = jnp.dot(flat_rows, matrices[1], preferred_element_type=jnp.float32).reshape(
        length, slot_count, -1
    )
    head_count = dt_bias.shape[0]
    state_count = conv_bc.shape[-1] // 2
    dt_raw = lax.dynamic_slice_in_dim(
        proj_bcd, 2 * state_count + lax.axis_index("tensor") * head_count, head_count, 2
    )
    conv_fn = partial(conv_piece, live_mask=live_mask, doc_ids=doc_ids)
    (conv_out, bc_out), conv_pull = jax.vjp(
        conv_fn, proj_zx[:, :, 1], proj_bcd[:, :, : 2 * state_count], conv_x, conv_bc
    )
    mixer_fn = partial(mixer_piece, live_mask=live_mask, doc_ids=doc_ids, block_len=SCAN_BLOCK)
    gated, mixer_pull = jax.vjp(
        mixer_fn, settle(conv_out), settle(bc_out), dt_raw, proj_zx[:, :, 0], dt_bias, a_log, d_skip
    )
    inner_inv = inner_scale(gated)
    normed_out = (
        (gated * inner_inv * gain_inner).astype(jnp.bfloat16).reshape(length * slot_count, -1)
    )
    return (row_scale, flat_rows, gated, inner_inv, normed_out, conv_pull, mixer_pull)


def layer_forward(residual_in, matrices, params, live_mask, doc_ids):
    residual = residual_in.astype(jnp.float32)
    row_scale, flat_rows, gated, inner_inv, normed_out, conv_pull, mixer_pull = layer_parts(
        residual, matrices, params, live_mask, doc_ids
    )
    branch = lax.psum_scatter(
        jnp.dot(normed_out, matrices[2], preferred_element_type=jnp.float32),
        "tensor",
        scatter_dimension=0,
        tiled=True,
    )
    return residual + branch.reshape(residual.shape)


def layer_backward(residual_in, grad_out, matrices, params, live_mask, doc_ids):
    gain_in, conv_x, conv_bc, dt_bias, a_log, d_skip, gain_inner = params
    residual = residual_in.astype(jnp.float32)
    row_scale, flat_rows, gated, inner_inv, normed_out, conv_pull, mixer_pull = layer_parts(
        residual, matrices, params, live_mask, doc_ids
    )
    grad_rows = lax.all_gather(grad_out, "tensor", axis=0, tiled=True)
    length, slot_count, model_width = grad_rows.shape
    grad_flat = grad_rows.reshape(length * slot_count, model_width)
    grad_wout = jnp.dot(normed_out.T, grad_flat, preferred_element_type=jnp.float32)
    grad_normed_out = jnp.dot(grad_flat, matrices[2].T, preferred_element_type=jnp.float32).reshape(
        gated.shape
    )
    grad_gain_inner = jnp.sum(grad_normed_out * gated * inner_inv, (0, 1))
    grad_scaled = grad_normed_out * gain_inner
    row_dot = lax.psum(jnp.sum(grad_scaled * gated, -1), "tensor")[..., None]
    grad_gated = inner_inv * grad_scaled - gated * inner_inv**3 * row_dot / DI
    grad_conv, grad_bc, grad_dt, grad_gate, grad_dt_bias, grad_a_log, grad_d_skip = mixer_pull(
        grad_gated
    )
    grad_x, grad_bcin, grad_conv_x, grad_conv_bc = conv_pull((grad_conv, grad_bc))
    grad_zx = (
        jnp.stack([grad_gate, grad_x], 2).astype(jnp.bfloat16).reshape(length * slot_count, 2, -1)
    )
    head_count = dt_bias.shape[0]
    dt_full = jnp.zeros(
        (length, slot_count, matrices[1].shape[1] - grad_bcin.shape[-1]), jnp.float32
    )
    dt_full = lax.dynamic_update_slice_in_dim(
        dt_full, grad_dt, lax.axis_index("tensor") * head_count, 2
    )
    grad_bcd = jnp.concatenate([grad_bcin, dt_full], -1).reshape(length * slot_count, -1)
    grad_wzx = jnp.einsum("rd,rkc->dkc", flat_rows, grad_zx, preferred_element_type=jnp.float32)
    grad_wbcd = jnp.dot(flat_rows.astype(jnp.float32).T, grad_bcd, precision=PRECISE)
    w_bcd_wide = matrices[1].astype(jnp.float32)
    from_zx = jnp.einsum("rkc,dkc->rd", grad_zx, matrices[0], preferred_element_type=jnp.float32)
    grad_normed = lax.psum_scatter(
        from_zx + jnp.dot(grad_bcd, w_bcd_wide.T, precision=PRECISE),
        "tensor",
        scatter_dimension=0,
        tiled=True,
    ).reshape(residual.shape)
    scaled_in = residual * row_scale
    grad_gain_in = jnp.sum(grad_normed * scaled_in, (0, 1))
    grad_scaled_in = grad_normed * gain_in
    grad_residual = grad_out.astype(jnp.float32) + row_scale * (
        grad_scaled_in - scaled_in * jnp.mean(grad_scaled_in * scaled_in, -1, keepdims=True)
    )
    grad_list = (
        grad_gain_in,
        grad_wzx,
        grad_wbcd,
        grad_conv_x,
        grad_conv_bc,
        grad_dt_bias,
        grad_a_log,
        grad_d_skip,
        grad_gain_inner,
        grad_wout,
    )
    return (grad_residual, grad_list)


def reduce_grads(grad_list):
    big_sums = (
        lax.psum_scatter(grad_list[1], "dp", scatter_dimension=0, tiled=True),
        lax.psum_scatter(grad_list[2], "dp", scatter_dimension=0, tiled=True),
        lax.psum_scatter(grad_list[9], "dp", scatter_dimension=1, tiled=True),
    )
    small_sums = lax.psum(
        (
            grad_list[0],
            grad_list[3],
            grad_list[4],
            grad_list[5],
            grad_list[6],
            grad_list[7],
            grad_list[8],
        ),
        "dp",
    )
    shared = lax.psum((big_sums[1], small_sums[0], small_sums[2]), "tensor")
    return (
        shared[1],
        big_sums[0],
        shared[0],
        small_sums[1],
        shared[2],
        small_sums[3],
        small_sums[4],
        small_sums[5],
        small_sums[6],
        big_sums[2],
    )


def on_device(
    x_in,
    d_out,
    doc_lengths,
    token_mask,
    gain_in,
    w_zx,
    w_bcdt,
    conv_x,
    conv_bc,
    dt_bias,
    a_log,
    d_skip,
    gain_inner,
    w_out,
):
    micro_count = x_in.shape[0]
    length = token_mask.shape[1]
    params = (gain_in[0], conv_x[0], conv_bc[0], dt_bias[0], a_log[0], d_skip[0], gain_inner[0])
    section_no = lax.axis_index("section")
    leading = section_no == 0

    def inputs_of(mb_index):
        picked = jnp.clip(mb_index, 0, micro_count - 1)
        live_mask = lax.dynamic_index_in_dim(token_mask, picked, 0, keepdims=False).astype(
            jnp.float32
        )[..., None]
        lengths = lax.dynamic_index_in_dim(doc_lengths, picked, 0, keepdims=False)
        return (live_mask, doc_index(lengths, length))

    received = jnp.zeros(x_in.shape[1:], jnp.float32)
    kept_inputs = []
    finals = []
    for tick_no in range(micro_count + 1):
        current = jnp.where(
            leading, x_in[min(tick_no, micro_count - 1)], received.astype(jnp.bfloat16)
        )
        kept_inputs.append(current)
        live_mask, doc_ids = inputs_of(tick_no - section_no)
        matrices = gather_weights(w_zx, w_bcdt, w_out)
        produced = layer_forward(current, matrices, params, live_mask, doc_ids)
        outgoing = jnp.where(leading, settle(produced), produced)
        received = from_behind(outgoing, "section", 1)
        if tick_no:
            finals.append(jnp.where(leading, received, produced))
    kept_all = jnp.stack(kept_inputs)
    passed = jnp.zeros(x_in.shape[1:], jnp.float32)
    summed = None
    input_grads = []
    for tick_no in range(micro_count + 1):
        mb_index = tick_no - 1 + section_no
        live_mask, doc_ids = inputs_of(mb_index)
        weight_on = ((mb_index >= 0) & (mb_index < micro_count)).astype(jnp.float32)
        grad_here = jnp.where(
            leading, passed.astype(jnp.bfloat16), d_out[min(tick_no, micro_count - 1)]
        )
        current = lax.dynamic_index_in_dim(
            kept_all, jnp.clip(mb_index, 0, micro_count - 1) + section_no, 0, keepdims=False
        )
        matrices = gather_weights(w_zx, w_bcdt, w_out)
        grad_prev, grad_list = layer_backward(
            current, grad_here, matrices, params, live_mask, doc_ids
        )
        grad_list = tuple((member * weight_on for member in grad_list))
        summed = (
            grad_list
            if summed is None
            else tuple((earlier + later for earlier, later in zip(summed, grad_list)))
        )
        outgoing = jnp.where(leading, grad_prev, settle(grad_prev))
        passed = from_behind(outgoing, "section", 1)
        if tick_no:
            input_grads.append(jnp.where(leading, grad_prev, passed))
    summed = reduce_grads(summed)
    reduced = tuple((member[None] for member in summed))
    grads_whole = jnp.stack(input_grads)
    half_width = grads_whole.shape[-1] // 2
    grads_half = lax.dynamic_slice_in_dim(grads_whole, section_no * half_width, half_width, 3)
    return (jnp.stack(finals), grads_half) + reduced


def solution(mesh):
    return jax.shard_map(
        on_device,
        mesh=mesh,
        in_specs=(
            P(None, "tensor", "dp", None),
            P(None, "tensor", "dp", None),
            P(None, "dp", None),
            P(None, None, "dp"),
            P("section", None),
            P("section", "dp", None, "tensor"),
            P("section", "dp", None),
            P("section", None, "tensor"),
            P("section", None, None),
            P("section", "tensor"),
            P("section", "tensor"),
            P("section", "tensor"),
            P("section", "tensor"),
            P("section", "tensor", "dp"),
        ),
        out_specs=(
            P(None, "tensor", "dp", None),
            P(None, "tensor", "dp", "section"),
            P("section", None),
            P("section", "dp", None, "tensor"),
            P("section", "dp", None),
            P("section", None, "tensor"),
            P("section", None, None),
            P("section", "tensor"),
            P("section", "tensor"),
            P("section", "tensor"),
            P("section", "tensor"),
            P("section", "tensor", "dp"),
        ),
        check_vma=False,
    )
```

profile of v0, /device:TPU:0, one launch (start us, length us, event | category | flops | bytes accessed | tf_op | source)
XLA Modules:
  0.0 2819.7 jit_solution(17086771245902090827)
XLA Ops:
  27.9 23.6 all-gather.1
  56.0 15.2 all-gather.16.cloned.1.call-done
  87.9 74.9 %all-gather.32.cloned.1.call-done = bf16[1,1536,2,768]{1,3,2,0:T(8,128)(2,1)} async-done(((bf16[1,384,2,768]{1,3,2,0:T(8,128)(2,1)}), bf16[1,1536,2,768]{1,3,2,0:T(8,128)(2,1)}) %all-gather.32.cloned.1.call-update) | async-done | bytes 4718608 | tf_op jit(solution)/shard_map/all_gather | solution.py:115
  162.8 10.8 convolution_bitcast_fusion.5
  197.3 16.2 fusion.26
  235.5 10.0 psum.133
  245.5 10.7 fusion.316
  256.5 91.6 %reduce-scatter.10.cloned.1.call-done = f32[384,1536]{1,0:T(8,128)} async-done(((f32[1536,1536]{1,0:T(8,128)}), f32[384,1536]{1,0:T(8,128)}) %reduce-scatter.10.cloned.1.call-update) | async-done | bytes 2359312 | tf_op jit(solution)/shard_map/reduce_scatter | solution.py:159
  362.5 50.6 %all-gather.18.cloned.1.call-done = bf16[1536,1,1536]{2,0,1:T(8,128)(2,1)} async-done(((bf16[384,1,1536]{2,0,1:T(8,128)(2,1)}), bf16[1536,1,1536]{2,0,1:T(8,128)(2,1)}) %all-gather.18.cloned.1.call-update) | async-done | bytes 4718608 | tf_op jit(solution)/shard_map/all_gather | solution.py:125
  449.6 10.8 convolution_bitcast_fusion.4
  485.4 16.2 fusion.19
  532.8 10.7 fusion.319
  543.7 94.9 %reduce-scatter.12.cloned.1.call-done = f32[384,1536]{1,0:T(8,128)} async-done(((f32[1536,1536]{1,0:T(8,128)}), f32[384,1536]{1,0:T(8,128)}) %reduce-scatter.12.cloned.1.call-update) | async-done | bytes 2359312 | tf_op jit(solution)/shard_map/reduce_scatter | solution.py:159
  693.8 23.3 all-gather.28.cloned.1.call-done
  721.0 55.5 %all-gather.24.cloned.1.call-done = bf16[1536,1,1536]{2,0,1:T(8,128)(2,1)} async-done(((bf16[384,1,1536]{2,0,1:T(8,128)(2,1)}), bf16[1536,1,1536]{2,0,1:T(8,128)(2,1)}) %all-gather.24.cloned.1.call-update) | async-done | bytes 4718608 | tf_op jit(solution)/shard_map/all_gather | solution.py:125
  781.8 54.3 %all-gather.22.cloned.1.call-done = bf16[1536,1,1536]{2,0,1:T(8,128)(2,1)} async-done(((bf16[384,1,1536]{2,0,1:T(8,128)(2,1)}), bf16[1536,1,1536]{2,0,1:T(8,128)(2,1)}) %all-gather.22.cloned.1.call-update) | async-done | bytes 4718608 | tf_op jit(solution)/shard_map/all_gather | solution.py:125
  917.3 11.3 convolution_bitcast_fusion.3
  932.8 11.1 convolution_bitcast_fusion
  961.6 11.0 convolution_bitcast_fusion.2
  976.4 13.7 multiply_convert_fusion.8
  996.0 23.8 multiply_convert_fusion.6
  1048.2 17.1 bitcast_add_fusion.5
  1065.4 16.7 bitcast_add_fusion.3
  1142.9 16.1 bitcast_add_fusion.1
  1171.7 18.0 multiply_reduce_fusion.23
  1199.0 13.7 multiply_reduce_fusion.8
  1212.7 15.3 all-reduce.137
  1287.2 19.2 bitcast_add_fusion.4
  1306.5 24.2 fusion.34
  1335.6 15.3 reduce-window.74
  1430.8 10.5 convolution_add_fusion.2
  1441.4 94.3 %reduce-scatter.16.cloned.1.call-done = f32[384,1536]{1,0:T(8,128)} async-done(((f32[1536,1536]{1,0:T(8,128)}), f32[384,1536]{1,0:T(8,128)}) %reduce-scatter.16.cloned.1.call-update) | async-done | bytes 2359312 | tf_op jit(solution)/shard_map/reduce_scatter | solution.py:204
  1553.4 49.7 %all-gather.26.cloned.1.call-done = bf16[1536,1,1536]{2,0,1:T(8,128)(2,1)} async-done(((bf16[384,1,1536]{2,0,1:T(8,128)(2,1)}), bf16[1536,1,1536]{2,0,1:T(8,128)(2,1)}) %all-gather.26.cloned.1.call-update) | async-done | bytes 4718608 | tf_op jit(solution)/shard_map/all_gather | solution.py:174
  1603.1 13.2 multiply_reduce_fusion.7
  1616.3 15.6 all-reduce.136
  1631.9 9.5 fusion.392
  1691.1 19.3 bitcast_add_fusion.2
  1710.3 24.2 fusion.36
  1739.4 15.3 reduce-window.80
  1833.4 10.7 convolution_add_fusion.1
  1844.2 95.0 %reduce-scatter.18.cloned.1.call-done = f32[384,1536]{1,0:T(8,128)} async-done(((f32[1536,1536]{1,0:T(8,128)}), f32[384,1536]{1,0:T(8,128)}) %reduce-scatter.18.cloned.1.call-update) | async-done | bytes 2359312 | tf_op jit(solution)/shard_map/reduce_scatter | solution.py:204
  1985.2 15.9 fusion.12
  2023.8 13.2 multiply_reduce_fusion.6
  2046.3 9.4 fusion.391
  2105.5 19.2 bitcast_add_fusion
  2124.8 24.2 fusion.38
  2153.8 15.3 reduce-window.86
  2204.1 12.4 multiply_reduce_fusion.12
  2255.3 10.3 convolution_add_fusion
  2320.0 40.3 %reduce-scatter.20.cloned.1.call-done = f32[384,1536]{1,0:T(8,128)} async-done(((f32[1536,1536]{1,0:T(8,128)}), f32[384,1536]{1,0:T(8,128)}) %reduce-scatter.20.cloned.1.call-update) | async-done | bytes 2359312 | tf_op jit(solution)/shard_map/reduce_scatter | solution.py:204
  2364.6 22.3 all-reduce.138
  2389.5 16.6 all-reduce.135
  2406.8 10.7 fusion.322
  2417.7 13.3 fusion.172
  2431.0 12.0 fusion.155
  2443.0 17.0 multiply_add_fusion
  2460.3 10.1 fusion.165
  2470.4 9.9 fusion.148
  2480.4 13.2 multiply_add_fusion.1
  2500.2 9.8 reduce-scatter.14.cloned.1.call-done
  2516.4 157.3 %reduce-scatter.22.cloned.1.call-done = f32[384,2,768]{2,0,1:T(8,128)} async-done(((f32[1536,2,768]{2,0,1:T(8,128)}), f32[384,2,768]{2,0,1:T(8,128)}) %reduce-scatter.22.cloned.1.call-update) | async-done | bytes 2359312 | tf_op jit(solution)/shard_map/reduce_scatter | solution.py:233
  2689.2 9.8 copy.991
  2699.0 23.4 all-reduce.141.cloned.1.call-done
  2722.4 88.4 %reduce-scatter.26.cloned.1.call-done = f32[768,384]{1,0:T(8,128)} async-done(((f32[768,1536]{1,0:T(8,128)}), f32[768,384]{1,0:T(8,128)}) %reduce-scatter.26.cloned.1.call-update) | async-done | bytes 1179664 | tf_op jit(solution)/shard_map/reduce_scatter | solution.py:235
  (1622 shorter events, 1036.9 us)
Async XLA Ops:
  7.2 64.0 %all-gather.16.cloned.1.call-start = ((), (), s32[]{:S(2)}) async-start(), calls=%async_computation.9 | async-start | bytes 5898240 | tf_op jit(solution)/shard_map/all_gather | solution.py:125
  9.8 645.1 %copy-start.166 = (f32[1536]{0:T(1024)}, f32[1536]{0:T(1024)S(1)}, u32[]{:S(2)}) copy-start(f32[1536]{0:T(1024)S(1)} %reduce.131) | copy-start | bytes 18436
  11.2 151.5 %all-gather.32.cloned.1.call-start = ((), (), s32[]{:S(2)}) async-start(), calls=%async_computation.27 | async-start | bytes 5898240 | tf_op jit(solution)/shard_map/all_gather | solution.py:115
  14.5 231.0 %all-gather.34.cloned.1.call-start = ((), (), s32[]{:S(2)}) async-start(), calls=%async_computation.28 | async-start | bytes 2949120 | tf_op jit(solution)/shard_map/all_gather | solution.py:117
  15.3 332.9 %reduce-scatter.10.cloned.1.call-start = ((), (), s32[]{:S(2)}) async-start(), calls=%async_computation.10 | async-start | bytes 11796480 | tf_op jit(solution)/shard_map/reduce_scatter | solution.py:159
  19.6 513.1 %copy-start.264 = (f32[768]{0:T(1024)}, f32[768]{0:T(1024)S(1)}, u32[]{:S(2)}) copy-start(f32[768]{0:T(1024)S(1)} %reduce.147) | copy-start | bytes 9220
  19.7 423.5 %copy-start.314 = (f32[1,1,256]{2,0,1:T(1,128)}, f32[1,1,256]{2,0,1:T(1,128)S(1)}, u32[]{:S(2)}) copy-start(f32[1,1,256]{2,0,1:T(1,128)S(1)} %get-tuple-element.489) | copy-start | bytes 3076
  19.7 423.5 %copy-start.319 = (f32[1,1,256]{2,0,1:T(1,128)}, f32[1,1,256]{2,0,1:T(1,128)S(1)}, u32[]{:S(2)}) copy-start(f32[1,1,256]{2,0,1:T(1,128)S(1)} %get-tuple-element.488) | copy-start | bytes 3076
  19.7 423.5 %copy-start.324 = (f32[1,1,256]{2,0,1:T(1,128)}, f32[1,1,256]{2,0,1:T(1,128)S(1)}, u32[]{:S(2)}) copy-start(f32[1,1,256]{2,0,1:T(1,128)S(1)} %get-tuple-element.491) | copy-start | bytes 3076
  19.7 423.5 %copy-start.329 = (f32[1,1,256]{2,0,1:T(1,128)}, f32[1,1,256]{2,0,1:T(1,128)S(1)}, u32[]{:S(2)}) copy-start(f32[1,1,256]{2,0,1:T(1,128)S(1)} %get-tuple-element.490) | copy-start | bytes 3076
  19.7 423.5 %copy-start.345 = (f32[1,1,256]{2,0,1:T(1,128)}, f32[1,1,256]{2,0,1:T(1,128)S(1)}, u32[]{:S(2)}) copy-start(f32[1,1,256]{2,0,1:T(1,128)S(1)} %get-tuple-element.487) | copy-start | bytes 3076
  27.1 489.7 %copy-start.195 = (f32[768]{0:T(1024)}, f32[768]{0:T(1024)S(1)}, u32[]{:S(2)}) copy-start(f32[768]{0:T(1024)S(1)} %mul.5384) | copy-start | bytes 9220
  27.2 433.7 %copy-start.229 = (f32[768]{0:T(1024)}, f32[768]{0:T(1024)S(1)}, u32[]{:S(2)}) copy-start(f32[768]{0:T(1024)S(1)} %get-tuple-element.170) | copy-start | bytes 9220
  27.2 433.7 %copy-start.234 = (f32[768]{0:T(1024)}, f32[768]{0:T(1024)S(1)}, u32[]{:S(2)}) copy-start(f32[768]{0:T(1024)S(1)} %get-tuple-element.171) | copy-start | bytes 9220
  27.2 433.7 %copy-start.239 = (f32[768]{0:T(1024)}, f32[768]{0:T(1024)S(1)}, u32[]{:S(2)}) copy-start(f32[768]{0:T(1024)S(1)} %get-tuple-element.169) | copy-start | bytes 9220
  27.2 433.7 %copy-start.244 = (f32[768]{0:T(1024)}, f32[768]{0:T(1024)S(1)}, u32[]{:S(2)}) copy-start(f32[768]{0:T(1024)S(1)} %get-tuple-element.172) | copy-start | bytes 9220
  27.2 433.7 %copy-start.285 = (f32[768]{0:T(1024)}, f32[768]{0:T(1024)S(1)}, u32[]{:S(2)}) copy-start(f32[768]{0:T(1024)S(1)} %get-tuple-element.168) | copy-start | bytes 9220
  51.5 784.6 %copy-start.63 = (bf16[1,1536,304]{1,2,0:T(8,128)(2,1)}, bf16[1,1536,304]{1,2,0:T(8,128)(2,1)S(1)}, u32[]{:S(2)}) copy-start(bf16[1,1536,304]{1,2,0:T(8,128)(2,1)S(1)} %all-gather.1) | copy-start | bytes 2801668
  256.3 156.8 %all-gather.18.cloned.1.call-start = ((), (), s32[]{:S(2)}) async-start(), calls=%async_computation.11 | async-start | bytes 5898240 | tf_op jit(solution)/shard_map/all_gather | solution.py:125
  351.1 2.9 collective-permute-start
  355.9 282.8 %reduce-scatter.12.cloned.1.call-start = ((), (), s32[]{:S(2)}) async-start(), calls=%async_computation.12 | async-start | bytes 11796480 | tf_op jit(solution)/shard_map/reduce_scatter | solution.py:159
  543.5 173.5 %all-gather.28.cloned.1.call-start = ((), (), s32[]{:S(2)}) async-start(), calls=%async_computation.20 | async-start | bytes 5898240 | tf_op jit(solution)/shard_map/all_gather | solution.py:125
  643.0 4.9 collective-permute-start.1
  659.8 116.8 %all-gather.24.cloned.1.call-start = ((), (), s32[]{:S(2)}) async-start(), calls=%async_computation.17 | async-start | bytes 5898240 | tf_op jit(solution)/shard_map/all_gather | solution.py:125
  660.6 175.5 %all-gather.22.cloned.1.call-start = ((), (), s32[]{:S(2)}) async-start(), calls=%async_computation.15 | async-start | bytes 5898240 | tf_op jit(solution)/shard_map/all_gather | solution.py:125
  661.3 234.2 %all-gather.20.cloned.1.call-start = ((), (), s32[]{:S(2)}) async-start(), calls=%async_computation.13 | async-start | bytes 5898240 | tf_op jit(solution)/shard_map/all_gather | solution.py:125
  661.9 537.1 %all-gather.36.cloned.1.call-start = ((), (), s32[]{:S(2)}) async-start(), calls=%async_computation.29 | async-start | bytes 5898240 | tf_op jit(solution)/shard_map/all_gather | solution.py:174
  663.1 872.6 %reduce-scatter.16.cloned.1.call-start = ((), (), s32[]{:S(2)}) async-start(), calls=%async_computation.16 | async-start | bytes 11796480 | tf_op jit(solution)/shard_map/reduce_scatter | solution.py:204
  691.8 189.7 %copy-start.280 = (f32[6,256]{1,0:T(8,128)}, f32[6,256]{1,0:T(8,128)S(1)}, u32[]{:S(2)}) copy-start(f32[6,256]{1,0:T(8,128)S(1)} %get-tuple-element.442) | copy-start | bytes 18436
  693.8 206.3 %copy-start.255 = (f32[1536]{0:T(1024)}, f32[1536]{0:T(1024)S(1)}, u32[]{:S(2)}) copy-start(f32[1536]{0:T(1024)S(1)} %get-tuple-element.527) | copy-start | bytes 18436
  721.0 119.1 %copy-start.70 = (f32[1536,304]{0,1:T(8,128)}, f32[1536,304]{0,1:T(8,128)S(1)}, u32[]{:S(2)}) copy-start(f32[1536,304]{0,1:T(8,128)S(1)} %fusion.141) | copy-start | bytes 5603332
  781.8 58.3 %copy-start.180 = (f32[1536]{0:T(1024)S(1)}, f32[1536]{0:T(1024)}, u32[]{:S(2)}) copy-start(f32[1536]{0:T(1024)} %get-tuple-element.173) | copy-start | bytes 18436
  781.8 58.3 %copy-start.182 = (f32[1536]{0:T(1024)S(1)}, f32[1536]{0:T(1024)}, u32[]{:S(2)}) copy-start(f32[1536]{0:T(1024)} %get-tuple-element.178) | copy-start | bytes 18436
  781.8 58.3 %copy-start.184 = (f32[1536]{0:T(1024)S(1)}, f32[1536]{0:T(1024)}, u32[]{:S(2)}) copy-start(f32[1536]{0:T(1024)} %get-tuple-element.174) | copy-start | bytes 18436
  781.8 58.4 %copy-start.349 = (f32[1,12]{1,0:T(1,128)S(1)}, f32[1,12]{1,0:T(1,128)}, u32[]{:S(2)}) copy-start(f32[1,12]{1,0:T(1,128)} %param.24) | copy-start | bytes 148
  781.8 58.4 %copy-start.356 = (f32[12]{0:T(128)S(1)}, f32[12]{0:T(128)}, u32[]{:S(2)}) copy-start(f32[12]{0:T(128)} %copy-done.354) | copy-start | bytes 148
  915.0 125.7 %copy-start.86 = (bf16[1536,1,128]{2,0,1:T(8,128)(2,1)}, bf16[1536,1,128]{2,0,1:T(8,128)(2,1)S(1)}, u32[]{:S(2)}) copy-start(bf16[1536,1,128]{2,0,1:T(8,128)(2,1)S(1)} %copy.892) | copy-start | bytes 1179652
  917.2 220.7 %copy-start.84 = (bf16[1536,1,128]{2,0,1:T(8,128)(2,1)}, bf16[1536,1,128]{2,0,1:T(8,128)(2,1)S(1)}, u32[]{:S(2)}) copy-start(bf16[1536,1,128]{2,0,1:T(8,128)(2,1)S(1)} %copy.939) | copy-start | bytes 1179652
  1019.7 151.9 %copy-start.17 = (bf16[1536,1,768]{0,2,1:T(8,128)(2,1)}, bf16[1536,1,768]{0,2,1:T(8,128)(2,1)S(1)}, u32[]{:S(2)}) copy-start(bf16[1536,1,768]{0,2,1:T(8,128)(2,1)S(1)} %get-tuple-element.433) | copy-start | bytes 7077892
  1441.3 94.4 %copy-start.2 = (bf16[3,384,1,1536]{3,1,2,0:T(8,128)(2,1)S(1)}, bf16[3,384,1,1536]{3,1,2,0:T(8,128)(2,1)}, u32[]{:S(2)}) copy-start(bf16[3,384,1,1536]{3,1,2,0:T(8,128)(2,1)} %copy-done.1) | copy-start | bytes 10616836
  1441.3 94.4 %copy-start.167 = (f32[1536]{0:T(1024)S(1)}, f32[1536]{0:T(1024)}, u32[]{:S(2)}) copy-start(f32[1536]{0:T(1024)} %copy-done.166) | copy-start | bytes 18436
  1441.3 161.8 %all-gather.26.cloned.1.call-start = ((), (), s32[]{:S(2)}) async-start(), calls=%async_computation.18 | async-start | bytes 5898240 | tf_op jit(solution)/shard_map/all_gather | solution.py:174
  1541.8 2.9 collective-permute-start.3
  1545.9 393.3 %reduce-scatter.18.cloned.1.call-start = ((), (), s32[]{:S(2)}) async-start(), calls=%async_computation.19 | async-start | bytes 11796480 | tf_op jit(solution)/shard_map/reduce_scatter | solution.py:204
  1546.0 57.2 %copy-start.19 = (bf16[1536,1,768]{0,2,1:T(8,128)(2,1)S(1)}, bf16[1536,1,768]{0,2,1:T(8,128)(2,1)}, u32[]{:S(2)}) copy-start(bf16[1536,1,768]{0,2,1:T(8,128)(2,1)} %get-tuple-element.303) | copy-start | bytes 7077892
  1553.4 88.0 %copy-start.270 = (f32[1536]{0:T(1024)}, f32[1536]{0:T(1024)S(1)}, u32[]{:S(2)}) copy-start(f32[1536]{0:T(1024)S(1)} %rsqrt_reduce_fusion.1) | copy-start | bytes 18436
  1844.1 95.1 %copy-start.3 = (bf16[3,384,1,1536]{3,1,2,0:T(8,128)(2,1)S(1)}, bf16[3,384,1,1536]{3,1,2,0:T(8,128)(2,1)}, u32[]{:S(2)}) copy-start(bf16[3,384,1,1536]{3,1,2,0:T(8,128)(2,1)} %copy-done.1) | copy-start | bytes 10616836
  1844.1 95.1 %copy-start.168 = (f32[1536]{0:T(1024)S(1)}, f32[1536]{0:T(1024)}, u32[]{:S(2)}) copy-start(f32[1536]{0:T(1024)} %copy-done.166) | copy-start | bytes 18436
  1844.1 95.1 %copy-start.343 = (f32[384]{0:T(512)S(1)}, f32[384]{0:T(512)}, u32[]{:S(2)}) copy-start(f32[384]{0:T(512)} %copy-done.342) | copy-start | bytes 4612
  1844.2 179.6 %all-gather.30.cloned.1.call-start = ((), (), s32[]{:S(2)}) async-start(), calls=%async_computation.21 | async-start | bytes 5898240 | tf_op jit(solution)/shard_map/all_gather | solution.py:174
  1944.7 4.6 collective-permute-start.4
  1952.0 408.4 %reduce-scatter.20.cloned.1.call-start = ((), (), s32[]{:S(2)}) async-start(), calls=%async_computation.22 | async-start | bytes 11796480 | tf_op jit(solution)/shard_map/reduce_scatter | solution.py:204
  2265.6 214.7 %reduce-scatter.24.cloned.1.call-start = ((), (), s32[]{:S(2)}) async-start(), calls=%async_computation.24 | async-start | bytes 2334720 | tf_op jit(solution)/shard_map/reduce_scatter | solution.py:234
  2281.0 79.3 %copy-start.4 = (bf16[3,384,1,1536]{3,1,2,0:T(8,128)(2,1)S(1)}, bf16[3,384,1,1536]{3,1,2,0:T(8,128)(2,1)}, u32[]{:S(2)}) copy-start(bf16[3,384,1,1536]{3,1,2,0:T(8,128)(2,1)} %copy-done.1) | copy-start | bytes 10616836
  2281.0 79.3 %copy-start.169 = (f32[1536]{0:T(1024)S(1)}, f32[1536]{0:T(1024)}, u32[]{:S(2)}) copy-start(f32[1536]{0:T(1024)} %copy-done.166) | copy-start | bytes 18436
  2281.0 79.3 %copy-start.341 = (f32[384]{0:T(512)S(1)}, f32[384]{0:T(512)}, u32[]{:S(2)}) copy-start(f32[384]{0:T(512)} %copy-done.340) | copy-start | bytes 4612
  2286.9 120.0 %copy-start.267 = (f32[768]{0:T(1024)S(1)}, f32[768]{0:T(1024)}, u32[]{:S(2)}) copy-start(f32[768]{0:T(1024)} %copy-done.264) | copy-start | bytes 9220
  2286.9 223.2 %reduce-scatter.14.cloned.1.call-start = ((), (), s32[]{:S(2)}) async-start(), calls=%async_computation.14 | async-start | bytes 11796480 | tf_op jit(solution)/shard_map/reduce_scatter | solution.py:159
  2417.6 256.1 %reduce-scatter.22.cloned.1.call-start = ((), (), s32[]{:S(2)}) async-start(), calls=%async_computation.23 | async-start | bytes 11796480 | tf_op jit(solution)/shard_map/reduce_scatter | solution.py:233
  2460.0 262.4 %all-reduce.141.cloned.1.call-start = ((), (), s32[]{:S(2)}) async-start(), calls=%async_computation.25 | async-start | bytes 933888 | tf_op jit(solution)/shard_map/psum | solution.py:249
  2480.4 330.5 %reduce-scatter.26.cloned.1.call-start = ((), (), s32[]{:S(2)}) async-start(), calls=%async_computation.26 | async-start | bytes 5898240 | tf_op jit(solution)/shard_map/reduce_scatter | solution.py:235
  2500.2 178.4 %collective-permute-start.5 = (f32[384,1,1536]{2,0,1:T(8,128)}, f32[384,1,1536]{2,0,1:T(8,128)}, u32[]{:S(2)}, u32[]{:S(2)}) collective-permute-start(f32[384,1,1536]{2,0,1:T(8,128)} %convert_select_fusion), channel_id=1, source_target_pairs={{0,16},{16,0},{1,17},{17,1},{2,18},{18,2},{3,19},{19,3},{4,20},{20... | collective-permute-start | bytes 7077896 | tf_op jit(solution)/shard_map/ppermute | solution.py:19
  2514.3 170.0 %collective-permute-start.2 = (f32[384,1,1536]{2,0,1:T(8,128)}, f32[384,1,1536]{2,0,1:T(8,128)}, u32[]{:S(2)}, u32[]{:S(2)}) collective-permute-start(f32[384,1,1536]{2,0,1:T(8,128)} %convert_select_fusion.2), channel_id=1, source_target_pairs={{0,16},{16,0},{1,17},{17,1},{2,18},{18,2},{3,19},{19,3},{4,20},{20... | collective-permute-start | bytes 7077896 | tf_op jit(solution)/shard_map/ppermute | solution.py:19
  2516.4 162.2 %copy-start.38 = (f32[384,1,1536]{2,0,1:T(8,128)S(1)}, f32[384,1,1536]{2,0,1:T(8,128)}, u32[]{:S(2)}) copy-start(f32[384,1,1536]{2,0,1:T(8,128)} %copy-done.37) | copy-start | bytes 7077892
  (421 other events, 3877.2 us)
Sparse Core Ops, SparseCore 0:
  11.3 59.7 all-gather.15
  73.4 89.3 all-gather.31
  164.4 48.7 all-gather.33
  256.4 91.6 reduce-scatter.9
  356.0 57.0 all-gather.17
  543.6 94.9 reduce-scatter.11
  659.9 57.1 all-gather.27
  719.5 57.0 all-gather.23
  779.0 57.0 all-gather.21
  838.4 57.0 all-gather.19
  897.3 57.0 all-gather.35
  1441.4 94.1 reduce-scatter.15
  1546.0 57.0 all-gather.25
  1844.3 94.8 reduce-scatter.17
  1952.1 57.1 all-gather.29
  2265.7 94.5 reduce-scatter.19
  2362.5 40.9 reduce-scatter.23
  2417.7 92.3 reduce-scatter.13
  2512.4 161.2 reduce-scatter.21
  2676.6 45.7 all-reduce.140
  2725.4 85.3 reduce-scatter.25
where the time goes:
time: 2830 us; the launch traced here: 2820 us
  waiting for transfers between devices  1040 us (37%)
  matrix products  658 us (23%)
  other arithmetic  545 us (19%)
  local copies, waits for them, and re-layouts  386 us (14%)
  blocking collectives  131 us (5%)
  between operations  55.3 us (2%)
    reduce_scatter x3, waiting for transfers between devices, layer_backward(): lax.psum_scatter(from_zx + jnp.dot(grad_bcd, w_bcd_wide.T, precision=PREC...  230 us
    dot_general x12, matrix products, ssd_slot(): within = jnp.einsum('ctsh,cshp->cthp', mixing, in_blocks, precision=PRECISE)  229 us
    all_gather x6, waiting for transfers between devices, layer_parts(): gathered = lax.all_gather(normed, 'tensor', axis=0, tiled=True)  205 us
    reduce_scatter x3, waiting for transfers between devices, layer_forward(): lax.psum_scatter(jnp.dot(normed_out, matrices[2], preferred_element_type=...  196 us
    reduce_scatter x1, waiting for transfers between devices, reduce_grads(): lax.psum_scatter(grad_list[1], 'dp', scatter_dimension=0, tiled=True)  157 us
    unnamed x948, local copies, waits for them, and re-layouts  116 us
    reduce_scatter x1, waiting for transfers between devices, reduce_grads(): lax.psum_scatter(grad_list[9], 'dp', scatter_dimension=1, tiled=True)  88.4 us
    convert_element_type x14, other arithmetic, settle(): values.astype(jnp.bfloat16)  76 us
  transfers between devices with their start and end apart: 27, of which 21 were waited for; matrix products, arithmetic and copies ran while one was open for 25% of the time, Pallas kernels for 0%

commit v1 on v0

v1 whole, which is shorter than its diff:
```python
from functools import partial

import jax
import jax.numpy as jnp
from jax import lax
from jax.experimental import pallas as pl
from jax.experimental.pallas import tpu as pltpu
from jax.sharding import PartitionSpec as P

EPS = 1e-05
F32 = jnp.float32
BF16 = jnp.bfloat16
HEAD = 64
CHUNK = 128
LANES = 128
VMEM_LIMIT = 56 * 1024 * 1024
NN = (((1,), (0,)), ((), ()))
NT = (((1,), (1,)), ((), ()))
TN = (((0,), (0,)), ((), ()))


def mm(left, right, dims=NN):
    return lax.dot_general(left, right, dims, preferred_element_type=F32)


def sigmoid(value):
    return 0.5 * jnp.tanh(0.5 * value) + 0.5


def softplus(value):
    return jnp.maximum(value, 0.0) + jnp.log1p(jnp.exp(-jnp.abs(value)))


def iota(shape, dim):
    return lax.broadcasted_iota(jnp.int32, shape, dim)


def split_two(value):
    high = value.astype(BF16)
    return high, (value - high.astype(F32)).astype(BF16)


def split_three(value):
    high = value.astype(BF16)
    rest = value - high.astype(F32)
    mid = rest.astype(BF16)
    return high, mid, (rest - mid.astype(F32)).astype(BF16)


def fold_rows(value):
    rows = value.shape[0]
    return jnp.sum(value.reshape(rows // 8, 8, value.shape[1]), 0)


def doc_of(places, e0, e1):
    return (places >= e0).astype(jnp.int32) + (places >= e1).astype(jnp.int32)


def same_behind(places, steps, e0, e1):
    crossed = ((places >= e0) & (places < e0 + steps)) | ((places >= e1) & (places < e1 + steps))
    return jnp.where(crossed, 0.0, 1.0)


def same_ahead(places, steps, e0, e1):
    crossed = ((places < e0) & (places >= e0 - steps)) | ((places < e1) & (places >= e1 - steps))
    return jnp.where(crossed, 0.0, 1.0)


def chunk_decays(log_decay, tri):
    high, mid, low = split_three(log_decay)
    cum = mm(jnp.concatenate([tri, tri, tri], 1), jnp.concatenate([high, mid, low], 0))
    return cum, cum.T


def column(values, at):
    return jnp.broadcast_to(values[:, at : at + 1], (values.shape[0], LANES))


def conv_tile(ubuf, cp, tile, rows, masks):
    lanes = slice(tile * LANES, (tile + 1) * LANES)
    summed = cp[4:5, lanes] + cp[3:4, lanes] * ubuf[8 : 8 + rows, lanes]
    for steps in (1, 2, 3):
        shifted = ubuf[8 - steps : 8 - steps + rows, lanes] * masks[steps - 1]
        summed = summed + cp[3 - steps : 4 - steps, lanes] * shifted
    return summed


def fwd_kernel(with_dot, inner, state, sc, *refs):
    pieces = refs[:8]
    refs = refs[8:]
    if with_dot:
        w, cp, hp, chp, live, gno, nrm, proj, y_out, st, gn, gsend, stats, carry, ubuf, act = refs
    else:
        w, cp, hp, chp, live, nrm, proj, y_out, st, gn, gsend, stats, carry, ubuf, act = refs
    step = pl.program_id(0)
    sec, ten, e0, e1 = sc[0], sc[1], sc[2], sc[3]
    rows = nrm.shape[0]
    half = rows // 2
    wide = inner + 2 * state
    tiles = wide // LANES
    pairs = inner // LANES

    @pl.when(step == 0)
    def _():
        carry[...] = jnp.zeros_like(carry)
        ubuf[0:8, :] = jnp.zeros((8, wide), F32)

    rel = jnp.bitwise_xor(ten, step)
    mine = pl.multiple_of(sec * half, half)
    theirs = pl.multiple_of((1 - sec) * half, half)
    for k in range(4):

        @pl.when(rel == k)
        def _(k=k):
            nrm[pl.ds(mine, half), :] = pieces[k][...]
            nrm[pl.ds(theirs, half), :] = pieces[4 + k][...]

    proj[...] = mm(nrm[...], w[...])
    lv = live[...]
    places = rows * step + iota((rows, LANES), 0)
    masks = [same_behind(places, steps, e0, e1) for steps in (1, 2, 3)]
    for tile in range(tiles):
        lanes = slice(tile * LANES, (tile + 1) * LANES)
        at = slice(inner + tile * LANES, inner + (tile + 1) * LANES)
        u = proj[:, at] * lv
        proj[:, at] = u
        ubuf[8 : 8 + rows, lanes] = u
    for tile in range(tiles):
        lanes = slice(tile * LANES, (tile + 1) * LANES)
        pre = conv_tile(ubuf, cp, tile, rows, masks)
        act[:, lanes] = (pre * sigmoid(pre)).astype(BF16)
    ubuf[0:8, :] = ubuf[rows : rows + 8, :]

    low_half = iota((CHUNK, LANES), 1) < HEAD
    tri = (iota((CHUNK, CHUNK), 0) >= iota((CHUNK, CHUNK), 1)).astype(F32).astype(BF16)
    gated_sq = []
    gated_dot = []
    for c in range(rows // CHUNK):
        r0 = c * CHUNK
        at = slice(r0, r0 + CHUNK)
        base = rows * step + r0
        t_at = base + iota((CHUNK, CHUNK), 0)
        s_at = base + iota((CHUNK, CHUNK), 1)
        id_t = doc_of(t_at, e0, e1)
        usable = (t_at >= s_at) & (id_t == doc_of(s_at, e0, e1))
        id_prev = doc_of(base - 1, e0, e1)
        id_end = doc_of(base + CHUNK - 1, e0, e1)
        from_prev = jnp.where(id_t == id_prev, 1.0, 0.0)
        tail_same = jnp.where(id_t == id_end, 1.0, 0.0)
        linked = jnp.where(id_end == id_prev, 1.0, 0.0).astype(F32)
        dt = softplus(proj[at, inner + wide : inner + wide + LANES] + hp[0:1, :]) * live[at, :]
        cum, cum_t = chunk_decays(dt * hp[1:2, :], tri)
        b_in = act[at, inner : inner + state]
        c_in = act[at, inner + state : wide]
        scores = jnp.where(usable, mm(c_in, b_in, NT), 0.0)
        sq = jnp.zeros((CHUNK, LANES), F32)
        rd = jnp.zeros((CHUNK, LANES), F32)
        for k in range(pairs):
            lanes = slice(k * LANES, (k + 1) * LANES)
            mixed, cums = [], []
            for h in (2 * k, 2 * k + 1):
                cum_col = column(cum, h)
                cums.append(cum_col)
                decay = jnp.exp(jnp.minimum(cum_col - cum_t[h : h + 1, :], 0.0))
                mixed.append((decay * scores).astype(BF16))
            cum_e = jnp.where(low_half, cums[0], cums[1])
            dt_e = jnp.where(low_half, column(dt, 2 * k), column(dt, 2 * k + 1))
            x_in = act[at, lanes].astype(F32)
            xdt = x_in * dt_e
            both = jnp.concatenate([jnp.where(low_half, xdt, 0.0), jnp.where(low_half, 0.0, xdt)], 0)
            within = mm(jnp.concatenate(mixed, 1), both.astype(BF16))
            old = carry[:, lanes]
            old_low = old.astype(BF16)
            st[c, :, lanes] = old_low
            across = mm(c_in, old_low) * (jnp.exp(cum_e) * from_prev)
            cum_end = cum_e[CHUNK - 1 : CHUNK, :]
            to_end = jnp.exp(cum_end - cum_e) * tail_same
            added = mm(b_in, (xdt * to_end).astype(BF16), TN)
            carry[:, lanes] = old * (jnp.exp(cum_end) * linked) + added
            y = within + across + chp[0:1, lanes] * x_in
            y_out[at, lanes] = y
            gate = proj[at, lanes]
            gated = y * (gate * sigmoid(gate))
            scaled = gated * chp[1:2, lanes]
            gn[at, lanes] = scaled.astype(BF16)
            sq = sq + gated * gated
            if with_dot:
                rd = rd + scaled * gno[at, lanes]
        gated_sq.append(sq)
        gated_dot.append(rd)
    ones = jnp.ones((8, LANES), F32)
    exact = partial(
        lax.dot_general,
        dimension_numbers=NT,
        precision=lax.Precision.HIGHEST,
        preferred_element_type=F32,
    )
    total = exact(ones, jnp.concatenate(gated_sq, 0))
    if with_dot:
        dots = exact(ones, jnp.concatenate(gated_dot, 0))
        total = jnp.where(iota((8, rows), 0) == 0, total, dots)
    stats[...] = total
    gsend[0] = gn[pl.ds(theirs, half), :]


def run_fwd(scalars, pieces, w, cp, hp, chp, live, gno, inner, state):
    half, width = pieces[0].shape
    rows = 2 * half
    length = live.shape[0]
    steps = length // rows
    cols = w.shape[1]
    chunks = rows // CHUNK
    whole = lambda shape: pl.BlockSpec(shape, lambda i, sc: (0,) * len(shape))
    by_row = lambda n: pl.BlockSpec((rows, n), lambda i, sc: (i, 0))
    in_specs = [whole((half, width))] * 8 + [
        whole(w.shape),
        whole(cp.shape),
        whole(hp.shape),
        whole(chp.shape),
        by_row(LANES),
    ]
    operands = [*pieces, w, cp, hp, chp, live]
    if gno is not None:
        in_specs.append(by_row(inner))
        operands.append(gno)
    flops = 2 * length * width * cols + 2 * length * inner * CHUNK * 6
    return pl.pallas_call(
        partial(fwd_kernel, gno is not None, inner, state),
        out_shape=(
            jax.ShapeDtypeStruct((length, width), BF16),
            jax.ShapeDtypeStruct((length, cols), F32),
            jax.ShapeDtypeStruct((length, inner), F32),
            jax.ShapeDtypeStruct((length // CHUNK, state, inner), BF16),
            jax.ShapeDtypeStruct((length, inner), BF16),
            jax.ShapeDtypeStruct((steps, half, inner), BF16),
            jax.ShapeDtypeStruct((8, length), F32),
        ),
        grid_spec=pltpu.PrefetchScalarGridSpec(
            num_scalar_prefetch=1,
            grid=(steps,),
            in_specs=in_specs,
            out_specs=(
                by_row(width),
                by_row(cols),
                by_row(inner),
                pl.BlockSpec((chunks, state, inner), lambda i, sc: (i, 0, 0)),
                by_row(inner),
                pl.BlockSpec((1, half, inner), lambda i, sc: (i, 0, 0)),
                pl.BlockSpec((8, rows), lambda i, sc: (0, i)),
            ),
            scratch_shapes=[
                pltpu.VMEM((state, inner), F32),
                pltpu.VMEM((rows + 8, inner + 2 * state), F32),
                pltpu.VMEM((rows, inner + 2 * state), BF16),
            ],
        ),
        compiler_params=pltpu.CompilerParams(
            dimension_semantics=("arbitrary",), vmem_limit_bytes=VMEM_LIMIT
        ),
        cost_estimate=pl.CostEstimate(
            flops=2 * flops, transcendentals=length * inner * 8, bytes_accessed=24 * 1024 * 1024
        ),
        name="layer_fwd",
    )(scalars, *operands)


def bwd_kernel(inner, state, total_inner, sc, *refs):
    gno, proj, halo, y_in, st, rc, live, cp, hp, chp = refs[:10]
    gz, gzsend, no_out, gcp, ghp, gch = refs[10:16]
    dstate, ubuf, gbuf, acc_c, acc_h, acc_n, acc_d = refs[16:]
    step = pl.program_id(0)
    steps = pl.num_programs(0)
    block = steps - 1 - step
    sec, e0, e1 = sc[0], sc[2], sc[3]
    rows = y_in.shape[0]
    half = rows // 2
    wide = inner + 2 * state
    tiles = wide // LANES
    pairs = inner // LANES
    theirs = pl.multiple_of((1 - sec) * half, half)

    @pl.when(step == 0)
    def _():
        dstate[...] = jnp.zeros_like(dstate)
        gbuf[rows : rows + 8, :] = jnp.zeros((8, wide), F32)
        acc_c[...] = jnp.zeros_like(acc_c)
        acc_h[...] = jnp.zeros_like(acc_h)
        acc_n[...] = jnp.zeros_like(acc_n)
        acc_d[...] = jnp.zeros_like(acc_d)

    ubuf[0:8, :] = jnp.where(block == 0, 0.0, halo[:, inner : inner + wide])
    ubuf[8 : 8 + rows, :] = proj[:, inner : inner + wide]
    places = rows * block + iota((rows, LANES), 0)
    masks = [same_behind(places, steps_, e0, e1) for steps_ in (1, 2, 3)]

    low_half = iota((CHUNK, LANES), 1) < HEAD
    row_at = iota((CHUNK, CHUNK), 0)
    col_at = iota((CHUNK, CHUNK), 1)
    tri = (row_at >= col_at).astype(F32).astype(BF16)
    tri_rev = (row_at <= col_at).astype(F32).astype(BF16)
    tri_strict = (row_at > col_at).astype(F32).astype(BF16)
    sums = jnp.concatenate([tri_rev, tri_rev, tri_strict, tri_strict], 1)
    to_head = [
        (iota((LANES, LANES), 1) == 2 * k + (iota((LANES, LANES), 0) >= HEAD).astype(jnp.int32))
        .astype(F32)
        .astype(BF16)
        for k in range(pairs)
    ]

    for c in reversed(range(rows // CHUNK)):
        r0 = c * CHUNK
        at = slice(r0, r0 + CHUNK)
        cmasks = [m[at, :] for m in masks]
        acts, slopes = [], []
        for tile in range(tiles):
            lanes = slice(tile * LANES, (tile + 1) * LANES)
            pre = cp[4:5, lanes] + cp[3:4, lanes] * ubuf[8 + r0 : 8 + r0 + CHUNK, lanes]
            for n in (1, 2, 3):
                shifted = ubuf[8 + r0 - n : 8 + r0 - n + CHUNK, lanes] * cmasks[n - 1]
                pre = pre + cp[3 - n : 4 - n, lanes] * shifted
            sig = sigmoid(pre)
            acts.append((pre * sig).astype(BF16))
            slopes.append(sig * (1.0 + pre * (1.0 - sig)))
        b_in, c_in = acts[pairs], acts[pairs + 1]
        base = rows * block + r0
        id_s = doc_of(base + row_at, e0, e1)
        usable = (row_at <= col_at) & (id_s == doc_of(base + col_at, e0, e1))
        id_prev = doc_of(base - 1, e0, e1)
        id_end = doc_of(base + CHUNK - 1, e0, e1)
        from_prev = jnp.where(id_s == id_prev, 1.0, 0.0)
        tail_same = jnp.where(id_s == id_end, 1.0, 0.0)
        linked = jnp.where(id_end == id_prev, 1.0, 0.0).astype(F32)
        lv = live[at, :]
        dt_in = proj[at, inner + wide : inner + wide + LANES] + hp[0:1, :]
        dt = softplus(dt_in) * lv
        log_decay = dt * hp[1:2, :]
        cum, cum_t = chunk_decays(log_decay, tri)
        scores = jnp.where(usable, mm(b_in, c_in, NT), 0.0)
        inv = column(rc[at, :], 0)
        coef = column(rc[at, :], 1)
        d_scores = jnp.zeros((CHUNK, CHUNK), F32)
        gb = jnp.zeros((CHUNK, state), F32)
        gc = jnp.zeros((CHUNK, state), F32)
        r1 = jnp.zeros((CHUNK, LANES), F32)
        r2 = jnp.zeros((CHUNK, LANES), F32)
        r3 = jnp.zeros((CHUNK, LANES), F32)
        kept = jnp.zeros((8, LANES), F32)
        for k in range(pairs):
            lanes = slice(k * LANES, (k + 1) * LANES)
            gate = proj[at, lanes]
            sig = sigmoid(gate)
            silu = gate * sig
            y = y_in[at, lanes]
            gated = y * silu
            g_no = gno[at, lanes]
            gain = chp[1:2, lanes]
            skip = chp[0:1, lanes]
            scaled = gated * inv
            acc_n[:, lanes] += fold_rows(g_no * scaled)
            no_out[at, lanes] = (scaled * gain).astype(BF16)
            gg = inv * (g_no * gain) - gated * coef
            gy = gg * silu
            gz[at, lanes] = (gg * y * (sig * (1.0 + gate * (1.0 - sig)))).astype(BF16)
            x_in = acts[k].astype(F32)
            acc_d[:, lanes] += fold_rows(gy * x_in)
            dt_e = jnp.where(low_half, column(dt, 2 * k), column(dt, 2 * k + 1))
            gy_b = gy.astype(BF16)
            gy_f = gy_b.astype(F32)
            xdt_b = (x_in * dt_e).astype(BF16)
            xdt_f = xdt_b.astype(F32)
            gy_halves = [jnp.where(low_half, gy_f, 0.0).astype(BF16), jnp.where(low_half, 0.0, gy_f).astype(BF16)]
            mixed, cums = [], []
            for n in (0, 1):
                h = 2 * k + n
                cum_col = column(cum, h)
                cums.append(cum_col)
                decay = jnp.exp(jnp.minimum(cum_t[h : h + 1, :] - cum_col, 0.0))
                mixed.append((decay * scores).astype(BF16))
                d_scores = d_scores + decay * mm(xdt_b, gy_halves[n], NT)
            cum_e = jnp.where(low_half, cums[0], cums[1])
            gx_in = mm(jnp.concatenate(mixed, 1), jnp.concatenate(gy_halves, 0))
            cum_end = cum_e[CHUNK - 1 : CHUNK, :]
            to_end = jnp.exp(cum_end - cum_e) * tail_same
            entering = jnp.exp(cum_e) * from_prev
            s_in = st[c, :, lanes]
            d_out = dstate[:, lanes]
            d_out_b = d_out.astype(BF16)
            gx_st = mm(b_in, d_out_b) * to_end
            gb = gb + mm((xdt_f * to_end).astype(BF16), d_out_b, NT)
            gye = (gy * entering).astype(BF16)
            gc = gc + mm(gye, s_in, NT)
            dec = jnp.exp(cum_end) * linked
            prod = fold_rows(s_in.astype(F32) * d_out) * dec
            p_hi, p_lo = split_two(prod)
            kept = kept + mm(p_hi, to_head[k]) + mm(p_lo, to_head[k])
            dstate[:, lanes] = d_out * dec + mm(c_in, gye, TN)
            gx = gx_in + gx_st
            t_hi, t_lo = split_two(gy_f * (y - skip * x_in) - xdt_f * gx_in)
            pair2 = jnp.concatenate([to_head[k], to_head[k]], 0)
            r1 = r1 + mm(jnp.concatenate([t_hi, t_lo], 1), pair2)
            t_hi, t_lo = split_two(x_in * gx)
            r2 = r2 + mm(jnp.concatenate([t_hi, t_lo], 1), pair2)
            t_hi, t_lo = split_two(x_in * gx_st)
            r3 = r3 + mm(jnp.concatenate([t_hi, t_lo], 1), pair2)
            gbuf[at, lanes] = (gx * dt_e + gy * skip) * slopes[k]
        d_scores = jnp.where(usable, d_scores, 0.0).astype(BF16)
        gb = gb + mm(d_scores, c_in)
        gc = gc + mm(d_scores, b_in, TN)
        for n in range(state // LANES):
            b_at = slice(inner + n * LANES, inner + (n + 1) * LANES)
            c_at = slice(inner + state + n * LANES, inner + state + (n + 1) * LANES)
            gbuf[at, b_at] = gb * slopes[pairs]
            gbuf[at, c_at] = gc * slopes[pairs + 1]
        a_hi, a_lo = split_two(r1)
        b_hi, b_lo = split_two(dt * r3)
        g_ld = mm(sums, jnp.concatenate([a_hi, a_lo, b_hi, b_lo], 0)) + jnp.sum(kept, 0, keepdims=True)
        g_dt = (r2 + g_ld * hp[1:2, :]) * (sigmoid(dt_in) * lv)
        acc_h[0:8, :] += fold_rows(g_dt)
        acc_h[8:16, :] += fold_rows(g_ld * log_decay)
        gz[at, inner + wide : inner + wide + LANES] = g_dt.astype(BF16)

    ahead = [same_ahead(places, n, e0, e1) for n in (1, 2, 3)]
    lv = live[...]
    for tile in range(tiles):
        lanes = slice(tile * LANES, (tile + 1) * LANES)
        gp = gbuf[0:rows, lanes]
        gu = cp[3:4, lanes] * gp
        acc_c[24:32, lanes] += fold_rows(gp * ubuf[8 : 8 + rows, lanes])
        acc_c[32:40, lanes] += fold_rows(gp)
        for n in (1, 2, 3):
            gu = gu + cp[3 - n : 4 - n, lanes] * (gbuf[n : n + rows, lanes] * ahead[n - 1])
            shifted = ubuf[8 - n : 8 - n + rows, lanes] * masks[n - 1]
            acc_c[8 * (3 - n) : 8 * (4 - n), lanes] += fold_rows(gp * shifted)
        at = slice(inner + tile * LANES, inner + (tile + 1) * LANES)
        gz[:, at] = (gu * lv).astype(BF16)
    gbuf[rows : rows + 8, :] = gbuf[0:8, :]
    gzsend[0] = gz[pl.ds(theirs, half), :]

    @pl.when(step == steps - 1)
    def _():
        gcp[...] = jnp.zeros_like(gcp)
        ghp[...] = jnp.zeros_like(ghp)
        gch[...] = jnp.zeros_like(gch)
        for n in range(5):
            gcp[n : n + 1, :] = jnp.sum(acc_c[8 * n : 8 * n + 8, :], 0, keepdims=True)
        for n in range(2):
            ghp[n : n + 1, :] = jnp.sum(acc_h[8 * n : 8 * n + 8, :], 0, keepdims=True)
        gch[0:1, :] = jnp.sum(acc_n[...], 0, keepdims=True)
        gch[1:2, :] = jnp.sum(acc_d[...], 0, keepdims=True)


def run_bwd(scalars, gno, proj, y, st, rc, live, cp, hp, chp, inner, state, rows):
    length, cols = proj.shape
    steps = length // rows
    half = rows // 2
    chunks = rows // CHUNK
    wide = inner + 2 * state
    whole = lambda shape: pl.BlockSpec(shape, lambda i, sc: (0,) * len(shape))
    by_row = lambda n: pl.BlockSpec((rows, n), lambda i, sc: (steps - 1 - i, 0))
    flops = 2 * length * inner * CHUNK * 24
    return pl.pallas_call(
        partial(bwd_kernel, inner, state, 0),
        out_shape=(
            jax.ShapeDtypeStruct((length, cols), BF16),
            jax.ShapeDtypeStruct((steps, half, cols), BF16),
            jax.ShapeDtypeStruct((length, inner), BF16),
            jax.ShapeDtypeStruct((8, wide), F32),
            jax.ShapeDtypeStruct((8, LANES), F32),
            jax.ShapeDtypeStruct((8, inner), F32),
        ),
        grid_spec=pltpu.PrefetchScalarGridSpec(
            num_scalar_prefetch=1,
            grid=(steps,),
            in_specs=[
                by_row(inner),
                by_row(cols),
                pl.BlockSpec(
                    (8, cols),
                    lambda i, sc: (jnp.maximum((steps - 1 - i) * (rows // 8) - 1, 0), 0),
                ),
                by_row(inner),
                pl.BlockSpec((chunks, state, inner), lambda i, sc: (steps - 1 - i, 0, 0)),
                by_row(LANES),
                by_row(LANES),
                whole(cp.shape),
                whole(hp.shape),
                whole(chp.shape),
            ],
            out_specs=(
                by_row(cols),
                pl.BlockSpec((1, half, cols), lambda i, sc: (steps - 1 - i, 0, 0)),
                by_row(inner),
                whole((8, wide)),
                whole((8, LANES)),
                whole((8, inner)),
            ),
            scratch_shapes=[
                pltpu.VMEM((state, inner), F32),
                pltpu.VMEM((rows + 8, wide), F32),
                pltpu.VMEM((rows + 8, wide), F32),
                pltpu.VMEM((40, wide), F32),
                pltpu.VMEM((16, LANES), F32),
                pltpu.VMEM((8, inner), F32),
                pltpu.VMEM((8, inner), F32),
            ],
        ),
        compiler_params=pltpu.CompilerParams(
            dimension_semantics=("arbitrary",), vmem_limit_bytes=VMEM_LIMIT
        ),
        cost_estimate=pl.CostEstimate(
            flops=8 * flops, transcendentals=length * inner * 12, bytes_accessed=24 * 1024 * 1024
        ),
        name="layer_bwd",
    )(scalars, gno, proj, proj, y, st, rc, live, cp, hp, chp)


def gn_kernel(with_rc, sc, *refs):
    pieces = refs[:8]
    refs = refs[8:]
    if with_rc:
        rcs, (w, gno, gout, rc) = refs[:8], refs[8:]
    else:
        w, gno, gout = refs
    sec, ten = sc[0], sc[1]
    half = gout.shape[0] // 2
    rel = jnp.bitwise_xor(ten, pl.program_id(0))
    mine = pl.multiple_of(sec * half, half)
    theirs = pl.multiple_of((1 - sec) * half, half)
    for k in range(4):

        @pl.when(rel == k)
        def _(k=k):
            gout[pl.ds(mine, half), :] = pieces[k][...]
            gout[pl.ds(theirs, half), :] = pieces[4 + k][...]
            if with_rc:
                rc[pl.ds(mine, half), :] = rcs[k][...]
                rc[pl.ds(theirs, half), :] = rcs[4 + k][...]

    gno[...] = mm(gout[...], w[...], NT)


def run_gn(scalars, pieces, w, rcs):
    half, width = pieces[0].shape
    inner = w.shape[0]
    rows, length = 2 * half, 8 * half
    whole = lambda shape: pl.BlockSpec(shape, lambda i, sc: (0,) * len(shape))
    by_row = lambda n: pl.BlockSpec((rows, n), lambda i, sc: (i, 0))
    in_specs = [whole((half, width))] * 8
    operands = list(pieces)
    outs = [
        jax.ShapeDtypeStruct((length, inner), F32),
        jax.ShapeDtypeStruct((length, width), BF16),
    ]
    out_specs = [by_row(inner), by_row(width)]
    if rcs is not None:
        in_specs += [whole((half, LANES))] * 8
        operands += list(rcs)
        outs.append(jax.ShapeDtypeStruct((length, LANES), F32))
        out_specs.append(by_row(LANES))
    return pl.pallas_call(
        partial(gn_kernel, rcs is not None),
        out_shape=tuple(outs),
        grid_spec=pltpu.PrefetchScalarGridSpec(
            num_scalar_prefetch=1,
            grid=(length // rows,),
            in_specs=in_specs + [whole(w.shape)],
            out_specs=tuple(out_specs),
        ),
        compiler_params=pltpu.CompilerParams(
            dimension_semantics=("arbitrary",), vmem_limit_bytes=VMEM_LIMIT
        ),
        cost_estimate=pl.CostEstimate(
            flops=2 * length * width * inner, transcendentals=0, bytes_accessed=13 * 1024 * 1024
        ),
        name="grad_rows",
    )(scalars, *operands, w)


def half_kernel(dims, sc, kept, got, wa, wb, *outs):
    total = mm(kept[...], wa[...], dims) + mm(got[0], wb[...], dims)
    for k in range(4):

        @pl.when(pl.program_id(0) == k)
        def _(k=k):
            outs[k][...] = total.astype(BF16)


def run_half(scalars, full, got, wa, wb, dims):
    groups, half, depth = got.shape
    width = wa.shape[1] if dims == NN else wa.shape[0]
    whole = lambda shape: pl.BlockSpec(shape, lambda i, sc: (0,) * len(shape))
    return pl.pallas_call(
        partial(half_kernel, dims),
        out_shape=(jax.ShapeDtypeStruct((half, width), BF16),) * 4,
        grid_spec=pltpu.PrefetchScalarGridSpec(
            num_scalar_prefetch=1,
            grid=(groups,),
            in_specs=[
                pl.BlockSpec(
                    (half, depth), lambda i, sc: (2 * jnp.bitwise_xor(sc[1], i) + sc[0], 0)
                ),
                pl.BlockSpec((1, half, depth), lambda i, sc: (jnp.bitwise_xor(sc[1], i), 0, 0)),
                whole(wa.shape),
                whole(wb.shape),
            ],
            out_specs=(whole((half, width)),) * 4,
        ),
        compiler_params=pltpu.CompilerParams(
            dimension_semantics=("arbitrary",), vmem_limit_bytes=VMEM_LIMIT
        ),
        cost_estimate=pl.CostEstimate(
            flops=4 * groups * half * depth * width, transcendentals=0, bytes_accessed=8 * 1024 * 1024
        ),
        name="half_rows",
    )(scalars, full, got, wa, wb)


def norm_kernel(x, gain, out):
    v = x[...].astype(F32)
    inv = lax.rsqrt(jnp.mean(v * v, -1, keepdims=True) + EPS)
    out[...] = (v * inv * gain[0:1, :]).astype(BF16)


def owner_kernel(final, u0, u1, u2, u3, x, rcol, gain, *outs):
    total = (u0[...].astype(F32) + u1[...].astype(F32)) + (u2[...].astype(F32) + u3[...].astype(F32))
    out = x[...].astype(F32) + rcol[:, 0:1] * total
    if final:
        outs[0][...] = out
        return
    h1, normed, kept = outs
    low = out.astype(BF16)
    h1[...] = low
    kept[...] = total
    v = low.astype(F32)
    inv = lax.rsqrt(jnp.mean(v * v, -1, keepdims=True) + EPS)
    normed[...] = (v * inv * gain[0:1, :]).astype(BF16)


def owner_back_kernel(last, inner_width, g0, g1, g2, g3, v_in, g_in, gain, *refs):
    g = (g0[...].astype(F32) + g1[...].astype(F32)) + (g2[...].astype(F32) + g3[...].astype(F32))
    v = v_in[...].astype(F32)
    inv = lax.rsqrt(jnp.mean(v * v, -1, keepdims=True) + EPS)
    scaled = v * inv
    p = g * gain[0:1, :]
    out = g_in[...].astype(F32) + inv * (p - scaled * jnp.mean(p * scaled, -1, keepdims=True))
    if last:
        g_v, ggain = refs
        g_v[...] = out
    else:
        kept, rcol, g_v, rc, ggain = refs
        low = out.astype(BF16)
        g_v[...] = low
        r = rcol[:, 0:1]
        dot = jnp.sum(low.astype(F32) * kept[...], -1, keepdims=True)
        coef = r * r * r * dot / inner_width
        lane = iota(rc.shape, 1)
        rc[...] = jnp.where(lane == 0, r, coef)
    ggain[...] = fold_rows(g * scaled)


def run_plain(kernel, name, out_shape, *operands):
    return pl.pallas_call(
        kernel,
        out_shape=out_shape,
        compiler_params=pltpu.CompilerParams(vmem_limit_bytes=VMEM_LIMIT),
        cost_estimate=pl.CostEstimate(
            flops=8 * 1024 * 1024, transcendentals=0, bytes_accessed=4 * 1024 * 1024
        ),
        name=name,
    )(*operands)


def across(value, step):
    count = lax.axis_size("tensor")
    return lax.ppermute(value, "tensor", [(i, i ^ step) for i in range(count)])


def swap(value):
    return lax.ppermute(value, "section", [(0, 1), (1, 0)])


def give(value, layer):
    return lax.ppermute(value, "section", [(1 - layer, layer)])


def spread(value):
    same = [value] + [across(value, k) for k in (1, 2, 3)]
    return same + [swap(piece) for piece in same]


def all_tensor(value):
    return value + across(value, 1) + across(value, 2) + across(value, 3)


def gather_dp(value, axis):
    count = lax.axis_size("dp")
    if count != 4:
        return lax.all_gather(value, "dp", axis=axis, tiled=True)
    up, down = [value], [value]
    for _ in range(3):
        up.append(lax.ppermute(up[-1], "dp", [(i, i + 1) for i in range(3)]))
        down.append(lax.ppermute(down[-1], "dp", [(i + 1, i) for i in range(3)]))
    at = lax.axis_index("dp")
    shards = []
    for j in range(4):
        shards.append(lax.select_n(at, *[up[i - j] if j <= i else down[j - i] for i in range(4)]))
    return jnp.concatenate(shards, axis)


def scatter_dp(value, axis):
    count = lax.axis_size("dp")
    if count != 4:
        return lax.psum_scatter(value, "dp", scatter_dimension=axis, tiled=True)
    at = lax.axis_index("dp")
    size = value.shape[axis] // 4
    total = lax.dynamic_slice_in_dim(value, at * size, size, axis)
    low = value.astype(BF16)
    for k in (1, 2, 3):
        part = lax.dynamic_slice_in_dim(low, ((at + k) % 4) * size, size, axis)
        got = lax.ppermute(part, "dp", [(i, (i + k) % 4) for i in range(4)])
        total = total + got.astype(F32)
    return total


def sum_dp(value):
    if lax.axis_size("dp") != 4:
        return lax.psum(value, "dp")
    total = value
    for k in (1, 2, 3):
        total = total + lax.ppermute(value, "dp", [(i, (i + k) % 4) for i in range(4)])
    return total


def on_device(
    x_in,
    d_out,
    doc_lengths,
    token_mask,
    gain_in,
    w_zx,
    w_bcdt,
    conv_x,
    conv_bc,
    dt_bias,
    a_log,
    d_skip,
    gain_inner,
    w_out,
):
    micro_count, local_rows, _, width = x_in.shape
    length = token_mask.shape[1]
    half = local_rows // 2
    inner = conv_x.shape[2] // 2
    heads = dt_bias.shape[1] // 2
    state = conv_bc.shape[2] // 2
    chip_inner = 2 * inner
    full_inner = chip_inner * lax.axis_size("tensor")
    full_heads = w_bcdt.shape[2] - 2 * state
    sec = lax.axis_index("section")
    ten = lax.axis_index("tensor")
    first = sec == 0
    micros = range(micro_count)

    def by_layer(own, other):
        return [jnp.where(first, own, other), jnp.where(first, other, own)]

    pad_to = lambda v, n: jnp.pad(v, ((0, 0), (0, n - v.shape[1])))
    pack = jnp.concatenate(
        [
            gain_in,
            pad_to(jnp.concatenate([conv_x[0], conv_bc[0]], 1), width),
            pad_to(gain_inner, width),
            pad_to(jnp.concatenate([dt_bias, a_log, d_skip], 1), width),
        ],
        0,
    )
    packs = by_layer(pack, swap(pack))

    zx = w_zx[0].reshape(w_zx.shape[1], 2, 2, inner)
    zx_own = lax.dynamic_index_in_dim(zx, sec, 2, keepdims=False).reshape(-1, 2 * inner)
    zx_send = lax.dynamic_index_in_dim(zx, 1 - sec, 2, keepdims=False).reshape(-1, 2 * inner)
    zx_shards = by_layer(zx_own, swap(zx_send))
    wo = w_out[0].reshape(2, inner, w_out.shape[2])
    wo_own = lax.dynamic_index_in_dim(wo, sec, 0, keepdims=False)
    wo_send = lax.dynamic_index_in_dim(wo, 1 - sec, 0, keepdims=False)
    wo_shards = by_layer(wo_own, swap(wo_send))
    zx_full, wo_full = [None, None], [None, None]
    zx_full[0] = gather_dp(zx_shards[0], 0)
    bcdt = gather_dp(w_bcdt[0], 0)
    bcdts = by_layer(bcdt, swap(bcdt))
    wo_full[0] = gather_dp(wo_shards[0], 1)
    zx_full[1] = gather_dp(zx_shards[1], 0)
    wo_full[1] = gather_dp(wo_shards[1], 1)

    def head_pick(core):
        row = lax.broadcasted_iota(jnp.int32, (full_heads, LANES), 0)
        col = lax.broadcasted_iota(jnp.int32, (full_heads, LANES), 1)
        return ((row == ten * 2 * heads + core * heads + col) & (col < heads)).astype(F32)

    layers = []
    for layer in range(2):
        bc = bcdts[layer][:, : 2 * state]
        dts = bcdts[layer][:, 2 * state :]
        pick = lambda core: jnp.dot(dts, head_pick(core).astype(BF16), preferred_element_type=BF16)
        w = jnp.concatenate([zx_full[layer], bc, pick(sec)], 1)
        w_other = jnp.concatenate([swap(zx_full[layer]), bc, pick(1 - sec)], 1)
        p = packs[layer]
        lane = lambda row, start, count: lax.dynamic_slice(p, (row, start), (1, count))
        taps = jnp.concatenate(
            [lax.dynamic_slice(p, (1, sec * inner), (5, inner)), p[1:6, chip_inner : chip_inner + 2 * state]], 1
        )
        cp = jnp.pad(taps, ((0, 3), (0, 0)))
        bias = pad_to(lane(7, sec * heads, heads), LANES)
        rate = pad_to(-jnp.exp(lane(7, 2 * heads + sec * heads, heads)), LANES)
        hp = jnp.concatenate([bias, rate, jnp.zeros((6, LANES), F32)], 0)
        skip = jnp.broadcast_to(
            lane(7, 4 * heads + sec * heads, heads).reshape(heads, 1), (heads, HEAD)
        ).reshape(1, inner)
        chp = jnp.concatenate([skip, lane(6, sec * inner, inner), jnp.zeros((6, inner), F32)], 0)
        gain = jnp.broadcast_to(p[0:1], (8, width))
        layers.append(
            dict(w=w, w_other=w_other, wo=wo_full[layer], wo_other=swap(wo_full[layer]), cp=cp, hp=hp, chp=chp, gain=gain)
        )

    rows_at = lambda v, m: lax.dynamic_slice_in_dim(v[m, :, 0, :], sec * half, half, 0)
    lane0 = lax.broadcasted_iota(jnp.int32, (1, LANES), 1) == 0
    wide = lambda kind, n=1: jax.ShapeDtypeStruct((n * half, width), kind)
    small = jax.ShapeDtypeStruct((8, width), F32)

    scalars, lives, xs, gs = [], [], [], []
    for m in micros:
        e0 = doc_lengths[m, 0, 0]
        e1 = e0 + doc_lengths[m, 0, 1]
        scalars.append(jnp.stack([sec, ten, e0, e1]).astype(jnp.int32))
        lives.append(jnp.broadcast_to(token_mask[m].astype(F32), (length, LANES)))
        xs.append(rows_at(x_in, m))
        gs.append(rows_at(d_out, m))

    def forward(layer, m, pieces, gno):
        k = layers[layer]
        nrm, proj, y, st, gn, gsend, stats = run_fwd(
            scalars[m], pieces, k["w"], k["cp"], k["hp"], k["chp"], lives[m], gno, inner, state
        )
        got = swap(gsend)
        part = stats + swap(stats)
        totals = all_tensor(part)
        inv = lax.rsqrt(totals[0] / full_inner + EPS)
        rcol = jnp.broadcast_to(
            lax.dynamic_slice_in_dim(inv, ten * 2 * half + sec * half, half)[:, None], (half, LANES)
        )
        outs = run_half(scalars[m], gn, got, k["wo"], k["wo_other"], NN)
        parts = [outs[0]] + [across(outs[n], n) for n in (1, 2, 3)]
        return dict(nrm=nrm, proj=proj, y=y, st=st, totals=totals, inv=inv, rcol=rcol, parts=parts)

    def backward(layer, m, gno, rc, kept):
        k = layers[layer]
        gz, gzsend, no, gcp, ghp, gch = run_bwd(
            scalars[m], gno, kept["proj"], kept["y"], kept["st"], rc, lives[m],
            k["cp"], k["hp"], k["chp"], inner, state, 2 * half,
        )
        outs = run_half(scalars[m], gz, swap(gzsend), k["w"], k["w_other"], NT)
        parts = [outs[0]] + [across(outs[n], n) for n in (1, 2, 3)]
        return parts, gz, no, (gcp, ghp, gch)

    normed0 = [
        run_plain(norm_kernel, "norm_rows", wide(BF16), xs[m], layers[0]["gain"]) for m in micros
    ]
    pieces0 = [spread(v) for v in normed0]
    kept0 = [forward(0, m, pieces0[m], None) for m in micros]
    grad_pieces1 = [spread(g) for g in gs]
    h1, pieces1, u0 = [], [], []
    for m in micros:
        h, normed, total = run_plain(
            partial(owner_kernel, False), "owner_mid", (wide(BF16), wide(BF16), wide(F32)),
            *kept0[m]["parts"], xs[m], kept0[m]["rcol"], layers[1]["gain"],
        )
        h1.append(h)
        u0.append(total)
        pieces1.append(spread(normed))
    rows1 = [run_gn(scalars[m], grad_pieces1[m], layers[1]["wo"], None) for m in micros]
    kept1 = [forward(1, m, pieces1[m], rows1[m][0]) for m in micros]

    weight_grads = [[], []]
    small_grads = [[], []]

    def weigh(layer, m, kept, gz, no, gout):
        weight_grads[layer].append(
            (mm(kept["nrm"], gz, TN), mm(no, gout, TN))
        )

    grad_rows, rcs0, gain_grads = [], [], [[], []]
    for m in micros:
        kept = kept1[m]
        coef = kept["inv"] ** 3 * kept["totals"][1] / full_inner
        rc = jnp.where(lane0, kept["inv"][:, None], coef[:, None])
        parts, gz, no, tiny = backward(1, m, rows1[m][0], rc, kept)
        g_h1, rc0, ggain = run_plain(
            partial(owner_back_kernel, False, full_inner), "owner_back",
            (wide(BF16), jax.ShapeDtypeStruct((half, LANES), F32), small),
            *parts, h1[m], gs[m], layers[1]["gain"], u0[m], kept0[m]["rcol"],
        )
        grad_rows.append(g_h1)
        rcs0.append(rc0)
        gain_grads[1].append(ggain)
        small_grads[1].append(tiny)
        weigh(1, m, kept, gz, no, rows1[m][1])
    rows0 = [
        run_gn(scalars[m], spread(grad_rows[m]), layers[0]["wo"], spread(rcs0[m])) for m in micros
    ]
    grads_in = []
    for m in micros:
        parts, gz, no, tiny = backward(0, m, rows0[m][0], rows0[m][2], kept0[m])
        g_v, ggain = run_plain(
            partial(owner_back_kernel, True, full_inner), "owner_last", (wide(F32), small),
            *parts, xs[m], grad_rows[m], layers[0]["gain"],
        )
        grads_in.append(g_v)
        gain_grads[0].append(ggain)
        small_grads[0].append(tiny)
        weigh(0, m, kept0[m], gz, no, rows0[m][1])

    finals = []
    for m in micros:
        out = run_plain(
            partial(owner_kernel, True), "owner_out", wide(F32),
            *kept1[m]["parts"], h1[m], kept1[m]["rcol"], layers[1]["gain"],
        )
        finals.append(jnp.concatenate(by_layer(out, swap(out)), 0))
    out_act = jnp.stack(finals)[:, :, None, :]

    halves = []
    for m in micros:
        cols = grads_in[m].reshape(half, 2, width // 2)
        mine = lax.dynamic_index_in_dim(cols, sec, 1, keepdims=False)
        theirs = lax.dynamic_index_in_dim(cols, 1 - sec, 1, keepdims=False)
        halves.append(jnp.concatenate(by_layer(mine, swap(theirs)), 0))
    grad_in = jnp.stack(halves)[:, :, None, :]

    zx_parts, wo_parts, bcdt_parts, packs_out = [], [], [], []
    for layer in range(2):
        g_w = weight_grads[layer][0][0] + weight_grads[layer][1][0]
        g_wo = weight_grads[layer][0][1] + weight_grads[layer][1][1]
        zx_parts.append(scatter_dp(g_w[:, : 2 * inner], 0))
        wo_parts.append(scatter_dp(g_wo, 1))
        g_dt = lax.dot_general(
            g_w[:, 2 * inner + 2 * state :], head_pick(sec), NT,
            precision=lax.Precision.HIGHEST, preferred_element_type=F32,
        )
        bcdt_parts.append(jnp.concatenate([g_w[:, 2 * inner : 2 * inner + 2 * state], g_dt], 1))
        gcp, ghp, gch = (a + b for a, b in zip(*small_grads[layer]))
        ggain = jnp.sum(gain_grads[layer][0] + gain_grads[layer][1], 0, keepdims=True)
        g_skip = jnp.sum(gch[1].reshape(heads, HEAD), -1)
        packed = jnp.concatenate([ggain, jnp.zeros((7, width), F32)], 0)
        put = lax.dynamic_update_slice
        packed = put(packed, gcp[:5, :inner], (1, sec * inner))
        packed = put(packed, gcp[:5, inner:], (1, chip_inner))
        packed = put(packed, gch[0:1], (6, sec * inner))
        packed = put(packed, ghp[0:1, :heads], (7, sec * heads))
        packed = put(packed, ghp[1:2, :heads], (7, 2 * heads + sec * heads))
        packed = put(packed, g_skip[None], (7, 4 * heads + sec * heads))
        packs_out.append(packed)

    def own_halves(parts):
        got = [give(parts[layer], layer) for layer in range(2)]
        return jnp.where(first, parts[0], got[1]), jnp.where(first, got[0], parts[1])

    lead, trail = own_halves(zx_parts)
    grad_w_zx = jnp.stack([lead.reshape(-1, 2, inner), trail.reshape(-1, 2, inner)], 2)
    grad_w_zx = grad_w_zx.reshape(1, -1, 2, chip_inner)
    grad_w_out = jnp.concatenate(own_halves(wo_parts), 0)[None]

    got = [give(bcdt_parts[layer].astype(BF16), layer).astype(F32) for layer in range(2)]
    summed = jnp.where(first, bcdt_parts[0] + got[0], bcdt_parts[1] + got[1])
    shard = scatter_dp(summed, 0)
    low = shard.astype(BF16)
    for k in (1, 2, 3):
        shard = shard + across(low, k).astype(F32)
    grad_w_bcdt = shard[None]

    got = [give(packs_out[layer], layer) for layer in range(2)]
    mine = sum_dp(jnp.where(first, packs_out[0] + got[0], packs_out[1] + got[1]))
    shared = all_tensor(mine)
    grad_conv_x = mine[None, 1:6, :chip_inner]
    grad_conv_bc = shared[None, 1:6, chip_inner : chip_inner + 2 * state]
    head_rows = mine[7:8, : 6 * heads].reshape(3, 1, 2 * heads)
    return (
        out_act,
        grad_in,
        shared[0:1],
        grad_w_zx,
        grad_w_bcdt,
        grad_conv_x,
        grad_conv_bc,
        head_rows[0],
        head_rows[1],
        head_rows[2],
        mine[6:7, :chip_inner],
        grad_w_out,
    )


def solution(mesh):
    return jax.shard_map(
        on_device,
        mesh=mesh,
        in_specs=(
            P(None, "tensor", "dp", None),
            P(None, "tensor", "dp", None),
            P(None, "dp", None),
            P(None, None, "dp"),
            P("section", None),
            P("section", "dp", None, "tensor"),
            P("section", "dp", None),
            P("section", None, "tensor"),
            P("section", None, None),
            P("section", "tensor"),
            P("section", "tensor"),
            P("section", "tensor"),
            P("section", "tensor"),
            P("section", "tensor", "dp"),
        ),
        out_specs=(
            P(None, "tensor", "dp", None),
            P(None, "tensor", "dp", "section"),
            P("section", None),
            P("section", "dp", None, "tensor"),
            P("section", "dp", None),
            P("section", None, "tensor"),
            P("section", None, None),
            P("section", "tensor"),
            P("section", "tensor"),
            P("section", "tensor"),
            P("section", "tensor"),
            P("section", "tensor", "dp"),
        ),
        check_vma=False,
    )
```

time: 2830 us -> 1230 us (0.43)
  waiting for transfers between devices: 1040 us -> 324 us
  matrix products: 658 us -> 52.4 us
  other arithmetic: 545 us -> 86.8 us
  Pallas kernels: 0 us -> 365 us
  local copies, waits for them, and re-layouts: 386 us -> 118 us
  starting transfers between devices: 1.63 us -> 266 us
  blocking collectives: 131 us -> 0 us
  between operations: 55.3 us -> 6.49 us
    reduce_scatter x9 -> x0, waiting for transfers between devices: 672 us -> none  [the longest x3 230 us: layer_backward(): lax.psum_scatter(from_zx + jnp.dot(grad_bcd, w_bcd_wide.T, precision=PREC...]
    dot_general x81 -> x14, matrix products: 658 us -> 52.4 us  [the longest x8 49.4 us: mm(): return lax.dot_general(left, right, dims, preferred_element_type=F32)]
    pallas_call x0 -> x30, Pallas kernels: none -> 365 us  [the longest x4 107 us: run_bwd(): pl.pallas_call(partial(bwd_kernel, inner, state, 0), out_shape=(jax.Shape...]
    all_gather x11 -> x0, waiting for transfers between devices: 330 us -> none  [the longest x6 205 us: layer_parts(): gathered = lax.all_gather(normed, 'tensor', axis=0, tiled=True)]
    ppermute x6 -> x192, waiting for transfers between devices: 15.1 us -> 324 us  [the longest x72 230 us: across(): return lax.ppermute(value, 'tensor', [(i, i ^ step) for i in range(count)])]
    ppermute x6 -> x192, starting transfers between devices: 0.22 us -> 266 us  [the longest x72 103 us: across(): return lax.ppermute(value, 'tensor', [(i, i ^ step) for i in range(count)])]
    reduce_sum x52 -> x4, other arithmetic: 196 us -> 2.39 us  [the longest x2 1.64 us: on_device(): jnp.sum(gain_grads[layer][0] + gain_grads[layer][1], 0, keepdims=True)]
    psum x8 -> x0, blocking collectives: 107 us -> none  [the longest x4 44.8 us: inner_scale(): summed = lax.psum(jnp.sum(gated * gated, -1), 'tensor')]
  transfers between devices with their start and end apart: 27 -> 192, of which waited for: 21 -> 55; matrix products, arithmetic and copies ran while one was open for 25% -> 19% of each run, Pallas kernels for 0% -> 30%
where the time goes in v1:
time: 1230 us; the launch traced here: 1220 us
  Pallas kernels  365 us (30%)
  waiting for transfers between devices  324 us (26%)
  starting transfers between devices  266 us (22%)
  local copies, waits for them, and re-layouts  118 us (10%)
  other arithmetic  86.8 us (7%)
  matrix products  52.4 us (4%)
    ppermute x72, waiting for transfers between devices, across(): return lax.ppermute(value, 'tensor', [(i, i ^ step) for i in range(count)])  230 us
    pallas_call x4, Pallas kernels, run_bwd(): pl.pallas_call(partial(bwd_kernel, inner, state, 0), out_shape=(jax.Shape...  107 us
    ppermute x72, starting transfers between devices, across(): return lax.ppermute(value, 'tensor', [(i, i ^ step) for i in range(count)])  103 us
    pallas_call x4, Pallas kernels, run_fwd(): pl.pallas_call(partial(fwd_kernel, gno is not None, inner, state), out_sh...  95.2 us
    pallas_call x8, Pallas kernels, run_half(): pl.pallas_call(partial(half_kernel, dims), out_shape=(jax.ShapeDtypeStruc...  94.2 us
    ppermute x15, starting transfers between devices, gather_dp(): up.append(lax.ppermute(up[-1], 'dp', [(i, i + 1) for i in range(3)]))  73.8 us
    ppermute x15, waiting for transfers between devices, scatter_dp(): got = lax.ppermute(part, 'dp', [(i, (i + k) % 4) for i in range(4)])  68.2 us
    dot_general x8, matrix products, mm(): return lax.dot_general(left, right, dims, preferred_element_type=F32)  49.4 us
  transfers between devices with their start and end apart: 192, of which 55 were waited for; matrix products, arithmetic and copies ran while one was open for 19% of the time, Pallas kernels for 30%

profile of v1, /device:TPU:0, one launch (start us, length us, event | category | flops | bytes accessed | tf_op | source)
XLA Modules:
  0.0 1218.6 jit_solution(7382141128431019655)
XLA Ops:
  2.5 5.6 collective-permute-start.15
  16.8 8.9 dynamic-slice_reduce_fusion
  43.7 5.4 collective-permute-start.16
  51.6 4.6 collective-permute-start.24
  72.3 15.5 %collective-permute-done.97.refs_2_ = bf16[192,1536]{1,0:T(8,128)(2,1)S(1)} collective-permute-done((bf16[192,1536]{1,0:T(8,128)(2,1)S(1)}, bf16[192,1536]{1,0:T(8,128)(2,1)S(1)}, u32[]{:S(2)}, u32[]{:S(2)}) %collective-permute-start.97) | collective-permute-done | bytes 589856 | tf_op jit(solution)/shard_map/ppermute | solution.py:675
  98.2 5.8 collective-permute-start.10
  119.5 5.0 collective-permute-start.25
  126.3 5.4 collective-permute-start.11
  136.1 5.5 collective-permute-start.45
  168.1 5.2 collective-permute-start.46
  207.3 5.4 collective-permute-done.1.refs_1_
  218.9 6.7 collective-permute-done.2.refs_2_
  228.6 11.8 fusion.3
  244.1 23.0 %layer_fwd.6 = (bf16[1536,1536]{1,0:T(8,128)(2,1)}, f32[1536,1152]{1,0:T(8,128)}, f32[1536,384]{1,0:T(8,128)}, bf16[12,128,384]{2,1,0:T(8,128)(2,1)}, bf16[1536,...) custom-call(s32[4]{0:T(128)} %pad_add_fusion.2.sc, bf16[192,1536]{1,0:T(8,128)(2,1)} %norm_rows.3.refs_0_, ...), custom_call_target="tpu_custom_call" | custom-call | flops 12683575296 | bytes 25165824 | tf_op jit(solution)/shard_map/layer_fwd/pallas_call | solution.py:227
  268.0 5.2 collective-permute-start.60
  276.5 23.1 %layer_fwd.4 = (bf16[1536,1536]{1,0:T(8,128)(2,1)}, f32[1536,1152]{1,0:T(8,128)}, f32[1536,384]{1,0:T(8,128)}, bf16[12,128,384]{2,1,0:T(8,128)(2,1)}, bf16[1536,...) custom-call(s32[4]{0:T(128)} %pad_add_fusion.sc, bf16[192,1536]{1,0:T(8,128)(2,1)} %norm_rows.2.refs_0_, ...), custom_call_target="tpu_custom_call" | custom-call | flops 12683575296 | bytes 25165824 | tf_op jit(solution)/shard_map/layer_fwd/pallas_call | solution.py:227
  300.4 7.6 half_rows.10
  314.7 9.7 collective-permute-done.88
  341.2 7.6 half_rows.8
  357.9 8.4 collective-permute-done.84.u3
  366.3 11.7 collective-permute-done.31.u1
  378.8 6.4 collective-permute-done.33.u3
  386.4 8.1 grad_rows.5
  411.7 8.1 grad_rows.4
  423.4 13.5 %collective-permute-done.90.refs_2_ = bf16[192,1536]{1,0:T(8,128)(2,1)S(1)} collective-permute-done((bf16[192,1536]{1,0:T(8,128)(2,1)S(1)}, bf16[192,1536]{1,0:T(8,128)(2,1)S(1)}, u32[]{:S(2)}, u32[]{:S(2)}) %collective-permute-start.90) | collective-permute-done | bytes 589856 | tf_op jit(solution)/shard_map/ppermute | solution.py:675
  437.5 10.6 collective-permute-done.38.refs_1_
  448.1 12.0 fusion.1
  463.7 24.3 %layer_fwd.7 = (bf16[1536,1536]{1,0:T(8,128)(2,1)}, f32[1536,1152]{1,0:T(8,128)}, f32[1536,384]{1,0:T(8,128)}, bf16[12,128,384]{2,1,0:T(8,128)(2,1)}, bf16[1536,...) custom-call(s32[4]{0:T(128)} %pad_add_fusion.2.sc, ...), custom_call_target="tpu_custom_call" | custom-call | flops 12683575296 | bytes 25165824 | tf_op jit(solution)/shard_map/layer_fwd/pallas_call | solution.py:227
  489.6 24.8 %layer_fwd.5 = (bf16[1536,1536]{1,0:T(8,128)(2,1)}, f32[1536,1152]{1,0:T(8,128)}, f32[1536,384]{1,0:T(8,128)}, bf16[12,128,384]{2,1,0:T(8,128)(2,1)}, bf16[1536,...) custom-call(s32[4]{0:T(128)} %pad_add_fusion.sc, bf16[192,1536]{1,0:T(8,128)(2,1)} %get-tuple-element.129.refs_0_, ...), custom_call_target="tpu_custom_call" | custom-call | flops 12683575296 | bytes 25165824 | tf_op jit(solution)/shard_map/layer_fwd/pallas_call | solution.py:227
  528.3 27.0 %layer_bwd.6 = (bf16[1536,1152]{1,0:T(8,128)(2,1)}, bf16[4,192,1152]{2,1,0:T(8,128)(2,1)}, bf16[1536,384]{1,0:T(8,128)(2,1)}, f32[8,640]{1,0:T(8,128)}, f32[8,128]{1,0:T(8,128)}, /*index=5*/f32[8,384]{1,0:T(8,128)}) custom-call(s32[4]{0:T(128)} %pad_add_fusion.2.sc, f32[1536,384]{1,0:T(8,128)} %get-tuple-element.147.refs_13_.refs_0_, ...), custom_call_target="tpu_custom_call" | custom-call | flops 28991029248 | bytes 25165824 | tf_op jit(solution)/shard_map/layer_bwd/pallas_call | solution.py:461
  558.7 27.2 %layer_bwd.4 = (bf16[1536,1152]{1,0:T(8,128)(2,1)}, bf16[4,192,1152]{2,1,0:T(8,128)(2,1)}, bf16[1536,384]{1,0:T(8,128)(2,1)}, f32[8,640]{1,0:T(8,128)}, f32[8,128]{1,0:T(8,128)}, /*index=5*/f32[8,384]{1,0:T(8,128)}) custom-call(s32[4]{0:T(128)} %pad_add_fusion.sc, f32[1536,384]{1,0:T(8,128)} %get-tuple-element.130.refs_13_.refs_0_, ...), custom_call_target="tpu_custom_call" | custom-call | flops 28991029248 | bytes 25165824 | tf_op jit(solution)/shard_map/layer_bwd/pallas_call | solution.py:461
  586.0 4.9 fusion.73
  595.3 8.8 fusion.76
  604.1 6.4 convolution_add_fusion
  618.8 7.9 half_rows.11
  626.7 7.5 collective-permute-done.188
  637.7 7.5 half_rows.9
  650.6 12.0 collective-permute-done.105.u2
  668.4 7.7 collective-permute-done.66.u1
  678.7 9.1 collective-permute-done.67.u2
  687.7 16.1 %collective-permute-start.172 = (bf16[384,768]{1,0:T(8,128)(2,1)}, bf16[384,768]{1,0:T(8,128)(2,1)}, u32[]{:S(2)}, u32[]{:S(2)}) collective-permute-start(bf16[384,768]{1,0:T(8,128)(2,1)} %get-tuple-element.287), channel_id=1, source_target_pairs={{0,8},{4,12},{8,0},{12,4},{1,9},{5,13},{9,1},{13,5},{2,10},{6,14},... | collective-permute-start | bytes 1769480 | tf_op jit(solution)/shard_map/ppermute | solution.py:720
  714.5 16.3 %half_rows.14 = (bf16[192,1536]{1,0:T(8,128)(2,1)}, bf16[192,1536]{1,0:T(8,128)(2,1)}, bf16[192,1536]{1,0:T(8,128)(2,1)}, bf16[192,1536]{1,0:T(8,128)(2,1)}) custom-call(s32[4]{0:T(128)} %pad_add_fusion.2.sc, bf16[1536,1152]{1,0:T(8,128)(2,1)} %get-tuple-element.183.kept, bf16[4,192,1152]{2,1,0:T(8,128)(2,1)} %collective-permute-done.137.got, ...), custom_call_target="tpu_custom_call" | custom-call | flops 5435817984 | bytes 8388608 | tf_op jit(solution)/shard_map/half_rows/pallas_call | solution.py:592
  730.7 10.4 collective-permute-done.172
  749.6 15.9 %half_rows.12 = (bf16[192,1536]{1,0:T(8,128)(2,1)}, bf16[192,1536]{1,0:T(8,128)(2,1)}, bf16[192,1536]{1,0:T(8,128)(2,1)}, bf16[192,1536]{1,0:T(8,128)(2,1)}) custom-call(s32[4]{0:T(128)} %pad_add_fusion.sc, bf16[1536,1152]{1,0:T(8,128)(2,1)} %get-tuple-element.159.kept, bf16[4,192,1152]{2,1,0:T(8,128)(2,1)} %collective-permute-done.112.got, ...), custom_call_target="tpu_custom_call" | custom-call | flops 5435817984 | bytes 8388608 | tf_op jit(solution)/shard_map/half_rows/pallas_call | solution.py:592
  783.3 11.6 collective-permute-done.115.g2
  799.9 22.7 %collective-permute-done.148.refs_9_ = f32[192,128]{1,0:T(8,128)S(1)} collective-permute-done((f32[192,128]{1,0:T(8,128)}, f32[192,128]{1,0:T(8,128)S(1)}, u32[]{:S(2)}, u32[]{:S(2)}) %collective-permute-start.148) | collective-permute-done | bytes 98336 | tf_op jit(solution)/shard_map/ppermute | solution.py:675
  823.1 5.0 collective-permute-done.150.refs_11_
  833.0 9.4 copy.90
  855.0 8.2 grad_rows.7
  863.2 5.8 collective-permute-done.124.refs_9_
  871.0 26.6 %layer_bwd.7 = (bf16[1536,1152]{1,0:T(8,128)(2,1)}, bf16[4,192,1152]{2,1,0:T(8,128)(2,1)}, bf16[1536,384]{1,0:T(8,128)(2,1)}, f32[8,640]{1,0:T(8,128)}, f32[8,128]{1,0:T(8,128)}, /*index=5*/f32[8,384]{1,0:T(8,128)}) custom-call(s32[4]{0:T(128)} %pad_add_fusion.2.sc, f32[1536,384]{1,0:T(8,128)} %get-tuple-element.192.refs_0_, ...), custom_call_target="tpu_custom_call" | custom-call | flops 28991029248 | bytes 25165824 | tf_op jit(solution)/shard_map/layer_bwd/pallas_call | solution.py:461
  898.9 11.2 fusion.75
  919.6 8.6 grad_rows.6
  928.2 26.6 %layer_bwd.5 = (bf16[1536,1152]{1,0:T(8,128)(2,1)}, bf16[4,192,1152]{2,1,0:T(8,128)(2,1)}, bf16[1536,384]{1,0:T(8,128)(2,1)}, f32[8,640]{1,0:T(8,128)}, f32[8,128]{1,0:T(8,128)}, /*index=5*/f32[8,384]{1,0:T(8,128)}) custom-call(s32[4]{0:T(128)} %pad_add_fusion.sc, f32[1536,384]{1,0:T(8,128)} %get-tuple-element.168.refs_0_, ...), custom_call_target="tpu_custom_call" | custom-call | flops 28991029248 | bytes 25165824 | tf_op jit(solution)/shard_map/layer_bwd/pallas_call | solution.py:461
  954.9 10.8 convolution_add_fusion.1
  975.9 6.5 collective-permute-done.186
  985.7 8.8 collective-permute-done.185
  1007.1 34.9 %collective-permute-done.169 = bf16[384,768]{1,0:T(8,128)(2,1)} collective-permute-done((bf16[384,768]{1,0:T(8,128)(2,1)}, bf16[384,768]{1,0:T(8,128)(2,1)}, u32[]{:S(2)}, u32[]{:S(2)}) %collective-permute-start.169) | collective-permute-done | bytes 589856 | tf_op jit(solution)/shard_map/ppermute | solution.py:720
  1063.4 15.8 %half_rows.15 = (bf16[192,1536]{1,0:T(8,128)(2,1)}, bf16[192,1536]{1,0:T(8,128)(2,1)}, bf16[192,1536]{1,0:T(8,128)(2,1)}, bf16[192,1536]{1,0:T(8,128)(2,1)}) custom-call(s32[4]{0:T(128)} %pad_add_fusion.2.sc, bf16[1536,1152]{1,0:T(8,128)(2,1)} %get-tuple-element.197.kept, bf16[4,192,1152]{2,1,0:T(8,128)(2,1)} %collective-permute-done.155.got, ...), custom_call_target="tpu_custom_call" | custom-call | flops 5435817984 | bytes 8388608 | tf_op jit(solution)/shard_map/half_rows/pallas_call | solution.py:592
  1079.3 14.3 %collective-permute-start.156 = (bf16[192,1536]{1,0:T(8,128)(2,1)}, bf16[192,1536]{1,0:T(8,128)(2,1)S(1)}, u32[]{:S(2)}, u32[]{:S(2)}) collective-permute-start(bf16[192,1536]{1,0:T(8,128)(2,1)} %get-tuple-element.200), channel_id=1, source_target_pairs={{0,1},{1,0},{2,3},{3,2},{4,5},{5,4},{6,7},{7,6},{8,9},{9,8},{10,11... | collective-permute-start | bytes 1769480 | tf_op jit(solution)/shard_map/ppermute | solution.py:675
  1093.7 7.3 collective-permute-start.183
  1102.6 15.8 %half_rows.13 = (bf16[192,1536]{1,0:T(8,128)(2,1)}, bf16[192,1536]{1,0:T(8,128)(2,1)}, bf16[192,1536]{1,0:T(8,128)(2,1)}, bf16[192,1536]{1,0:T(8,128)(2,1)}) custom-call(s32[4]{0:T(128)} %pad_add_fusion.sc, bf16[1536,1152]{1,0:T(8,128)(2,1)} %get-tuple-element.173.kept, bf16[4,192,1152]{2,1,0:T(8,128)(2,1)} %collective-permute-done.131.got, ...), custom_call_target="tpu_custom_call" | custom-call | flops 5435817984 | bytes 8388608 | tf_op jit(solution)/shard_map/half_rows/pallas_call | solution.py:592
  1128.6 18.9 %collective-permute-done.157.g2 = bf16[192,1536]{1,0:T(8,128)(2,1)} collective-permute-done((bf16[192,1536]{1,0:T(8,128)(2,1)}, bf16[192,1536]{1,0:T(8,128)(2,1)}, u32[]{:S(2)}, u32[]{:S(2)}) %collective-permute-start.157) | collective-permute-done | bytes 589856 | tf_op jit(solution)/shard_map/ppermute | solution.py:675
  1154.1 18.6 %collective-permute-done.134.g2 = bf16[192,1536]{1,0:T(8,128)(2,1)} collective-permute-done((bf16[192,1536]{1,0:T(8,128)(2,1)}, bf16[192,1536]{1,0:T(8,128)(2,1)}, u32[]{:S(2)}, u32[]{:S(2)}) %collective-permute-start.134) | collective-permute-done | bytes 589856 | tf_op jit(solution)/shard_map/ppermute | solution.py:675
  (907 shorter events, 445.5 us)
Async XLA Ops:
  2.5 39.7 %collective-permute-start.15 = (bf16[384,304]{1,0:T(8,128)(2,1)}, bf16[384,304]{1,0:T(8,128)(2,1)}, u32[]{:S(2)}, u32[]{:S(2)}) collective-permute-start(bf16[384,304]{1,0:T(8,128)(2,1)} %bitcast.5), channel_id=1, source_target_pairs={{0,4},{4,8},{8,12},{1,5},{5,9},{9,13},{2,6},{6,10},{10,14},{3,7},{... | collective-permute-start | bytes 700424 | tf_op jit(solution)/shard_map/ppermute | solution.py:701
  8.1 35.6 %collective-permute-start.18 = (bf16[384,304]{1,0:T(8,128)(2,1)}, bf16[384,304]{1,0:T(8,128)(2,1)}, u32[]{:S(2)}, u32[]{:S(2)}) collective-permute-start(bf16[384,304]{1,0:T(8,128)(2,1)} %bitcast.5), channel_id=1, source_target_pairs={{4,0},{8,4},{12,8},{5,1},{9,5},{13,9},{6,2},{10,6},{14,10},{7,3},{... | collective-permute-start | bytes 700424 | tf_op jit(solution)/shard_map/ppermute | solution.py:702
  13.0 38.6 %collective-permute-start = (f32[8,1536]{1,0:T(8,128)}, f32[8,1536]{1,0:T(8,128)}, u32[]{:S(2)}, u32[]{:S(2)}) collective-permute-start(f32[8,1536]{1,0:T(8,128)} %fusion.18), channel_id=1, source_target_pairs={{0,16},{16,0},{1,17},{17,1},{2,18},{18,2},{3,19},{19,3},{4,20},{20... | collective-permute-start | bytes 147464 | tf_op jit(solution)/shard_map/ppermute | solution.py:679
  26.6 35.5 %collective-permute-start.8 = (bf16[384,768]{1,0:T(8,128)(2,1)}, bf16[384,768]{1,0:T(8,128)(2,1)}, u32[]{:S(2)}, u32[]{:S(2)}) collective-permute-start(bf16[384,768]{1,0:T(8,128)(2,1)} %bitcast.40), channel_id=1, source_target_pairs={{0,16},{16,0},{1,17},{17,1},{2,18},{18,2},{3,19},{19,3},{4,20},{20... | collective-permute-start | bytes 1769480 | tf_op jit(solution)/shard_map/ppermute | solution.py:679
  66.4 31.8 %collective-permute-start.9 = (bf16[384,768]{1,0:T(8,128)(2,1)S(1)}, bf16[384,768]{1,0:T(8,128)(2,1)S(1)}, u32[]{:S(2)}, u32[]{:S(2)}) collective-permute-start(bf16[384,768]{1,0:T(8,128)(2,1)S(1)} %get-tuple-element.324), channel_id=1, source_target_pairs={{0,4},{4,8},{8,12},{1,5},{5,9},{9,13},{2,6},{6,10},{10,14},{3,7},{... | collective-permute-start | bytes 1769480 | tf_op jit(solution)/shard_map/ppermute | solution.py:701
  70.1 34.0 %collective-permute-start.12 = (bf16[384,768]{1,0:T(8,128)(2,1)S(1)}, bf16[384,768]{1,0:T(8,128)(2,1)S(1)}, u32[]{:S(2)}, u32[]{:S(2)}) collective-permute-start(bf16[384,768]{1,0:T(8,128)(2,1)S(1)} %get-tuple-element.324), channel_id=1, source_target_pairs={{4,0},{8,4},{12,8},{5,1},{9,5},{13,9},{6,2},{10,6},{14,10},{7,3},{... | collective-permute-start | bytes 1769480 | tf_op jit(solution)/shard_map/ppermute | solution.py:702
  136.1 32.0 %collective-permute-start.45 = (bf16[384,768]{1,0:T(8,128)(2,1)S(1)}, bf16[384,768]{1,0:T(8,128)(2,1)}, u32[]{:S(2)}, u32[]{:S(2)}) collective-permute-start(bf16[384,768]{1,0:T(8,128)(2,1)S(1)} %copy-done.19), channel_id=1, source_target_pairs={{0,4},{4,8},{8,12},{1,5},{5,9},{9,13},{2,6},{6,10},{10,14},{3,7},{... | collective-permute-start | bytes 1769480 | tf_op jit(solution)/shard_map/ppermute | solution.py:701
  141.6 31.7 %collective-permute-start.48 = (bf16[384,768]{1,0:T(8,128)(2,1)S(1)}, bf16[384,768]{1,0:T(8,128)(2,1)}, u32[]{:S(2)}, u32[]{:S(2)}) collective-permute-start(bf16[384,768]{1,0:T(8,128)(2,1)S(1)} %copy-done.19), channel_id=1, source_target_pairs={{4,0},{8,4},{12,8},{5,1},{9,5},{13,9},{6,2},{10,6},{14,10},{7,3},{... | collective-permute-start | bytes 1769480 | tf_op jit(solution)/shard_map/ppermute | solution.py:702
  142.9 33.3 %collective-permute-start.21 = (bf16[1536,304]{0,1:T(8,128)(2,1)}, bf16[1536,304]{0,1:T(8,128)(2,1)S(1)}, u32[]{:S(2)}, u32[]{:S(2)}) collective-permute-start(bf16[1536,304]{0,1:T(8,128)(2,1)} %copy.72), channel_id=1, source_target_pairs={{0,16},{16,0},{1,17},{17,1},{2,18},{18,2},{3,19},{19,3},{4,20},{20... | collective-permute-start | bytes 2801672 | tf_op jit(solution)/shard_map/ppermute | solution.py:679
  176.2 51.9 %collective-permute-start.132 = (bf16[1536,768]{1,0:T(8,128)(2,1)}, bf16[1536,768]{1,0:T(8,128)(2,1)}, u32[]{:S(2)}, u32[]{:S(2)}) collective-permute-start(bf16[1536,768]{1,0:T(8,128)(2,1)} %pad_maximum_fusion.4), channel_id=1, source_target_pairs={{0,16},{16,0},{1,17},{17,1},{2,18},{18,2},{3,19},{19,3},{4,20},{20... | collective-permute-start | bytes 7077896 | tf_op jit(solution)/shard_map/ppermute | solution.py:679
  241.0 32.1 %collective-permute-start.6 = (bf16[192,1536]{1,0:T(8,128)(2,1)}, bf16[192,1536]{1,0:T(8,128)(2,1)}, u32[]{:S(2)}, u32[]{:S(2)}) collective-permute-start(bf16[192,1536]{1,0:T(8,128)(2,1)} %collective-permute-done.2.refs_2_), channel_id=1, source_target_pairs={{0,16},{16,0},{1,17},{17,1},{2,18},{18,2},{3,19},{19,3},{4,20},{20... | collective-permute-start | bytes 1769480 | tf_op jit(solution)/shard_map/ppermute | solution.py:679
  241.1 33.5 %collective-permute-start.7 = (bf16[192,1536]{1,0:T(8,128)(2,1)}, bf16[192,1536]{1,0:T(8,128)(2,1)}, u32[]{:S(2)}, u32[]{:S(2)}) collective-permute-start(bf16[192,1536]{1,0:T(8,128)(2,1)} %collective-permute-done.3.refs_3_), channel_id=1, source_target_pairs={{0,16},{16,0},{1,17},{17,1},{2,18},{18,2},{3,19},{19,3},{4,20},{20... | collective-permute-start | bytes 1769480 | tf_op jit(solution)/shard_map/ppermute | solution.py:679
  242.1 32.7 %collective-permute-start.30 = (bf16[384,1536]{1,0:T(8,128)(2,1)S(1)}, bf16[384,1536]{1,0:T(8,128)(2,1)S(1)}, u32[]{:S(2)}, u32[]{:S(2)}) collective-permute-start(bf16[384,1536]{1,0:T(8,128)(2,1)S(1)} %copy-done.27), channel_id=1, source_target_pairs={{0,16},{16,0},{1,17},{17,1},{2,18},{18,2},{3,19},{19,3},{4,20},{20... | collective-permute-start | bytes 3538952 | tf_op jit(solution)/shard_map/ppermute | solution.py:679
  267.1 40.9 %collective-permute-start.102 = (bf16[192,1536]{1,0:T(8,128)(2,1)}, bf16[192,1536]{1,0:T(8,128)(2,1)S(1)}, u32[]{:S(2)}, u32[]{:S(2)}) collective-permute-start(bf16[192,1536]{1,0:T(8,128)(2,1)} %collective-permute-done.98.refs_3_), channel_id=1, source_target_pairs={{0,16},{16,0},{1,17},{17,1},{2,18},{18,2},{3,19},{19,3},{4,20},{20... | collective-permute-start | bytes 1769480 | tf_op jit(solution)/shard_map/ppermute | solution.py:679
  268.0 40.6 %collective-permute-start.60 = (bf16[384,384]{1,0:T(8,128)(2,1)S(1)}, bf16[384,384]{1,0:T(8,128)(2,1)S(1)}, u32[]{:S(2)}, u32[]{:S(2)}) collective-permute-start(bf16[384,384]{1,0:T(8,128)(2,1)S(1)} %collective-permute-done.59), channel_id=1, source_target_pairs={{0,4},{4,8},{8,12},{1,5},{5,9},{9,13},{2,6},{6,10},{10,14},{3,7},{... | collective-permute-start | bytes 884744 | tf_op jit(solution)/shard_map/ppermute | solution.py:701
  273.2 36.1 %collective-permute-start.63 = (bf16[384,384]{1,0:T(8,128)(2,1)S(1)}, bf16[384,384]{1,0:T(8,128)(2,1)S(1)}, u32[]{:S(2)}, u32[]{:S(2)}) collective-permute-start(bf16[384,384]{1,0:T(8,128)(2,1)S(1)} %collective-permute-done.62), channel_id=1, source_target_pairs={{4,0},{8,4},{12,8},{5,1},{9,5},{13,9},{6,2},{10,6},{14,10},{7,3},{... | collective-permute-start | bytes 884744 | tf_op jit(solution)/shard_map/ppermute | solution.py:702
  274.7 135.4 %collective-permute-start.113 = (bf16[1536,768]{1,0:T(8,128)(2,1)}, bf16[1536,768]{1,0:T(8,128)(2,1)}, u32[]{:S(2)}, u32[]{:S(2)}) collective-permute-start(bf16[1536,768]{1,0:T(8,128)(2,1)} %pad_maximum_fusion.5), channel_id=1, source_target_pairs={{0,16},{16,0},{1,17},{17,1},{2,18},{18,2},{3,19},{19,3},{4,20},{20... | collective-permute-start | bytes 7077896 | tf_op jit(solution)/shard_map/ppermute | solution.py:679
  299.5 41.4 %collective-permute-start.22 = (bf16[4,192,384]{2,1,0:T(8,128)(2,1)}, bf16[4,192,384]{2,1,0:T(8,128)(2,1)}, u32[]{:S(2)}, u32[]{:S(2)}) collective-permute-start(bf16[4,192,384]{2,1,0:T(8,128)(2,1)} %get-tuple-element.123), channel_id=1, source_target_pairs={{0,16},{16,0},{1,17},{17,1},{2,18},{18,2},{3,19},{19,3},{4,20},{20... | collective-permute-start | bytes 1769480 | tf_op jit(solution)/shard_map/ppermute | solution.py:679
  308.0 43.8 %collective-permute-start.82 = (bf16[192,1536]{1,0:T(8,128)(2,1)}, bf16[192,1536]{1,0:T(8,128)(2,1)}, u32[]{:S(2)}, u32[]{:S(2)}) collective-permute-start(bf16[192,1536]{1,0:T(8,128)(2,1)} %get-tuple-element.142), channel_id=1, source_target_pairs={{0,1},{1,0},{2,3},{3,2},{4,5},{5,4},{6,7},{7,6},{8,9},{9,8},{10,11... | collective-permute-start | bytes 1769480 | tf_op jit(solution)/shard_map/ppermute | solution.py:675
  308.6 44.4 %collective-permute-start.83 = (bf16[192,1536]{1,0:T(8,128)(2,1)}, bf16[192,1536]{1,0:T(8,128)(2,1)}, u32[]{:S(2)}, u32[]{:S(2)}) collective-permute-start(bf16[192,1536]{1,0:T(8,128)(2,1)} %get-tuple-element.143), channel_id=1, source_target_pairs={{0,2},{1,3},{2,0},{3,1},{4,6},{5,7},{6,4},{7,5},{8,10},{9,11},{10,... | collective-permute-start | bytes 1769480 | tf_op jit(solution)/shard_map/ppermute | solution.py:675
  353.0 32.1 %collective-permute-start.33 = (bf16[192,1536]{1,0:T(8,128)(2,1)}, bf16[192,1536]{1,0:T(8,128)(2,1)S(1)}, u32[]{:S(2)}, u32[]{:S(2)}) collective-permute-start(bf16[192,1536]{1,0:T(8,128)(2,1)} %get-tuple-element.127), channel_id=1, source_target_pairs={{0,3},{1,2},{2,1},{3,0},{4,7},{5,6},{6,5},{7,4},{8,11},{9,10},{10,... | collective-permute-start | bytes 1769480 | tf_op jit(solution)/shard_map/ppermute | solution.py:675
  366.3 40.2 %collective-permute-start.54 = (bf16[192,1536]{1,0:T(8,128)(2,1)S(1)}, bf16[192,1536]{1,0:T(8,128)(2,1)}, u32[]{:S(2)}, u32[]{:S(2)}) collective-permute-start(bf16[192,1536]{1,0:T(8,128)(2,1)S(1)} %copy-done.17), channel_id=1, source_target_pairs={{0,16},{16,0},{1,17},{17,1},{2,18},{18,2},{3,19},{19,3},{4,20},{20... | collective-permute-start | bytes 1769480 | tf_op jit(solution)/shard_map/ppermute | solution.py:679
  378.0 30.1 %collective-permute-start.55 = (bf16[192,1536]{1,0:T(8,128)(2,1)}, bf16[192,1536]{1,0:T(8,128)(2,1)}, u32[]{:S(2)}, u32[]{:S(2)}) collective-permute-start(bf16[192,1536]{1,0:T(8,128)(2,1)} %collective-permute-done.51.refs_1_), channel_id=1, source_target_pairs={{0,16},{16,0},{1,17},{17,1},{2,18},{18,2},{3,19},{19,3},{4,20},{20... | collective-permute-start | bytes 1769480 | tf_op jit(solution)/shard_map/ppermute | solution.py:679
  378.7 29.8 %collective-permute-start.56 = (bf16[192,1536]{1,0:T(8,128)(2,1)}, bf16[192,1536]{1,0:T(8,128)(2,1)}, u32[]{:S(2)}, u32[]{:S(2)}) collective-permute-start(bf16[192,1536]{1,0:T(8,128)(2,1)} %collective-permute-done.52.refs_2_), channel_id=1, source_target_pairs={{0,16},{16,0},{1,17},{17,1},{2,18},{18,2},{3,19},{19,3},{4,20},{20... | collective-permute-start | bytes 1769480 | tf_op jit(solution)/shard_map/ppermute | solution.py:679
  410.1 37.9 %collective-permute-start.38 = (bf16[192,1536]{1,0:T(8,128)(2,1)}, bf16[192,1536]{1,0:T(8,128)(2,1)S(1)}, u32[]{:S(2)}, u32[]{:S(2)}) collective-permute-start(bf16[192,1536]{1,0:T(8,128)(2,1)} %get-tuple-element.129.refs_0_), channel_id=1, source_target_pairs={{0,1},{1,0},{2,3},{3,2},{4,5},{5,4},{6,7},{7,6},{8,9},{9,8},{10,11... | collective-permute-start | bytes 1769480 | tf_op jit(solution)/shard_map/ppermute | solution.py:675
  422.8 38.7 %collective-permute-start.39 = (bf16[192,1536]{1,0:T(8,128)(2,1)S(1)}, bf16[192,1536]{1,0:T(8,128)(2,1)S(1)}, u32[]{:S(2)}, u32[]{:S(2)}) collective-permute-start(bf16[192,1536]{1,0:T(8,128)(2,1)S(1)} %copy-done.118), channel_id=1, source_target_pairs={{0,2},{1,3},{2,0},{3,1},{4,6},{5,7},{6,4},{7,5},{8,10},{9,11},{10,... | collective-permute-start | bytes 1769480 | tf_op jit(solution)/shard_map/ppermute | solution.py:675
  518.5 95.3 %collective-permute-start.65 = (bf16[384,1536]{1,0:T(8,128)(2,1)S(1)}, bf16[384,1536]{1,0:T(8,128)(2,1)}, u32[]{:S(2)}, u32[]{:S(2)}) collective-permute-start(bf16[384,1536]{1,0:T(8,128)(2,1)S(1)} %copy-done.28), channel_id=1, source_target_pairs={{0,16},{16,0},{1,17},{17,1},{2,18},{18,2},{3,19},{19,3},{4,20},{20... | collective-permute-start | bytes 3538952 | tf_op jit(solution)/shard_map/ppermute | solution.py:679
  518.5 100.3 %collective-permute-start.103 = (bf16[4,192,384]{2,1,0:T(8,128)(2,1)}, bf16[4,192,384]{2,1,0:T(8,128)(2,1)}, u32[]{:S(2)}, u32[]{:S(2)}) collective-permute-start(bf16[4,192,384]{2,1,0:T(8,128)(2,1)} %get-tuple-element.149), channel_id=1, source_target_pairs={{0,16},{16,0},{1,17},{17,1},{2,18},{18,2},{3,19},{19,3},{4,20},{20... | collective-permute-start | bytes 1769480 | tf_op jit(solution)/shard_map/ppermute | solution.py:679
  525.3 109.8 %collective-permute-start.64 = (bf16[4,192,384]{2,1,0:T(8,128)(2,1)}, bf16[4,192,384]{2,1,0:T(8,128)(2,1)}, u32[]{:S(2)}, u32[]{:S(2)}) collective-permute-start(bf16[4,192,384]{2,1,0:T(8,128)(2,1)} %get-tuple-element.132), channel_id=1, source_target_pairs={{0,16},{16,0},{1,17},{17,1},{2,18},{18,2},{3,19},{19,3},{4,20},{20... | collective-permute-start | bytes 1769480 | tf_op jit(solution)/shard_map/ppermute | solution.py:679
  618.8 95.7 %collective-permute-start.137 = (bf16[4,192,1152]{2,1,0:T(8,128)(2,1)}, bf16[4,192,1152]{2,1,0:T(8,128)(2,1)}, u32[]{:S(2)}, u32[]{:S(2)}) collective-permute-start(bf16[4,192,1152]{2,1,0:T(8,128)(2,1)} %get-tuple-element.184), channel_id=1, source_target_pairs={{0,16},{16,0},{1,17},{17,1},{2,18},{18,2},{3,19},{19,3},{4,20},{20... | collective-permute-start | bytes 5308424 | tf_op jit(solution)/shard_map/ppermute | solution.py:679
  645.2 30.9 %collective-permute-start.66 = (bf16[192,1536]{1,0:T(8,128)(2,1)}, bf16[192,1536]{1,0:T(8,128)(2,1)}, u32[]{:S(2)}, u32[]{:S(2)}) collective-permute-start(bf16[192,1536]{1,0:T(8,128)(2,1)} %get-tuple-element.134), channel_id=1, source_target_pairs={{0,1},{1,0},{2,3},{3,2},{4,5},{5,4},{6,7},{7,6},{8,9},{9,8},{10,11... | collective-permute-start | bytes 1769480 | tf_op jit(solution)/shard_map/ppermute | solution.py:675
  650.6 96.4 %collective-permute-start.112 = (bf16[4,192,1152]{2,1,0:T(8,128)(2,1)}, bf16[4,192,1152]{2,1,0:T(8,128)(2,1)}, u32[]{:S(2)}, u32[]{:S(2)}) collective-permute-start(bf16[4,192,1152]{2,1,0:T(8,128)(2,1)} %get-tuple-element.160), channel_id=1, source_target_pairs={{0,16},{16,0},{1,17},{17,1},{2,18},{18,2},{3,19},{19,3},{4,20},{20... | collective-permute-start | bytes 5308424 | tf_op jit(solution)/shard_map/ppermute | solution.py:679
  663.5 40.4 %collective-permute-start.68 = (bf16[192,1536]{1,0:T(8,128)(2,1)}, bf16[192,1536]{1,0:T(8,128)(2,1)}, u32[]{:S(2)}, u32[]{:S(2)}) collective-permute-start(bf16[192,1536]{1,0:T(8,128)(2,1)} %get-tuple-element.136), channel_id=1, source_target_pairs={{0,3},{1,2},{2,1},{3,0},{4,7},{5,6},{6,5},{7,4},{8,11},{9,10},{10,... | collective-permute-start | bytes 1769480 | tf_op jit(solution)/shard_map/ppermute | solution.py:675
  676.0 65.5 %collective-permute-start.177 = (bf16[1536,304]{0,1:T(8,128)(2,1)}, bf16[1536,304]{0,1:T(8,128)(2,1)}, u32[]{:S(2)}, u32[]{:S(2)}) collective-permute-start(bf16[1536,304]{0,1:T(8,128)(2,1)} %copy.88), channel_id=1, source_target_pairs={{0,16},{1,17},{2,18},{3,19},{4,20},{5,21},{6,22},{7,23},{8,24},{9,... | collective-permute-start | bytes 2801672 | tf_op jit(solution)/shard_map/ppermute | solution.py:683
  687.7 53.4 %collective-permute-start.172 = (bf16[384,768]{1,0:T(8,128)(2,1)}, bf16[384,768]{1,0:T(8,128)(2,1)}, u32[]{:S(2)}, u32[]{:S(2)}) collective-permute-start(bf16[384,768]{1,0:T(8,128)(2,1)} %get-tuple-element.287), channel_id=1, source_target_pairs={{0,8},{4,12},{8,0},{12,4},{1,9},{5,13},{9,1},{13,5},{2,10},{6,14},... | collective-permute-start | bytes 1769480 | tf_op jit(solution)/shard_map/ppermute | solution.py:720
  703.8 37.3 %collective-permute-start.171 = (bf16[384,768]{1,0:T(8,128)(2,1)}, bf16[384,768]{1,0:T(8,128)(2,1)}, u32[]{:S(2)}, u32[]{:S(2)}) collective-permute-start(bf16[384,768]{1,0:T(8,128)(2,1)} %get-tuple-element.285), channel_id=1, source_target_pairs={{0,4},{4,8},{8,12},{12,0},{1,5},{5,9},{9,13},{13,1},{2,6},{6,10},{... | collective-permute-start | bytes 1769480 | tf_op jit(solution)/shard_map/ppermute | solution.py:720
  714.5 51.0 %collective-permute-start.111 = (f32[192,1536]{1,0:T(8,128)}, f32[192,1536]{1,0:T(8,128)}, u32[]{:S(2)}, u32[]{:S(2)}) collective-permute-start(f32[192,1536]{1,0:T(8,128)} %owner_out.3), channel_id=1, source_target_pairs={{0,16},{16,0},{1,17},{17,1},{2,18},{18,2},{3,19},{19,3},{4,20},{20... | collective-permute-start | bytes 3538952 | tf_op jit(solution)/shard_map/ppermute | solution.py:679
  741.1 38.2 %collective-permute-start.73 = (f32[192,1536]{1,0:T(8,128)S(1)}, f32[192,1536]{1,0:T(8,128)}, u32[]{:S(2)}, u32[]{:S(2)}) collective-permute-start(f32[192,1536]{1,0:T(8,128)S(1)} %copy-done.12), channel_id=1, source_target_pairs={{0,16},{16,0},{1,17},{17,1},{2,18},{18,2},{3,19},{19,3},{4,20},{20... | collective-permute-start | bytes 3538952 | tf_op jit(solution)/shard_map/ppermute | solution.py:679
  765.9 29.0 %collective-permute-start.115 = (bf16[192,1536]{1,0:T(8,128)(2,1)}, bf16[192,1536]{1,0:T(8,128)(2,1)S(1)}, u32[]{:S(2)}, u32[]{:S(2)}) collective-permute-start(bf16[192,1536]{1,0:T(8,128)(2,1)} %get-tuple-element.163), channel_id=1, source_target_pairs={{0,2},{1,3},{2,0},{3,1},{4,6},{5,7},{6,4},{7,5},{8,10},{9,11},{10,... | collective-permute-start | bytes 1769480 | tf_op jit(solution)/shard_map/ppermute | solution.py:675
  778.7 49.9 %collective-permute-start.141 = (bf16[192,1536]{1,0:T(8,128)(2,1)}, bf16[192,1536]{1,0:T(8,128)(2,1)}, u32[]{:S(2)}, u32[]{:S(2)}) collective-permute-start(bf16[192,1536]{1,0:T(8,128)(2,1)} %get-tuple-element.190.refs_0_.g_in), channel_id=1, source_target_pairs={{0,1},{1,0},{2,3},{3,2},{4,5},{5,4},{6,7},{7,6},{8,9},{9,8},{10,11... | collective-permute-start | bytes 1769480 | tf_op jit(solution)/shard_map/ppermute | solution.py:675
  779.3 49.4 %collective-permute-start.142 = (bf16[192,1536]{1,0:T(8,128)(2,1)}, bf16[192,1536]{1,0:T(8,128)(2,1)}, u32[]{:S(2)}, u32[]{:S(2)}) collective-permute-start(bf16[192,1536]{1,0:T(8,128)(2,1)} %get-tuple-element.190.refs_0_.g_in), channel_id=1, source_target_pairs={{0,2},{1,3},{2,0},{3,1},{4,6},{5,7},{6,4},{7,5},{8,10},{9,11},{10,... | collective-permute-start | bytes 1769480 | tf_op jit(solution)/shard_map/ppermute | solution.py:675
  782.9 46.3 %collective-permute-start.143 = (bf16[192,1536]{1,0:T(8,128)(2,1)}, bf16[192,1536]{1,0:T(8,128)(2,1)}, u32[]{:S(2)}, u32[]{:S(2)}) collective-permute-start(bf16[192,1536]{1,0:T(8,128)(2,1)} %get-tuple-element.190.refs_0_.g_in), channel_id=1, source_target_pairs={{0,3},{1,2},{2,1},{3,0},{4,7},{5,6},{6,5},{7,4},{8,11},{9,10},{10,... | collective-permute-start | bytes 1769480 | tf_op jit(solution)/shard_map/ppermute | solution.py:675
  850.4 47.9 %collective-permute-start.117 = (bf16[192,1536]{1,0:T(8,128)(2,1)}, bf16[192,1536]{1,0:T(8,128)(2,1)S(1)}, u32[]{:S(2)}, u32[]{:S(2)}) collective-permute-start(bf16[192,1536]{1,0:T(8,128)(2,1)} %get-tuple-element.166.refs_0_.g_in), channel_id=1, source_target_pairs={{0,1},{1,0},{2,3},{3,2},{4,5},{5,4},{6,7},{7,6},{8,9},{9,8},{10,11... | collective-permute-start | bytes 1769480 | tf_op jit(solution)/shard_map/ppermute | solution.py:675
  850.9 47.6 %collective-permute-start.118 = (bf16[192,1536]{1,0:T(8,128)(2,1)}, bf16[192,1536]{1,0:T(8,128)(2,1)S(1)}, u32[]{:S(2)}, u32[]{:S(2)}) collective-permute-start(bf16[192,1536]{1,0:T(8,128)(2,1)} %get-tuple-element.166.refs_0_.g_in), channel_id=1, source_target_pairs={{0,2},{1,3},{2,0},{3,1},{4,6},{5,7},{6,4},{7,5},{8,10},{9,11},{10,... | collective-permute-start | bytes 1769480 | tf_op jit(solution)/shard_map/ppermute | solution.py:675
  869.0 29.9 %collective-permute-start.119 = (bf16[192,1536]{1,0:T(8,128)(2,1)S(1)}, bf16[192,1536]{1,0:T(8,128)(2,1)S(1)}, u32[]{:S(2)}, u32[]{:S(2)}) collective-permute-start(bf16[192,1536]{1,0:T(8,128)(2,1)S(1)} %copy-done.35), channel_id=1, source_target_pairs={{0,3},{1,2},{2,1},{3,0},{4,7},{5,6},{6,5},{7,4},{8,11},{9,10},{10,... | collective-permute-start | bytes 1769480 | tf_op jit(solution)/shard_map/ppermute | solution.py:675
  912.7 59.6 %collective-permute-start.190 = (f32[384,384]{1,0:T(8,128)}, f32[384,384]{1,0:T(8,128)}, u32[]{:S(2)}, u32[]{:S(2)}) collective-permute-start(f32[384,384]{1,0:T(8,128)} %convert_add_fusion.2), channel_id=1, source_target_pairs={{0,16},{1,17},{2,18},{3,19},{4,20},{5,21},{6,22},{7,23},{8,24},{9,... | collective-permute-start | bytes 1769480 | tf_op jit(solution)/shard_map/ppermute | solution.py:683
  915.5 87.7 %collective-permute-start.174 = (f32[384,768]{1,0:T(8,128)}, f32[384,768]{1,0:T(8,128)}, u32[]{:S(2)}, u32[]{:S(2)}) collective-permute-start(f32[384,768]{1,0:T(8,128)} %convert_add_fusion), channel_id=1, source_target_pairs={{0,16},{1,17},{2,18},{3,19},{4,20},{5,21},{6,22},{7,23},{8,24},{9,... | collective-permute-start | bytes 3538952 | tf_op jit(solution)/shard_map/ppermute | solution.py:683
  972.3 32.9 %collective-permute-start.170 = (bf16[384,768]{1,0:T(8,128)(2,1)}, bf16[384,768]{1,0:T(8,128)(2,1)}, u32[]{:S(2)}, u32[]{:S(2)}) collective-permute-start(bf16[384,768]{1,0:T(8,128)(2,1)} %get-tuple-element.283), channel_id=1, source_target_pairs={{0,12},{4,0},{8,4},{12,8},{1,13},{5,1},{9,5},{13,9},{2,14},{6,2},{... | collective-permute-start | bytes 1769480 | tf_op jit(solution)/shard_map/ppermute | solution.py:720
  982.5 59.5 %collective-permute-start.169 = (bf16[384,768]{1,0:T(8,128)(2,1)}, bf16[384,768]{1,0:T(8,128)(2,1)}, u32[]{:S(2)}, u32[]{:S(2)}) collective-permute-start(bf16[384,768]{1,0:T(8,128)(2,1)} %get-tuple-element.284), channel_id=1, source_target_pairs={{0,8},{4,12},{8,0},{12,4},{1,9},{5,13},{9,1},{13,5},{2,10},{6,14},... | collective-permute-start | bytes 1769480 | tf_op jit(solution)/shard_map/ppermute | solution.py:720
  994.5 47.5 %collective-permute-start.168 = (bf16[384,768]{1,0:T(8,128)(2,1)}, bf16[384,768]{1,0:T(8,128)(2,1)}, u32[]{:S(2)}, u32[]{:S(2)}) collective-permute-start(bf16[384,768]{1,0:T(8,128)(2,1)} %get-tuple-element.282), channel_id=1, source_target_pairs={{0,4},{4,8},{8,12},{12,0},{1,5},{5,9},{9,13},{13,1},{2,6},{6,10},{... | collective-permute-start | bytes 1769480 | tf_op jit(solution)/shard_map/ppermute | solution.py:720
  995.6 54.0 %collective-permute-start.191 = (f32[384,384]{1,0:T(8,128)}, f32[384,384]{1,0:T(8,128)}, u32[]{:S(2)}, u32[]{:S(2)}) collective-permute-start(f32[384,384]{1,0:T(8,128)} %get-tuple-element.273), channel_id=1, source_target_pairs={{16,0},{17,1},{18,2},{19,3},{20,4},{21,5},{22,6},{23,7},{24,8},{25... | collective-permute-start | bytes 1769480 | tf_op jit(solution)/shard_map/ppermute | solution.py:683
  1003.2 58.2 %collective-permute-start.155 = (bf16[4,192,1152]{2,1,0:T(8,128)(2,1)}, bf16[4,192,1152]{2,1,0:T(8,128)(2,1)}, u32[]{:S(2)}, u32[]{:S(2)}) collective-permute-start(bf16[4,192,1152]{2,1,0:T(8,128)(2,1)} %get-tuple-element.198), channel_id=1, source_target_pairs={{0,16},{16,0},{1,17},{17,1},{2,18},{18,2},{3,19},{19,3},{4,20},{20... | collective-permute-start | bytes 5308424 | tf_op jit(solution)/shard_map/ppermute | solution.py:679
  1005.3 47.6 %collective-permute-start.176 = (bf16[1536,304]{0,1:T(8,128)(2,1)}, bf16[1536,304]{0,1:T(8,128)(2,1)}, u32[]{:S(2)}, u32[]{:S(2)}) collective-permute-start(bf16[1536,304]{0,1:T(8,128)(2,1)} %copy.85), channel_id=1, source_target_pairs={{16,0},{17,1},{18,2},{19,3},{20,4},{21,5},{22,6},{23,7},{24,8},{25... | collective-permute-start | bytes 2801672 | tf_op jit(solution)/shard_map/ppermute | solution.py:683
  1042.0 60.6 %collective-permute-start.131 = (bf16[4,192,1152]{2,1,0:T(8,128)(2,1)}, bf16[4,192,1152]{2,1,0:T(8,128)(2,1)}, u32[]{:S(2)}, u32[]{:S(2)}) collective-permute-start(bf16[4,192,1152]{2,1,0:T(8,128)(2,1)} %get-tuple-element.174), channel_id=1, source_target_pairs={{0,16},{16,0},{1,17},{17,1},{2,18},{18,2},{3,19},{19,3},{4,20},{20... | collective-permute-start | bytes 5308424 | tf_op jit(solution)/shard_map/ppermute | solution.py:679
  1045.5 76.9 %collective-permute-start.175 = (f32[384,768]{1,0:T(8,128)}, f32[384,768]{1,0:T(8,128)}, u32[]{:S(2)}, u32[]{:S(2)}) collective-permute-start(f32[384,768]{1,0:T(8,128)} %get-tuple-element.277), channel_id=1, source_target_pairs={{16,0},{17,1},{18,2},{19,3},{20,4},{21,5},{22,6},{23,7},{24,8},{25... | collective-permute-start | bytes 3538952 | tf_op jit(solution)/shard_map/ppermute | solution.py:683
  1058.0 35.6 %collective-permute-start.179 = (bf16[384,304]{1,0:T(8,128)(2,1)S(1)}, bf16[384,304]{1,0:T(8,128)(2,1)S(1)}, u32[]{:S(2)}, u32[]{:S(2)}) collective-permute-start(bf16[384,304]{1,0:T(8,128)(2,1)S(1)} %get-tuple-element.314), channel_id=1, source_target_pairs={{0,8},{4,12},{8,0},{12,4},{1,9},{5,13},{9,1},{13,5},{2,10},{6,14},... | collective-permute-start | bytes 700424 | tf_op jit(solution)/shard_map/ppermute | solution.py:720
  1061.5 32.1 %collective-permute-start.178 = (bf16[384,304]{1,0:T(8,128)(2,1)S(1)}, bf16[384,304]{1,0:T(8,128)(2,1)S(1)}, u32[]{:S(2)}, u32[]{:S(2)}) collective-permute-start(bf16[384,304]{1,0:T(8,128)(2,1)S(1)} %get-tuple-element.312), channel_id=1, source_target_pairs={{0,4},{4,8},{8,12},{12,0},{1,5},{5,9},{9,13},{13,1},{2,6},{6,10},{... | collective-permute-start | bytes 700424 | tf_op jit(solution)/shard_map/ppermute | solution.py:720
  1079.3 43.6 %collective-permute-start.156 = (bf16[192,1536]{1,0:T(8,128)(2,1)}, bf16[192,1536]{1,0:T(8,128)(2,1)S(1)}, u32[]{:S(2)}, u32[]{:S(2)}) collective-permute-start(bf16[192,1536]{1,0:T(8,128)(2,1)} %get-tuple-element.200), channel_id=1, source_target_pairs={{0,1},{1,0},{2,3},{3,2},{4,5},{5,4},{6,7},{7,6},{8,9},{9,8},{10,11... | collective-permute-start | bytes 1769480 | tf_op jit(solution)/shard_map/ppermute | solution.py:675
  1118.3 29.2 %collective-permute-start.157 = (bf16[192,1536]{1,0:T(8,128)(2,1)}, bf16[192,1536]{1,0:T(8,128)(2,1)}, u32[]{:S(2)}, u32[]{:S(2)}) collective-permute-start(bf16[192,1536]{1,0:T(8,128)(2,1)} %get-tuple-element.201), channel_id=1, source_target_pairs={{0,2},{1,3},{2,0},{3,1},{4,6},{5,7},{6,4},{7,5},{8,10},{9,11},{10,... | collective-permute-start | bytes 1769480 | tf_op jit(solution)/shard_map/ppermute | solution.py:675
  1119.0 31.1 %collective-permute-start.158 = (bf16[192,1536]{1,0:T(8,128)(2,1)}, bf16[192,1536]{1,0:T(8,128)(2,1)}, u32[]{:S(2)}, u32[]{:S(2)}) collective-permute-start(bf16[192,1536]{1,0:T(8,128)(2,1)} %get-tuple-element.202), channel_id=1, source_target_pairs={{0,3},{1,2},{2,1},{3,0},{4,7},{5,6},{6,5},{7,4},{8,11},{9,10},{10,... | collective-permute-start | bytes 1769480 | tf_op jit(solution)/shard_map/ppermute | solution.py:675
  1121.9 32.2 %collective-permute-start.133 = (bf16[192,1536]{1,0:T(8,128)(2,1)}, bf16[192,1536]{1,0:T(8,128)(2,1)S(1)}, u32[]{:S(2)}, u32[]{:S(2)}) collective-permute-start(bf16[192,1536]{1,0:T(8,128)(2,1)} %get-tuple-element.176), channel_id=1, source_target_pairs={{0,1},{1,0},{2,3},{3,2},{4,5},{5,4},{6,7},{7,6},{8,9},{9,8},{10,11... | collective-permute-start | bytes 1769480 | tf_op jit(solution)/shard_map/ppermute | solution.py:675
  1122.3 50.4 %collective-permute-start.134 = (bf16[192,1536]{1,0:T(8,128)(2,1)}, bf16[192,1536]{1,0:T(8,128)(2,1)}, u32[]{:S(2)}, u32[]{:S(2)}) collective-permute-start(bf16[192,1536]{1,0:T(8,128)(2,1)} %get-tuple-element.177), channel_id=1, source_target_pairs={{0,2},{1,3},{2,0},{3,1},{4,6},{5,7},{6,4},{7,5},{8,10},{9,11},{10,... | collective-permute-start | bytes 1769480 | tf_op jit(solution)/shard_map/ppermute | solution.py:675
  1122.8 49.9 %collective-permute-start.135 = (bf16[192,1536]{1,0:T(8,128)(2,1)}, bf16[192,1536]{1,0:T(8,128)(2,1)}, u32[]{:S(2)}, u32[]{:S(2)}) collective-permute-start(bf16[192,1536]{1,0:T(8,128)(2,1)} %get-tuple-element.178), channel_id=1, source_target_pairs={{0,3},{1,2},{2,1},{3,0},{4,7},{5,6},{6,5},{7,4},{8,11},{9,10},{10,... | collective-permute-start | bytes 1769480 | tf_op jit(solution)/shard_map/ppermute | solution.py:675
  1147.5 49.9 %collective-permute-start.161 = (f32[8,1536]{1,0:T(8,128)}, f32[8,1536]{1,0:T(8,128)}, u32[]{:S(2)}, u32[]{:S(2)}) collective-permute-start(f32[8,1536]{1,0:T(8,128)} %copy-done.71), channel_id=1, source_target_pairs={{0,16},{1,17},{2,18},{3,19},{4,20},{5,21},{6,22},{7,23},{8,24},{9,... | collective-permute-start | bytes 147464 | tf_op jit(solution)/shard_map/ppermute | solution.py:683
  (305 other events, 4806.5 us)

commit v2 on v1

v2 whole, which is shorter than its diff:
```python
from functools import partial

import jax
import jax.numpy as jnp
from jax import lax
from jax.experimental import pallas as pl
from jax.experimental.pallas import tpu as pltpu
from jax.sharding import PartitionSpec as P

EPS = 1e-05
F32 = jnp.float32
BF16 = jnp.bfloat16
HEAD = 64
CHUNK = 128
LANES = 128
VMEM_LIMIT = 56 * 1024 * 1024
NN = (((1,), (0,)), ((), ()))
NT = (((1,), (1,)), ((), ()))
TN = (((0,), (0,)), ((), ()))


def mm(left, right, dims=NN):
    return lax.dot_general(left, right, dims, preferred_element_type=F32)


def sigmoid(value):
    return 0.5 * jnp.tanh(0.5 * value) + 0.5


def softplus(value):
    return jnp.maximum(value, 0.0) + jnp.log1p(jnp.exp(-jnp.abs(value)))


def iota(shape, dim):
    return lax.broadcasted_iota(jnp.int32, shape, dim)


def split_two(value):
    high = value.astype(BF16)
    return high, (value - high.astype(F32)).astype(BF16)


def split_three(value):
    high = value.astype(BF16)
    rest = value - high.astype(F32)
    mid = rest.astype(BF16)
    return high, mid, (rest - mid.astype(F32)).astype(BF16)


def fold_rows(value):
    rows = value.shape[0]
    return jnp.sum(value.reshape(rows // 8, 8, value.shape[1]), 0)


def doc_of(places, e0, e1):
    return (places >= e0).astype(jnp.int32) + (places >= e1).astype(jnp.int32)


def same_behind(places, steps, e0, e1):
    crossed = ((places >= e0) & (places < e0 + steps)) | ((places >= e1) & (places < e1 + steps))
    return jnp.where(crossed, 0.0, 1.0)


def same_ahead(places, steps, e0, e1):
    crossed = ((places < e0) & (places >= e0 - steps)) | ((places < e1) & (places >= e1 - steps))
    return jnp.where(crossed, 0.0, 1.0)


def chunk_decays(log_decay, tri):
    high, mid, low = split_three(log_decay)
    cum = mm(jnp.concatenate([tri, tri, tri], 1), jnp.concatenate([high, mid, low], 0))
    return cum, cum.T


def column(values, at):
    return jnp.broadcast_to(values[:, at : at + 1], (values.shape[0], LANES))


def conv_tile(ubuf, cp, tile, rows, masks):
    lanes = slice(tile * LANES, (tile + 1) * LANES)
    summed = cp[4:5, lanes] + cp[3:4, lanes] * ubuf[8 : 8 + rows, lanes]
    for steps in (1, 2, 3):
        shifted = ubuf[8 - steps : 8 - steps + rows, lanes] * masks[steps - 1]
        summed = summed + cp[3 - steps : 4 - steps, lanes] * shifted
    return summed


def bring(out, blocks, step, sec, ten, order):
    half = out.shape[0] // 2
    mine = pl.multiple_of(sec * half, half)
    theirs = pl.multiple_of((1 - sec) * half, half)
    far = (jnp.bitwise_xor(ten, step) >> (1 - order)) & 1
    width = out.shape[1]
    for k in range(2):

        @pl.when(far == k)
        def _(k=k):
            out[pl.ds(mine, half), :] = blocks[k][0, :, :width]
            out[pl.ds(theirs, half), :] = blocks[2 + k][0, :, :width]


def piece_spec(shape, order):
    return pl.BlockSpec(
        (1,) + shape[1:], lambda i, sc: ((jnp.bitwise_xor(sc[1], i) >> order) & 1, 0, 0)
    )


def fwd_kernel(with_dot, shards, inner, state, heads, order, sc, *refs):
    pieces = refs[:4]
    refs = refs[4:]
    if shards > 1:
        parts, refs, whole_w = refs[:shards], refs[shards:-1], refs[-1]

        @pl.when(pl.program_id(0) == 0)
        def _():
            size = parts[0].shape[0]
            for k in range(shards):
                at = pl.multiple_of(((sc[4] - k) & 3) * size, size)
                whole_w[pl.ds(at, size), :] = parts[k][...]

        refs = (whole_w, *refs)
    if with_dot:
        w, cp, hp, chp, live, gno, nrm, proj, y_out, st, gated_out, stats, carry, ubuf, act = refs
    else:
        w, cp, hp, chp, live, nrm, proj, y_out, st, gated_out, stats, carry, ubuf, act = refs
    step = pl.program_id(0)
    sec, ten, e0, e1 = sc[0], sc[1], sc[2], sc[3]
    rows = nrm.shape[0]
    wide = inner + 2 * state
    tiles = wide // LANES
    pairs = inner // LANES

    @pl.when(step == 0)
    def _():
        carry[...] = jnp.zeros_like(carry)
        ubuf[0:8, :] = jnp.zeros((8, wide), F32)

    bring(nrm, pieces, step, sec, ten, order)
    proj[...] = mm(nrm[...], w[...])
    lv = live[...]
    dt_at = slice(inner + wide, inner + wide + LANES)
    offset = ten * (2 * heads) + sec * heads
    proj[:, dt_at] = pltpu.roll(proj[:, dt_at], (LANES - offset) % LANES, 1) + hp[0:1, :]
    places = rows * step + iota((rows, LANES), 0)
    masks = [same_behind(places, steps, e0, e1) for steps in (1, 2, 3)]
    for tile in range(tiles):
        lanes = slice(tile * LANES, (tile + 1) * LANES)
        at = slice(inner + tile * LANES, inner + (tile + 1) * LANES)
        u = proj[:, at] * lv
        proj[:, at] = u
        ubuf[8 : 8 + rows, lanes] = u
    for tile in range(tiles):
        lanes = slice(tile * LANES, (tile + 1) * LANES)
        pre = conv_tile(ubuf, cp, tile, rows, masks)
        act[:, lanes] = (pre * sigmoid(pre)).astype(BF16)
    ubuf[0:8, :] = ubuf[rows : rows + 8, :]

    low_half = iota((CHUNK, LANES), 1) < HEAD
    tri = (iota((CHUNK, CHUNK), 0) >= iota((CHUNK, CHUNK), 1)).astype(F32).astype(BF16)
    gated_sq = []
    gated_dot = []
    for c in range(rows // CHUNK):
        r0 = c * CHUNK
        at = slice(r0, r0 + CHUNK)
        base = rows * step + r0
        t_at = base + iota((CHUNK, CHUNK), 0)
        s_at = base + iota((CHUNK, CHUNK), 1)
        id_t = doc_of(t_at, e0, e1)
        usable = (t_at >= s_at) & (id_t == doc_of(s_at, e0, e1))
        id_prev = doc_of(base - 1, e0, e1)
        id_end = doc_of(base + CHUNK - 1, e0, e1)
        from_prev = jnp.where(id_t == id_prev, 1.0, 0.0)
        tail_same = jnp.where(id_t == id_end, 1.0, 0.0)
        linked = jnp.where(id_end == id_prev, 1.0, 0.0).astype(F32)
        dt = softplus(proj[at, dt_at]) * live[at, :]
        cum, cum_t = chunk_decays(dt * hp[1:2, :], tri)
        b_in = act[at, inner : inner + state]
        c_in = act[at, inner + state : wide]
        scores = jnp.where(usable, mm(c_in, b_in, NT), 0.0)
        sq = jnp.zeros((CHUNK, LANES), F32)
        rd = jnp.zeros((CHUNK, LANES), F32)
        for k in range(pairs):
            lanes = slice(k * LANES, (k + 1) * LANES)
            mixed, cums = [], []
            for h in (2 * k, 2 * k + 1):
                cum_col = column(cum, h)
                cums.append(cum_col)
                decay = jnp.exp(jnp.minimum(cum_col - cum_t[h : h + 1, :], 0.0))
                mixed.append((decay * scores).astype(BF16))
            cum_e = jnp.where(low_half, cums[0], cums[1])
            dt_e = jnp.where(low_half, column(dt, 2 * k), column(dt, 2 * k + 1))
            x_in = act[at, lanes].astype(F32)
            xdt = x_in * dt_e
            both = jnp.concatenate([jnp.where(low_half, xdt, 0.0), jnp.where(low_half, 0.0, xdt)], 0)
            within = mm(jnp.concatenate(mixed, 1), both.astype(BF16))
            old = carry[:, lanes]
            old_low = old.astype(BF16)
            st[c, :, lanes] = old_low
            across = mm(c_in, old_low) * (jnp.exp(cum_e) * from_prev)
            cum_end = cum_e[CHUNK - 1 : CHUNK, :]
            to_end = jnp.exp(cum_end - cum_e) * tail_same
            added = mm(b_in, (xdt * to_end).astype(BF16), TN)
            carry[:, lanes] = old * (jnp.exp(cum_end) * linked) + added
            y = within + across + chp[0:1, lanes] * x_in
            y_out[at, lanes] = y
            gate = proj[at, lanes]
            gated = y * (gate * sigmoid(gate))
            gated_out[at, lanes] = gated
            sq = sq + gated * gated
            if with_dot:
                rd = rd + gated * chp[1:2, lanes] * gno[at, lanes]
        gated_sq.append(sq)
        gated_dot.append(rd)
    ones = jnp.ones((8, LANES), F32)
    exact = partial(
        lax.dot_general,
        dimension_numbers=NT,
        precision=lax.Precision.HIGHEST,
        preferred_element_type=F32,
    )
    total = exact(ones, jnp.concatenate(gated_sq, 0))
    if with_dot:
        dots = exact(ones, jnp.concatenate(gated_dot, 0))
        total = jnp.where(iota((8, rows), 0) == 0, total, dots)
    stats[...] = total


def call(kernel, name, scalars, grid, ins, outs, scratch, deps, flops, extra, moved):
    count = len(ins)
    specs = [spec for spec, _ in ins] + [pl.BlockSpec(memory_space=pl.ANY)] * len(deps)

    def body(sc, *refs):
        kernel(sc, *refs[:count], *refs[count + len(deps) :])

    return pl.pallas_call(
        body,
        out_shape=tuple(jax.ShapeDtypeStruct(shape, kind) for _, shape, kind in outs),
        grid_spec=pltpu.PrefetchScalarGridSpec(
            num_scalar_prefetch=1,
            grid=grid,
            in_specs=specs,
            out_specs=tuple(spec for spec, _, _ in outs),
            scratch_shapes=scratch,
        ),
        compiler_params=pltpu.CompilerParams(
            dimension_semantics=("arbitrary",) * len(grid), vmem_limit_bytes=VMEM_LIMIT
        ),
        cost_estimate=pl.CostEstimate(flops=flops, transcendentals=extra, bytes_accessed=moved),
        name=name,
    )(scalars, *[operand for _, operand in ins], *deps)


def whole(shape):
    return pl.BlockSpec(shape, lambda i, sc: (0,) * len(shape))


def fixed(array):
    return (whole(array.shape), array)


def bring_coef(out, blocks, width, step, sec, ten, order):
    half = out.shape[0] // 2
    mine = pl.multiple_of(sec * half, half)
    theirs = pl.multiple_of((1 - sec) * half, half)
    far = (jnp.bitwise_xor(ten, step) >> (1 - order)) & 1
    for k in range(2):

        @pl.when(far == k)
        def _(k=k):
            for at, block in ((mine, blocks[k]), (theirs, blocks[2 + k])):
                parts = block[0, :, width:].astype(F32)
                total = parts[:, 0:1] + parts[:, 1:2] + parts[:, 2:3]
                out[pl.ds(at, half), :] = jnp.broadcast_to(total, (half, LANES))


def turn_kernel(count, sc, *refs):
    parts, wo_t, w_t, wo = refs[:count], *refs[count:]
    if count == 1:
        w_t[...] = parts[0][...].T
    else:
        pick = (sc[4] - pl.program_id(0)) & 3
        for k in range(count):

            @pl.when(pick == k)
            def _(k=k):
                w_t[...] = parts[k][...].T

    wo[...] = wo_t[...].T


def run_turn(scalars, parts, wo_t, deps):
    depth, cols = wo_t.shape[0], parts[0].shape[1]
    rows = depth // 4
    by_row = lambda n: pl.BlockSpec((rows, n), lambda i, sc: (i, 0))
    by_col = lambda n: pl.BlockSpec((n, rows), lambda i, sc: (0, i))
    if len(parts) == 1:
        ins = [(by_row(cols), parts[0])]
    else:
        ins = [fixed(part) for part in parts]
    return call(
        partial(turn_kernel, len(parts)), "turn_weights", scalars, (4,),
        ins + [(by_row(wo_t.shape[1]), wo_t)],
        [
            (by_col(cols), (cols, depth), BF16),
            (by_col(wo_t.shape[1]), (wo_t.shape[1], depth), BF16),
        ],
        [], deps, 4 * 1024**3, 0, 10 * 1024 * 1024,
    )


def outer_kernel(count, start, sc, *refs):
    total = mm(refs[0][...], refs[1][...], TN)
    for k in range(1, count):
        total = total + mm(refs[2 * k][...], refs[2 * k + 1][...], TN)
    if start:
        total = total + refs[2 * count][...]
    refs[-1][...] = total


def run_outer(scalars, pairs, start, tall, deps):
    depth = pairs[0][0].shape[0]
    rows, cols = pairs[0][0].shape[1], pairs[0][1].shape[1]
    if tall:
        tile, grid = 3 * LANES, (rows // (3 * LANES),)
        cut = pl.BlockSpec((depth, tile), lambda i, sc: (0, i))
        out = pl.BlockSpec((tile, cols), lambda i, sc: (i, 0))
        ins = [item for a, b in pairs for item in ((cut, a), fixed(b))]
    else:
        tile, grid = 4 * LANES, (cols // (4 * LANES),)
        cut = pl.BlockSpec((depth, tile), lambda i, sc: (0, i))
        out = pl.BlockSpec((rows, tile), lambda i, sc: (0, i))
        ins = [item for a, b in pairs for item in (fixed(a), (cut, b))]
    if start is not None:
        ins.append((out, start))
    return call(
        partial(outer_kernel, len(pairs), start is not None), "outer_rows", scalars, grid, ins,
        [(out, (rows, cols), F32)], [], deps, 9 * 1024**3 * len(pairs), 0, 16 * 1024 * 1024,
    )[0]


def join_kernel(sc, mine, theirs, out):
    half = mine.shape[1]
    out[0, pl.ds(sc[0] * half, half), 0, :] = mine[0]
    out[0, pl.ds((1 - sc[0]) * half, half), 0, :] = theirs[0]


def run_join(scalars, mine, theirs):
    count, half, width = mine.shape
    spec = pl.BlockSpec((1, half, width), lambda i, sc: (i, 0, 0))
    return call(
        join_kernel, "join_rows", scalars, (count,), [(spec, mine), (spec, theirs)],
        [
            (
                pl.BlockSpec((1, 2 * half, 1, width), lambda i, sc: (i, 0, 0, 0)),
                (count, 2 * half, 1, width),
                F32,
            )
        ],
        [], [], 0, 0, 16 * 1024 * 1024,
    )[0]


def weave_kernel(sc, mine, theirs, out):
    size = mine.shape[1] // 2
    own = pl.ds(pl.multiple_of(sc[0] * size, LANES), size)
    other = pl.ds(pl.multiple_of((1 - sc[0]) * size, LANES), size)
    for k in range(2):
        out[:, k, own] = mine[:, k * size : (k + 1) * size]
        out[:, k, other] = theirs[:, k * size : (k + 1) * size]


def run_weave(scalars, mine, theirs):
    depth, width = mine.shape
    rows = depth if depth % 32 else depth // 4
    spec = pl.BlockSpec((rows, width), lambda i, sc: (i, 0))
    return call(
        weave_kernel, "weave_cols", scalars, (depth // rows,), [(spec, mine), (spec, theirs)],
        [(pl.BlockSpec((rows, 2, width), lambda i, sc: (i, 0, 0)), (depth, 2, width), F32)],
        [], [], 0, 0, 5 * 1024 * 1024,
    )[0]


def run_fwd(scalars, pieces, order, w, cp, hp, chp, live, gno, inner, state, heads, deps):
    half, width = pieces[0].shape[1:]
    rows = 2 * half
    length = live.shape[0]
    steps = length // rows
    cols = w[0].shape[1]
    chunks = rows // CHUNK
    by_row = lambda n: pl.BlockSpec((rows, n), lambda i, sc: (i, 0))
    ins = [(piece_spec(piece.shape, order), piece) for piece in pieces]
    ins += [fixed(part) for part in w]
    ins += [fixed(cp), fixed(hp), fixed(chp), (by_row(LANES), live)]
    joined = [pltpu.VMEM((width, cols), BF16)] if len(w) > 1 else []
    if gno is not None:
        ins.append((by_row(inner), gno))
    return call(
        partial(fwd_kernel, gno is not None, len(w), inner, state, heads, order), "layer_fwd", scalars, (steps,),
        ins,
        [
            (by_row(width), (length, width), BF16),
            (by_row(cols), (length, cols), F32),
            (by_row(inner), (length, inner), F32),
            (pl.BlockSpec((chunks, state, inner), lambda i, sc: (i, 0, 0)), (length // CHUNK, state, inner), BF16),
            (by_row(inner), (length, inner), F32),
            (pl.BlockSpec((8, rows), lambda i, sc: (0, i)), (8, length), F32),
        ],
        [
            pltpu.VMEM((state, inner), F32),
            pltpu.VMEM((rows + 8, inner + 2 * state), F32),
            pltpu.VMEM((rows, inner + 2 * state), BF16),
        ]
        + joined,
        deps, 24 * 1024**3, length * inner * 8, 24 * 1024**2,
    )


def scale_kernel(inner_width, sc, gated, sa, sb, chp, no_out, send, rc):
    rows = gated.shape[0]
    half = rows // 2
    theirs = pl.multiple_of((1 - sc[0]) * half, half)
    total = sa[...] + sb[...]
    inv = lax.rsqrt(total / inner_width + EPS)
    coef = jnp.concatenate([total[1:8], total[0:1]], 0) * (inv * inv * inv) / inner_width
    both = jnp.where(iota(total.shape, 0) == 0, inv, pltpu.roll(coef, 1, 0))
    for c in range(rows // CHUNK):
        at = slice(c * CHUNK, (c + 1) * CHUNK)
        cols = jnp.concatenate([both[:, at]] * (CHUNK // 8), 0).T
        rc[at, :] = cols
        col = column(cols, 0)
        for k in range(gated.shape[1] // LANES):
            lanes = slice(k * LANES, (k + 1) * LANES)
            no_out[at, lanes] = (gated[at, lanes] * col * chp[1:2, lanes]).astype(BF16)
    send[0] = no_out[pl.ds(theirs, half), :]


def run_scale(scalars, gated, sa, sb, chp, rows, inner_width, deps):
    length, inner = gated.shape
    steps = length // rows
    by_row = lambda n: pl.BlockSpec((rows, n), lambda i, sc: (i, 0))
    by_lane = pl.BlockSpec((8, rows), lambda i, sc: (0, i))
    return call(
        partial(scale_kernel, inner_width), "scale_rows", scalars, (steps,),
        [(by_row(inner), gated), (by_lane, sa), (by_lane, sb), fixed(chp)],
        [
            (by_row(inner), (length, inner), BF16),
            (pl.BlockSpec((1, rows // 2, inner), lambda i, sc: (i, 0, 0)), (steps, rows // 2, inner), BF16),
            (by_row(LANES), (length, LANES), F32),
        ],
        [], deps, 4 * 1024**3, 0, 8 * 1024**2,
    )


def bwd_kernel(inner, state, heads, order, sc, *refs):
    if order is None:
        gno, cc, proj, halo, y_in, st, rc, live, cp, hp, chp = refs[:11]
        refs = refs[11:]
    else:
        pieces, wo_t = refs[:4], refs[4]
        proj, halo, y_in, st, rc, live, cp, hp, chp = refs[5:14]
        gout, gno, cc = refs[14], refs[-2], refs[-1]
        refs = refs[15:-2]
    gz, gzsend, gpack, dstate, ubuf, gbuf, acc_c, acc_h, acc_n, acc_d = refs
    step = pl.program_id(0)
    steps = pl.num_programs(0)
    block = steps - 1 - step
    sec, ten, e0, e1 = sc[0], sc[1], sc[2], sc[3]
    offset = ten * (2 * heads) + sec * heads
    rows = y_in.shape[0]
    half = rows // 2
    wide = inner + 2 * state
    tiles = wide // LANES
    pairs = inner // LANES
    theirs = pl.multiple_of((1 - sec) * half, half)

    @pl.when(step == 0)
    def _():
        dstate[...] = jnp.zeros_like(dstate)
        gbuf[rows : rows + 8, :] = jnp.zeros((8, wide), F32)
        acc_c[...] = jnp.zeros_like(acc_c)
        acc_h[...] = jnp.zeros_like(acc_h)
        acc_n[...] = jnp.zeros_like(acc_n)
        acc_d[...] = jnp.zeros_like(acc_d)

    if order is not None:
        bring(gout, pieces, block, sec, ten, order)
        bring_coef(cc, pieces, gout.shape[1], block, sec, ten, order)
        gno[...] = mm(gout[...], wo_t[...])

    ubuf[0:8, :] = jnp.where(block == 0, 0.0, halo[:, inner : inner + wide])
    ubuf[8 : 8 + rows, :] = proj[:, inner : inner + wide]
    places = rows * block + iota((rows, LANES), 0)
    masks = [same_behind(places, steps_, e0, e1) for steps_ in (1, 2, 3)]

    low_half = iota((CHUNK, LANES), 1) < HEAD
    row_at = iota((CHUNK, CHUNK), 0)
    col_at = iota((CHUNK, CHUNK), 1)
    tri = (row_at >= col_at).astype(F32).astype(BF16)
    tri_rev = (row_at <= col_at).astype(F32).astype(BF16)
    tri_strict = (row_at > col_at).astype(F32).astype(BF16)
    sums = jnp.concatenate([tri_rev, tri_rev, tri_strict, tri_strict], 1)
    to_head = [
        (iota((LANES, LANES), 1) == 2 * k + (iota((LANES, LANES), 0) >= HEAD).astype(jnp.int32))
        .astype(F32)
        .astype(BF16)
        for k in range(pairs)
    ]

    for c in reversed(range(rows // CHUNK)):
        r0 = c * CHUNK
        at = slice(r0, r0 + CHUNK)
        cmasks = [m[at, :] for m in masks]
        acts, slopes = [], []
        for tile in range(tiles):
            lanes = slice(tile * LANES, (tile + 1) * LANES)
            pre = cp[4:5, lanes] + cp[3:4, lanes] * ubuf[8 + r0 : 8 + r0 + CHUNK, lanes]
            for n in (1, 2, 3):
                shifted = ubuf[8 + r0 - n : 8 + r0 - n + CHUNK, lanes] * cmasks[n - 1]
                pre = pre + cp[3 - n : 4 - n, lanes] * shifted
            sig = sigmoid(pre)
            acts.append((pre * sig).astype(BF16))
            slopes.append(sig * (1.0 + pre * (1.0 - sig)))
        b_in, c_in = acts[pairs], acts[pairs + 1]
        base = rows * block + r0
        id_s = doc_of(base + row_at, e0, e1)
        usable = (row_at <= col_at) & (id_s == doc_of(base + col_at, e0, e1))
        id_prev = doc_of(base - 1, e0, e1)
        id_end = doc_of(base + CHUNK - 1, e0, e1)
        from_prev = jnp.where(id_s == id_prev, 1.0, 0.0)
        tail_same = jnp.where(id_s == id_end, 1.0, 0.0)
        linked = jnp.where(id_end == id_prev, 1.0, 0.0).astype(F32)
        lv = live[at, :]
        dt_in = proj[at, inner + wide : inner + wide + LANES]
        dt = softplus(dt_in) * lv
        log_decay = dt * hp[1:2, :]
        cum, cum_t = chunk_decays(log_decay, tri)
        scores = jnp.where(usable, mm(b_in, c_in, NT), 0.0)
        inv = column(rc[at, :], 0)
        coef = column(cc[at, :], 1)
        d_scores = jnp.zeros((CHUNK, CHUNK), F32)
        gb = jnp.zeros((CHUNK, state), F32)
        gc = jnp.zeros((CHUNK, state), F32)
        r1 = jnp.zeros((CHUNK, LANES), F32)
        r2 = jnp.zeros((CHUNK, LANES), F32)
        r3 = jnp.zeros((CHUNK, LANES), F32)
        kept = jnp.zeros((8, LANES), F32)
        for k in range(pairs):
            lanes = slice(k * LANES, (k + 1) * LANES)
            gate = proj[at, lanes]
            sig = sigmoid(gate)
            silu = gate * sig
            y = y_in[at, lanes]
            gated = y * silu
            g_no = gno[at, lanes]
            gain = chp[1:2, lanes]
            skip = chp[0:1, lanes]
            scaled = gated * inv
            acc_n[:, lanes] += fold_rows(g_no * scaled)
            gg = inv * (g_no * gain) - gated * coef
            gy = gg * silu
            gz[at, lanes] = (gg * y * (sig * (1.0 + gate * (1.0 - sig)))).astype(BF16)
            x_in = acts[k].astype(F32)
            acc_d[:, lanes] += fold_rows(gy * x_in)
            dt_e = jnp.where(low_half, column(dt, 2 * k), column(dt, 2 * k + 1))
            gy_b = gy.astype(BF16)
            gy_f = gy_b.astype(F32)
            xdt_b = (x_in * dt_e).astype(BF16)
            xdt_f = xdt_b.astype(F32)
            gy_halves = [jnp.where(low_half, gy_f, 0.0).astype(BF16), jnp.where(low_half, 0.0, gy_f).astype(BF16)]
            mixed, cums = [], []
            for n in (0, 1):
                h = 2 * k + n
                cum_col = column(cum, h)
                cums.append(cum_col)
                decay = jnp.exp(jnp.minimum(cum_t[h : h + 1, :] - cum_col, 0.0))
                mixed.append((decay * scores).astype(BF16))
                d_scores = d_scores + decay * mm(xdt_b, gy_halves[n], NT)
            cum_e = jnp.where(low_half, cums[0], cums[1])
            gx_in = mm(jnp.concatenate(mixed, 1), jnp.concatenate(gy_halves, 0))
            cum_end = cum_e[CHUNK - 1 : CHUNK, :]
            to_end = jnp.exp(cum_end - cum_e) * tail_same
            entering = jnp.exp(cum_e) * from_prev
            s_in = st[c, :, lanes]
            d_out = dstate[:, lanes]
            d_out_b = d_out.astype(BF16)
            gx_st = mm(b_in, d_out_b) * to_end
            gb = gb + mm((xdt_f * to_end).astype(BF16), d_out_b, NT)
            gye = (gy * entering).astype(BF16)
            gc = gc + mm(gye, s_in, NT)
            dec = jnp.exp(cum_end) * linked
            prod = fold_rows(s_in.astype(F32) * d_out) * dec
            p_hi, p_lo = split_two(prod)
            kept = kept + mm(p_hi, to_head[k]) + mm(p_lo, to_head[k])
            dstate[:, lanes] = d_out * dec + mm(c_in, gye, TN)
            gx = gx_in + gx_st
            t_hi, t_lo = split_two(gy_f * (y - skip * x_in) - xdt_f * gx_in)
            pair2 = jnp.concatenate([to_head[k], to_head[k]], 0)
            r1 = r1 + mm(jnp.concatenate([t_hi, t_lo], 1), pair2)
            t_hi, t_lo = split_two(x_in * gx)
            r2 = r2 + mm(jnp.concatenate([t_hi, t_lo], 1), pair2)
            t_hi, t_lo = split_two(x_in * gx_st)
            r3 = r3 + mm(jnp.concatenate([t_hi, t_lo], 1), pair2)
            gbuf[at, lanes] = (gx * dt_e + gy * skip) * slopes[k]
        d_scores = jnp.where(usable, d_scores, 0.0).astype(BF16)
        gb = gb + mm(d_scores, c_in)
        gc = gc + mm(d_scores, b_in, TN)
        for n in range(state // LANES):
            b_at = slice(inner + n * LANES, inner + (n + 1) * LANES)
            c_at = slice(inner + state + n * LANES, inner + state + (n + 1) * LANES)
            gbuf[at, b_at] = gb * slopes[pairs]
            gbuf[at, c_at] = gc * slopes[pairs + 1]
        a_hi, a_lo = split_two(r1)
        b_hi, b_lo = split_two(dt * r3)
        g_ld = mm(sums, jnp.concatenate([a_hi, a_lo, b_hi, b_lo], 0)) + jnp.sum(kept, 0, keepdims=True)
        g_dt = (r2 + g_ld * hp[1:2, :]) * (sigmoid(dt_in) * lv)
        acc_h[0:8, :] += fold_rows(g_dt)
        acc_h[8:16, :] += fold_rows(g_ld * log_decay)
        gz[at, inner + wide : inner + wide + LANES] = pltpu.roll(g_dt, offset, 1).astype(BF16)

    ahead = [same_ahead(places, n, e0, e1) for n in (1, 2, 3)]
    lv = live[...]
    for tile in range(tiles):
        lanes = slice(tile * LANES, (tile + 1) * LANES)
        gp = gbuf[0:rows, lanes]
        gu = cp[3:4, lanes] * gp
        acc_c[24:32, lanes] += fold_rows(gp * ubuf[8 : 8 + rows, lanes])
        acc_c[32:40, lanes] += fold_rows(gp)
        for n in (1, 2, 3):
            gu = gu + cp[3 - n : 4 - n, lanes] * (gbuf[n : n + rows, lanes] * ahead[n - 1])
            shifted = ubuf[8 - n : 8 - n + rows, lanes] * masks[n - 1]
            acc_c[8 * (3 - n) : 8 * (4 - n), lanes] += fold_rows(gp * shifted)
        at = slice(inner + tile * LANES, inner + (tile + 1) * LANES)
        gz[:, at] = (gu * lv).astype(BF16)
    gbuf[rows : rows + 8, :] = gbuf[0:8, :]
    gzsend[0] = gz[pl.ds(theirs, half), :]

    @pl.when(step == steps - 1)
    def _():
        gpack[...] = jnp.zeros_like(gpack)
        own = pl.ds(pl.multiple_of(sec * inner, LANES), inner)
        for n in range(5):
            line = jnp.sum(acc_c[8 * n : 8 * n + 8, :], 0, keepdims=True)
            gpack[1 + n : 2 + n, own] = line[:, :inner]
            gpack[1 + n : 2 + n, 2 * inner : 2 * inner + 2 * state] = line[:, inner:]
        gpack[6:7, own] = jnp.sum(acc_n[...], 0, keepdims=True)
        skips = jnp.zeros((8, LANES), F32)
        for k in range(pairs):
            d_hi, d_mid, d_low = split_three(acc_d[:, k * LANES : (k + 1) * LANES])
            skips = skips + (mm(d_hi, to_head[k]) + mm(d_mid, to_head[k]) + mm(d_low, to_head[k]))
        heads_sums = [acc_h[0:8, :], acc_h[8:16, :], skips]
        for n in range(3):
            line = jnp.sum(pltpu.roll(heads_sums[n], sec * heads, 1), 0, keepdims=True)
            gpack[7 + n : 8 + n, 0:LANES] = line


def run_bwd(scalars, rows_in, order, proj, y, st, rc, live, cp, hp, chp, inner, state, heads, rows, width, deps):
    length, cols = proj.shape
    steps = length // rows
    half = rows // 2
    chunks = rows // CHUNK
    wide = inner + 2 * state
    back = lambda i: steps - 1 - i
    by_row = lambda n: pl.BlockSpec((rows, n), lambda i, sc: (back(i), 0))
    halo = pl.BlockSpec((8, cols), lambda i, sc: (jnp.maximum(back(i) * (rows // 8) - 1, 0), 0))
    scratch = [
        pltpu.VMEM((state, inner), F32),
        pltpu.VMEM((rows + 8, wide), F32),
        pltpu.VMEM((rows + 8, wide), F32),
        pltpu.VMEM((40, wide), F32),
        pltpu.VMEM((16, LANES), F32),
        pltpu.VMEM((8, inner), F32),
        pltpu.VMEM((8, inner), F32),
    ]
    if order is None:
        gno, cc = rows_in
        ins, outs = [(by_row(inner), gno), (by_row(LANES), cc)], []
    else:
        pieces, wo_t = rows_in
        shape = pieces[0].shape
        spec = pl.BlockSpec(
            (1,) + shape[1:],
            lambda i, sc: ((jnp.bitwise_xor(sc[1], back(i)) >> order) & 1, 0, 0),
        )
        ins = [(spec, piece) for piece in pieces] + [fixed(wo_t)]
        outs = [(by_row(width), (length, width), BF16)]
        scratch += [pltpu.VMEM((rows, inner), F32), pltpu.VMEM((rows, LANES), F32)]
    ins += [
        (by_row(cols), proj),
        (halo, proj),
        (by_row(inner), y),
        (pl.BlockSpec((chunks, state, inner), lambda i, sc: (back(i), 0, 0)), st),
        (by_row(LANES), rc),
        (by_row(LANES), live),
        fixed(cp),
        fixed(hp),
        fixed(chp),
    ]
    outs += [
        (by_row(cols), (length, cols), BF16),
        (pl.BlockSpec((1, half, cols), lambda i, sc: (back(i), 0, 0)), (steps, half, cols), BF16),
        (whole((16, width)), (16, width), F32),
    ]
    return call(
        partial(bwd_kernel, inner, state, heads, order), "layer_bwd", scalars, (steps,),
        ins, outs, scratch, deps, 28 * 1024**3, length * inner * 12, 24 * 1024**2,
    )


def gn_kernel(order, sc, *refs):
    pieces, w, gno, gout = refs[:4], refs[4], refs[5], refs[6]
    step, sec, ten = pl.program_id(0), sc[0], sc[1]
    bring(gout, pieces, step, sec, ten, order)
    if len(refs) > 7:
        bring_coef(refs[7], pieces, gout.shape[1], step, sec, ten, order)
    gno[...] = mm(gout[...], w[...])


def run_gn(scalars, pieces, order, w, width, deps):
    half, cols = pieces[0].shape[1:]
    inner = w.shape[1]
    rows, length = 2 * half, 8 * half
    by_row = lambda n: pl.BlockSpec((rows, n), lambda i, sc: (i, 0))
    outs = [(by_row(inner), (length, inner), F32), (by_row(width), (length, width), BF16)]
    if cols > width:
        outs.append((by_row(LANES), (length, LANES), F32))
    return call(
        partial(gn_kernel, order), "grad_rows", scalars, (length // rows,),
        [(piece_spec(piece.shape, order), piece) for piece in pieces] + [fixed(w)],
        outs, [], deps, 8 * 1024**3, 0, 18 * 1024**2,
    )


def half_kernel(axis, sc, kept, got, wa, wb, own, near, far):
    ten = sc[1]
    groups = [jnp.bitwise_xor(ten, k) for k in (0, 3 - axis, axis, 3)]
    half = own.shape[0]
    left = jnp.concatenate([kept[g, 0] for g in groups], 0)
    right = jnp.concatenate([got[g] for g in groups], 0)
    total = mm(jnp.concatenate([left, right], 1), jnp.concatenate([wa[...], wb[...]], 0))
    own[...] = total[:half]
    near[...] = total[half : 2 * half]
    far[0] = total[2 * half : 3 * half].astype(BF16)
    far[1] = total[3 * half :].astype(BF16)


def run_half(scalars, full, got, wa, wb, axis, deps):
    groups, half, depth = got.shape
    width = wa.shape[1]
    tile = 4 * LANES
    w_spec = pl.BlockSpec((depth, tile), lambda i, sc: (0, i))
    part = pl.BlockSpec((half, tile), lambda i, sc: (0, i))
    return call(
        partial(half_kernel, axis), "half_rows", scalars, (width // tile,),
        [
            (
                pl.BlockSpec((groups, 1, half, depth), lambda i, sc: (0, sc[0], 0, 0)),
                full.reshape(groups, 2, half, depth),
            ),
            fixed(got),
            (w_spec, wa),
            (w_spec, wb),
        ],
        [
            (part, (half, width), F32),
            (part, (half, width), F32),
            (pl.BlockSpec((2, half, tile), lambda i, sc: (0, 0, i)), (2, half, width), BF16),
        ],
        [], deps, 8 * 1024**3, 0, 10 * 1024**2,
    )


def norm_kernel(x, gain, out):
    v = x[...].astype(F32)
    inv = lax.rsqrt(jnp.mean(v * v, -1, keepdims=True) + EPS)
    out[...] = (v * inv * gain[0:1, :]).astype(BF16)


def owner_kernel(final, own, far, near, x, gain, *outs):
    total = own[...] + far[0].astype(F32) + near[...].astype(F32)
    out = x[...].astype(F32) + total
    if final:
        outs[0][...] = out
        return
    h1, normed, kept = outs
    low = out.astype(BF16)
    h1[...] = low
    kept[...] = total
    v = low.astype(F32)
    inv = lax.rsqrt(jnp.mean(v * v, -1, keepdims=True) + EPS)
    normed[...] = (v * inv * gain[0:1, :]).astype(BF16)


def owner_back_kernel(last, inner_width, own, far, near, v_in, g_in, gain, *refs):
    g = own[...] + far[0].astype(F32) + near[...].astype(F32)
    v = v_in[...].astype(F32)
    width = v.shape[1]
    inv = lax.rsqrt(jnp.mean(v * v, -1, keepdims=True) + EPS)
    scaled = v * inv
    p = g * gain[0:1, :]
    out = g_in[:, :width].astype(F32) + inv * (p - scaled * jnp.mean(p * scaled, -1, keepdims=True))
    if last:
        g_v, ggain = refs
        g_v[...] = out
    else:
        kept, rcol, g_v, ggain = refs
        low = out.astype(BF16)
        g_v[:, :width] = low
        r = rcol[:, 0:1]
        coef = r * r * jnp.sum(low.astype(F32) * kept[...], -1, keepdims=True) / inner_width
        shape = (v.shape[0], LANES)
        high, mid, small = [
            jnp.broadcast_to(part.astype(F32), shape) for part in split_three(coef)
        ]
        lane = iota(shape, 1)
        parts = jnp.where(lane == 0, high, jnp.where(lane == 1, mid, small))
        g_v[:, width:] = parts.astype(BF16)
    ggain[...] = jnp.zeros_like(ggain)
    ggain[0:1, :] = jnp.sum(g * scaled, 0, keepdims=True)


def run_plain(kernel, name, out_shape, operands, deps):
    count = len(operands)
    vmem = pl.BlockSpec(memory_space=pltpu.VMEM)

    def body(*refs):
        kernel(*refs[:count], *refs[count + len(deps) :])

    return pl.pallas_call(
        body,
        in_specs=[vmem] * count + [pl.BlockSpec(memory_space=pl.ANY)] * len(deps),
        out_shape=out_shape,
        compiler_params=pltpu.CompilerParams(vmem_limit_bytes=VMEM_LIMIT),
        cost_estimate=pl.CostEstimate(
            flops=3 * 1024**3, transcendentals=0, bytes_accessed=6 * 1024**2
        ),
        name=name,
    )(*operands, *deps)


def across(value, step):
    count = lax.axis_size("tensor")
    return lax.ppermute(value, "tensor", [(i, i ^ step) for i in range(count)])


def swap(value):
    return lax.ppermute(value, "section", [(0, 1), (1, 0)])


def reach(value, order):
    return value, across(value, 1 + order)


def widen(pair, order, *waits):
    near = jnp.stack([after(pair[0], *waits), pair[1]])
    return near, across(near, 2 - order)


def share(near, far):
    return [near, far, swap(near), swap(far)]


def spread(value, order):
    return share(*widen(reach(value, order), order))


def hand(outs, order):
    return outs[0], outs[1], across(outs[2], 2 - order)


def settle(held, order, *waits):
    own, near, far = held
    send = (after(near, *waits) + far[1].astype(F32)).astype(BF16)
    return own, far, across(send, 1 + order)


def all_tensor(value):
    value = value + across(value, 1)
    return value + across(value, 2)


def cycle(value, steps):
    count = lax.axis_size("dp")
    return lax.ppermute(value, "dp", [(i, (i + steps) % count) for i in range(count)])


def pieces_dp(value):
    if lax.axis_size("dp") != 4:
        return [lax.all_gather(value, "dp", axis=0, tiled=True)]
    return [value] + [cycle(value, k) for k in (1, 2, 3)]


def gather_dp(value):
    got = pieces_dp(value)
    if len(got) == 1:
        return got[0]
    at = lax.axis_index("dp")
    shards = [lax.select_n(at, *[got[(i - j) % 4] for i in range(4)]) for j in range(4)]
    return jnp.concatenate(shards, 0)


def trade(value, bit):
    return lax.ppermute(value, "dp", [(i, i ^ bit) for i in range(4)])


def deal_one(value):
    at = lax.axis_index("dp")
    odd = (at & 1) == 1
    shards = value.reshape(4, value.shape[0] // 4, value.shape[1])
    kept = jnp.where(odd, shards[1::2], shards[0::2])
    sent = jnp.where(odd, shards[0::2], shards[1::2]).astype(BF16)
    return sent, kept, trade(sent, 1)


def deal_two(kept, got):
    high = lax.axis_index("dp") >= 2
    both = kept + got.astype(F32)
    sent = jnp.where(high, both[0], both[1]).astype(BF16)
    return jnp.where(high, both[1], both[0]), trade(sent, 2)


def scatter_dp(value):
    return lax.psum_scatter(value, "dp", scatter_dimension=0, tiled=True)


def sum_dp(value):
    if lax.axis_size("dp") != 4:
        return lax.psum(value, "dp")
    return value + cycle(value, 1) + cycle(value, 2) + cycle(value, 3)


def after(value, *waits):
    return lax.optimization_barrier((value, *waits))[0]


def on_device(
    x_in,
    d_out,
    doc_lengths,
    token_mask,
    gain_in,
    w_zx,
    w_bcdt,
    conv_x,
    conv_bc,
    dt_bias,
    a_log,
    d_skip,
    gain_inner,
    w_out,
):
    micro_count, local_rows, _, width = x_in.shape
    length = token_mask.shape[1]
    half = local_rows // 2
    rows = local_rows
    inner = conv_x.shape[2] // 2
    heads = dt_bias.shape[1] // 2
    state = conv_bc.shape[2] // 2
    chip_inner = 2 * inner
    full_inner = chip_inner * lax.axis_size("tensor")
    sec = lax.axis_index("section")
    ten = lax.axis_index("tensor")
    first = sec == 0
    micros = range(micro_count)

    def by_layer(own, other):
        return [jnp.where(first, own, other), jnp.where(first, other, own)]

    pad_to = lambda v, n: jnp.pad(v, ((0, 0), (0, n - v.shape[1])))
    pack = jnp.concatenate(
        [
            gain_in,
            pad_to(jnp.concatenate([conv_x[0], conv_bc[0]], 1), width),
            pad_to(gain_inner, width),
            pad_to(jnp.concatenate([dt_bias, a_log, d_skip], 1), width),
        ],
        0,
    )
    packs = by_layer(pack, swap(pack))
    gains = [jnp.broadcast_to(p[0:1], (8, width)) for p in packs]

    gate_w, x_w = w_zx[0, :, 0, :], w_zx[0, :, 1, :]
    ends = [jnp.concatenate([gate_w[:, at], x_w[:, at]], 1) for at in (slice(inner), slice(inner, None))]
    zx_own, zx_send = by_layer(*ends)
    bc_own = pad_to(w_bcdt[0], 2 * state + LANES)
    got = swap(jnp.concatenate([zx_send, bc_own], 1))
    zx_shards = by_layer(jnp.concatenate([zx_own, bc_own], 1), got)
    wo_own, wo_send = by_layer(w_out[0, :inner].T, w_out[0, inner:].T)
    wo_shards = by_layer(wo_own, swap(wo_send))
    first_parts = pieces_dp(zx_shards[0])

    rows_at = lambda v, m: jnp.where(first, v[m, :half, 0, :], v[m, half:, 0, :])
    xs = [rows_at(x_in, m) for m in micros]
    gs = [rows_at(d_out, m) for m in micros]
    wide = lambda kind, n=0: jax.ShapeDtypeStruct((half, width + n), kind)
    small = jax.ShapeDtypeStruct((16, width), F32)
    pieces0 = [
        widen(reach(run_plain(norm_kernel, "norm_rows", wide(BF16), (xs[m], gains[0]), ()), 0), 0)
        for m in micros
    ]
    wide0 = pieces0
    pieces0 = [share(wide0[0][0], after(wide0[0][1], *first_parts[1:2]))]
    later = lambda v: lax.all_gather(after(v, *first_parts), "dp", axis=0, tiled=True)
    wo_t0, wo_t1 = later(wo_shards[0]), later(wo_shards[1])
    w1 = later(zx_shards[1])

    scalars, lives = [], []
    for m in micros:
        e0 = doc_lengths[m, 0, 0]
        e1 = e0 + doc_lengths[m, 0, 1]
        scalars.append(jnp.stack([sec, ten, e0, e1, lax.axis_index("dp")]).astype(jnp.int32))
        lives.append(jnp.broadcast_to(token_mask[m].astype(F32), (length, LANES)))
    places = scalars[0]

    layers = []
    for layer in range(2):
        p = packs[layer]
        pick = lambda row, start, count: jnp.where(
            first, p[row : row + 1, start : start + count],
            p[row : row + 1, start + count : start + 2 * count],
        )
        taps = jnp.concatenate(
            [
                jnp.where(first, p[1:6, :inner], p[1:6, inner:chip_inner]),
                p[1:6, chip_inner : chip_inner + 2 * state],
            ],
            1,
        )
        cp = jnp.pad(taps, ((0, 3), (0, 0)))
        bias = pad_to(pick(7, 0, heads), LANES)
        rate = pad_to(-jnp.exp(pick(7, 2 * heads, heads)), LANES)
        hp = jnp.concatenate([bias, rate, jnp.zeros((6, LANES), F32)], 0)
        skip = jnp.broadcast_to(pick(7, 4 * heads, heads).reshape(heads, 1), (heads, HEAD))
        chp = jnp.concatenate(
            [skip.reshape(1, inner), pick(6, 0, inner), jnp.zeros((6, inner), F32)], 0
        )
        layers.append(dict(cp=cp, hp=hp, chp=chp))
    early, late = layers

    def fwd(k, m, pieces, gno, deps):
        nrm, proj, y, st, gated, stats = run_fwd(
            scalars[m], pieces, 0, k["w"], k["cp"], k["hp"], k["chp"], lives[m], gno,
            inner, state, heads, deps,
        )
        part = stats + swap(stats)
        part = part + across(part, 1 + m)
        got = across(part, 2 - m)
        return dict(nrm=nrm, proj=proj, y=y, st=st, gated=gated, stats=stats, part=part, got=got)

    def scale(k, m, r, deps):
        r["no"], send, r["rc"] = run_scale(
            scalars[m], r["gated"], r["part"], r["got"], k["chp"], rows, full_inner, deps
        )
        r["sent"] = swap(send)

    def project(k, m, r, deps):
        return run_half(scalars[m], r["no"], r["sent"], k["wo"], k["wo_other"], 2, deps)

    def back(k, m, rows_in, order, r, deps):
        out = run_bwd(
            scalars[m], rows_in, order, r["proj"], r["y"], r["st"], r["rc"], lives[m],
            k["cp"], k["hp"], k["chp"], inner, state, heads, rows, width, deps,
        )
        gz, gzsend, gpack = out[-3:]
        return gz, swap(gzsend), gpack, out[0]

    def unproject(k, m, gz, got, deps):
        return run_half(scalars[m], gz, got, k["w_t"], k["w_t_other"], 2, deps)

    def middle(m, parts, deps):
        return run_plain(
            partial(owner_kernel, False), "owner_mid", (wide(BF16), wide(BF16), wide(F32)),
            (*parts, xs[m], gains[1]), deps,
        )

    early["w"], late["w"] = first_parts, [w1]
    near_g = [reach(after(gs[m], *first_parts), m) for m in micros]

    a0 = fwd(early, 0, pieces0[0], None, ())
    early["wo_t"], late["wo_t"] = wo_t0, wo_t1
    wide_g = [widen(near_g[m], m, a0["stats"]) for m in micros]
    pieces0.append(share(wide0[1][0], after(wide0[1][1], a0["stats"])))
    a1 = fwd(early, 1, pieces0[1], None, [a0["stats"]] + [pair[1] for pair in near_g])
    early["wo"] = wo_t0.T
    early["wo_other"] = swap(early["wo"])
    scale(early, 0, a0, [a1["stats"]])
    pieces_g = [share(*wide_g[m]) for m in micros]
    outs0 = project(early, 0, a0, ())
    held0 = hand(outs0, 0)
    scale(early, 1, a1, [outs0[0]])
    outs1 = project(early, 1, a1, [pair[1] for pair in wide_g])
    held1 = hand(outs1, 0)
    gno0, gout1_0 = run_gn(scalars[0], pieces_g[0], 0, late["wo_t"], width, [outs1[0]])
    parts0 = settle(held0, 0, gno0)
    gno1, gout1_1 = run_gn(scalars[1], pieces_g[1], 1, late["wo_t"], width, [gno0, held0[2]])
    parts1 = settle(held1, 0, gno1)
    h_0, normed_0, u_0 = middle(0, parts0, [gno1, held1[2]])
    pair0 = reach(normed_0, 0)
    h_1, normed_1, u_1 = middle(1, parts1, [normed_0])
    pair1 = reach(normed_1, 0)
    late["w_t"], late["wo"] = run_turn(places, late["w"], late["wo_t"], [normed_1])
    wide0 = widen(pair0, 0, late["wo"])
    wide1 = widen(pair1, 0, late["wo"])
    early["w_t"], _ = run_turn(places, early["w"], early["wo_t"], [late["wo"], pair0[1], pair1[1]])
    late["wo_other"] = swap(late["wo"])
    for k in layers:
        k["w_t_other"] = swap(k["w_t"])

    b0 = fwd(late, 0, share(*wide0), gno0, [early["w_t"]])
    b1 = fwd(late, 1, share(*wide1), gno1, [b0["stats"]])
    scale(late, 0, b0, [b1["stats"], early["w_t_other"]])
    gz0, got0, pack0, _ = back(late, 0, (gno0, b0["rc"]), None, b0, [b0["no"]])
    scale(late, 1, b1, [pack0])
    outs0 = unproject(late, 0, gz0, got0, [b1["no"]])
    held0 = hand(outs0, 0)
    gz1, got1, pack1, _ = back(late, 1, (gno1, b1["rc"]), None, b1, [outs0[0]])
    parts0 = settle(held0, 0, pack1)
    g_wo1 = run_outer(
        places, [(b0["no"], gout1_0), (b1["no"], gout1_1)], None, False, [pack1, held0[2]]
    )
    outs1 = unproject(late, 1, gz1, got1, [g_wo1])
    held1 = hand(outs1, 0)

    own_at = ten * rows + sec * half
    rcol = lambda r: lax.dynamic_slice_in_dim(r["rc"], own_at, half, 0)

    def turn(m, parts, h, u, r, deps):
        return run_plain(
            partial(owner_back_kernel, False, full_inner), "owner_back",
            (wide(BF16, LANES), small), (*parts, h, gs[m], gains[1], u, rcol(r)), deps,
        )

    gh_0, gain1_0 = turn(0, parts0, h_0, u_0, a0, [outs1[0]])
    pair0 = reach(gh_0, 0)
    g_w1 = run_outer(places, [(b0["nrm"], gz0), (b1["nrm"], gz1)], None, True, [gh_0])
    parts1 = settle(held1, 0, g_w1)
    wide0 = widen(pair0, 0, g_w1)
    final0 = project(late, 0, b0, [g_w1])
    gh_1, gain1_1 = turn(1, parts1, h_1, u_1, a1, [final0[0]])
    pair1 = reach(gh_1, 0)
    wide1 = widen(pair1, 0)
    turned0, turned1 = share(*wide0), share(*wide1)
    spill = lambda g, axis: lax.psum_scatter(g, "dp", scatter_dimension=axis, tiled=True)
    narrow = lambda g, axis: spill(g.astype(BF16), axis).astype(F32)
    wo1_sum = narrow(g_wo1, 1)
    zx1_sum = narrow(after(g_w1, pair0[1])[:, : 2 * inner], 0)
    tiny1 = pack0 + pack1 + gain1_0 + gain1_1
    bcdt_at = slice(2 * inner, 2 * inner + w_bcdt.shape[2])

    gz0, got0, pack0, gout0_0 = back(early, 0, (turned0, early["wo_t"]), 0, a0, [gh_1, pair1[1]])
    final1 = project(late, 1, b1, [pack0, wide1[1]])
    outs0 = unproject(early, 0, gz0, got0, [final1[0]])
    held0 = hand(outs0, 0)
    g_w0 = run_outer(places, [(a0["nrm"], gz0)], None, True, [outs0[0]])
    gno0_1, gout0_1, cc0_1 = run_gn(scalars[1], turned1, 0, early["wo_t"], width, [g_w0])
    g_wo0 = run_outer(
        places, [(a0["no"], gout0_0), (a1["no"], gout0_1)], None, False, [gno0_1]
    )
    wo0_sum = narrow(g_wo0, 1)
    hold = lambda outs: (after(outs[0], gno0_1), outs[1], after(outs[2], gno0_1))
    heldf = [hand(hold(outs), 0) for outs in (final0, final1)]
    gz1, got1, pack1, _ = back(early, 1, (gno0_1, cc0_1), None, a1, [g_wo0])
    g_w0 = run_outer(places, [(a1["nrm"], gz1)], g_w0, True, [pack1, held0[2], heldf[0][2]])
    zx0_sum = narrow(g_w0[:, : 2 * inner], 0)
    outs1 = unproject(early, 1, gz1, got1, [g_w0, heldf[1][2]])
    held1 = hand(outs1, 0)
    pair = by_layer(g_w0[:, bcdt_at], g_w1[:, bcdt_at])
    bc_got = swap(pair[1].astype(BF16))
    parts0 = settle(held0, 0, outs1[0])
    def finish(m, h, deps):
        return run_plain(
            partial(owner_kernel, True), "owner_out", wide(F32), (*partsf[m], h, gains[1]), deps
        )

    def last(m, parts, gh, deps):
        return run_plain(
            partial(owner_back_kernel, True, full_inner), "owner_last", (wide(F32), small),
            (*parts, xs[m], gh, gains[0]), deps,
        )

    paired = after(pair[0], outs1[0]) + bc_got.astype(F32)
    gv_0, gain0_0 = last(0, parts0, gh_0, [outs1[0]])
    partsf = [settle(heldf[m], 0, outs1[0]) for m in micros]
    if lax.axis_size("dp") == 4:
        _, b_kept, b_got = deal_one(paired)
        finals = [finish(0, h_0, [gv_0, b_got])]
        b_kept, b_got = deal_two(b_kept, b_got)
        shard = b_kept + b_got.astype(F32)
    else:
        shard = scatter_dp(paired)
        finals = [finish(0, h_0, [gv_0])]
    finals.append(finish(1, h_1, [finals[0], held1[2]]))
    parts1 = settle(held1, 0, finals[1])
    gv_1, gain0_1 = last(1, parts1, gh_1, ())
    tiny0 = pack0 + pack1 + gain0_0 + gain0_1

    finals = jnp.stack(finals)
    out_act = run_join(places, finals, swap(finals))
    both = jnp.stack([gv_0, gv_1])
    mine, theirs = by_layer(both[:, :, : width // 2], both[:, :, width // 2 :])
    grad_in = run_join(places, mine, swap(theirs))

    kept, sent = by_layer(tiny0, tiny1)
    mine = sum_dp(kept + swap(sent))
    shared = all_tensor(mine)
    for bit in (1, 2):
        shard = shard + across(shard.astype(BF16), bit).astype(F32)
    grad_w_bcdt = shard[None]

    def owned(parts):
        kept, sent = by_layer(parts[0], parts[1])
        return kept, swap(sent)

    grad_w_zx = run_weave(places, *owned([zx0_sum, zx1_sum]))[None]
    grad_w_out = jnp.concatenate(by_layer(*owned([wo0_sum, wo1_sum])), 0)[None]
    return (
        out_act,
        grad_in,
        shared[0:1],
        grad_w_zx,
        grad_w_bcdt,
        mine[None, 1:6, :chip_inner],
        shared[None, 1:6, chip_inner : chip_inner + 2 * state],
        mine[7:8, : 2 * heads],
        mine[8:9, : 2 * heads],
        mine[9:10, : 2 * heads],
        mine[6:7, :chip_inner],
        grad_w_out,
    )


def solution(mesh):
    return jax.shard_map(
        on_device,
        mesh=mesh,
        in_specs=(
            P(None, "tensor", "dp", None),
            P(None, "tensor", "dp", None),
            P(None, "dp", None),
            P(None, None, "dp"),
            P("section", None),
            P("section", "dp", None, "tensor"),
            P("section", "dp", None),
            P("section", None, "tensor"),
            P("section", None, None),
            P("section", "tensor"),
            P("section", "tensor"),
            P("section", "tensor"),
            P("section", "tensor"),
            P("section", "tensor", "dp"),
        ),
        out_specs=(
            P(None, "tensor", "dp", None),
            P(None, "tensor", "dp", "section"),
            P("section", None),
            P("section", "dp", None, "tensor"),
            P("section", "dp", None),
            P("section", None, "tensor"),
            P("section", None, None),
            P("section", "tensor"),
            P("section", "tensor"),
            P("section", "tensor"),
            P("section", "tensor"),
            P("section", "tensor", "dp"),
        ),
        check_vma=False,
    )
```

time: 1230 us -> 962 us (0.78)
  starting transfers between devices: 266 us -> 83.4 us
  Pallas kernels: 365 us -> 445 us
  matrix products: 52.4 us -> 0 us
  local copies, waits for them, and re-layouts: 118 us -> 67.7 us
  other arithmetic: 86.8 us -> 48.7 us
  waiting for transfers between devices: 324 us -> 287 us
    ppermute x56 -> x8, starting transfers between devices: 149 us -> 21.9 us  [the longest x2 12.4 us: trade(): return lax.ppermute(value, 'dp', [(i, i ^ bit) for i in range(4)])]
    pallas_call x30 -> x43, Pallas kernels: 365 us -> 445 us  [the longest x33 410 us: call(): pl.pallas_call(body, out_shape=tuple((jax.ShapeDtypeStruct(shape, kind) f...]
    dot_general x14 -> x0, matrix products: 52.4 us -> none  [the longest x8 49.4 us: mm(): return lax.dot_general(left, right, dims, preferred_element_type=F32)]
    ppermute x72 -> x44, starting transfers between devices: 103 us -> 53.7 us  [across(): return lax.ppermute(value, 'tensor', [(i, i ^ step) for i in range(count)])]
    concatenate x10 -> x4, other arithmetic: 32.1 us -> 1.96 us  [the longest x2 1.21 us: on_device(): jnp.concatenate([jnp.where(first, p[1:6, :inner], p[1:6, inner:chip_inner...]
    ppermute x56 -> x8, waiting for transfers between devices: 91.1 us -> 63.2 us  [the longest x6 35.4 us: cycle(): lax.ppermute(value, 'dp', [(i, (i + steps) % count) for i in range(count)])]
    ppermute x72 -> x44, waiting for transfers between devices: 230 us -> 207 us  [across(): return lax.ppermute(value, 'tensor', [(i, i ^ step) for i in range(count)])]
    dynamic_slice x16 -> x2, local copies, waits for them, and re-layouts: 19 us -> 3.08 us  [on_device(): rcol = lambda r: lax.dynamic_slice_in_dim(r['rc'], own_at, half, 0)]
  transfers between devices with their start and end apart: 192 -> 100, of which waited for: 55 -> 34; matrix products, arithmetic and copies ran while one was open for 19% -> 9% of each run, Pallas kernels for 30% -> 45%
where the time goes in v2:
time: 962 us; the launch traced here: 950 us
  Pallas kernels  445 us (46%)
  waiting for transfers between devices  287 us (30%)
  starting transfers between devices  83.4 us (9%)
  local copies, waits for them, and re-layouts  67.7 us (7%)
  other arithmetic  48.7 us (5%)
  between operations  18.1 us (2%)
    pallas_call x33, Pallas kernels, call(): pl.pallas_call(body, out_shape=tuple((jax.ShapeDtypeStruct(shape, kind) f...  410 us
    ppermute x44, waiting for transfers between devices, across(): return lax.ppermute(value, 'tensor', [(i, i ^ step) for i in range(count)])  207 us
    ppermute x44, starting transfers between devices, across(): return lax.ppermute(value, 'tensor', [(i, i ^ step) for i in range(count)])  53.7 us
    ppermute x6, waiting for transfers between devices, cycle(): lax.ppermute(value, 'dp', [(i, (i + steps) % count) for i in range(count)])  35.4 us
    pallas_call x10, Pallas kernels, run_plain(): pl.pallas_call(body, in_specs=[vmem] * count + [pl.BlockSpec(memory_space...  35.3 us
    unnamed x195, local copies, waits for them, and re-layouts  34.4 us
    ppermute x2, waiting for transfers between devices, trade(): return lax.ppermute(value, 'dp', [(i, i ^ bit) for i in range(4)])  27.8 us
  transfers between devices with their start and end apart: 100, of which 34 were waited for; matrix products, arithmetic and copies ran while one was open for 9% of the time, Pallas kernels for 45%

profile of v2, /device:TPU:0, one launch (start us, length us, event | category | flops | bytes accessed | tf_op | source)
XLA Modules:
  0.0 950.4 jit_solution(749756141321016146)
XLA Ops:
  10.7 3.7 fusion.27
  26.0 12.8 %collective-permute-done.1 = bf16[192,1536]{1,0:T(8,128)(2,1)} collective-permute-done((bf16[192,1536]{1,0:T(8,128)(2,1)}, bf16[192,1536]{1,0:T(8,128)(2,1)}, u32[]{:S(2)}, u32[]{:S(2)}) %collective-permute-start.1) | collective-permute-done | bytes 589856 | tf_op jit(solution)/shard_map/ppermute | solution.py:842
  53.7 13.8 %collective-permute-done.4.refs_5_.refs_1_ = bf16[384,1152]{1,0:T(8,128)(2,1)} collective-permute-done((bf16[384,1152]{1,0:T(8,128)(2,1)S(1)}, bf16[384,1152]{1,0:T(8,128)(2,1)}, u32[]{:S(2)}, u32[]{:S(2)}) %collective-permute-start.4) | collective-permute-done | bytes 884768 | tf_op jit(solution)/shard_map/ppermute | solution.py:883
  79.5 10.8 %collective-permute-done.12 = bf16[192,1536]{1,0:T(8,128)(2,1)S(1)} collective-permute-done((bf16[192,1536]{1,0:T(8,128)(2,1)}, bf16[192,1536]{1,0:T(8,128)(2,1)S(1)}, u32[]{:S(2)}, u32[]{:S(2)}) %collective-permute-start.12) | collective-permute-done | bytes 589856 | tf_op jit(solution)/shard_map/ppermute | solution.py:842
  92.9 18.7 %collective-permute-done.7.refs_6_.refs_2_ = bf16[384,1152]{1,0:T(8,128)(2,1)} collective-permute-done((bf16[384,1152]{1,0:T(8,128)(2,1)S(1)}, bf16[384,1152]{1,0:T(8,128)(2,1)}, u32[]{:S(2)}, u32[]{:S(2)}) %collective-permute-start.7) | collective-permute-done | bytes 884768 | tf_op jit(solution)/shard_map/ppermute | solution.py:883
  112.9 22.9 %layer_fwd.4 = (bf16[1536,1536]{1,0:T(8,128)(2,1)}, f32[1536,1152]{1,0:T(8,128)}, f32[1536,384]{1,0:T(8,128)}, bf16[12,128,384]{2,1,0:T(8,128)(2,1)}, f32[1536,384]{1,0:T(8,128)}, /*index=5*/f32[8,1536]{1,0:T(8,128)}) custom-call(s32[5]{0:T(128)} %stack.118.sc, bf16[2,192,1536]{2,1,0:T(8,128)(2,1)} %copy-done.16, ...), custom_call_target="tpu_custom_call" | custom-call | flops 25769803776 | bytes 25165824 | tf_op jit(solution)/shard_map/layer_fwd/pallas_call | solution.py:235
  144.2 10.0 %collective-permute-done.10 = f32[8,1536]{1,0:T(8,128)S(1)} collective-permute-done((f32[8,1536]{1,0:T(8,128)S(1)}, f32[8,1536]{1,0:T(8,128)S(1)}, u32[]{:S(2)}, u32[]{:S(2)}) %collective-permute-start.10) | collective-permute-done | bytes 49184 | tf_op jit(solution)/shard_map/ppermute | solution.py:842
  154.7 7.5 all-gather.4.cloned.1.call-done.refs_4_
  163.5 22.8 %layer_fwd.5 = (bf16[1536,1536]{1,0:T(8,128)(2,1)}, f32[1536,1152]{1,0:T(8,128)}, f32[1536,384]{1,0:T(8,128)}, bf16[12,128,384]{2,1,0:T(8,128)(2,1)}, f32[1536,384]{1,0:T(8,128)}, /*index=5*/f32[8,1536]{1,0:T(8,128)}) custom-call(s32[5]{0:T(128)} %stack.123.sc, bf16[2,192,1536]{2,1,0:T(8,128)(2,1)} %pad_maximum_fusion.5.refs_0_, ...), custom_call_target="tpu_custom_call" | custom-call | flops 25769803776 | bytes 25165824 | tf_op jit(solution)/shard_map/layer_fwd/pallas_call | solution.py:235
  186.9 5.2 scale_rows.4
  202.9 6.1 half_rows.8
  209.0 13.8 %collective-permute-done.27.refs_2_ = f32[8,1536]{1,0:T(8,128)S(1)} collective-permute-done((f32[8,1536]{1,0:T(8,128)S(1)}, f32[8,1536]{1,0:T(8,128)S(1)}, u32[]{:S(2)}, u32[]{:S(2)}) %collective-permute-start.27) | collective-permute-done | bytes 49184 | tf_op jit(solution)/shard_map/ppermute | solution.py:842
  223.4 5.1 scale_rows.5
  232.2 6.0 half_rows.9
  240.1 9.2 grad_rows.3
  249.3 10.5 %collective-permute-done.21.refs_6_.refs_1_ = bf16[2,192,1536]{2,1,0:T(8,128)(2,1)} collective-permute-done((bf16[2,192,1536]{2,1,0:T(8,128)(2,1)}, bf16[2,192,1536]{2,1,0:T(8,128)(2,1)}, u32[]{:S(2)}, u32[]{:S(2)}) %collective-permute-start.21) | collective-permute-done | bytes 1179680 | tf_op jit(solution)/shard_map/ppermute | solution.py:842
  262.6 8.9 grad_rows.4
  271.5 12.7 %collective-permute-done.33.refs_6_.refs_1_ = bf16[2,192,1536]{2,1,0:T(8,128)(2,1)S(1)} collective-permute-done((bf16[2,192,1536]{2,1,0:T(8,128)(2,1)}, bf16[2,192,1536]{2,1,0:T(8,128)(2,1)S(1)}, u32[]{:S(2)}, u32[]{:S(2)}) %collective-permute-start.33) | collective-permute-done | bytes 1179680 | tf_op jit(solution)/shard_map/ppermute | solution.py:842
  286.7 3.7 owner_mid.2
  291.2 9.5 collective-permute-done.34.refs_2_
  301.5 3.7 owner_mid.3
  305.2 6.3 turn_weights.2
  315.4 11.9 %collective-permute-done.39.refs_7_ = bf16[192,1536]{1,0:T(8,128)(2,1)S(1)} collective-permute-done((bf16[192,1536]{1,0:T(8,128)(2,1)S(1)}, bf16[192,1536]{1,0:T(8,128)(2,1)S(1)}, u32[]{:S(2)}, u32[]{:S(2)}) %collective-permute-start.39) | collective-permute-done | bytes 589856 | tf_op jit(solution)/shard_map/ppermute | solution.py:842
  328.8 12.6 %collective-permute-done.36.refs_1_ = bf16[2,192,1536]{2,1,0:T(8,128)(2,1)} collective-permute-done((bf16[2,192,1536]{2,1,0:T(8,128)(2,1)S(1)}, bf16[2,192,1536]{2,1,0:T(8,128)(2,1)}, u32[]{:S(2)}, u32[]{:S(2)}) %collective-permute-start.36) | collective-permute-done | bytes 1179680 | tf_op jit(solution)/shard_map/ppermute | solution.py:842
  342.6 6.5 turn_weights.3
  349.1 14.9 %collective-permute-done.43.refs_1_ = bf16[2,192,1536]{2,1,0:T(8,128)(2,1)S(1)} collective-permute-done((bf16[2,192,1536]{2,1,0:T(8,128)(2,1)S(1)}, bf16[2,192,1536]{2,1,0:T(8,128)(2,1)S(1)}, u32[]{:S(2)}, u32[]{:S(2)}) %collective-permute-start.43) | collective-permute-done | bytes 1179680 | tf_op jit(solution)/shard_map/ppermute | solution.py:842
  364.0 24.6 %layer_fwd.6 = (bf16[1536,1536]{1,0:T(8,128)(2,1)}, f32[1536,1152]{1,0:T(8,128)}, f32[1536,384]{1,0:T(8,128)}, bf16[12,128,384]{2,1,0:T(8,128)(2,1)}, f32[1536,384]{1,0:T(8,128)}, /*index=5*/f32[8,1536]{1,0:T(8,128)}) custom-call(s32[5]{0:T(128)} %stack.118.sc, bf16[2,192,1536]{2,1,0:T(8,128)(2,1)} %copy-done.23, ...), custom_call_target="tpu_custom_call" | custom-call | flops 25769803776 | bytes 25165824 | tf_op jit(solution)/shard_map/layer_fwd/pallas_call | solution.py:235
  396.7 24.4 %layer_fwd.7 = (bf16[1536,1536]{1,0:T(8,128)(2,1)}, f32[1536,1152]{1,0:T(8,128)}, f32[1536,384]{1,0:T(8,128)}, bf16[12,128,384]{2,1,0:T(8,128)(2,1)}, f32[1536,384]{1,0:T(8,128)}, /*index=5*/f32[8,1536]{1,0:T(8,128)}) custom-call(s32[5]{0:T(128)} %stack.123.sc, bf16[2,192,1536]{2,1,0:T(8,128)(2,1)} %copy-done.21, bf16[2,192,1536]{2,1,0:T(8,128)(2,1)} %copy-done.79, ...), custom_call_target="tpu_custom_call" | custom-call | flops 25769803776 | bytes 25165824 | tf_op jit(solution)/shard_map/layer_fwd/pallas_call | solution.py:235
  423.0 5.1 scale_rows.6
  428.0 27.6 %layer_bwd.4 = (bf16[1536,1152]{1,0:T(8,128)(2,1)}, bf16[4,192,1152]{2,1,0:T(8,128)(2,1)}, f32[16,1536]{1,0:T(8,128)}) custom-call(s32[5]{0:T(128)} %stack.118.sc, f32[1536,384]{1,0:T(8,128)} %get-tuple-element.155.refs_5_.refs_9_.refs_0_, f32[1536,128]{1,0:T(8,128)} %get-tuple-element.174.refs_1_.refs_6_, f32[1536,1152]{1,0:T(8,128)} %get-tuple-element.175.refs_2_.refs_3_, ...), custom_call_target="tpu_custom_call" | custom-call | flops 30064771072 | bytes 25165824 | tf_op jit(solution)/shard_map/layer_bwd/pallas_call | solution.py:235
  459.7 3.5 collective-permute-done.50
  468.0 5.1 scale_rows.7
  474.3 10.4 %half_rows.10 = (f32[192,1536]{1,0:T(8,128)}, f32[192,1536]{1,0:T(8,128)}, bf16[2,192,1536]{2,1,0:T(8,128)(2,1)}) custom-call(s32[5]{0:T(128)} %stack.118.sc, bf16[4,2,192,1152]{3,2,1,0:T(8,128)(2,1)} %bitcast.158, bf16[4,192,1152]{2,1,0:T(8,128)(2,1)} %copy-done.70, bf16[1152,1536]{1,0:T(8,128)(2,1)} %get-tuple-element.187.refs_2_, ...), custom_call_target="tpu_custom_call" | custom-call | flops 8589934592 | bytes 10485760 | tf_op jit(solution)/shard_map/half_rows/pallas_call | solution.py:235
  485.3 27.3 %layer_bwd.5 = (bf16[1536,1152]{1,0:T(8,128)(2,1)}, bf16[4,192,1152]{2,1,0:T(8,128)(2,1)}, f32[16,1536]{1,0:T(8,128)}) custom-call(s32[5]{0:T(128)} %stack.123.sc, f32[1536,384]{1,0:T(8,128)} %get-tuple-element.157.refs_5_.refs_9_.refs_0_, f32[1536,128]{1,0:T(8,128)} %get-tuple-element.182.refs_1_.refs_6_, f32[1536,1152]{1,0:T(8,128)} %get-tuple-element.183.refs_2_.refs_3_, ...), custom_call_target="tpu_custom_call" | custom-call | flops 30064771072 | bytes 25165824 | tf_op jit(solution)/shard_map/layer_bwd/pallas_call | solution.py:235
  515.2 9.2 outer_rows.5.refs_4_
  525.7 10.4 %half_rows.11 = (f32[192,1536]{1,0:T(8,128)}, f32[192,1536]{1,0:T(8,128)}, bf16[2,192,1536]{2,1,0:T(8,128)(2,1)}) custom-call(s32[5]{0:T(128)} %stack.123.sc, bf16[4,2,192,1152]{3,2,1,0:T(8,128)(2,1)} %bitcast.160, bf16[4,192,1152]{2,1,0:T(8,128)(2,1)} %copy-done.71, bf16[1152,1536]{1,0:T(8,128)(2,1)} %get-tuple-element.187.refs_2_, ...), custom_call_target="tpu_custom_call" | custom-call | flops 8589934592 | bytes 10485760 | tf_op jit(solution)/shard_map/half_rows/pallas_call | solution.py:235
  538.4 4.5 owner_back.2
  543.5 18.9 %outer_rows.6.refs_4_ = f32[1536,1152]{1,0:T(8,128)} custom-call(s32[5]{0:T(128)} %stack.118.sc, bf16[1536,1536]{1,0:T(8,128)(2,1)} %get-tuple-element.173.refs_0_, bf16[1536,1152]{1,0:T(8,128)(2,1)} %get-tuple-element.178.refs_1_, bf16[1536,1536]{1,0:T(8,128)(2,1)} %get-tuple-element.179.refs_2_, bf16[1536,1152]{1,0:T(8,128)(2,1)} %get-tuple-element.190.refs_3_, ...), custom_call_target="tpu_custom_call" | custom-call | flops 19327352832 | bytes 16777216 | tf_op jit(solution)/shard_map/outer_rows/pallas_call | solution.py:235
  568.7 23.6 %collective-permute-done.64.refs_1_ = bf16[2,192,1664]{2,1,0:T(8,128)(2,1)S(1)} collective-permute-done((bf16[2,192,1664]{2,1,0:T(8,128)(2,1)S(1)}, bf16[2,192,1664]{2,1,0:T(8,128)(2,1)S(1)}, u32[]{:S(2)}, u32[]{:S(2)}) %collective-permute-start.64) | collective-permute-done | bytes 1277984 | tf_op jit(solution)/shard_map/ppermute | solution.py:842
  593.4 6.4 half_rows.12
  599.8 4.5 owner_back.3
  605.8 15.5 %collective-permute-done.59.refs_15_ = bf16[192,1664]{1,0:T(8,128)(2,1)S(1)} collective-permute-done((bf16[192,1664]{1,0:T(8,128)(2,1)}, bf16[192,1664]{1,0:T(8,128)(2,1)S(1)}, u32[]{:S(2)}, u32[]{:S(2)}) %collective-permute-start.59) | collective-permute-done | bytes 639008 | tf_op jit(solution)/shard_map/ppermute | solution.py:842
  624.9 32.1 %layer_bwd.6 = (bf16[1536,1536]{1,0:T(8,128)(2,1)}, bf16[1536,1152]{1,0:T(8,128)(2,1)}, bf16[4,192,1152]{2,1,0:T(8,128)(2,1)}, f32[16,1536]{1,0:T(8,128)}) custom-call(s32[5]{0:T(128)} %stack.118.sc, bf16[2,192,1664]{2,1,0:T(8,128)(2,1)} %copy-done.11, bf16[2,192,1664]{2,1,0:T(8,128)(2,1)} %copy-done.72, ...), custom_call_target="tpu_custom_call" | custom-call | flops 30064771072 | bytes 25165824 | tf_op jit(solution)/shard_map/layer_bwd/pallas_call | solution.py:235
  662.2 6.1 half_rows.13
  668.3 10.4 %half_rows.14 = (f32[192,1536]{1,0:T(8,128)}, f32[192,1536]{1,0:T(8,128)}, bf16[2,192,1536]{2,1,0:T(8,128)(2,1)}) custom-call(s32[5]{0:T(128)} %stack.118.sc, bf16[4,2,192,1152]{3,2,1,0:T(8,128)(2,1)} %bitcast.159, bf16[4,192,1152]{2,1,0:T(8,128)(2,1)} %collective-permute-done.67.refs_1_, bf16[1152,1536]{1,0:T(8,128)(2,1)} %get-tuple-element.166.refs_10_.refs_2_, ...), custom_call_target="tpu_custom_call" | custom-call | flops 8589934592 | bytes 10485760 | tf_op jit(solution)/shard_map/half_rows/pallas_call | solution.py:235
  678.7 11.4 %outer_rows.7.refs_5_.refs_2_ = f32[1536,1152]{1,0:T(8,128)} custom-call(s32[5]{0:T(128)} %stack.118.sc, bf16[1536,1536]{1,0:T(8,128)(2,1)} %get-tuple-element.211.refs_0_, bf16[1536,1152]{1,0:T(8,128)(2,1)} %get-tuple-element.216.refs_1_, f32[192,1536]{1,0:T(8,128)} %get-tuple-element.221.refs_2_.refs_0_), custom_call_target="tpu_custom_call" | custom-call | flops 9663676416 | bytes 16777216 | tf_op jit(solution)/shard_map/outer_rows/pallas_call | solution.py:235
  692.3 9.7 %grad_rows.5 = (f32[1536,384]{1,0:T(8,128)}, bf16[1536,1536]{1,0:T(8,128)(2,1)}, f32[1536,128]{1,0:T(8,128)}) custom-call(s32[5]{0:T(128)} %stack.123.sc, bf16[2,192,1664]{2,1,0:T(8,128)(2,1)} %copy-done.10, bf16[2,192,1664]{2,1,0:T(8,128)(2,1)} %collective-permute-done.60.refs_5_.refs_1_, bf16[2,192,1664]{2,1,0:T(8,128)(2,1)} %copy-done.74, ...), custom_call_target="tpu_custom_call" | custom-call | flops 8589934592 | bytes 18874368 | tf_op jit(solution)/shard_map/grad_rows/pallas_call | solution.py:235
  702.0 9.2 outer_rows.8.refs_11_
  714.5 4.0 slice.427
  722.7 26.4 %layer_bwd.7 = (bf16[1536,1152]{1,0:T(8,128)(2,1)}, bf16[4,192,1152]{2,1,0:T(8,128)(2,1)}, f32[16,1536]{1,0:T(8,128)}) custom-call(s32[5]{0:T(128)} %stack.123.sc, f32[1536,384]{1,0:T(8,128)} %get-tuple-element.222.refs_4_.refs_0_, f32[1536,128]{1,0:T(8,128)} %get-tuple-element.227.refs_1_, f32[1536,1152]{1,0:T(8,128)} %get-tuple-element.228.refs_2_.refs_3_, ...), custom_call_target="tpu_custom_call" | custom-call | flops 30064771072 | bytes 25165824 | tf_op jit(solution)/shard_map/layer_bwd/pallas_call | solution.py:235
  750.2 24.5 %collective-permute-done.71.refs_4_.refs_1_ = bf16[2,192,1536]{2,1,0:T(8,128)(2,1)S(1)} collective-permute-done((bf16[2,192,1536]{2,1,0:T(8,128)(2,1)S(1)}, bf16[2,192,1536]{2,1,0:T(8,128)(2,1)S(1)}, u32[]{:S(2)}, u32[]{:S(2)}) %collective-permute-start.71) | collective-permute-done | bytes 1179680 | tf_op jit(solution)/shard_map/ppermute | solution.py:842
  775.7 12.7 %outer_rows.9.refs_4_ = f32[1536,1152]{1,0:T(8,128)} custom-call(s32[5]{0:T(128)} %stack.118.sc, bf16[1536,1536]{1,0:T(8,128)(2,1)} %get-tuple-element.235.refs_0_, bf16[1536,1152]{1,0:T(8,128)(2,1)} %get-tuple-element.233.refs_1_, f32[1536,1152]{1,0:T(8,128)} %outer_rows.7.refs_5_.refs_2_, f32[16,1536]{1,0:T(8,128)} %get-tuple-element.236.refs_3_, ...), custom_call_target="tpu_custom_call" | custom-call | flops 9663676416 | bytes 16777216 | tf_op jit(solution)/shard_map/outer_rows/pallas_call | solution.py:235
  788.4 4.0 slice.428
  799.5 10.6 %half_rows.15 = (f32[192,1536]{1,0:T(8,128)}, f32[192,1536]{1,0:T(8,128)}, bf16[2,192,1536]{2,1,0:T(8,128)(2,1)}) custom-call(s32[5]{0:T(128)} %stack.123.sc, bf16[4,2,192,1152]{3,2,1,0:T(8,128)(2,1)} %bitcast.161, bf16[4,192,1152]{2,1,0:T(8,128)(2,1)} %collective-permute-done.70.refs_1_, bf16[1152,1536]{1,0:T(8,128)(2,1)} %get-tuple-element.166.refs_10_.refs_2_, ...), custom_call_target="tpu_custom_call" | custom-call | flops 8589934592 | bytes 10485760 | tf_op jit(solution)/shard_map/half_rows/pallas_call | solution.py:235
  824.8 11.7 %collective-permute-start.76 = (bf16[2,384,304]{1,2,0:T(8,128)(2,1)}, bf16[2,384,304]{1,2,0:T(8,128)(2,1)S(1)}, u32[]{:S(2)}, u32[]{:S(2)}) collective-permute-start(bf16[2,384,304]{1,2,0:T(8,128)(2,1)} %select_convert_fusion.1), channel_id=1, source_target_pairs={{0,4},{4,0},{8,12},{12,8},{1,5},{5,1},{9,13},{13,9},{2,6},{6,2},{1... | collective-permute-start | bytes 1400840 | tf_op jit(solution)/shard_map/ppermute | solution.py:902
  838.6 4.0 owner_last.2
  842.6 19.8 %collective-permute-done.76 = bf16[2,384,304]{1,2,0:T(8,128)(2,1)S(1)} collective-permute-done((bf16[2,384,304]{1,2,0:T(8,128)(2,1)}, bf16[2,384,304]{1,2,0:T(8,128)(2,1)S(1)}, u32[]{:S(2)}, u32[]{:S(2)}) %collective-permute-start.76) | collective-permute-done | bytes 466976 | tf_op jit(solution)/shard_map/ppermute | solution.py:902
  867.6 8.0 collective-permute-done.89
  887.7 10.1 %collective-permute-done.80.refs_2_ = bf16[192,1536]{1,0:T(8,128)(2,1)} collective-permute-done((bf16[192,1536]{1,0:T(8,128)(2,1)S(1)}, bf16[192,1536]{1,0:T(8,128)(2,1)}, u32[]{:S(2)}, u32[]{:S(2)}) %collective-permute-start.80) | collective-permute-done | bytes 589856 | tf_op jit(solution)/shard_map/ppermute | solution.py:842
  897.8 4.1 owner_last.3
  919.1 4.1 collective-permute-done.86
  929.2 3.5 join_rows.3
  932.7 4.9 join_rows.2
  938.6 4.7 weave_cols.1
  (484 shorter events, 205.8 us)
Async XLA Ops:
  7.2 155.0 %all-gather.4.cloned.1.call-start = ((), (), s32[]{:S(2)}) async-start(), calls=%async_computation.4 | async-start | bytes 1474560 | tf_op jit(solution)/shard_map/all_gather | solution.py:1002
  16.1 26.0 %collective-permute-start.3 = (bf16[384,1152]{1,0:T(8,128)(2,1)S(1)}, bf16[384,1152]{1,0:T(8,128)(2,1)}, u32[]{:S(2)}, u32[]{:S(2)}) collective-permute-start(bf16[384,1152]{1,0:T(8,128)(2,1)S(1)} %pad_maximum_fusion.11), channel_id=1, source_target_pairs={{0,16},{16,0},{1,17},{17,1},{2,18},{18,2},{3,19},{19,3},{4,20},{20... | collective-permute-start | bytes 2654216 | tf_op jit(solution)/shard_map/ppermute | solution.py:846
  25.8 49.1 %collective-permute-start.19 = (bf16[384,384]{1,0:T(8,128)(2,1)}, bf16[384,384]{1,0:T(8,128)(2,1)}, u32[]{:S(2)}, u32[]{:S(2)}) collective-permute-start(bf16[384,384]{1,0:T(8,128)(2,1)} %select_bitcast_fusion.4), channel_id=1, source_target_pairs={{0,16},{16,0},{1,17},{17,1},{2,18},{18,2},{3,19},{19,3},{4,20},{20... | collective-permute-start | bytes 884744 | tf_op jit(solution)/shard_map/ppermute | solution.py:846
  40.2 28.0 %collective-permute-start.2 = (bf16[2,192,1536]{2,1,0:T(8,128)(2,1)S(1)}, bf16[2,192,1536]{2,1,0:T(8,128)(2,1)}, u32[]{:S(2)}, u32[]{:S(2)}) collective-permute-start(bf16[2,192,1536]{2,1,0:T(8,128)(2,1)S(1)} %pad_maximum_fusion.4.refs_0_), channel_id=1, source_target_pairs={{0,2},{1,3},{2,0},{3,1},{4,6},{5,7},{6,4},{7,5},{8,10},{9,11},{10,... | collective-permute-start | bytes 3538952 | tf_op jit(solution)/shard_map/ppermute | solution.py:842
  53.7 58.1 %collective-permute-start.5 = (bf16[2,192,1536]{2,1,0:T(8,128)(2,1)S(1)}, bf16[2,192,1536]{2,1,0:T(8,128)(2,1)}, u32[]{:S(2)}, u32[]{:S(2)}) collective-permute-start(bf16[2,192,1536]{2,1,0:T(8,128)(2,1)S(1)} %pad_maximum_fusion.4.refs_0_), channel_id=1, source_target_pairs={{0,16},{16,0},{1,17},{17,1},{2,18},{18,2},{3,19},{19,3},{4,20},{20... | collective-permute-start | bytes 3538952 | tf_op jit(solution)/shard_map/ppermute | solution.py:846
  68.2 43.6 %collective-permute-start.6 = (bf16[2,192,1536]{2,1,0:T(8,128)(2,1)}, bf16[2,192,1536]{2,1,0:T(8,128)(2,1)}, u32[]{:S(2)}, u32[]{:S(2)}) collective-permute-start(bf16[2,192,1536]{2,1,0:T(8,128)(2,1)} %collective-permute-done.2.refs_1_), channel_id=1, source_target_pairs={{0,16},{16,0},{1,17},{17,1},{2,18},{18,2},{3,19},{19,3},{4,20},{20... | collective-permute-start | bytes 3538952 | tf_op jit(solution)/shard_map/ppermute | solution.py:846
  69.2 42.5 %collective-permute-start.7 = (bf16[384,1152]{1,0:T(8,128)(2,1)S(1)}, bf16[384,1152]{1,0:T(8,128)(2,1)}, u32[]{:S(2)}, u32[]{:S(2)}) collective-permute-start(bf16[384,1152]{1,0:T(8,128)(2,1)S(1)} %get-tuple-element.310.refs_4_.refs_0_), channel_id=1, source_target_pairs={{0,8},{4,12},{8,0},{12,4},{1,9},{5,13},{9,1},{13,5},{2,10},{6,14},... | collective-permute-start | bytes 2654216 | tf_op jit(solution)/shard_map/ppermute | solution.py:883
  71.9 39.8 %collective-permute-start.8 = (bf16[384,1152]{1,0:T(8,128)(2,1)S(1)}, bf16[384,1152]{1,0:T(8,128)(2,1)}, u32[]{:S(2)}, u32[]{:S(2)}) collective-permute-start(bf16[384,1152]{1,0:T(8,128)(2,1)S(1)} %get-tuple-element.310.refs_4_.refs_0_), channel_id=1, source_target_pairs={{0,12},{4,0},{8,4},{12,8},{1,13},{5,1},{9,5},{13,9},{2,14},{6,2},{... | collective-permute-start | bytes 2654216 | tf_op jit(solution)/shard_map/ppermute | solution.py:883
  91.4 44.4 %collective-permute-start.13 = (bf16[2,192,1536]{2,1,0:T(8,128)(2,1)}, bf16[2,192,1536]{2,1,0:T(8,128)(2,1)}, u32[]{:S(2)}, u32[]{:S(2)}) collective-permute-start(bf16[2,192,1536]{2,1,0:T(8,128)(2,1)} %pad_maximum_fusion.5.refs_0_), channel_id=1, source_target_pairs={{0,2},{1,3},{2,0},{3,1},{4,6},{5,7},{6,4},{7,5},{8,10},{9,11},{10,... | collective-permute-start | bytes 3538952 | tf_op jit(solution)/shard_map/ppermute | solution.py:842
  111.7 43.1 %collective-permute-start.14 = (bf16[2,192,1536]{2,1,0:T(8,128)(2,1)}, bf16[2,192,1536]{2,1,0:T(8,128)(2,1)}, u32[]{:S(2)}, u32[]{:S(2)}) collective-permute-start(bf16[2,192,1536]{2,1,0:T(8,128)(2,1)} %pad_maximum_fusion.5.refs_0_), channel_id=1, source_target_pairs={{0,16},{16,0},{1,17},{17,1},{2,18},{18,2},{3,19},{19,3},{4,20},{20... | collective-permute-start | bytes 3538952 | tf_op jit(solution)/shard_map/ppermute | solution.py:846
  111.7 128.3 %all-gather.6.cloned.1.call-start = ((), (), s32[]{:S(2)}) async-start(), calls=%async_computation.5 | async-start | bytes 1474560 | tf_op jit(solution)/shard_map/all_gather | solution.py:1002
  135.8 26.4 %collective-permute-start.15 = (bf16[2,192,1536]{2,1,0:T(8,128)(2,1)}, bf16[2,192,1536]{2,1,0:T(8,128)(2,1)}, u32[]{:S(2)}, u32[]{:S(2)}) collective-permute-start(bf16[2,192,1536]{2,1,0:T(8,128)(2,1)} %collective-permute-done.13.refs_1_), channel_id=1, source_target_pairs={{0,16},{16,0},{1,17},{17,1},{2,18},{18,2},{3,19},{19,3},{4,20},{20... | collective-permute-start | bytes 3538952 | tf_op jit(solution)/shard_map/ppermute | solution.py:846
  136.5 25.7 %collective-permute-start.17 = (bf16[192,1536]{1,0:T(8,128)(2,1)S(1)}, bf16[192,1536]{1,0:T(8,128)(2,1)S(1)}, u32[]{:S(2)}, u32[]{:S(2)}) collective-permute-start(bf16[192,1536]{1,0:T(8,128)(2,1)S(1)} %get-tuple-element.153.refs_4_), channel_id=1, source_target_pairs={{0,2},{1,3},{2,0},{3,1},{4,6},{5,7},{6,4},{7,5},{8,10},{9,11},{10,... | collective-permute-start | bytes 1769480 | tf_op jit(solution)/shard_map/ppermute | solution.py:842
  138.2 24.0 %collective-permute-start.16 = (bf16[192,1536]{1,0:T(8,128)(2,1)S(1)}, bf16[192,1536]{1,0:T(8,128)(2,1)S(1)}, u32[]{:S(2)}, u32[]{:S(2)}) collective-permute-start(bf16[192,1536]{1,0:T(8,128)(2,1)S(1)} %get-tuple-element.148.refs_4_), channel_id=1, source_target_pairs={{0,1},{1,0},{2,3},{3,2},{4,5},{5,4},{6,7},{7,6},{8,9},{9,8},{10,11... | collective-permute-start | bytes 1769480 | tf_op jit(solution)/shard_map/ppermute | solution.py:842
  144.0 161.1 %all-gather.8.cloned.1.call-start = ((), (), s32[]{:S(2)}) async-start(), calls=%async_computation.6 | async-start | bytes 4423680 | tf_op jit(solution)/shard_map/all_gather | solution.py:1002
  154.2 32.1 %collective-permute-start.11 = (f32[8,1536]{1,0:T(8,128)S(1)}, f32[8,1536]{1,0:T(8,128)S(1)}, u32[]{:S(2)}, u32[]{:S(2)}) collective-permute-start(f32[8,1536]{1,0:T(8,128)S(1)} %add.144.refs_1_), channel_id=1, source_target_pairs={{0,2},{1,3},{2,0},{3,1},{4,6},{5,7},{6,4},{7,5},{8,10},{9,11},{10,... | collective-permute-start | bytes 147464 | tf_op jit(solution)/shard_map/ppermute | solution.py:842
  162.2 38.3 %collective-permute-start.20 = (bf16[384,1536]{0,1:T(8,128)(2,1)}, bf16[384,1536]{0,1:T(8,128)(2,1)}, u32[]{:S(2)}, u32[]{:S(2)}) collective-permute-start(bf16[384,1536]{0,1:T(8,128)(2,1)} %bitcast.137), channel_id=1, source_target_pairs={{0,16},{16,0},{1,17},{17,1},{2,18},{18,2},{3,19},{19,3},{4,20},{20... | collective-permute-start | bytes 3538952 | tf_op jit(solution)/shard_map/ppermute | solution.py:846
  192.6 526.0 %reduce-scatter.15.cloned.1.call-start = ((), (), s32[]{:S(2)}) async-start(), calls=%async_computation.10 | async-start | bytes 1474560
  193.3 36.2 %collective-permute-start.29 = (bf16[2,192,1536]{2,1,0:T(8,128)(2,1)S(1)}, bf16[2,192,1536]{2,1,0:T(8,128)(2,1)}, u32[]{:S(2)}, u32[]{:S(2)}) collective-permute-start(bf16[2,192,1536]{2,1,0:T(8,128)(2,1)S(1)} %pad_maximum_fusion.7.refs_0_), channel_id=1, source_target_pairs={{0,1},{1,0},{2,3},{3,2},{4,5},{5,4},{6,7},{7,6},{8,9},{9,8},{10,11... | collective-permute-start | bytes 3538952 | tf_op jit(solution)/shard_map/ppermute | solution.py:842
  197.5 31.5 %collective-permute-start.22 = (bf16[2,192,1536]{2,1,0:T(8,128)(2,1)}, bf16[2,192,1536]{2,1,0:T(8,128)(2,1)}, u32[]{:S(2)}, u32[]{:S(2)}) collective-permute-start(bf16[2,192,1536]{2,1,0:T(8,128)(2,1)} %pad_maximum_fusion.6.refs_0_), channel_id=1, source_target_pairs={{0,2},{1,3},{2,0},{3,1},{4,6},{5,7},{6,4},{7,5},{8,10},{9,11},{10,... | collective-permute-start | bytes 3538952 | tf_op jit(solution)/shard_map/ppermute | solution.py:842
  199.5 23.2 %collective-permute-start.27 = (f32[8,1536]{1,0:T(8,128)S(1)}, f32[8,1536]{1,0:T(8,128)S(1)}, u32[]{:S(2)}, u32[]{:S(2)}) collective-permute-start(f32[8,1536]{1,0:T(8,128)S(1)} %add.147.refs_1_), channel_id=1, source_target_pairs={{0,1},{1,0},{2,3},{3,2},{4,5},{5,4},{6,7},{7,6},{8,9},{9,8},{10,11... | collective-permute-start | bytes 147464 | tf_op jit(solution)/shard_map/ppermute | solution.py:842
  229.0 33.5 %collective-permute-start.31 = (bf16[2,192,1536]{2,1,0:T(8,128)(2,1)S(1)}, bf16[2,192,1536]{2,1,0:T(8,128)(2,1)}, u32[]{:S(2)}, u32[]{:S(2)}) collective-permute-start(bf16[2,192,1536]{2,1,0:T(8,128)(2,1)S(1)} %pad_maximum_fusion.7.refs_0_), channel_id=1, source_target_pairs={{0,16},{16,0},{1,17},{17,1},{2,18},{18,2},{3,19},{19,3},{4,20},{20... | collective-permute-start | bytes 3538952 | tf_op jit(solution)/shard_map/ppermute | solution.py:846
  229.5 33.0 %collective-permute-start.32 = (bf16[2,192,1536]{2,1,0:T(8,128)(2,1)}, bf16[2,192,1536]{2,1,0:T(8,128)(2,1)}, u32[]{:S(2)}, u32[]{:S(2)}) collective-permute-start(bf16[2,192,1536]{2,1,0:T(8,128)(2,1)} %collective-permute-done.29.refs_5_.refs_1_), channel_id=1, source_target_pairs={{0,16},{16,0},{1,17},{17,1},{2,18},{18,2},{3,19},{19,3},{4,20},{20... | collective-permute-start | bytes 3538952 | tf_op jit(solution)/shard_map/ppermute | solution.py:846
  230.7 29.1 %collective-permute-start.21 = (bf16[2,192,1536]{2,1,0:T(8,128)(2,1)}, bf16[2,192,1536]{2,1,0:T(8,128)(2,1)}, u32[]{:S(2)}, u32[]{:S(2)}) collective-permute-start(bf16[2,192,1536]{2,1,0:T(8,128)(2,1)} %get-tuple-element.146), channel_id=1, source_target_pairs={{0,2},{1,3},{2,0},{3,1},{4,6},{5,7},{6,4},{7,5},{8,10},{9,11},{10,... | collective-permute-start | bytes 3538952 | tf_op jit(solution)/shard_map/ppermute | solution.py:842
  239.3 44.9 %collective-permute-start.33 = (bf16[2,192,1536]{2,1,0:T(8,128)(2,1)}, bf16[2,192,1536]{2,1,0:T(8,128)(2,1)S(1)}, u32[]{:S(2)}, u32[]{:S(2)}) collective-permute-start(bf16[2,192,1536]{2,1,0:T(8,128)(2,1)} %get-tuple-element.158), channel_id=1, source_target_pairs={{0,2},{1,3},{2,0},{3,1},{4,6},{5,7},{6,4},{7,5},{8,10},{9,11},{10,... | collective-permute-start | bytes 3538952 | tf_op jit(solution)/shard_map/ppermute | solution.py:842
  261.0 24.9 %collective-permute-start.30 = (bf16[192,1536]{1,0:T(8,128)(2,1)S(1)}, bf16[192,1536]{1,0:T(8,128)(2,1)S(1)}, u32[]{:S(2)}, u32[]{:S(2)}) collective-permute-start(bf16[192,1536]{1,0:T(8,128)(2,1)S(1)} %fusion.9), channel_id=1, source_target_pairs={{0,1},{1,0},{2,3},{3,2},{4,5},{5,4},{6,7},{7,6},{8,9},{9,8},{10,11... | collective-permute-start | bytes 1769480 | tf_op jit(solution)/shard_map/ppermute | solution.py:842
  312.4 29.0 %collective-permute-start.36 = (bf16[2,192,1536]{2,1,0:T(8,128)(2,1)S(1)}, bf16[2,192,1536]{2,1,0:T(8,128)(2,1)}, u32[]{:S(2)}, u32[]{:S(2)}) collective-permute-start(bf16[2,192,1536]{2,1,0:T(8,128)(2,1)S(1)} %pad_maximum_fusion.8.refs_0_), channel_id=1, source_target_pairs={{0,2},{1,3},{2,0},{3,1},{4,6},{5,7},{6,4},{7,5},{8,10},{9,11},{10,... | collective-permute-start | bytes 3538952 | tf_op jit(solution)/shard_map/ppermute | solution.py:842
  328.1 35.9 %collective-permute-start.43 = (bf16[2,192,1536]{2,1,0:T(8,128)(2,1)S(1)}, bf16[2,192,1536]{2,1,0:T(8,128)(2,1)S(1)}, u32[]{:S(2)}, u32[]{:S(2)}) collective-permute-start(bf16[2,192,1536]{2,1,0:T(8,128)(2,1)S(1)} %pad_maximum_fusion.9.refs_0_), channel_id=1, source_target_pairs={{0,2},{1,3},{2,0},{3,1},{4,6},{5,7},{6,4},{7,5},{8,10},{9,11},{10,... | collective-permute-start | bytes 3538952 | tf_op jit(solution)/shard_map/ppermute | solution.py:842
  328.8 35.2 %collective-permute-start.37 = (bf16[2,192,1536]{2,1,0:T(8,128)(2,1)S(1)}, bf16[2,192,1536]{2,1,0:T(8,128)(2,1)}, u32[]{:S(2)}, u32[]{:S(2)}) collective-permute-start(bf16[2,192,1536]{2,1,0:T(8,128)(2,1)S(1)} %pad_maximum_fusion.8.refs_0_), channel_id=1, source_target_pairs={{0,16},{16,0},{1,17},{17,1},{2,18},{18,2},{3,19},{19,3},{4,20},{20... | collective-permute-start | bytes 3538952 | tf_op jit(solution)/shard_map/ppermute | solution.py:846
  342.1 54.7 %collective-permute-start.44 = (bf16[2,192,1536]{2,1,0:T(8,128)(2,1)S(1)}, bf16[2,192,1536]{2,1,0:T(8,128)(2,1)}, u32[]{:S(2)}, u32[]{:S(2)}) collective-permute-start(bf16[2,192,1536]{2,1,0:T(8,128)(2,1)S(1)} %pad_maximum_fusion.9.refs_0_), channel_id=1, source_target_pairs={{0,16},{16,0},{1,17},{17,1},{2,18},{18,2},{3,19},{19,3},{4,20},{20... | collective-permute-start | bytes 3538952 | tf_op jit(solution)/shard_map/ppermute | solution.py:846
  349.1 72.1 %collective-permute-start.46 = (bf16[1152,1536]{1,0:T(8,128)(2,1)}, bf16[1152,1536]{1,0:T(8,128)(2,1)S(1)}, u32[]{:S(2)}, u32[]{:S(2)}) collective-permute-start(bf16[1152,1536]{1,0:T(8,128)(2,1)} %get-tuple-element.166.refs_10_.refs_2_), channel_id=1, source_target_pairs={{0,16},{16,0},{1,17},{17,1},{2,18},{18,2},{3,19},{19,3},{4,20},{20... | collective-permute-start | bytes 10616840 | tf_op jit(solution)/shard_map/ppermute | solution.py:846
  364.0 32.8 %collective-permute-start.45 = (bf16[2,192,1536]{2,1,0:T(8,128)(2,1)S(1)}, bf16[2,192,1536]{2,1,0:T(8,128)(2,1)}, u32[]{:S(2)}, u32[]{:S(2)}) collective-permute-start(bf16[2,192,1536]{2,1,0:T(8,128)(2,1)S(1)} %collective-permute-done.43.refs_1_), channel_id=1, source_target_pairs={{0,16},{16,0},{1,17},{17,1},{2,18},{18,2},{3,19},{19,3},{4,20},{20... | collective-permute-start | bytes 3538952 | tf_op jit(solution)/shard_map/ppermute | solution.py:846
  392.6 80.5 %collective-permute-start.53 = (bf16[1152,1536]{1,0:T(8,128)(2,1)}, bf16[1152,1536]{1,0:T(8,128)(2,1)}, u32[]{:S(2)}, u32[]{:S(2)}) collective-permute-start(bf16[1152,1536]{1,0:T(8,128)(2,1)} %get-tuple-element.187.refs_2_), channel_id=1, source_target_pairs={{0,16},{16,0},{1,17},{17,1},{2,18},{18,2},{3,19},{19,3},{4,20},{20... | collective-permute-start | bytes 10616840 | tf_op jit(solution)/shard_map/ppermute | solution.py:846
  395.2 26.0 %collective-permute-start.42 = (f32[8,1536]{1,0:T(8,128)S(1)}, f32[8,1536]{1,0:T(8,128)S(1)}, u32[]{:S(2)}, u32[]{:S(2)}) collective-permute-start(f32[8,1536]{1,0:T(8,128)S(1)} %add.151.refs_1_), channel_id=1, source_target_pairs={{0,2},{1,3},{2,0},{3,1},{4,6},{5,7},{6,4},{7,5},{8,10},{9,11},{10,... | collective-permute-start | bytes 147464 | tf_op jit(solution)/shard_map/ppermute | solution.py:842
  484.7 27.9 %collective-permute-start.54 = (bf16[2,192,1536]{2,1,0:T(8,128)(2,1)}, bf16[2,192,1536]{2,1,0:T(8,128)(2,1)S(1)}, u32[]{:S(2)}, u32[]{:S(2)}) collective-permute-start(bf16[2,192,1536]{2,1,0:T(8,128)(2,1)} %get-tuple-element.191), channel_id=1, source_target_pairs={{0,2},{1,3},{2,0},{3,1},{4,6},{5,7},{6,4},{7,5},{8,10},{9,11},{10,... | collective-permute-start | bytes 3538952 | tf_op jit(solution)/shard_map/ppermute | solution.py:842
  513.7 23.8 %collective-permute-start.55 = (bf16[192,1536]{1,0:T(8,128)(2,1)S(1)}, bf16[192,1536]{1,0:T(8,128)(2,1)S(1)}, u32[]{:S(2)}, u32[]{:S(2)}) collective-permute-start(bf16[192,1536]{1,0:T(8,128)(2,1)S(1)} %fusion.7), channel_id=1, source_target_pairs={{0,1},{1,0},{2,3},{3,2},{4,5},{5,4},{6,7},{7,6},{8,9},{9,8},{10,11... | collective-permute-start | bytes 1769480 | tf_op jit(solution)/shard_map/ppermute | solution.py:842
  536.1 30.1 %collective-permute-start.57 = (bf16[2,192,1536]{2,1,0:T(8,128)(2,1)}, bf16[2,192,1536]{2,1,0:T(8,128)(2,1)S(1)}, u32[]{:S(2)}, u32[]{:S(2)}) collective-permute-start(bf16[2,192,1536]{2,1,0:T(8,128)(2,1)} %get-tuple-element.204), channel_id=1, source_target_pairs={{0,2},{1,3},{2,0},{3,1},{4,6},{5,7},{6,4},{7,5},{8,10},{9,11},{10,... | collective-permute-start | bytes 3538952 | tf_op jit(solution)/shard_map/ppermute | solution.py:842
  562.5 29.7 %collective-permute-start.64 = (bf16[2,192,1664]{2,1,0:T(8,128)(2,1)S(1)}, bf16[2,192,1664]{2,1,0:T(8,128)(2,1)S(1)}, u32[]{:S(2)}, u32[]{:S(2)}) collective-permute-start(bf16[2,192,1664]{2,1,0:T(8,128)(2,1)S(1)} %pad_maximum_fusion.2.refs_0_), channel_id=1, source_target_pairs={{0,2},{1,3},{2,0},{3,1},{4,6},{5,7},{6,4},{7,5},{8,10},{9,11},{10,... | collective-permute-start | bytes 3833864 | tf_op jit(solution)/shard_map/ppermute | solution.py:842
  564.1 28.1 %collective-permute-start.48 = (bf16[384,1536]{1,0:T(8,128)(2,1)S(1)}, bf16[384,1536]{1,0:T(8,128)(2,1)S(1)}, u32[]{:S(2)}, u32[]{:S(2)}) collective-permute-start(bf16[384,1536]{1,0:T(8,128)(2,1)S(1)} %copy-done.76), channel_id=1, source_target_pairs={{0,16},{16,0},{1,17},{17,1},{2,18},{18,2},{3,19},{19,3},{4,20},{20... | collective-permute-start | bytes 3538952 | tf_op jit(solution)/shard_map/ppermute | solution.py:846
  564.1 28.2 %collective-permute-start.47 = (bf16[4,192,384]{2,1,0:T(8,128)(2,1)}, bf16[4,192,384]{2,1,0:T(8,128)(2,1)}, u32[]{:S(2)}, u32[]{:S(2)}) collective-permute-start(bf16[4,192,384]{2,1,0:T(8,128)(2,1)} %get-tuple-element.172), channel_id=1, source_target_pairs={{0,16},{16,0},{1,17},{17,1},{2,18},{18,2},{3,19},{19,3},{4,20},{20... | collective-permute-start | bytes 1769480 | tf_op jit(solution)/shard_map/ppermute | solution.py:846
  566.2 57.7 %collective-permute-start.65 = (bf16[2,192,1664]{2,1,0:T(8,128)(2,1)S(1)}, bf16[2,192,1664]{2,1,0:T(8,128)(2,1)}, u32[]{:S(2)}, u32[]{:S(2)}) collective-permute-start(bf16[2,192,1664]{2,1,0:T(8,128)(2,1)S(1)} %pad_maximum_fusion.2.refs_0_), channel_id=1, source_target_pairs={{0,16},{16,0},{1,17},{17,1},{2,18},{18,2},{3,19},{19,3},{4,20},{20... | collective-permute-start | bytes 3833864 | tf_op jit(solution)/shard_map/ppermute | solution.py:846
  567.2 32.6 %collective-permute-start.58 = (bf16[192,1536]{1,0:T(8,128)(2,1)S(1)}, bf16[192,1536]{1,0:T(8,128)(2,1)}, u32[]{:S(2)}, u32[]{:S(2)}) collective-permute-start(bf16[192,1536]{1,0:T(8,128)(2,1)S(1)} %fusion.6), channel_id=1, source_target_pairs={{0,1},{1,0},{2,3},{3,2},{4,5},{5,4},{6,7},{7,6},{8,9},{9,8},{10,11... | collective-permute-start | bytes 1769480 | tf_op jit(solution)/shard_map/ppermute | solution.py:842
  592.2 31.6 %collective-permute-start.66 = (bf16[2,192,1664]{2,1,0:T(8,128)(2,1)S(1)}, bf16[2,192,1664]{2,1,0:T(8,128)(2,1)S(1)}, u32[]{:S(2)}, u32[]{:S(2)}) collective-permute-start(bf16[2,192,1664]{2,1,0:T(8,128)(2,1)S(1)} %collective-permute-done.64.refs_1_), channel_id=1, source_target_pairs={{0,16},{16,0},{1,17},{17,1},{2,18},{18,2},{3,19},{19,3},{4,20},{20... | collective-permute-start | bytes 3833864 | tf_op jit(solution)/shard_map/ppermute | solution.py:846
  622.8 36.6 %collective-permute-start.60 = (bf16[2,192,1664]{2,1,0:T(8,128)(2,1)S(1)}, bf16[2,192,1664]{2,1,0:T(8,128)(2,1)}, u32[]{:S(2)}, u32[]{:S(2)}) collective-permute-start(bf16[2,192,1664]{2,1,0:T(8,128)(2,1)S(1)} %pad_maximum_fusion.1.refs_0_), channel_id=1, source_target_pairs={{0,2},{1,3},{2,0},{3,1},{4,6},{5,7},{6,4},{7,5},{8,10},{9,11},{10,... | collective-permute-start | bytes 3833864 | tf_op jit(solution)/shard_map/ppermute | solution.py:842
  659.2 177.3 %reduce-scatter.13.cloned.1.call-start = ((), (), s32[]{:S(2)}) async-start(), calls=%async_computation.9 | async-start | bytes 1474560
  659.2 30.9 %collective-permute-start.61 = (bf16[2,192,1664]{2,1,0:T(8,128)(2,1)S(1)}, bf16[2,192,1664]{2,1,0:T(8,128)(2,1)S(1)}, u32[]{:S(2)}, u32[]{:S(2)}) collective-permute-start(bf16[2,192,1664]{2,1,0:T(8,128)(2,1)S(1)} %pad_maximum_fusion.1.refs_0_), channel_id=1, source_target_pairs={{0,16},{16,0},{1,17},{17,1},{2,18},{18,2},{3,19},{19,3},{4,20},{20... | collective-permute-start | bytes 3833864 | tf_op jit(solution)/shard_map/ppermute | solution.py:846
  659.4 30.8 %collective-permute-start.62 = (bf16[2,192,1664]{2,1,0:T(8,128)(2,1)}, bf16[2,192,1664]{2,1,0:T(8,128)(2,1)S(1)}, u32[]{:S(2)}, u32[]{:S(2)}) collective-permute-start(bf16[2,192,1664]{2,1,0:T(8,128)(2,1)} %collective-permute-done.60.refs_5_.refs_1_), channel_id=1, source_target_pairs={{0,16},{16,0},{1,17},{17,1},{2,18},{18,2},{3,19},{19,3},{4,20},{20... | collective-permute-start | bytes 3833864 | tf_op jit(solution)/shard_map/ppermute | solution.py:846
  714.4 194.6 %reduce-scatter.11.cloned.1.call-start = ((), (), s32[]{:S(2)}) async-start(), calls=%async_computation.8 | async-start | bytes 2949120 | tf_op jit(solution)/shard_map/reduce_scatter | solution.py:1142
  718.5 190.5 %reduce-scatter.9.cloned.1.call-start = ((), (), s32[]{:S(2)}) async-start(), calls=%async_computation.7 | async-start | bytes 2949120 | tf_op jit(solution)/shard_map/reduce_scatter | solution.py:1142
  720.6 29.6 %collective-permute-start.69 = (bf16[2,192,1536]{2,1,0:T(8,128)(2,1)S(1)}, bf16[2,192,1536]{2,1,0:T(8,128)(2,1)S(1)}, u32[]{:S(2)}, u32[]{:S(2)}) collective-permute-start(bf16[2,192,1536]{2,1,0:T(8,128)(2,1)S(1)} %copy-done.77), channel_id=1, source_target_pairs={{0,2},{1,3},{2,0},{3,1},{4,6},{5,7},{6,4},{7,5},{8,10},{9,11},{10,... | collective-permute-start | bytes 3538952 | tf_op jit(solution)/shard_map/ppermute | solution.py:842
  721.7 53.0 %collective-permute-start.71 = (bf16[2,192,1536]{2,1,0:T(8,128)(2,1)S(1)}, bf16[2,192,1536]{2,1,0:T(8,128)(2,1)S(1)}, u32[]{:S(2)}, u32[]{:S(2)}) collective-permute-start(bf16[2,192,1536]{2,1,0:T(8,128)(2,1)S(1)} %copy-done.80), channel_id=1, source_target_pairs={{0,2},{1,3},{2,0},{3,1},{4,6},{5,7},{6,4},{7,5},{8,10},{9,11},{10,... | collective-permute-start | bytes 3538952 | tf_op jit(solution)/shard_map/ppermute | solution.py:842
  749.0 50.5 %collective-permute-start.70 = (bf16[4,192,1152]{2,1,0:T(8,128)(2,1)}, bf16[4,192,1152]{2,1,0:T(8,128)(2,1)}, u32[]{:S(2)}, u32[]{:S(2)}) collective-permute-start(bf16[4,192,1152]{2,1,0:T(8,128)(2,1)} %get-tuple-element.234), channel_id=1, source_target_pairs={{0,16},{16,0},{1,17},{17,1},{2,18},{18,2},{3,19},{19,3},{4,20},{20... | collective-permute-start | bytes 5308424 | tf_op jit(solution)/shard_map/ppermute | solution.py:846
  749.1 50.4 %collective-permute-start.72 = (bf16[2,192,1536]{2,1,0:T(8,128)(2,1)}, bf16[2,192,1536]{2,1,0:T(8,128)(2,1)}, u32[]{:S(2)}, u32[]{:S(2)}) collective-permute-start(bf16[2,192,1536]{2,1,0:T(8,128)(2,1)} %get-tuple-element.239), channel_id=1, source_target_pairs={{0,2},{1,3},{2,0},{3,1},{4,6},{5,7},{6,4},{7,5},{8,10},{9,11},{10,... | collective-permute-start | bytes 3538952 | tf_op jit(solution)/shard_map/ppermute | solution.py:842
  795.6 23.1 %collective-permute-start.75 = (bf16[1536,304]{0,1:T(8,128)(2,1)S(1)}, bf16[1536,304]{0,1:T(8,128)(2,1)}, u32[]{:S(2)}, u32[]{:S(2)}) collective-permute-start(bf16[1536,304]{0,1:T(8,128)(2,1)S(1)} %copy.63), channel_id=1, source_target_pairs={{0,16},{16,0},{1,17},{17,1},{2,18},{18,2},{3,19},{19,3},{4,20},{20... | collective-permute-start | bytes 2801672 | tf_op jit(solution)/shard_map/ppermute | solution.py:846
  811.1 27.5 %collective-permute-start.74 = (bf16[192,1536]{1,0:T(8,128)(2,1)}, bf16[192,1536]{1,0:T(8,128)(2,1)}, u32[]{:S(2)}, u32[]{:S(2)}) collective-permute-start(bf16[192,1536]{1,0:T(8,128)(2,1)} %fusion.4), channel_id=1, source_target_pairs={{0,1},{1,0},{2,3},{3,2},{4,5},{5,4},{6,7},{7,6},{8,9},{9,8},{10,11... | collective-permute-start | bytes 1769480 | tf_op jit(solution)/shard_map/ppermute | solution.py:842
  813.1 51.3 %collective-permute-start.73 = (bf16[192,1536]{1,0:T(8,128)(2,1)}, bf16[192,1536]{1,0:T(8,128)(2,1)}, u32[]{:S(2)}, u32[]{:S(2)}) collective-permute-start(bf16[192,1536]{1,0:T(8,128)(2,1)} %fusion.5), channel_id=1, source_target_pairs={{0,1},{1,0},{2,3},{3,2},{4,5},{5,4},{6,7},{7,6},{8,9},{9,8},{10,11... | collective-permute-start | bytes 1769480 | tf_op jit(solution)/shard_map/ppermute | solution.py:842
  816.1 62.4 %collective-permute-start.77 = (bf16[192,1536]{1,0:T(8,128)(2,1)}, bf16[192,1536]{1,0:T(8,128)(2,1)}, u32[]{:S(2)}, u32[]{:S(2)}) collective-permute-start(bf16[192,1536]{1,0:T(8,128)(2,1)} %fusion.3), channel_id=1, source_target_pairs={{0,1},{1,0},{2,3},{3,2},{4,5},{5,4},{6,7},{7,6},{8,9},{9,8},{10,11... | collective-permute-start | bytes 1769480 | tf_op jit(solution)/shard_map/ppermute | solution.py:842
  817.2 61.3 %collective-permute-start.78 = (bf16[2,192,1536]{2,1,0:T(8,128)(2,1)}, bf16[2,192,1536]{2,1,0:T(8,128)(2,1)}, u32[]{:S(2)}, u32[]{:S(2)}) collective-permute-start(bf16[2,192,1536]{2,1,0:T(8,128)(2,1)} %get-tuple-element.249), channel_id=1, source_target_pairs={{0,2},{1,3},{2,0},{3,1},{4,6},{5,7},{6,4},{7,5},{8,10},{9,11},{10,... | collective-permute-start | bytes 3538952 | tf_op jit(solution)/shard_map/ppermute | solution.py:842
  824.8 37.6 %collective-permute-start.76 = (bf16[2,384,304]{1,2,0:T(8,128)(2,1)}, bf16[2,384,304]{1,2,0:T(8,128)(2,1)S(1)}, u32[]{:S(2)}, u32[]{:S(2)}) collective-permute-start(bf16[2,384,304]{1,2,0:T(8,128)(2,1)} %select_convert_fusion.1), channel_id=1, source_target_pairs={{0,4},{4,0},{8,12},{12,8},{1,5},{5,1},{9,13},{13,9},{2,6},{6,2},{1... | collective-permute-start | bytes 1400840 | tf_op jit(solution)/shard_map/ppermute | solution.py:902
  838.6 38.7 %collective-permute-start.92 = (f32[384,384]{1,0:T(8,128)}, f32[384,384]{1,0:T(8,128)}, u32[]{:S(2)}, u32[]{:S(2)}) collective-permute-start(f32[384,384]{1,0:T(8,128)} %convert_select_fusion.2), channel_id=1, source_target_pairs={{0,16},{16,0},{1,17},{17,1},{2,18},{18,2},{3,19},{19,3},{4,20},{20... | collective-permute-start | bytes 1769480 | tf_op jit(solution)/shard_map/ppermute | solution.py:846
  885.9 46.8 %collective-permute-start.79 = (f32[2,192,1536]{2,1,0:T(8,128)S(1)}, f32[2,192,1536]{2,1,0:T(8,128)}, u32[]{:S(2)}, u32[]{:S(2)}) collective-permute-start(f32[2,192,1536]{2,1,0:T(8,128)S(1)} %pad_maximum_fusion.refs_0_), channel_id=1, source_target_pairs={{0,16},{16,0},{1,17},{17,1},{2,18},{18,2},{3,19},{19,3},{4,20},{20... | collective-permute-start | bytes 7077896 | tf_op jit(solution)/shard_map/ppermute | solution.py:846
  886.1 25.4 %collective-permute-start.91 = (bf16[384,304]{0,1:T(8,128)(2,1)S(1)}, bf16[384,304]{0,1:T(8,128)(2,1)}, u32[]{:S(2)}, u32[]{:S(2)}) collective-permute-start(bf16[384,304]{0,1:T(8,128)(2,1)S(1)} %fusion.12), channel_id=1, source_target_pairs={{0,2},{1,3},{2,0},{3,1},{4,6},{5,7},{6,4},{7,5},{8,10},{9,11},{10,... | collective-permute-start | bytes 700424 | tf_op jit(solution)/shard_map/ppermute | solution.py:842
  906.1 23.0 %collective-permute-start.81 = (f32[2,192,768]{2,1,0:T(8,128)}, f32[2,192,768]{2,1,0:T(8,128)}, u32[]{:S(2)}, u32[]{:S(2)}) collective-permute-start(f32[2,192,768]{2,1,0:T(8,128)} %get-tuple-element.301), channel_id=1, source_target_pairs={{0,16},{16,0},{1,17},{17,1},{2,18},{18,2},{3,19},{19,3},{4,20},{20... | collective-permute-start | bytes 3538952 | tf_op jit(solution)/shard_map/ppermute | solution.py:846
  914.3 23.3 %collective-permute-start.88 = (f32[384,768]{1,0:T(8,128)S(1)}, f32[384,768]{1,0:T(8,128)S(1)}, u32[]{:S(2)}, u32[]{:S(2)}) collective-permute-start(f32[384,768]{1,0:T(8,128)S(1)} %get-tuple-element.313), channel_id=1, source_target_pairs={{0,16},{16,0},{1,17},{17,1},{2,18},{18,2},{3,19},{19,3},{4,20},{20... | collective-permute-start | bytes 3538952 | tf_op jit(solution)/shard_map/ppermute | solution.py:846
  (127 other events, 1300.4 us)
Sparse Core Ops, SparseCore 0:
  111.8 50.3 all-gather.3
  164.3 29.5 all-gather.5
  195.5 79.5 all-gather.7
  659.3 41.0 reduce-scatter.14
  714.5 41.1 reduce-scatter.12
  757.9 46.7 reduce-scatter.10
  807.6 58.2 reduce-scatter.8

commit v3 on v2

--- a/solution.py
+++ b/solution.py
@@ -105,9 +105,14 @@
     )
 
 
+def shard_place(at, k):
+    place = at - k if k < 4 else at + (k - 3)
+    return place, (place >= 0) & (place < 4)
+
+
 def fwd_kernel(with_dot, shards, inner, state, heads, order, sc, *refs):
-    pieces = refs[:4]
-    refs = refs[4:]
+    gathered = order is None
+    pieces, refs = (refs[:1], refs[1:]) if gathered else (refs[:4], refs[4:])
     if shards > 1:
         parts, refs, whole_w = refs[:shards], refs[shards:-1], refs[-1]
 
@@ -115,14 +120,22 @@
         def _():
             size = parts[0].shape[0]
             for k in range(shards):
-                at = pl.multiple_of(((sc[4] - k) & 3) * size, size)
-                whole_w[pl.ds(at, size), :] = parts[k][...]
+                place, held = shard_place(sc[4], k)
+
+                @pl.when(held)
+                def _(k=k, place=place):
+                    whole_w[pl.ds(pl.multiple_of(place * size, size), size), :] = parts[k][...]
 
         refs = (whole_w, *refs)
+    w, cp, hp, chp, live = refs[:5]
+    refs = refs[5:]
     if with_dot:
-        w, cp, hp, chp, live, gno, nrm, proj, y_out, st, gated_out, stats, carry, ubuf, act = refs
+        gno, refs = refs[0], refs[1:]
+    if gathered:
+        nrm = pieces[0]
     else:
-        w, cp, hp, chp, live, nrm, proj, y_out, st, gated_out, stats, carry, ubuf, act = refs
+        nrm, refs = refs[0], refs[1:]
+    proj, y_out, st, gated_out, stats, carry, ubuf, act = refs
     step = pl.program_id(0)
     sec, ten, e0, e1 = sc[0], sc[1], sc[2], sc[3]
     rows = nrm.shape[0]
@@ -135,7 +148,8 @@
         carry[...] = jnp.zeros_like(carry)
         ubuf[0:8, :] = jnp.zeros((8, wide), F32)
 
-    bring(nrm, pieces, step, sec, ten, order)
+    if not gathered:
+        bring(nrm, pieces, step, sec, ten, order)
     proj[...] = mm(nrm[...], w[...])
     lv = live[...]
     dt_at = slice(inner + wide, inner + wide + LANES)
@@ -181,28 +195,40 @@
         rd = jnp.zeros((CHUNK, LANES), F32)
         for k in range(pairs):
             lanes = slice(k * LANES, (k + 1) * LANES)
-            mixed, cums = [], []
+            mixed, fine, cums = [], [], []
             for h in (2 * k, 2 * k + 1):
                 cum_col = column(cum, h)
                 cums.append(cum_col)
                 decay = jnp.exp(jnp.minimum(cum_col - cum_t[h : h + 1, :], 0.0))
-                mixed.append((decay * scores).astype(BF16))
+                high, low = split_two(decay * scores)
+                mixed.append(high)
+                fine.append(low)
             cum_e = jnp.where(low_half, cums[0], cums[1])
             dt_e = jnp.where(low_half, column(dt, 2 * k), column(dt, 2 * k + 1))
             x_in = act[at, lanes].astype(F32)
             xdt = x_in * dt_e
             both = jnp.concatenate([jnp.where(low_half, xdt, 0.0), jnp.where(low_half, 0.0, xdt)], 0)
-            within = mm(jnp.concatenate(mixed, 1), both.astype(BF16))
+            both, both_low = split_two(both)
+            mixed = jnp.concatenate(mixed, 1)
+            within = mm(mixed, both)
             old = carry[:, lanes]
-            old_low = old.astype(BF16)
-            st[c, :, lanes] = old_low
-            across = mm(c_in, old_low) * (jnp.exp(cum_e) * from_prev)
+            old_high, old_low = split_two(old)
+            st[c, :, lanes] = old_high
+            entering = jnp.exp(cum_e) * from_prev
+            across = mm(c_in, old_high) * entering
             cum_end = cum_e[CHUNK - 1 : CHUNK, :]
             to_end = jnp.exp(cum_end - cum_e) * tail_same
-            added = mm(b_in, (xdt * to_end).astype(BF16), TN)
+            if with_dot:
+                added = mm(b_in, (xdt * to_end).astype(BF16), TN)
+            else:
+                into = jnp.concatenate(split_two(xdt * to_end), 0)
+                added = mm(jnp.concatenate([b_in, b_in], 0), into, TN)
             carry[:, lanes] = old * (jnp.exp(cum_end) * linked) + added
             y = within + across + chp[0:1, lanes] * x_in
             y_out[at, lanes] = y
+            if not with_dot:
+                y = y + mm(jnp.concatenate(fine, 1), both) + mm(mixed, both_low)
+                y = y + mm(c_in, old_low) * entering
             gate = proj[at, lanes]
             gated = y * (gate * sigmoid(gate))
             gated_out[at, lanes] = gated
@@ -278,10 +304,10 @@
     if count == 1:
         w_t[...] = parts[0][...].T
     else:
-        pick = (sc[4] - pl.program_id(0)) & 3
         for k in range(count):
-
-            @pl.when(pick == k)
+            place, held = shard_place(sc[4], k)
+
+            @pl.when(held & (place == pl.program_id(0)))
             def _(k=k):
                 w_t[...] = parts[k][...].T
 
@@ -314,27 +340,25 @@
         total = total + mm(refs[2 * k][...], refs[2 * k + 1][...], TN)
     if start:
         total = total + refs[2 * count][...]
-    refs[-1][...] = total
-
-
-def run_outer(scalars, pairs, start, tall, deps):
+    refs[-1][...] = total.astype(refs[-1].dtype)
+
+
+def run_outer(scalars, pairs, start, tall, kind, deps):
     depth = pairs[0][0].shape[0]
     rows, cols = pairs[0][0].shape[1], pairs[0][1].shape[1]
+    tile = 3 * LANES if tall else 4 * LANES
+    cut = pl.BlockSpec((depth, tile), lambda i, sc: (0, i))
     if tall:
-        tile, grid = 3 * LANES, (rows // (3 * LANES),)
-        cut = pl.BlockSpec((depth, tile), lambda i, sc: (0, i))
-        out = pl.BlockSpec((tile, cols), lambda i, sc: (i, 0))
+        grid, out = (rows // tile,), pl.BlockSpec((tile, cols), lambda i, sc: (i, 0))
         ins = [item for a, b in pairs for item in ((cut, a), fixed(b))]
     else:
-        tile, grid = 4 * LANES, (cols // (4 * LANES),)
-        cut = pl.BlockSpec((depth, tile), lambda i, sc: (0, i))
-        out = pl.BlockSpec((rows, tile), lambda i, sc: (0, i))
+        grid, out = (cols // tile,), pl.BlockSpec((rows, tile), lambda i, sc: (0, i))
         ins = [item for a, b in pairs for item in (fixed(a), (cut, b))]
     if start is not None:
         ins.append((out, start))
     return call(
         partial(outer_kernel, len(pairs), start is not None), "outer_rows", scalars, grid, ins,
-        [(out, (rows, cols), F32)], [], deps, 9 * 1024**3 * len(pairs), 0, 16 * 1024 * 1024,
+        [(out, (rows, cols), kind)], [], deps, 9 * 1024**3 * len(pairs), 0, 16 * 1024 * 1024,
     )[0]
 
 
@@ -365,8 +389,8 @@
     own = pl.ds(pl.multiple_of(sc[0] * size, LANES), size)
     other = pl.ds(pl.multiple_of((1 - sc[0]) * size, LANES), size)
     for k in range(2):
-        out[:, k, own] = mine[:, k * size : (k + 1) * size]
-        out[:, k, other] = theirs[:, k * size : (k + 1) * size]
+        out[:, k, own] = mine[:, k * size : (k + 1) * size].astype(F32)
+        out[:, k, other] = theirs[:, k * size : (k + 1) * size].astype(F32)
 
 
 def run_weave(scalars, mine, theirs):
@@ -381,14 +405,18 @@
 
 
 def run_fwd(scalars, pieces, order, w, cp, hp, chp, live, gno, inner, state, heads, deps):
-    half, width = pieces[0].shape[1:]
-    rows = 2 * half
+    width = pieces[0].shape[-1]
     length = live.shape[0]
-    steps = length // rows
+    steps = 4
+    rows = length // steps
     cols = w[0].shape[1]
     chunks = rows // CHUNK
     by_row = lambda n: pl.BlockSpec((rows, n), lambda i, sc: (i, 0))
-    ins = [(piece_spec(piece.shape, order), piece) for piece in pieces]
+    if order is None:
+        ins, outs = [(by_row(width), pieces[0])], []
+    else:
+        ins = [(piece_spec(piece.shape, order), piece) for piece in pieces]
+        outs = [(by_row(width), (length, width), BF16)]
     ins += [fixed(part) for part in w]
     ins += [fixed(cp), fixed(hp), fixed(chp), (by_row(LANES), live)]
     joined = [pltpu.VMEM((width, cols), BF16)] if len(w) > 1 else []
@@ -397,8 +425,8 @@
     return call(
         partial(fwd_kernel, gno is not None, len(w), inner, state, heads, order), "layer_fwd", scalars, (steps,),
         ins,
-        [
-            (by_row(width), (length, width), BF16),
+        outs
+        + [
             (by_row(cols), (length, cols), F32),
             (by_row(inner), (length, inner), F32),
             (pl.BlockSpec((chunks, state, inner), lambda i, sc: (i, 0, 0)), (length // CHUNK, state, inner), BF16),
@@ -415,11 +443,11 @@
     )
 
 
-def scale_kernel(inner_width, sc, gated, sa, sb, chp, no_out, send, rc):
+def scale_kernel(inner_width, sc, gated, s0, s1, s2, s3, chp, no_out, send, rc):
     rows = gated.shape[0]
     half = rows // 2
     theirs = pl.multiple_of((1 - sc[0]) * half, half)
-    total = sa[...] + sb[...]
+    total = (s0[...] + s1[...]) + (s2[...] + s3[...])
     inv = lax.rsqrt(total / inner_width + EPS)
     coef = jnp.concatenate([total[1:8], total[0:1]], 0) * (inv * inv * inv) / inner_width
     both = jnp.where(iota(total.shape, 0) == 0, inv, pltpu.roll(coef, 1, 0))
@@ -434,14 +462,14 @@
     send[0] = no_out[pl.ds(theirs, half), :]
 
 
-def run_scale(scalars, gated, sa, sb, chp, rows, inner_width, deps):
+def run_scale(scalars, gated, sums, chp, rows, inner_width, deps):
     length, inner = gated.shape
     steps = length // rows
     by_row = lambda n: pl.BlockSpec((rows, n), lambda i, sc: (i, 0))
     by_lane = pl.BlockSpec((8, rows), lambda i, sc: (0, i))
     return call(
         partial(scale_kernel, inner_width), "scale_rows", scalars, (steps,),
-        [(by_row(inner), gated), (by_lane, sa), (by_lane, sb), fixed(chp)],
+        [(by_row(inner), gated)] + [(by_lane, part) for part in sums] + [fixed(chp)],
         [
             (by_row(inner), (length, inner), BF16),
             (pl.BlockSpec((1, rows // 2, inner), lambda i, sc: (i, 0, 0)), (steps, rows // 2, inner), BF16),
@@ -730,42 +758,51 @@
     )
 
 
-def half_kernel(axis, sc, kept, got, wa, wb, own, near, far):
-    ten = sc[1]
-    groups = [jnp.bitwise_xor(ten, k) for k in (0, 3 - axis, axis, 3)]
-    half = own.shape[0]
-    left = jnp.concatenate([kept[g, 0] for g in groups], 0)
-    right = jnp.concatenate([got[g] for g in groups], 0)
+def half_kernel(axis, sc, kept, got, wa, wb, *outs):
+    half = got.shape[1]
+    if axis:
+        groups = [jnp.bitwise_xor(sc[1], k) for k in (0, 3 - axis, axis, 3)]
+        left = jnp.concatenate([kept[g, 0] for g in groups], 0)
+        right = jnp.concatenate([got[g] for g in groups], 0)
+    else:
+        kept1, got1, *outs = outs
+        left = jnp.concatenate([ref[g, 0] for g in range(4) for ref in (kept, kept1)], 0)
+        right = jnp.concatenate([ref[g] for g in range(4) for ref in (got, got1)], 0)
     total = mm(jnp.concatenate([left, right], 1), jnp.concatenate([wa[...], wb[...]], 0))
-    own[...] = total[:half]
-    near[...] = total[half : 2 * half]
-    far[0] = total[2 * half : 3 * half].astype(BF16)
-    far[1] = total[3 * half :].astype(BF16)
-
-
-def run_half(scalars, full, got, wa, wb, axis, deps):
+    if axis:
+        own, near, far = outs
+        own[...] = total[:half]
+        near[...] = total[half : 2 * half]
+        far[0] = total[2 * half : 3 * half].astype(far.dtype)
+        far[1] = total[3 * half :].astype(far.dtype)
+    else:
+        outs[0][...] = total.astype(BF16)
+
+
+def run_half(scalars, full, got, wa, wb, axis, deps, more=None, kind=BF16):
     groups, half, depth = got.shape
     width = wa.shape[1]
     tile = 4 * LANES
     w_spec = pl.BlockSpec((depth, tile), lambda i, sc: (0, i))
-    part = pl.BlockSpec((half, tile), lambda i, sc: (0, i))
+    part = lambda n: pl.BlockSpec((n, tile), lambda i, sc: (0, i))
+    if axis:
+        outs = [
+            (part(half), (half, width), F32),
+            (part(half), (half, width), F32),
+            (pl.BlockSpec((2, half, tile), lambda i, sc: (0, 0, i)), (2, half, width), kind),
+        ]
+    else:
+        outs = [(part(2 * groups * half), (2 * groups * half, width), BF16)]
+    own = lambda v: (
+        pl.BlockSpec((groups, 1, half, depth), lambda i, sc: (0, sc[0], 0, 0)),
+        v.reshape(groups, 2, half, depth),
+    )
+    ins = [own(full), fixed(got), (w_spec, wa), (w_spec, wb)]
+    if more is not None:
+        ins += [own(more[0]), fixed(more[1])]
     return call(
-        partial(half_kernel, axis), "half_rows", scalars, (width // tile,),
-        [
-            (
-                pl.BlockSpec((groups, 1, half, depth), lambda i, sc: (0, sc[0], 0, 0)),
-                full.reshape(groups, 2, half, depth),
-            ),
-            fixed(got),
-            (w_spec, wa),
-            (w_spec, wb),
-        ],
-        [
-            (part, (half, width), F32),
-            (part, (half, width), F32),
-            (pl.BlockSpec((2, half, tile), lambda i, sc: (0, 0, i)), (2, half, width), BF16),
-        ],
-        [], deps, 8 * 1024**3, 0, 10 * 1024**2,
+        partial(half_kernel, axis), "half_rows", scalars, (width // tile,), ins,
+        outs, [], deps, 8 * 1024**3, 0, 10 * 1024**2,
     )
 
 
@@ -775,13 +812,14 @@
     out[...] = (v * inv * gain[0:1, :]).astype(BF16)
 
 
-def owner_kernel(final, own, far, near, x, gain, *outs):
+def final_kernel(total, x0, x1, out):
+    out[0] = x0[...].astype(F32) + total[0].astype(F32)
+    out[1] = x1[...].astype(F32) + total[1].astype(F32)
+
+
+def owner_kernel(own, far, near, x, gain, h1, normed, kept):
     total = own[...] + far[0].astype(F32) + near[...].astype(F32)
     out = x[...].astype(F32) + total
-    if final:
-        outs[0][...] = out
-        return
-    h1, normed, kept = outs
     low = out.astype(BF16)
     h1[...] = low
     kept[...] = total
@@ -869,8 +907,8 @@
 
 def settle(held, order, *waits):
     own, near, far = held
-    send = (after(near, *waits) + far[1].astype(F32)).astype(BF16)
-    return own, far, across(send, 1 + order)
+    send = (after(near, *waits) + far[1].astype(F32)).astype(far.dtype)
+    return (own, far, across(send, 1 + order)), send
 
 
 def all_tensor(value):
@@ -886,46 +924,19 @@
 def pieces_dp(value):
     if lax.axis_size("dp") != 4:
         return [lax.all_gather(value, "dp", axis=0, tiled=True)]
-    return [value] + [cycle(value, k) for k in (1, 2, 3)]
-
-
-def gather_dp(value):
-    got = pieces_dp(value)
-    if len(got) == 1:
-        return got[0]
-    at = lax.axis_index("dp")
-    shards = [lax.select_n(at, *[got[(i - j) % 4] for i in range(4)]) for j in range(4)]
-    return jnp.concatenate(shards, 0)
-
-
-def trade(value, bit):
-    return lax.ppermute(value, "dp", [(i, i ^ bit) for i in range(4)])
-
-
-def deal_one(value):
-    at = lax.axis_index("dp")
-    odd = (at & 1) == 1
-    shards = value.reshape(4, value.shape[0] // 4, value.shape[1])
-    kept = jnp.where(odd, shards[1::2], shards[0::2])
-    sent = jnp.where(odd, shards[0::2], shards[1::2]).astype(BF16)
-    return sent, kept, trade(sent, 1)
-
-
-def deal_two(kept, got):
-    high = lax.axis_index("dp") >= 2
-    both = kept + got.astype(F32)
-    sent = jnp.where(high, both[0], both[1]).astype(BF16)
-    return jnp.where(high, both[1], both[0]), trade(sent, 2)
-
-
-def scatter_dp(value):
-    return lax.psum_scatter(value, "dp", scatter_dimension=0, tiled=True)
-
-
-def sum_dp(value):
+    up, down = [value], [value]
+    for _ in range(3):
+        waits = (up[-1], down[-1])
+        up.append(lax.ppermute(after(up[-1], *waits), "dp", [(i, i + 1) for i in range(3)]))
+        down.append(lax.ppermute(after(down[-1], *waits), "dp", [(i + 1, i) for i in range(3)]))
+    return up + down[1:]
+
+
+def sum_dp(value, *waits):
     if lax.axis_size("dp") != 4:
         return lax.psum(value, "dp")
-    return value + cycle(value, 1) + cycle(value, 2) + cycle(value, 3)
+    got = [cycle(value, k) for k in (1, 2, 3)]
+    return value + sum(after(part, *waits) for part in got)
 
 
 def after(value, *waits):
@@ -989,20 +1000,23 @@
     first_parts = pieces_dp(zx_shards[0])
 
     rows_at = lambda v, m: jnp.where(first, v[m, :half, 0, :], v[m, half:, 0, :])
-    xs = [rows_at(x_in, m) for m in micros]
+    early_in = (first_parts[1], first_parts[4]) if len(first_parts) > 1 else (zx_shards[0],)
+    xs = [rows_at(after(x_in, *(early_in if m else zx_shards[:1])), m) for m in micros]
     gs = [rows_at(d_out, m) for m in micros]
     wide = lambda kind, n=0: jax.ShapeDtypeStruct((half, width + n), kind)
     small = jax.ShapeDtypeStruct((16, width), F32)
+    rows_of = lambda v: lax.all_gather(v, ("tensor", "section"), axis=0, tiled=True)
     pieces0 = [
-        widen(reach(run_plain(norm_kernel, "norm_rows", wide(BF16), (xs[m], gains[0]), ()), 0), 0)
+        [rows_of(run_plain(norm_kernel, "norm_rows", wide(BF16), (xs[m], gains[0]), ()))]
         for m in micros
     ]
-    wide0 = pieces0
-    pieces0 = [share(wide0[0][0], after(wide0[0][1], *first_parts[1:2]))]
     later = lambda v: lax.all_gather(after(v, *first_parts), "dp", axis=0, tiled=True)
     wo_t0, wo_t1 = later(wo_shards[0]), later(wo_shards[1])
     w1 = later(zx_shards[1])
 
+    doc_lengths, token_mask, *packs = lax.optimization_barrier(
+        (doc_lengths, token_mask, *packs, *early_in)
+    )[:4]
     scalars, lives = [], []
     for m in micros:
         e0 = doc_lengths[m, 0, 0]
@@ -1036,39 +1050,48 @@
         layers.append(dict(cp=cp, hp=hp, chp=chp))
     early, late = layers
 
-    def fwd(k, m, pieces, gno, deps):
-        nrm, proj, y, st, gated, stats = run_fwd(
-            scalars[m], pieces, 0, k["w"], k["cp"], k["hp"], k["chp"], lives[m], gno,
+    def fwd(k, m, pieces, gno, deps, *waits):
+        order = None if len(pieces) == 1 else 0
+        *nrm, proj, y, st, gated, stats = run_fwd(
+            scalars[m], pieces, order, k["w"], k["cp"], k["hp"], k["chp"], lives[m], gno,
             inner, state, heads, deps,
         )
-        part = stats + swap(stats)
-        part = part + across(part, 1 + m)
-        got = across(part, 2 - m)
-        return dict(nrm=nrm, proj=proj, y=y, st=st, gated=gated, stats=stats, part=part, got=got)
+        held = after(stats, *waits)
+        part = held + swap(held)
+        sums = [part] + [across(part, n) for n in (1, 2, 3)]
+        nrm = nrm[0] if nrm else pieces[0]
+        return dict(nrm=nrm, proj=proj, y=y, st=st, gated=gated, stats=stats, sums=sums)
 
     def scale(k, m, r, deps):
         r["no"], send, r["rc"] = run_scale(
-            scalars[m], r["gated"], r["part"], r["got"], k["chp"], rows, full_inner, deps
+            scalars[m], r["gated"], r["sums"], k["chp"], rows, full_inner, deps
         )
         r["sent"] = swap(send)
 
-    def project(k, m, r, deps):
-        return run_half(scalars[m], r["no"], r["sent"], k["wo"], k["wo_other"], 2, deps)
-
-    def back(k, m, rows_in, order, r, deps):
+    def project(k, m, r, deps, axis):
+        return run_half(
+            scalars[m], r["no"], r["sent"], k["wo"], k["wo_other"], axis, deps, kind=F32
+        )
+
+    def project_both(k, r0, r1, deps):
+        return run_half(
+            scalars[0], r0["no"], r0["sent"], k["wo"], k["wo_other"], 0, deps, (r1["no"], r1["sent"])
+        )[0]
+
+    def back(k, m, rows_in, order, r, deps, *waits):
         out = run_bwd(
             scalars[m], rows_in, order, r["proj"], r["y"], r["st"], r["rc"], lives[m],
             k["cp"], k["hp"], k["chp"], inner, state, heads, rows, width, deps,
         )
         gz, gzsend, gpack = out[-3:]
-        return gz, swap(gzsend), gpack, out[0]
+        return gz, swap(after(gzsend, *waits)), gpack, out[0]
 
     def unproject(k, m, gz, got, deps):
         return run_half(scalars[m], gz, got, k["w_t"], k["w_t_other"], 2, deps)
 
     def middle(m, parts, deps):
         return run_plain(
-            partial(owner_kernel, False), "owner_mid", (wide(BF16), wide(BF16), wide(F32)),
+            owner_kernel, "owner_mid", (wide(BF16), wide(BF16), wide(F32)),
             (*parts, xs[m], gains[1]), deps,
         )
 
@@ -1078,44 +1101,44 @@
     a0 = fwd(early, 0, pieces0[0], None, ())
     early["wo_t"], late["wo_t"] = wo_t0, wo_t1
     wide_g = [widen(near_g[m], m, a0["stats"]) for m in micros]
-    pieces0.append(share(wide0[1][0], after(wide0[1][1], a0["stats"])))
     a1 = fwd(early, 1, pieces0[1], None, [a0["stats"]] + [pair[1] for pair in near_g])
-    early["wo"] = wo_t0.T
+    early["wo"] = after(wo_t0, a1["stats"]).T
     early["wo_other"] = swap(early["wo"])
-    scale(early, 0, a0, [a1["stats"]])
+    scale(early, 0, a0, [a1["stats"]] + [pair[1] for pair in wide_g])
     pieces_g = [share(*wide_g[m]) for m in micros]
-    outs0 = project(early, 0, a0, ())
+    outs0 = project(early, 0, a0, (), 2)
     held0 = hand(outs0, 0)
     scale(early, 1, a1, [outs0[0]])
-    outs1 = project(early, 1, a1, [pair[1] for pair in wide_g])
-    held1 = hand(outs1, 0)
+    outs1 = project(early, 1, a1, (), 1)
+    held1 = hand(outs1, 1)
     gno0, gout1_0 = run_gn(scalars[0], pieces_g[0], 0, late["wo_t"], width, [outs1[0]])
-    parts0 = settle(held0, 0, gno0)
-    gno1, gout1_1 = run_gn(scalars[1], pieces_g[1], 1, late["wo_t"], width, [gno0, held0[2]])
-    parts1 = settle(held1, 0, gno1)
-    h_0, normed_0, u_0 = middle(0, parts0, [gno1, held1[2]])
+    parts0, sent0 = settle(held0, 0, gno0)
+    gno1, gout1_1 = run_gn(scalars[1], pieces_g[1], 1, late["wo_t"], width, [gno0, sent0])
+    parts1, sent1 = settle(held1, 1, gno1)
+    h_0, normed_0, u_0 = middle(0, parts0, [gno1])
     pair0 = reach(normed_0, 0)
     h_1, normed_1, u_1 = middle(1, parts1, [normed_0])
     pair1 = reach(normed_1, 0)
-    late["w_t"], late["wo"] = run_turn(places, late["w"], late["wo_t"], [normed_1])
-    wide0 = widen(pair0, 0, late["wo"])
+    wide0 = widen(pair0, 0, normed_1)
+    late["w_t"], late["wo"] = run_turn(places, late["w"], late["wo_t"], [wide0[0]])
     wide1 = widen(pair1, 0, late["wo"])
-    early["w_t"], _ = run_turn(places, early["w"], early["wo_t"], [late["wo"], pair0[1], pair1[1]])
-    late["wo_other"] = swap(late["wo"])
-    for k in layers:
-        k["w_t_other"] = swap(k["w_t"])
-
-    b0 = fwd(late, 0, share(*wide0), gno0, [early["w_t"]])
-    b1 = fwd(late, 1, share(*wide1), gno1, [b0["stats"]])
+    early["w_t"], _ = run_turn(places, early["w"], early["wo_t"], [late["wo"], wide1[0]])
+    late["wo_other"] = swap(after(late["wo"], wide1[0]))
+    late["w_t_other"] = swap(after(late["w_t"], early["w_t"]))
+    early["w_t_other"] = swap(early["w_t"])
+
+    b0 = fwd(late, 0, share(wide0[0], after(wide0[1], early["w_t"])), gno0, [early["w_t"]], wide1[1])
+    last1 = share(wide1[0], after(wide1[1], b0["stats"]))
+    b1 = fwd(late, 1, last1, gno1, [b0["stats"]])
     scale(late, 0, b0, [b1["stats"], early["w_t_other"]])
-    gz0, got0, pack0, _ = back(late, 0, (gno0, b0["rc"]), None, b0, [b0["no"]])
+    gz0, got0, pack0, _ = back(late, 0, (gno0, b0["rc"]), None, b0, [b0["no"], b1["sums"][0]], *b1["sums"][1:])
     scale(late, 1, b1, [pack0])
     outs0 = unproject(late, 0, gz0, got0, [b1["no"]])
     held0 = hand(outs0, 0)
     gz1, got1, pack1, _ = back(late, 1, (gno1, b1["rc"]), None, b1, [outs0[0]])
-    parts0 = settle(held0, 0, pack1)
+    parts0, sent0 = settle(held0, 0, pack1)
     g_wo1 = run_outer(
-        places, [(b0["no"], gout1_0), (b1["no"], gout1_1)], None, False, [pack1, held0[2]]
+        places, [(gout1_0, b0["no"]), (gout1_1, b1["no"])], None, True, BF16, [pack1, sent0]
     )
     outs1 = unproject(late, 1, gz1, got1, [g_wo1])
     held1 = hand(outs1, 0)
@@ -1131,45 +1154,42 @@
 
     gh_0, gain1_0 = turn(0, parts0, h_0, u_0, a0, [outs1[0]])
     pair0 = reach(gh_0, 0)
-    g_w1 = run_outer(places, [(b0["nrm"], gz0), (b1["nrm"], gz1)], None, True, [gh_0])
-    parts1 = settle(held1, 0, g_w1)
-    wide0 = widen(pair0, 0, g_w1)
-    final0 = project(late, 0, b0, [g_w1])
-    gh_1, gain1_1 = turn(1, parts1, h_1, u_1, a1, [final0[0]])
+    w1_out = run_outer(
+        places, [(b0["nrm"], gz0), (b1["nrm"], gz1)], None, True, BF16, [gh_0]
+    )
+    parts1, sent1 = settle(held1, 0, w1_out, pair0[1])
+    wide0 = widen(pair0, 0, w1_out, sent1)
+    final = project_both(late, b0, b1, [w1_out, sent1, wide0[0]])
+    gh_1, gain1_1 = turn(1, parts1, h_1, u_1, a1, [final])
     pair1 = reach(gh_1, 0)
+    turned0 = share(wide0[0], after(wide0[1], gh_1))
+    spill = lambda g, axis: lax.psum_scatter(g, "dp", scatter_dimension=axis, tiled=True)
+    wo1_sum = spill(g_wo1, 0)
+    w1_sum = spill(after(w1_out, sent1), 0)
+    over_tensor = lambda v: lax.psum_scatter(v, "tensor", scatter_dimension=0, tiled=True)
+    sums = over_tensor(after(final, gh_1))
+    tiny1 = pack0 + pack1 + gain1_0 + gain1_1
+
     wide1 = widen(pair1, 0)
-    turned0, turned1 = share(*wide0), share(*wide1)
-    spill = lambda g, axis: lax.psum_scatter(g, "dp", scatter_dimension=axis, tiled=True)
-    narrow = lambda g, axis: spill(g.astype(BF16), axis).astype(F32)
-    wo1_sum = narrow(g_wo1, 1)
-    zx1_sum = narrow(after(g_w1, pair0[1])[:, : 2 * inner], 0)
-    tiny1 = pack0 + pack1 + gain1_0 + gain1_1
-    bcdt_at = slice(2 * inner, 2 * inner + w_bcdt.shape[2])
-
-    gz0, got0, pack0, gout0_0 = back(early, 0, (turned0, early["wo_t"]), 0, a0, [gh_1, pair1[1]])
-    final1 = project(late, 1, b1, [pack0, wide1[1]])
-    outs0 = unproject(early, 0, gz0, got0, [final1[0]])
+    gz0, got0, pack0, gout0_0 = back(
+        early, 0, (turned0, early["wo_t"]), 0, a0, [gh_1, wo1_sum, wide1[0]], wide1[1]
+    )
+    outs0 = unproject(early, 0, gz0, got0, [pack0, wide1[0]])
     held0 = hand(outs0, 0)
-    g_w0 = run_outer(places, [(a0["nrm"], gz0)], None, True, [outs0[0]])
-    gno0_1, gout0_1, cc0_1 = run_gn(scalars[1], turned1, 0, early["wo_t"], width, [g_w0])
+    g_w0 = run_outer(places, [(a0["nrm"], gz0)], None, True, F32, [outs0[0]])
+    turned1 = share(wide1[0], after(wide1[1], g_w0))
+    gno0_1, gout0_1, cc0_1 = run_gn(scalars[1], turned1, 0, early["wo_t"], width, [g_w0, w1_sum])
+    gz1, got1, pack1, _ = back(early, 1, (gno0_1, cc0_1), None, a1, [gno0_1])
+    w0_out = run_outer(places, [(a1["nrm"], gz1)], g_w0, True, BF16, [pack1, held0[2]])
+    w0_sum = spill(w0_out, 0)
+    outs1 = unproject(early, 1, gz1, got1, [w0_out])
+    held1 = hand(outs1, 0)
+    parts0, _ = settle(held0, 0, pack1)
     g_wo0 = run_outer(
-        places, [(a0["no"], gout0_0), (a1["no"], gout0_1)], None, False, [gno0_1]
-    )
-    wo0_sum = narrow(g_wo0, 1)
-    hold = lambda outs: (after(outs[0], gno0_1), outs[1], after(outs[2], gno0_1))
-    heldf = [hand(hold(outs), 0) for outs in (final0, final1)]
-    gz1, got1, pack1, _ = back(early, 1, (gno0_1, cc0_1), None, a1, [g_wo0])
-    g_w0 = run_outer(places, [(a1["nrm"], gz1)], g_w0, True, [pack1, held0[2], heldf[0][2]])
-    zx0_sum = narrow(g_w0[:, : 2 * inner], 0)
-    outs1 = unproject(early, 1, gz1, got1, [g_w0, heldf[1][2]])
-    held1 = hand(outs1, 0)
-    pair = by_layer(g_w0[:, bcdt_at], g_w1[:, bcdt_at])
-    bc_got = swap(pair[1].astype(BF16))
-    parts0 = settle(held0, 0, outs1[0])
-    def finish(m, h, deps):
-        return run_plain(
-            partial(owner_kernel, True), "owner_out", wide(F32), (*partsf[m], h, gains[1]), deps
-        )
+        places, [(gout0_0, a0["no"]), (gout0_1, a1["no"])], None, True, BF16, [outs1[0]]
+    )
+    wo0_sum = spill(after(g_wo0, w0_sum), 0)
+    parts1, sent1 = settle(held1, 0, g_wo0)
 
     def last(m, parts, gh, deps):
         return run_plain(
@@ -1177,41 +1197,35 @@
             (*parts, xs[m], gh, gains[0]), deps,
         )
 
-    paired = after(pair[0], outs1[0]) + bc_got.astype(F32)
-    gv_0, gain0_0 = last(0, parts0, gh_0, [outs1[0]])
-    partsf = [settle(heldf[m], 0, outs1[0]) for m in micros]
-    if lax.axis_size("dp") == 4:
-        _, b_kept, b_got = deal_one(paired)
-        finals = [finish(0, h_0, [gv_0, b_got])]
-        b_kept, b_got = deal_two(b_kept, b_got)
-        shard = b_kept + b_got.astype(F32)
-    else:
-        shard = scatter_dp(paired)
-        finals = [finish(0, h_0, [gv_0])]
-    finals.append(finish(1, h_1, [finals[0], held1[2]]))
-    parts1 = settle(held1, 0, finals[1])
-    gv_1, gain0_1 = last(1, parts1, gh_1, ())
+    gv_0, gain0_0 = last(0, parts0, gh_0, [sent1, g_wo0])
+    finals = run_plain(
+        final_kernel, "owner_out", jax.ShapeDtypeStruct((2, half, width), F32),
+        (sums.reshape(2, half, width), h_0, h_1), [gv_0],
+    )
+    out_act = run_join(places, finals, swap(finals))
+    gv_1, gain0_1 = last(1, parts1, gh_1, [out_act])
     tiny0 = pack0 + pack1 + gain0_0 + gain0_1
 
-    finals = jnp.stack(finals)
-    out_act = run_join(places, finals, swap(finals))
     both = jnp.stack([gv_0, gv_1])
     mine, theirs = by_layer(both[:, :, : width // 2], both[:, :, width // 2 :])
     grad_in = run_join(places, mine, swap(theirs))
 
+    def owned(parts):
+        kept, sent = by_layer(parts[0], parts[1])
+        return kept, swap(sent)
+
+    kept, got = owned([v[:, : 2 * inner] for v in (w0_sum, w1_sum)])
+    grad_w_zx = run_weave(places, kept, got)[None]
     kept, sent = by_layer(tiny0, tiny1)
-    mine = sum_dp(kept + swap(sent))
+    mine = sum_dp(kept + swap(sent), grad_in, grad_w_zx)
     shared = all_tensor(mine)
+    grad_w_out = jnp.concatenate(by_layer(*owned([wo0_sum, wo1_sum])), 1).T[None].astype(F32)
+    cut = lambda v: after(v, got)[:, 2 * inner : 2 * inner + w_bcdt.shape[2]]
+    kept, got = owned([cut(v) for v in (w0_sum, w1_sum)])
+    shard = kept.astype(F32) + got.astype(F32)
     for bit in (1, 2):
         shard = shard + across(shard.astype(BF16), bit).astype(F32)
     grad_w_bcdt = shard[None]
-
-    def owned(parts):
-        kept, sent = by_layer(parts[0], parts[1])
-        return kept, swap(sent)
-
-    grad_w_zx = run_weave(places, *owned([zx0_sum, zx1_sum]))[None]
-    grad_w_out = jnp.concatenate(by_layer(*owned([wo0_sum, wo1_sum])), 0)[None]
     return (
         out_act,
         grad_in,

time: 962 us -> 844 us (0.88)
  waiting for transfers between devices: 287 us -> 221 us
  other arithmetic: 48.7 us -> 27.6 us
  local copies, waits for them, and re-layouts: 67.7 us -> 49.7 us
    ppermute x44 -> x40, waiting for transfers between devices: 207 us -> 145 us  [across(): return lax.ppermute(value, 'tensor', [(i, i ^ step) for i in range(count)])]
    ppermute x6 -> x3, waiting for transfers between devices: 35.4 us -> 5.69 us  [cycle(): lax.ppermute(value, 'dp', [(i, (i + steps) % count) for i in range(count)])]
    ppermute x2 -> x6, waiting for transfers between devices: 27.8 us -> 53.3 us  [the longest x3 39.1 us: pieces_dp(): lax.ppermute(after(up[-1], *waits), 'dp', [(i, i + 1) for i in range(3)])]
    ppermute x44 -> x40, starting transfers between devices: 53.7 us -> 46.6 us  [across(): return lax.ppermute(value, 'tensor', [(i, i ^ step) for i in range(count)])]
    unnamed x195 -> x205, local copies, waits for them, and re-layouts: 34.4 us -> 29.6 us
    pallas_call x33 -> x32, Pallas kernels: 410 us -> 413 us  [call(): pl.pallas_call(body, out_shape=tuple((jax.ShapeDtypeStruct(shape, kind) f...]
    pallas_call x10 -> x9, Pallas kernels: 35.3 us -> 33.3 us  [run_plain(): pl.pallas_call(body, in_specs=[vmem] * count + [pl.BlockSpec(memory_space...]
  transfers between devices with their start and end apart: 100 -> 96, of which waited for: 34 -> 39; matrix products, arithmetic and copies ran while one was open for 9% -> 5% of each run, Pallas kernels for 45% -> 52%
where the time goes in v3:
time: 844 us; the launch traced here: 837 us
  Pallas kernels  446 us (53%)
  waiting for transfers between devices  221 us (26%)
  starting transfers between devices  74.4 us (9%)
  local copies, waits for them, and re-layouts  49.7 us (6%)
  other arithmetic  27.6 us (3%)
  between operations  18.1 us (2%)
    pallas_call x32, Pallas kernels, call(): pl.pallas_call(body, out_shape=tuple((jax.ShapeDtypeStruct(shape, kind) f...  413 us
    ppermute x40, waiting for transfers between devices, across(): return lax.ppermute(value, 'tensor', [(i, i ^ step) for i in range(count)])  145 us
    ppermute x40, starting transfers between devices, across(): return lax.ppermute(value, 'tensor', [(i, i ^ step) for i in range(count)])  46.6 us
    ppermute x3, waiting for transfers between devices, pieces_dp(): lax.ppermute(after(up[-1], *waits), 'dp', [(i, i + 1) for i in range(3)])  39.1 us
    pallas_call x9, Pallas kernels, run_plain(): pl.pallas_call(body, in_specs=[vmem] * count + [pl.BlockSpec(memory_space...  33.3 us
    unnamed x205, local copies, waits for them, and re-layouts  29.6 us
  transfers between devices with their start and end apart: 96, of which 39 were waited for; matrix products, arithmetic and copies ran while one was open for 5% of the time, Pallas kernels for 52%

profile of v3, /device:TPU:0, one launch (start us, length us, event | category | flops | bytes accessed | tf_op | source)
XLA Modules:
  0.0 836.6 jit_solution(2382687967186611265)
XLA Ops:
  7.2 3.7 fusion.21
  22.2 5.8 collective-permute-start.2
  29.3 17.0 %collective-permute-done.2.refs_2_.refs_1_ = bf16[384,1152]{1,0:T(8,128)(2,1)} collective-permute-done((bf16[384,1152]{1,0:T(8,128)(2,1)S(1)}, bf16[384,1152]{1,0:T(8,128)(2,1)}, u32[]{:S(2)}, u32[]{:S(2)}) %collective-permute-start.2) | collective-permute-done | bytes 884768 | tf_op jit(solution)/shard_map/ppermute | solution.py:930
  46.3 5.2 collective-permute-done.3.refs_5_.refs_4_
  57.0 3.4 collective-permute-start.4
  72.0 7.4 collective-permute-done.4.refs_3_.refs_2_
  79.4 5.0 collective-permute-done.5.refs_6_.refs_5_
  91.1 14.7 %collective-permute-done.6.refs_4_.refs_3_ = bf16[384,1152]{1,0:T(8,128)(2,1)S(1)} collective-permute-done((bf16[384,1152]{1,0:T(8,128)(2,1)}, bf16[384,1152]{1,0:T(8,128)(2,1)S(1)}, u32[]{:S(2)}, u32[]{:S(2)}) %collective-permute-start.6) | collective-permute-done | bytes 884768 | tf_op jit(solution)/shard_map/ppermute | solution.py:930
  105.8 4.1 collective-permute-done.7.refs_7_.refs_6_
  114.3 25.1 %layer_fwd.4 = (f32[1536,1152]{1,0:T(8,128)}, f32[1536,384]{1,0:T(8,128)}, bf16[12,128,384]{2,1,0:T(8,128)(2,1)}, f32[1536,384]{1,0:T(8,128)}, f32[8,1536]{1,0:T(8,128)}) custom-call(s32[5]{0:T(128)} %stack.91.sc, bf16[1536,1536]{1,0:T(8,128)(2,1)} %all-gather.6.cloned.1.call-done.refs_0_, bf16[384,1152]{1,0:T(8,128)(2,1)} %copy-done.24, ...), custom_call_target="tpu_custom_call" | custom-call | flops 25769803776 | bytes 25165824 | tf_op jit(solution)/shard_map/layer_fwd/pallas_call | solution.py:261
  143.9 25.0 %layer_fwd.5 = (f32[1536,1152]{1,0:T(8,128)}, f32[1536,384]{1,0:T(8,128)}, bf16[12,128,384]{2,1,0:T(8,128)(2,1)}, f32[1536,384]{1,0:T(8,128)}, f32[8,1536]{1,0:T(8,128)}) custom-call(s32[5]{0:T(128)} %stack.93.sc, bf16[1536,1536]{1,0:T(8,128)(2,1)} %all-gather.8.cloned.1.call-done.refs_0_, bf16[384,1152]{1,0:T(8,128)(2,1)} %copy-done.24, ...), custom_call_target="tpu_custom_call" | custom-call | flops 25769803776 | bytes 25165824 | tf_op jit(solution)/shard_map/layer_fwd/pallas_call | solution.py:261
  181.3 5.3 scale_rows.4
  194.9 6.2 half_rows.7
  201.8 5.1 scale_rows.5
  209.3 6.4 half_rows.8
  218.4 9.4 %grad_rows.3 = (f32[1536,384]{1,0:T(8,128)}, bf16[1536,1536]{1,0:T(8,128)(2,1)}) custom-call(s32[5]{0:T(128)} %stack.91.sc, bf16[2,192,1536]{2,1,0:T(8,128)(2,1)} %pad_maximum_fusion.3.refs_0_, bf16[2,192,1536]{2,1,0:T(8,128)(2,1)} %collective-permute-done.14.refs_7_.refs_1_, bf16[2,192,1536]{2,1,0:T(8,128)(2,1)} %copy-done.69, ...), custom_call_target="tpu_custom_call" | custom-call | flops 8589934592 | bytes 18874368 | tf_op jit(solution)/shard_map/grad_rows/pallas_call | solution.py:261
  227.8 33.1 %collective-permute-done.19.refs_1_ = f32[2,192,1536]{2,1,0:T(8,128)} collective-permute-done((f32[2,192,1536]{2,1,0:T(8,128)}, f32[2,192,1536]{2,1,0:T(8,128)}, u32[]{:S(2)}, u32[]{:S(2)}) %collective-permute-start.19) | collective-permute-done | bytes 2359328 | tf_op jit(solution)/shard_map/ppermute | solution.py:880
  263.6 8.9 %grad_rows.4 = (f32[1536,384]{1,0:T(8,128)}, bf16[1536,1536]{1,0:T(8,128)(2,1)}) custom-call(s32[5]{0:T(128)} %stack.93.sc, bf16[2,192,1536]{2,1,0:T(8,128)(2,1)} %copy-done.15, bf16[2,192,1536]{2,1,0:T(8,128)(2,1)} %collective-permute-done.15.refs_8_.refs_1_, bf16[2,192,1536]{2,1,0:T(8,128)(2,1)} %collective-permute-done.28.refs_2_, ...), custom_call_target="tpu_custom_call" | custom-call | flops 8589934592 | bytes 18874368 | tf_op jit(solution)/shard_map/grad_rows/pallas_call | solution.py:261
  275.7 18.7 %collective-permute-done.27.refs_2_ = f32[192,1536]{1,0:T(8,128)S(1)} collective-permute-done((f32[192,1536]{1,0:T(8,128)S(1)}, f32[192,1536]{1,0:T(8,128)S(1)}, u32[]{:S(2)}, u32[]{:S(2)}) %collective-permute-start.27) | collective-permute-done | bytes 1179680 | tf_op jit(solution)/shard_map/ppermute | solution.py:880
  295.5 4.2 owner_mid.2
  302.4 4.2 owner_mid.3
  307.8 8.4 collective-permute-done.32
  318.0 6.1 turn_weights.2
  328.2 7.5 turn_weights.3
  335.7 5.2 collective-permute-done.33.refs_1_
  344.2 24.5 %layer_fwd.6 = (bf16[1536,1536]{1,0:T(8,128)(2,1)}, f32[1536,1152]{1,0:T(8,128)}, f32[1536,384]{1,0:T(8,128)}, bf16[12,128,384]{2,1,0:T(8,128)(2,1)}, f32[1536,384]{1,0:T(8,128)}, /*index=5*/f32[8,1536]{1,0:T(8,128)}) custom-call(s32[5]{0:T(128)} %stack.91.sc, bf16[2,192,1536]{2,1,0:T(8,128)(2,1)} %copy-done.17, ...), custom_call_target="tpu_custom_call" | custom-call | flops 25769803776 | bytes 25165824 | tf_op jit(solution)/shard_map/layer_fwd/pallas_call | solution.py:261
  370.6 3.3 collective-permute-done.43.refs_3_
  374.9 24.6 %layer_fwd.7 = (bf16[1536,1536]{1,0:T(8,128)(2,1)}, f32[1536,1152]{1,0:T(8,128)}, f32[1536,384]{1,0:T(8,128)}, bf16[12,128,384]{2,1,0:T(8,128)(2,1)}, f32[1536,384]{1,0:T(8,128)}, /*index=5*/f32[8,1536]{1,0:T(8,128)}) custom-call(s32[5]{0:T(128)} %stack.93.sc, bf16[2,192,1536]{2,1,0:T(8,128)(2,1)} %pad_maximum_fusion.6.refs_9_.refs_0_, ...), custom_call_target="tpu_custom_call" | custom-call | flops 25769803776 | bytes 25165824 | tf_op jit(solution)/shard_map/layer_fwd/pallas_call | solution.py:261
  408.4 5.1 scale_rows.6
  413.4 27.0 %layer_bwd.4 = (bf16[1536,1152]{1,0:T(8,128)(2,1)}, bf16[4,192,1152]{2,1,0:T(8,128)(2,1)}, f32[16,1536]{1,0:T(8,128)}) custom-call(s32[5]{0:T(128)} %stack.91.sc, f32[1536,384]{1,0:T(8,128)} %get-tuple-element.175.refs_5_.refs_9_.refs_0_, f32[1536,128]{1,0:T(8,128)} %get-tuple-element.199.refs_1_.refs_6_, f32[1536,1152]{1,0:T(8,128)} %get-tuple-element.200.refs_2_.refs_3_, ...), custom_call_target="tpu_custom_call" | custom-call | flops 30064771072 | bytes 25165824 | tf_op jit(solution)/shard_map/layer_bwd/pallas_call | solution.py:261
  442.1 5.1 scale_rows.7
  448.5 10.6 %half_rows.9 = (f32[192,1536]{1,0:T(8,128)}, f32[192,1536]{1,0:T(8,128)}, bf16[2,192,1536]{2,1,0:T(8,128)(2,1)}) custom-call(s32[5]{0:T(128)} %stack.91.sc, bf16[4,2,192,1152]{3,2,1,0:T(8,128)(2,1)} %bitcast.128, bf16[4,192,1152]{2,1,0:T(8,128)(2,1)} %copy-done.65, bf16[1152,1536]{1,0:T(8,128)(2,1)} %get-tuple-element.216.refs_2_, ...), custom_call_target="tpu_custom_call" | custom-call | flops 8589934592 | bytes 10485760 | tf_op jit(solution)/shard_map/half_rows/pallas_call | solution.py:261
  460.7 27.0 %layer_bwd.5 = (bf16[1536,1152]{1,0:T(8,128)(2,1)}, bf16[4,192,1152]{2,1,0:T(8,128)(2,1)}, f32[16,1536]{1,0:T(8,128)}) custom-call(s32[5]{0:T(128)} %stack.93.sc, f32[1536,384]{1,0:T(8,128)} %get-tuple-element.177.refs_5_.refs_9_.refs_0_, f32[1536,128]{1,0:T(8,128)} %get-tuple-element.209.refs_1_.refs_6_, f32[1536,1152]{1,0:T(8,128)} %get-tuple-element.210.refs_2_.refs_3_, ...), custom_call_target="tpu_custom_call" | custom-call | flops 30064771072 | bytes 25165824 | tf_op jit(solution)/shard_map/layer_bwd/pallas_call | solution.py:261
  490.3 9.9 %outer_rows.5.refs_4_ = bf16[1536,384]{1,0:T(8,128)(2,1)} custom-call(s32[5]{0:T(128)} %stack.91.sc, bf16[1536,1536]{1,0:T(8,128)(2,1)} %get-tuple-element.227.refs_0_, bf16[1536,384]{1,0:T(8,128)(2,1)} %get-tuple-element.195.refs_11_.refs_1_, bf16[1536,1536]{1,0:T(8,128)(2,1)} %get-tuple-element.228.refs_2_, ...), custom_call_target="tpu_custom_call" | custom-call | flops 19327352832 | bytes 16777216 | tf_op jit(solution)/shard_map/outer_rows/pallas_call | solution.py:261
  501.4 10.6 %half_rows.10 = (f32[192,1536]{1,0:T(8,128)}, f32[192,1536]{1,0:T(8,128)}, bf16[2,192,1536]{2,1,0:T(8,128)(2,1)}) custom-call(s32[5]{0:T(128)} %stack.93.sc, bf16[4,2,192,1152]{3,2,1,0:T(8,128)(2,1)} %bitcast.129, bf16[4,192,1152]{2,1,0:T(8,128)(2,1)} %copy-done.66, bf16[1152,1536]{1,0:T(8,128)(2,1)} %get-tuple-element.216.refs_2_, ...), custom_call_target="tpu_custom_call" | custom-call | flops 8589934592 | bytes 10485760 | tf_op jit(solution)/shard_map/half_rows/pallas_call | solution.py:261
  512.0 4.6 owner_back.2
  518.6 18.6 %outer_rows.6.refs_6_ = bf16[1536,1152]{1,0:T(8,128)(2,1)} custom-call(s32[5]{0:T(128)} %stack.91.sc, bf16[1536,1536]{1,0:T(8,128)(2,1)} %get-tuple-element.206.refs_0_, bf16[1536,1152]{1,0:T(8,128)(2,1)} %get-tuple-element.207.refs_1_, bf16[1536,1536]{1,0:T(8,128)(2,1)} %get-tuple-element.208.refs_2_, bf16[1536,1152]{1,0:T(8,128)(2,1)} %get-tuple-element.218.refs_3_, ...), custom_call_target="tpu_custom_call" | custom-call | flops 19327352832 | bytes 16777216 | tf_op jit(solution)/shard_map/outer_rows/pallas_call | solution.py:261
  537.2 8.2 collective-permute-done.58.refs_1_
  552.6 8.6 %half_rows.11.refs_8_ = bf16[1536,1536]{1,0:T(8,128)(2,1)} custom-call(s32[5]{0:T(128)} %stack.91.sc, bf16[4,2,192,384]{3,2,1,0:T(8,128)(2,1)} %bitcast.134, bf16[4,192,384]{2,1,0:T(8,128)(2,1)} %copy-done.81, bf16[384,1536]{1,0:T(8,128)(2,1)} %get-tuple-element.197.refs_8_.refs_2_, bf16[384,1536]{1,0:T(8,128)(2,1)} %copy-done.73, ...), custom_call_target="tpu_custom_call" | custom-call | flops 8589934592 | bytes 10485760 | tf_op jit(solution)/shard_map/half_rows/pallas_call | solution.py:261
  561.2 4.0 collective-permute-done.59.refs_2_
  566.0 4.7 owner_back.3
  570.6 7.5 collective-permute-done.60.refs_1_
  579.1 16.0 %collective-permute-done.63 = bf16[192,1664]{1,0:T(8,128)(2,1)S(1)} collective-permute-done((bf16[192,1664]{1,0:T(8,128)(2,1)}, bf16[192,1664]{1,0:T(8,128)(2,1)S(1)}, u32[]{:S(2)}, u32[]{:S(2)}) %collective-permute-start.63) | collective-permute-done | bytes 639008 | tf_op jit(solution)/shard_map/ppermute | solution.py:880
  597.4 32.0 %layer_bwd.6 = (bf16[1536,1536]{1,0:T(8,128)(2,1)}, bf16[1536,1152]{1,0:T(8,128)(2,1)}, bf16[4,192,1152]{2,1,0:T(8,128)(2,1)}, f32[16,1536]{1,0:T(8,128)}) custom-call(s32[5]{0:T(128)} %stack.91.sc, bf16[2,192,1664]{2,1,0:T(8,128)(2,1)} %copy-done.7, bf16[2,192,1664]{2,1,0:T(8,128)(2,1)} %collective-permute-done.60.refs_1_, ...), custom_call_target="tpu_custom_call" | custom-call | flops 30064771072 | bytes 25165824 | tf_op jit(solution)/shard_map/layer_bwd/pallas_call | solution.py:261
  634.6 10.5 %half_rows.12 = (f32[192,1536]{1,0:T(8,128)}, f32[192,1536]{1,0:T(8,128)}, bf16[2,192,1536]{2,1,0:T(8,128)(2,1)}) custom-call(s32[5]{0:T(128)} %stack.91.sc, bf16[4,2,192,1152]{3,2,1,0:T(8,128)(2,1)} %bitcast.131, bf16[4,192,1152]{2,1,0:T(8,128)(2,1)} %copy-done.67, bf16[1152,1536]{1,0:T(8,128)(2,1)} %get-tuple-element.187.refs_10_.refs_2_, ...), custom_call_target="tpu_custom_call" | custom-call | flops 8589934592 | bytes 10485760 | tf_op jit(solution)/shard_map/half_rows/pallas_call | solution.py:261
  645.1 11.7 %outer_rows.7.refs_5_.refs_2_ = f32[1536,1152]{1,0:T(8,128)} custom-call(s32[5]{0:T(128)} %stack.91.sc, bf16[1536,1536]{1,0:T(8,128)(2,1)} %all-gather.6.cloned.1.call-done.refs_0_, bf16[1536,1152]{1,0:T(8,128)(2,1)} %get-tuple-element.244.refs_1_, f32[192,1536]{1,0:T(8,128)} %get-tuple-element.248.refs_2_.refs_0_), custom_call_target="tpu_custom_call" | custom-call | flops 9663676416 | bytes 16777216 | tf_op jit(solution)/shard_map/outer_rows/pallas_call | solution.py:261
  660.2 9.7 %grad_rows.5 = (f32[1536,384]{1,0:T(8,128)}, bf16[1536,1536]{1,0:T(8,128)(2,1)}, f32[1536,128]{1,0:T(8,128)}) custom-call(s32[5]{0:T(128)} %stack.93.sc, bf16[2,192,1664]{2,1,0:T(8,128)(2,1)} %copy-done.8, bf16[2,192,1664]{2,1,0:T(8,128)(2,1)} %collective-permute-done.64.refs_1_, bf16[2,192,1664]{2,1,0:T(8,128)(2,1)} %copy-done.68, ...), custom_call_target="tpu_custom_call" | custom-call | flops 8589934592 | bytes 18874368 | tf_op jit(solution)/shard_map/grad_rows/pallas_call | solution.py:261
  669.9 26.2 %layer_bwd.7 = (bf16[1536,1152]{1,0:T(8,128)(2,1)}, bf16[4,192,1152]{2,1,0:T(8,128)(2,1)}, f32[16,1536]{1,0:T(8,128)}) custom-call(s32[5]{0:T(128)} %stack.93.sc, f32[1536,384]{1,0:T(8,128)} %get-tuple-element.253.refs_0_.refs_11_, f32[1536,128]{1,0:T(8,128)} %get-tuple-element.254.refs_1_, f32[1536,1152]{1,0:T(8,128)} %get-tuple-element.255.refs_2_.refs_3_, ...), custom_call_target="tpu_custom_call" | custom-call | flops 30064771072 | bytes 25165824 | tf_op jit(solution)/shard_map/layer_bwd/pallas_call | solution.py:261
  697.8 12.1 %outer_rows.8.refs_4_ = bf16[1536,1152]{1,0:T(8,128)(2,1)} custom-call(s32[5]{0:T(128)} %stack.91.sc, bf16[1536,1536]{1,0:T(8,128)(2,1)} %all-gather.8.cloned.1.call-done.refs_0_, bf16[1536,1152]{1,0:T(8,128)(2,1)} %get-tuple-element.260.refs_1_, f32[1536,1152]{1,0:T(8,128)} %outer_rows.7.refs_5_.refs_2_, f32[16,1536]{1,0:T(8,128)} %get-tuple-element.258.refs_3_, ...), custom_call_target="tpu_custom_call" | custom-call | flops 9663676416 | bytes 16777216 | tf_op jit(solution)/shard_map/outer_rows/pallas_call | solution.py:261
  713.2 11.2 %half_rows.13 = (f32[192,1536]{1,0:T(8,128)}, f32[192,1536]{1,0:T(8,128)}, bf16[2,192,1536]{2,1,0:T(8,128)(2,1)}) custom-call(s32[5]{0:T(128)} %stack.93.sc, bf16[4,2,192,1152]{3,2,1,0:T(8,128)(2,1)} %bitcast.130, bf16[4,192,1152]{2,1,0:T(8,128)(2,1)} %collective-permute-done.70.refs_1_, bf16[1152,1536]{1,0:T(8,128)(2,1)} %get-tuple-element.187.refs_10_.refs_2_, ...), custom_call_target="tpu_custom_call" | custom-call | flops 8589934592 | bytes 10485760 | tf_op jit(solution)/shard_map/half_rows/pallas_call | solution.py:261
  724.5 10.0 %outer_rows.9.refs_7_ = bf16[1536,384]{1,0:T(8,128)(2,1)} custom-call(s32[5]{0:T(128)} %stack.91.sc, bf16[1536,1536]{1,0:T(8,128)(2,1)} %get-tuple-element.263.refs_0_, bf16[1536,384]{1,0:T(8,128)(2,1)} %get-tuple-element.163.refs_1_, bf16[1536,1536]{1,0:T(8,128)(2,1)} %get-tuple-element.264.refs_2_, bf16[1536,384]{1,0:T(8,128)(2,1)} %get-tuple-element.172.refs_3_, ...), custom_call_target="tpu_custom_call" | custom-call | flops 19327352832 | bytes 16777216 | tf_op jit(solution)/shard_map/outer_rows/pallas_call | solution.py:261
  734.5 16.9 %collective-permute-done.71.refs_1_ = bf16[2,192,1536]{2,1,0:T(8,128)(2,1)S(1)} collective-permute-done((bf16[2,192,1536]{2,1,0:T(8,128)(2,1)}, bf16[2,192,1536]{2,1,0:T(8,128)(2,1)S(1)}, u32[]{:S(2)}, u32[]{:S(2)}) %collective-permute-start.71) | collective-permute-done | bytes 1179680 | tf_op jit(solution)/shard_map/ppermute | solution.py:880
  753.4 4.1 owner_last.2
  757.5 3.3 owner_out.1.refs_0_
  761.5 4.1 collective-permute-done.72.refs_1_
  767.0 4.9 join_rows.2.refs_6_
  771.8 4.7 collective-permute-done.73.refs_2_
  777.4 4.0 owner_last.3
  787.2 3.2 collective-permute-start.79
  791.7 3.5 join_rows.3
  796.1 4.6 weave_cols.1
  800.7 5.7 collective-permute-done.78
  809.0 3.1 collective-permute-done.80
  820.7 6.1 collective-permute-done.84
  (465 shorter events, 162.0 us)
Async XLA Ops:
  7.2 105.9 %all-gather.6.cloned.1.call-start = ((), (), s32[]{:S(2)}) async-start(), calls=%async_computation.5 | async-start | bytes 5308416 | tf_op jit(solution)/shard_map/all_gather | solution.py:1008
  22.2 120.6 %all-gather.8.cloned.1.call-start = ((), (), s32[]{:S(2)}) async-start(), calls=%async_computation.6 | async-start | bytes 5308416 | tf_op jit(solution)/shard_map/all_gather | solution.py:1008
  22.2 24.1 %collective-permute-start.2 = (bf16[384,1152]{1,0:T(8,128)(2,1)S(1)}, bf16[384,1152]{1,0:T(8,128)(2,1)}, u32[]{:S(2)}, u32[]{:S(2)}) collective-permute-start(bf16[384,1152]{1,0:T(8,128)(2,1)S(1)} %get-tuple-element.146.refs_1_.refs_0_), channel_id=1, source_target_pairs={{0,4},{4,8},{8,12},{1,5},{5,9},{9,13},{2,6},{6,10},{10,14},{3,7},{... | collective-permute-start | bytes 2654216 | tf_op jit(solution)/shard_map/ppermute | solution.py:930
  28.0 23.4 %collective-permute-start.3 = (bf16[384,1152]{1,0:T(8,128)(2,1)S(1)}, bf16[384,1152]{1,0:T(8,128)(2,1)}, u32[]{:S(2)}, u32[]{:S(2)}) collective-permute-start(bf16[384,1152]{1,0:T(8,128)(2,1)S(1)} %get-tuple-element.146.refs_1_.refs_0_), channel_id=1, source_target_pairs={{4,0},{8,4},{12,8},{5,1},{9,5},{13,9},{6,2},{10,6},{14,10},{7,3},{... | collective-permute-start | bytes 2654216 | tf_op jit(solution)/shard_map/ppermute | solution.py:931
  54.5 114.4 %all-gather.10.cloned.1.call-start = ((), (), s32[]{:S(2)}) async-start(), calls=%async_computation.7 | async-start | bytes 1474560 | tf_op jit(solution)/shard_map/all_gather | solution.py:1013
  57.0 22.4 %collective-permute-start.4 = (bf16[384,1152]{1,0:T(8,128)(2,1)}, bf16[384,1152]{1,0:T(8,128)(2,1)}, u32[]{:S(2)}, u32[]{:S(2)}) collective-permute-start(bf16[384,1152]{1,0:T(8,128)(2,1)} %collective-permute-done.2.refs_2_.refs_1_), channel_id=1, source_target_pairs={{0,4},{4,8},{8,12},{1,5},{5,9},{9,13},{2,6},{6,10},{10,14},{3,7},{... | collective-permute-start | bytes 2654216 | tf_op jit(solution)/shard_map/ppermute | solution.py:930
  60.4 24.0 %collective-permute-start.5 = (bf16[384,1152]{1,0:T(8,128)(2,1)}, bf16[384,1152]{1,0:T(8,128)(2,1)}, u32[]{:S(2)}, u32[]{:S(2)}) collective-permute-start(bf16[384,1152]{1,0:T(8,128)(2,1)} %collective-permute-done.3.refs_5_.refs_4_), channel_id=1, source_target_pairs={{4,0},{8,4},{12,8},{5,1},{9,5},{13,9},{6,2},{10,6},{14,10},{7,3},{... | collective-permute-start | bytes 2654216 | tf_op jit(solution)/shard_map/ppermute | solution.py:931
  84.4 21.4 %collective-permute-start.6 = (bf16[384,1152]{1,0:T(8,128)(2,1)}, bf16[384,1152]{1,0:T(8,128)(2,1)S(1)}, u32[]{:S(2)}, u32[]{:S(2)}) collective-permute-start(bf16[384,1152]{1,0:T(8,128)(2,1)} %collective-permute-done.4.refs_3_.refs_2_), channel_id=1, source_target_pairs={{0,4},{4,8},{8,12},{1,5},{5,9},{9,13},{2,6},{6,10},{10,14},{3,7},{... | collective-permute-start | bytes 2654216 | tf_op jit(solution)/shard_map/ppermute | solution.py:930
  87.1 22.8 %collective-permute-start.7 = (bf16[384,1152]{1,0:T(8,128)(2,1)}, bf16[384,1152]{1,0:T(8,128)(2,1)S(1)}, u32[]{:S(2)}, u32[]{:S(2)}) collective-permute-start(bf16[384,1152]{1,0:T(8,128)(2,1)} %collective-permute-done.5.refs_6_.refs_5_), channel_id=1, source_target_pairs={{4,0},{8,4},{12,8},{5,1},{9,5},{13,9},{6,2},{10,6},{14,10},{7,3},{... | collective-permute-start | bytes 2654216 | tf_op jit(solution)/shard_map/ppermute | solution.py:931
  109.8 29.6 %collective-permute-start.12 = (bf16[192,1536]{1,0:T(8,128)(2,1)S(1)}, bf16[192,1536]{1,0:T(8,128)(2,1)S(1)}, u32[]{:S(2)}, u32[]{:S(2)}) collective-permute-start(bf16[192,1536]{1,0:T(8,128)(2,1)S(1)} %copy-done.4), channel_id=1, source_target_pairs={{0,1},{1,0},{2,3},{3,2},{4,5},{5,4},{6,7},{7,6},{8,9},{9,8},{10,11... | collective-permute-start | bytes 1769480 | tf_op jit(solution)/shard_map/ppermute | solution.py:880
  111.3 29.7 %collective-permute-start.13 = (bf16[192,1536]{1,0:T(8,128)(2,1)S(1)}, bf16[192,1536]{1,0:T(8,128)(2,1)S(1)}, u32[]{:S(2)}, u32[]{:S(2)}) collective-permute-start(bf16[192,1536]{1,0:T(8,128)(2,1)S(1)} %get-tuple-element.162.refs_4_), channel_id=1, source_target_pairs={{0,2},{1,3},{2,0},{3,1},{4,6},{5,7},{6,4},{7,5},{8,10},{9,11},{10,... | collective-permute-start | bytes 1769480 | tf_op jit(solution)/shard_map/ppermute | solution.py:880
  112.9 104.5 %all-gather.12.cloned.1.call-start = ((), (), s32[]{:S(2)}) async-start(), calls=%async_computation.8 | async-start | bytes 1474560 | tf_op jit(solution)/shard_map/all_gather | solution.py:1013
  140.7 39.9 %collective-permute-start.14 = (bf16[2,192,1536]{2,1,0:T(8,128)(2,1)}, bf16[2,192,1536]{2,1,0:T(8,128)(2,1)}, u32[]{:S(2)}, u32[]{:S(2)}) collective-permute-start(bf16[2,192,1536]{2,1,0:T(8,128)(2,1)} %pad_maximum_fusion.3.refs_0_), channel_id=1, source_target_pairs={{0,2},{1,3},{2,0},{3,1},{4,6},{5,7},{6,4},{7,5},{8,10},{9,11},{10,... | collective-permute-start | bytes 3538952 | tf_op jit(solution)/shard_map/ppermute | solution.py:880
  141.9 38.8 %collective-permute-start.15 = (bf16[2,192,1536]{2,1,0:T(8,128)(2,1)S(1)}, bf16[2,192,1536]{2,1,0:T(8,128)(2,1)}, u32[]{:S(2)}, u32[]{:S(2)}) collective-permute-start(bf16[2,192,1536]{2,1,0:T(8,128)(2,1)S(1)} %pad_maximum_fusion.4.refs_0_), channel_id=1, source_target_pairs={{0,1},{1,0},{2,3},{3,2},{4,5},{5,4},{6,7},{7,6},{8,9},{9,8},{10,11... | collective-permute-start | bytes 3538952 | tf_op jit(solution)/shard_map/ppermute | solution.py:880
  168.8 24.6 %collective-permute-start.18 = (bf16[384,1536]{0,1:T(8,128)(2,1)}, bf16[384,1536]{0,1:T(8,128)(2,1)S(1)}, u32[]{:S(2)}, u32[]{:S(2)}) collective-permute-start(bf16[384,1536]{0,1:T(8,128)(2,1)} %bitcast.113), channel_id=1, source_target_pairs={{0,16},{16,0},{1,17},{17,1},{2,18},{18,2},{3,19},{19,3},{4,20},{20... | collective-permute-start | bytes 3538952 | tf_op jit(solution)/shard_map/ppermute | solution.py:884
  187.1 130.9 %all-gather.14.cloned.1.call-start = ((), (), s32[]{:S(2)}) async-start(), calls=%async_computation.9 | async-start | bytes 4423680 | tf_op jit(solution)/shard_map/all_gather | solution.py:1013
  189.9 11.3 %collective-permute-start.23 = (f32[8,1536]{1,0:T(8,128)S(1)}, f32[8,1536]{1,0:T(8,128)S(1)}, u32[]{:S(2)}, u32[]{:S(2)}) collective-permute-start(f32[8,1536]{1,0:T(8,128)S(1)} %add.123.refs_1_), channel_id=1, source_target_pairs={{0,1},{1,0},{2,3},{3,2},{4,5},{5,4},{6,7},{7,6},{8,9},{9,8},{10,11... | collective-permute-start | bytes 147464 | tf_op jit(solution)/shard_map/ppermute | solution.py:880
  191.1 10.0 %collective-permute-start.24 = (f32[8,1536]{1,0:T(8,128)S(1)}, f32[8,1536]{1,0:T(8,128)S(1)}, u32[]{:S(2)}, u32[]{:S(2)}) collective-permute-start(f32[8,1536]{1,0:T(8,128)S(1)} %add.123.refs_1_), channel_id=1, source_target_pairs={{0,2},{1,3},{2,0},{3,1},{4,6},{5,7},{6,4},{7,5},{8,10},{9,11},{10,... | collective-permute-start | bytes 147464 | tf_op jit(solution)/shard_map/ppermute | solution.py:880
  206.9 54.0 %collective-permute-start.19 = (f32[2,192,1536]{2,1,0:T(8,128)}, f32[2,192,1536]{2,1,0:T(8,128)}, u32[]{:S(2)}, u32[]{:S(2)}) collective-permute-start(f32[2,192,1536]{2,1,0:T(8,128)} %get-tuple-element.168), channel_id=1, source_target_pairs={{0,2},{1,3},{2,0},{3,1},{4,6},{5,7},{6,4},{7,5},{8,10},{9,11},{10,... | collective-permute-start | bytes 7077896 | tf_op jit(solution)/shard_map/ppermute | solution.py:880
  209.2 387.8 %reduce-scatter.8.cloned.1.call-start = ((), (), s32[]{:S(2)}) async-start(), calls=%async_computation.11 | async-start | bytes 1474560 | tf_op jit(solution)/shard_map/reduce_scatter | solution.py:1166
  215.6 56.9 %collective-permute-start.30 = (f32[2,192,1536]{2,1,0:T(8,128)}, f32[2,192,1536]{2,1,0:T(8,128)}, u32[]{:S(2)}, u32[]{:S(2)}) collective-permute-start(f32[2,192,1536]{2,1,0:T(8,128)} %get-tuple-element.179), channel_id=1, source_target_pairs={{0,1},{1,0},{2,3},{3,2},{4,5},{5,4},{6,7},{7,6},{8,9},{9,8},{10,11... | collective-permute-start | bytes 7077896 | tf_op jit(solution)/shard_map/ppermute | solution.py:880
  216.8 46.8 %collective-permute-start.28 = (bf16[2,192,1536]{2,1,0:T(8,128)(2,1)S(1)}, bf16[2,192,1536]{2,1,0:T(8,128)(2,1)}, u32[]{:S(2)}, u32[]{:S(2)}) collective-permute-start(bf16[2,192,1536]{2,1,0:T(8,128)(2,1)S(1)} %pad_maximum_fusion.4.refs_0_), channel_id=1, source_target_pairs={{0,16},{16,0},{1,17},{17,1},{2,18},{18,2},{3,19},{19,3},{4,20},{20... | collective-permute-start | bytes 3538952 | tf_op jit(solution)/shard_map/ppermute | solution.py:884
  216.8 46.7 %collective-permute-start.29 = (bf16[2,192,1536]{2,1,0:T(8,128)(2,1)}, bf16[2,192,1536]{2,1,0:T(8,128)(2,1)}, u32[]{:S(2)}, u32[]{:S(2)}) collective-permute-start(bf16[2,192,1536]{2,1,0:T(8,128)(2,1)} %collective-permute-done.15.refs_8_.refs_1_), channel_id=1, source_target_pairs={{0,16},{16,0},{1,17},{17,1},{2,18},{18,2},{3,19},{19,3},{4,20},{20... | collective-permute-start | bytes 3538952 | tf_op jit(solution)/shard_map/ppermute | solution.py:884
  262.3 32.1 %collective-permute-start.27 = (f32[192,1536]{1,0:T(8,128)S(1)}, f32[192,1536]{1,0:T(8,128)S(1)}, u32[]{:S(2)}, u32[]{:S(2)}) collective-permute-start(f32[192,1536]{1,0:T(8,128)S(1)} %fusion.3.refs_6_), channel_id=1, source_target_pairs={{0,1},{1,0},{2,3},{3,2},{4,5},{5,4},{6,7},{7,6},{8,9},{9,8},{10,11... | collective-permute-start | bytes 3538952 | tf_op jit(solution)/shard_map/ppermute | solution.py:880
  273.9 27.4 %collective-permute-start.31 = (f32[192,1536]{1,0:T(8,128)S(1)}, f32[192,1536]{1,0:T(8,128)S(1)}, u32[]{:S(2)}, u32[]{:S(2)}) collective-permute-start(f32[192,1536]{1,0:T(8,128)S(1)} %fusion.2), channel_id=1, source_target_pairs={{0,2},{1,3},{2,0},{3,1},{4,6},{5,7},{6,4},{7,5},{8,10},{9,11},{10,... | collective-permute-start | bytes 3538952 | tf_op jit(solution)/shard_map/ppermute | solution.py:880
  299.7 16.5 %collective-permute-start.32 = (bf16[192,1536]{1,0:T(8,128)(2,1)}, bf16[192,1536]{1,0:T(8,128)(2,1)S(1)}, u32[]{:S(2)}, u32[]{:S(2)}) collective-permute-start(bf16[192,1536]{1,0:T(8,128)(2,1)} %get-tuple-element.183.refs_5_), channel_id=1, source_target_pairs={{0,1},{1,0},{2,3},{3,2},{4,5},{5,4},{6,7},{7,6},{8,9},{9,8},{10,11... | collective-permute-start | bytes 1769480 | tf_op jit(solution)/shard_map/ppermute | solution.py:880
  306.6 20.5 %collective-permute-start.34 = (bf16[192,1536]{1,0:T(8,128)(2,1)}, bf16[192,1536]{1,0:T(8,128)(2,1)S(1)}, u32[]{:S(2)}, u32[]{:S(2)}) collective-permute-start(bf16[192,1536]{1,0:T(8,128)(2,1)} %get-tuple-element.186), channel_id=1, source_target_pairs={{0,1},{1,0},{2,3},{3,2},{4,5},{5,4},{6,7},{7,6},{8,9},{9,8},{10,11... | collective-permute-start | bytes 1769480 | tf_op jit(solution)/shard_map/ppermute | solution.py:880
  316.3 24.7 %collective-permute-start.33 = (bf16[2,192,1536]{2,1,0:T(8,128)(2,1)S(1)}, bf16[2,192,1536]{2,1,0:T(8,128)(2,1)}, u32[]{:S(2)}, u32[]{:S(2)}) collective-permute-start(bf16[2,192,1536]{2,1,0:T(8,128)(2,1)S(1)} %pad_maximum_fusion.5.refs_2_.refs_0_), channel_id=1, source_target_pairs={{0,2},{1,3},{2,0},{3,1},{4,6},{5,7},{6,4},{7,5},{8,10},{9,11},{10,... | collective-permute-start | bytes 3538952 | tf_op jit(solution)/shard_map/ppermute | solution.py:880
  318.0 25.5 %collective-permute-start.35 = (bf16[2,192,1536]{2,1,0:T(8,128)(2,1)S(1)}, bf16[2,192,1536]{2,1,0:T(8,128)(2,1)}, u32[]{:S(2)}, u32[]{:S(2)}) collective-permute-start(bf16[2,192,1536]{2,1,0:T(8,128)(2,1)S(1)} %pad_maximum_fusion.5.refs_2_.refs_0_), channel_id=1, source_target_pairs={{0,16},{16,0},{1,17},{17,1},{2,18},{18,2},{3,19},{19,3},{4,20},{20... | collective-permute-start | bytes 3538952 | tf_op jit(solution)/shard_map/ppermute | solution.py:884
  341.6 28.4 %collective-permute-start.37 = (bf16[2,192,1536]{2,1,0:T(8,128)(2,1)S(1)}, bf16[2,192,1536]{2,1,0:T(8,128)(2,1)S(1)}, u32[]{:S(2)}, u32[]{:S(2)}) collective-permute-start(bf16[2,192,1536]{2,1,0:T(8,128)(2,1)S(1)} %copy-done.16), channel_id=1, source_target_pairs={{0,2},{1,3},{2,0},{3,1},{4,6},{5,7},{6,4},{7,5},{8,10},{9,11},{10,... | collective-permute-start | bytes 3538952 | tf_op jit(solution)/shard_map/ppermute | solution.py:880
  343.2 27.3 %collective-permute-start.42 = (bf16[2,192,1536]{2,1,0:T(8,128)(2,1)S(1)}, bf16[2,192,1536]{2,1,0:T(8,128)(2,1)S(1)}, u32[]{:S(2)}, u32[]{:S(2)}) collective-permute-start(bf16[2,192,1536]{2,1,0:T(8,128)(2,1)S(1)} %copy-done.16), channel_id=1, source_target_pairs={{0,16},{16,0},{1,17},{17,1},{2,18},{18,2},{3,19},{19,3},{4,20},{20... | collective-permute-start | bytes 3538952 | tf_op jit(solution)/shard_map/ppermute | solution.py:884
  370.0 38.4 %collective-permute-start.44 = (bf16[1152,1536]{1,0:T(8,128)(2,1)}, bf16[1152,1536]{1,0:T(8,128)(2,1)}, u32[]{:S(2)}, u32[]{:S(2)}) collective-permute-start(bf16[1152,1536]{1,0:T(8,128)(2,1)} %get-tuple-element.187.refs_10_.refs_2_), channel_id=1, source_target_pairs={{0,16},{16,0},{1,17},{17,1},{2,18},{18,2},{3,19},{19,3},{4,20},{20... | collective-permute-start | bytes 10616840 | tf_op jit(solution)/shard_map/ppermute | solution.py:884
  370.5 29.3 %collective-permute-start.38 = (f32[8,1536]{1,0:T(8,128)}, f32[8,1536]{1,0:T(8,128)S(1)}, u32[]{:S(2)}, u32[]{:S(2)}) collective-permute-start(f32[8,1536]{1,0:T(8,128)} %get-tuple-element.192.refs_10_), channel_id=1, source_target_pairs={{0,16},{16,0},{1,17},{17,1},{2,18},{18,2},{3,19},{19,3},{4,20},{20... | collective-permute-start | bytes 147464 | tf_op jit(solution)/shard_map/ppermute | solution.py:884
  403.3 43.9 %collective-permute-start.53 = (bf16[1152,1536]{1,0:T(8,128)(2,1)}, bf16[1152,1536]{1,0:T(8,128)(2,1)}, u32[]{:S(2)}, u32[]{:S(2)}) collective-permute-start(bf16[1152,1536]{1,0:T(8,128)(2,1)} %get-tuple-element.216.refs_2_), channel_id=1, source_target_pairs={{0,16},{16,0},{1,17},{17,1},{2,18},{18,2},{3,19},{19,3},{4,20},{20... | collective-permute-start | bytes 10616840 | tf_op jit(solution)/shard_map/ppermute | solution.py:884
  404.2 36.3 %collective-permute-start.48 = (f32[8,1536]{1,0:T(8,128)S(1)}, f32[8,1536]{1,0:T(8,128)S(1)}, u32[]{:S(2)}, u32[]{:S(2)}) collective-permute-start(f32[8,1536]{1,0:T(8,128)S(1)} %add.127.refs_12_.refs_1_), channel_id=1, source_target_pairs={{0,1},{1,0},{2,3},{3,2},{4,5},{5,4},{6,7},{7,6},{8,9},{9,8},{10,11... | collective-permute-start | bytes 147464 | tf_op jit(solution)/shard_map/ppermute | solution.py:880
  405.5 35.0 %collective-permute-start.49 = (f32[8,1536]{1,0:T(8,128)S(1)}, f32[8,1536]{1,0:T(8,128)S(1)}, u32[]{:S(2)}, u32[]{:S(2)}) collective-permute-start(f32[8,1536]{1,0:T(8,128)S(1)} %add.127.refs_12_.refs_1_), channel_id=1, source_target_pairs={{0,2},{1,3},{2,0},{3,1},{4,6},{5,7},{6,4},{7,5},{8,10},{9,11},{10,... | collective-permute-start | bytes 147464 | tf_op jit(solution)/shard_map/ppermute | solution.py:880
  407.7 32.8 %collective-permute-start.50 = (f32[8,1536]{1,0:T(8,128)S(1)}, f32[8,1536]{1,0:T(8,128)S(1)}, u32[]{:S(2)}, u32[]{:S(2)}) collective-permute-start(f32[8,1536]{1,0:T(8,128)S(1)} %add.127.refs_12_.refs_1_), channel_id=1, source_target_pairs={{0,3},{1,2},{2,1},{3,0},{4,7},{5,6},{6,5},{7,4},{8,11},{9,10},{10,... | collective-permute-start | bytes 147464 | tf_op jit(solution)/shard_map/ppermute | solution.py:880
  459.1 28.9 %collective-permute-start.54 = (bf16[2,192,1536]{2,1,0:T(8,128)(2,1)}, bf16[2,192,1536]{2,1,0:T(8,128)(2,1)S(1)}, u32[]{:S(2)}, u32[]{:S(2)}) collective-permute-start(bf16[2,192,1536]{2,1,0:T(8,128)(2,1)} %get-tuple-element.219), channel_id=1, source_target_pairs={{0,2},{1,3},{2,0},{3,1},{4,6},{5,7},{6,4},{7,5},{8,10},{9,11},{10,... | collective-permute-start | bytes 3538952 | tf_op jit(solution)/shard_map/ppermute | solution.py:880
  487.7 12.5 %collective-permute-start.56 = (bf16[4,192,1152]{2,1,0:T(8,128)(2,1)}, bf16[4,192,1152]{2,1,0:T(8,128)(2,1)S(1)}, u32[]{:S(2)}, u32[]{:S(2)}) collective-permute-start(bf16[4,192,1152]{2,1,0:T(8,128)(2,1)} %get-tuple-element.226), channel_id=1, source_target_pairs={{0,16},{16,0},{1,17},{17,1},{2,18},{18,2},{3,19},{19,3},{4,20},{20... | collective-permute-start | bytes 5308424 | tf_op jit(solution)/shard_map/ppermute | solution.py:884
  489.0 23.0 %collective-permute-start.55 = (bf16[192,1536]{1,0:T(8,128)(2,1)S(1)}, bf16[192,1536]{1,0:T(8,128)(2,1)}, u32[]{:S(2)}, u32[]{:S(2)}) collective-permute-start(bf16[192,1536]{1,0:T(8,128)(2,1)S(1)} %fusion.7.refs_5_), channel_id=1, source_target_pairs={{0,1},{1,0},{2,3},{3,2},{4,5},{5,4},{6,7},{7,6},{8,9},{9,8},{10,11... | collective-permute-start | bytes 1769480 | tf_op jit(solution)/shard_map/ppermute | solution.py:880
  500.2 160.0 %reduce-scatter.10.cloned.1.call-start = ((), (), s32[]{:S(2)}) async-start(), calls=%async_computation.12 | async-start | bytes 4423680 | tf_op jit(solution)/shard_map/reduce_scatter | solution.py:1166
  516.7 20.5 %collective-permute-start.57 = (bf16[192,1664]{1,0:T(8,128)(2,1)}, bf16[192,1664]{1,0:T(8,128)(2,1)S(1)}, u32[]{:S(2)}, u32[]{:S(2)}) collective-permute-start(bf16[192,1664]{1,0:T(8,128)(2,1)} %get-tuple-element.234.refs_4_), channel_id=1, source_target_pairs={{0,1},{1,0},{2,3},{3,2},{4,5},{5,4},{6,7},{7,6},{8,9},{9,8},{10,11... | collective-permute-start | bytes 1916936 | tf_op jit(solution)/shard_map/ppermute | solution.py:880
  517.4 28.0 %collective-permute-start.58 = (bf16[2,192,1536]{2,1,0:T(8,128)(2,1)S(1)}, bf16[2,192,1536]{2,1,0:T(8,128)(2,1)}, u32[]{:S(2)}, u32[]{:S(2)}) collective-permute-start(bf16[2,192,1536]{2,1,0:T(8,128)(2,1)S(1)} %copy-done.74), channel_id=1, source_target_pairs={{0,2},{1,3},{2,0},{3,1},{4,6},{5,7},{6,4},{7,5},{8,10},{9,11},{10,... | collective-permute-start | bytes 3538952 | tf_op jit(solution)/shard_map/ppermute | solution.py:880
  546.7 210.8 %reduce-scatter.6.cloned.1.call-start = ((), (), s32[]{:S(2)}) async-start(), calls=%async_computation.10 | async-start | bytes 5898240 | tf_op jit(solution)/shard_map/reduce_scatter | solution.py:1169
  548.1 30.0 %collective-permute-start.60 = (bf16[2,192,1664]{2,1,0:T(8,128)(2,1)S(1)}, bf16[2,192,1664]{2,1,0:T(8,128)(2,1)}, u32[]{:S(2)}, u32[]{:S(2)}) collective-permute-start(bf16[2,192,1664]{2,1,0:T(8,128)(2,1)S(1)} %pad_maximum_fusion.refs_8_.refs_0_), channel_id=1, source_target_pairs={{0,2},{1,3},{2,0},{3,1},{4,6},{5,7},{6,4},{7,5},{8,10},{9,11},{10,... | collective-permute-start | bytes 3833864 | tf_op jit(solution)/shard_map/ppermute | solution.py:880
  550.3 14.9 %collective-permute-start.59 = (bf16[192,1536]{1,0:T(8,128)(2,1)S(1)}, bf16[192,1536]{1,0:T(8,128)(2,1)S(1)}, u32[]{:S(2)}, u32[]{:S(2)}) collective-permute-start(bf16[192,1536]{1,0:T(8,128)(2,1)S(1)} %fusion.6.refs_7_), channel_id=1, source_target_pairs={{0,1},{1,0},{2,3},{3,2},{4,5},{5,4},{6,7},{7,6},{8,9},{9,8},{10,11... | collective-permute-start | bytes 1769480 | tf_op jit(solution)/shard_map/ppermute | solution.py:880
  551.2 45.8 %collective-permute-start.61 = (bf16[2,192,1664]{2,1,0:T(8,128)(2,1)S(1)}, bf16[2,192,1664]{2,1,0:T(8,128)(2,1)}, u32[]{:S(2)}, u32[]{:S(2)}) collective-permute-start(bf16[2,192,1664]{2,1,0:T(8,128)(2,1)S(1)} %pad_maximum_fusion.refs_8_.refs_0_), channel_id=1, source_target_pairs={{0,16},{16,0},{1,17},{17,1},{2,18},{18,2},{3,19},{19,3},{4,20},{20... | collective-permute-start | bytes 3833864 | tf_op jit(solution)/shard_map/ppermute | solution.py:884
  578.1 18.8 %collective-permute-start.62 = (bf16[2,192,1664]{2,1,0:T(8,128)(2,1)}, bf16[2,192,1664]{2,1,0:T(8,128)(2,1)}, u32[]{:S(2)}, u32[]{:S(2)}) collective-permute-start(bf16[2,192,1664]{2,1,0:T(8,128)(2,1)} %collective-permute-done.60.refs_1_), channel_id=1, source_target_pairs={{0,16},{16,0},{1,17},{17,1},{2,18},{18,2},{3,19},{19,3},{4,20},{20... | collective-permute-start | bytes 3833864 | tf_op jit(solution)/shard_map/ppermute | solution.py:884
  578.1 17.0 %collective-permute-start.63 = (bf16[192,1664]{1,0:T(8,128)(2,1)}, bf16[192,1664]{1,0:T(8,128)(2,1)S(1)}, u32[]{:S(2)}, u32[]{:S(2)}) collective-permute-start(bf16[192,1664]{1,0:T(8,128)(2,1)} %get-tuple-element.238.refs_14_.refs_4_), channel_id=1, source_target_pairs={{0,1},{1,0},{2,3},{3,2},{4,5},{5,4},{6,7},{7,6},{8,9},{9,8},{10,11... | collective-permute-start | bytes 1916936 | tf_op jit(solution)/shard_map/ppermute | solution.py:880
  596.4 33.0 %collective-permute-start.64 = (bf16[2,192,1664]{2,1,0:T(8,128)(2,1)S(1)}, bf16[2,192,1664]{2,1,0:T(8,128)(2,1)}, u32[]{:S(2)}, u32[]{:S(2)}) collective-permute-start(bf16[2,192,1664]{2,1,0:T(8,128)(2,1)S(1)} %pad_maximum_fusion.1.refs_16_.refs_5_.refs_0_), channel_id=1, source_target_pairs={{0,2},{1,3},{2,0},{3,1},{4,6},{5,7},{6,4},{7,5},{8,10},{9,11},{10,... | collective-permute-start | bytes 3833864 | tf_op jit(solution)/shard_map/ppermute | solution.py:880
  629.5 155.4 %reduce-scatter.12.cloned.1.call-start = ((), (), s32[]{:S(2)}) async-start(), calls=%async_computation.13 | async-start | bytes 4423680 | tf_op jit(solution)/shard_map/reduce_scatter | solution.py:1166
  630.7 27.3 %collective-permute-start.67 = (bf16[2,192,1664]{2,1,0:T(8,128)(2,1)S(1)}, bf16[2,192,1664]{2,1,0:T(8,128)(2,1)S(1)}, u32[]{:S(2)}, u32[]{:S(2)}) collective-permute-start(bf16[2,192,1664]{2,1,0:T(8,128)(2,1)S(1)} %copy-done.9), channel_id=1, source_target_pairs={{0,16},{16,0},{1,17},{17,1},{2,18},{18,2},{3,19},{19,3},{4,20},{20... | collective-permute-start | bytes 3833864 | tf_op jit(solution)/shard_map/ppermute | solution.py:884
  656.8 40.0 %collective-permute-start.66 = (bf16[2,192,1536]{2,1,0:T(8,128)(2,1)}, bf16[2,192,1536]{2,1,0:T(8,128)(2,1)S(1)}, u32[]{:S(2)}, u32[]{:S(2)}) collective-permute-start(bf16[2,192,1536]{2,1,0:T(8,128)(2,1)} %get-tuple-element.249), channel_id=1, source_target_pairs={{0,2},{1,3},{2,0},{3,1},{4,6},{5,7},{6,4},{7,5},{8,10},{9,11},{10,... | collective-permute-start | bytes 3538952 | tf_op jit(solution)/shard_map/ppermute | solution.py:880
  696.1 17.1 %collective-permute-start.70 = (bf16[4,192,1152]{2,1,0:T(8,128)(2,1)}, bf16[4,192,1152]{2,1,0:T(8,128)(2,1)}, u32[]{:S(2)}, u32[]{:S(2)}) collective-permute-start(bf16[4,192,1152]{2,1,0:T(8,128)(2,1)} %get-tuple-element.261), channel_id=1, source_target_pairs={{0,16},{16,0},{1,17},{17,1},{2,18},{18,2},{3,19},{19,3},{4,20},{20... | collective-permute-start | bytes 5308424 | tf_op jit(solution)/shard_map/ppermute | solution.py:884
  710.0 109.1 %reduce-scatter.14.cloned.1.call-start = ((), (), s32[]{:S(2)}) async-start(), calls=%async_computation.14 | async-start | bytes 1474560 | tf_op jit(solution)/shard_map/reduce_scatter | solution.py:1166
  711.7 40.9 %collective-permute-start.69 = (bf16[192,1536]{1,0:T(8,128)(2,1)S(1)}, bf16[192,1536]{1,0:T(8,128)(2,1)S(1)}, u32[]{:S(2)}, u32[]{:S(2)}) collective-permute-start(bf16[192,1536]{1,0:T(8,128)(2,1)S(1)} %fusion.5), channel_id=1, source_target_pairs={{0,1},{1,0},{2,3},{3,2},{4,5},{5,4},{6,7},{7,6},{8,9},{9,8},{10,11... | collective-permute-start | bytes 1769480 | tf_op jit(solution)/shard_map/ppermute | solution.py:880
  724.5 26.9 %collective-permute-start.71 = (bf16[2,192,1536]{2,1,0:T(8,128)(2,1)}, bf16[2,192,1536]{2,1,0:T(8,128)(2,1)S(1)}, u32[]{:S(2)}, u32[]{:S(2)}) collective-permute-start(bf16[2,192,1536]{2,1,0:T(8,128)(2,1)} %get-tuple-element.267), channel_id=1, source_target_pairs={{0,2},{1,3},{2,0},{3,1},{4,6},{5,7},{6,4},{7,5},{8,10},{9,11},{10,... | collective-permute-start | bytes 3538952 | tf_op jit(solution)/shard_map/ppermute | solution.py:880
  760.8 15.7 %collective-permute-start.73 = (bf16[192,1536]{1,0:T(8,128)(2,1)S(1)}, bf16[192,1536]{1,0:T(8,128)(2,1)S(1)}, u32[]{:S(2)}, u32[]{:S(2)}) collective-permute-start(bf16[192,1536]{1,0:T(8,128)(2,1)S(1)} %copy-done.30), channel_id=1, source_target_pairs={{0,1},{1,0},{2,3},{3,2},{4,5},{5,4},{6,7},{7,6},{8,9},{9,8},{10,11... | collective-permute-start | bytes 1769480 | tf_op jit(solution)/shard_map/ppermute | solution.py:880
  787.2 13.4 %collective-permute-start.79 = (f32[16,1536]{1,0:T(8,128)S(1)}, f32[16,1536]{1,0:T(8,128)S(1)}, u32[]{:S(2)}, u32[]{:S(2)}) collective-permute-start(f32[16,1536]{1,0:T(8,128)S(1)} %select_add_fusion), channel_id=1, source_target_pairs={{0,12},{4,0},{8,4},{12,8},{1,13},{5,1},{9,5},{13,9},{2,14},{6,2},{... | collective-permute-start | bytes 294920 | tf_op jit(solution)/shard_map/ppermute | solution.py:921
  790.4 10.3 %collective-permute-start.76 = (f32[16,1536]{1,0:T(8,128)S(1)}, f32[16,1536]{1,0:T(8,128)S(1)}, u32[]{:S(2)}, u32[]{:S(2)}) collective-permute-start(f32[16,1536]{1,0:T(8,128)S(1)} %select_add_fusion), channel_id=1, source_target_pairs={{0,4},{4,8},{8,12},{12,0},{1,5},{5,9},{9,13},{13,1},{2,6},{6,10},{... | collective-permute-start | bytes 294920 | tf_op jit(solution)/shard_map/ppermute | solution.py:921
  790.4 15.9 %collective-permute-start.78 = (f32[16,1536]{1,0:T(8,128)S(1)}, f32[16,1536]{1,0:T(8,128)S(1)}, u32[]{:S(2)}, u32[]{:S(2)}) collective-permute-start(f32[16,1536]{1,0:T(8,128)S(1)} %select_add_fusion), channel_id=1, source_target_pairs={{0,8},{4,12},{8,0},{12,4},{1,9},{5,13},{9,1},{13,5},{2,10},{6,14},... | collective-permute-start | bytes 294920 | tf_op jit(solution)/shard_map/ppermute | solution.py:921
  808.2 9.9 %collective-permute-start.83 = (bf16[384,304]{1,0:T(8,128)(2,1)S(1)}, bf16[384,304]{1,0:T(8,128)(2,1)S(1)}, u32[]{:S(2)}, u32[]{:S(2)}) collective-permute-start(bf16[384,304]{1,0:T(8,128)(2,1)S(1)} %get-tuple-element.294), channel_id=1, source_target_pairs={{0,1},{1,0},{2,3},{3,2},{4,5},{5,4},{6,7},{7,6},{8,9},{9,8},{10,11... | collective-permute-start | bytes 700424 | tf_op jit(solution)/shard_map/ppermute | solution.py:880
  818.2 8.7 %collective-permute-start.84 = (bf16[384,304]{1,0:T(8,128)(2,1)S(1)}, bf16[384,304]{1,0:T(8,128)(2,1)S(1)}, u32[]{:S(2)}, u32[]{:S(2)}) collective-permute-start(bf16[384,304]{1,0:T(8,128)(2,1)S(1)} %fusion.9), channel_id=1, source_target_pairs={{0,2},{1,3},{2,0},{3,1},{4,6},{5,7},{6,4},{7,5},{8,10},{9,11},{10,... | collective-permute-start | bytes 700424 | tf_op jit(solution)/shard_map/ppermute | solution.py:880
  819.1 8.9 %collective-permute-start.85 = (bf16[384,384]{1,0:T(8,128)(2,1)S(1)}, bf16[384,384]{1,0:T(8,128)(2,1)S(1)}, u32[]{:S(2)}, u32[]{:S(2)}) collective-permute-start(bf16[384,384]{1,0:T(8,128)(2,1)S(1)} %broadcast_select_fusion.13), channel_id=1, source_target_pairs={{0,16},{16,0},{1,17},{17,1},{2,18},{18,2},{3,19},{19,3},{4,20},{20... | collective-permute-start | bytes 884744 | tf_op jit(solution)/shard_map/ppermute | solution.py:884
  (129 other events, 825.6 us)
Sparse Core Ops, SparseCore 0:
  22.3 41.5 all-gather.5
  66.3 38.9 all-gather.7
  113.0 27.1 all-gather.9
  187.2 28.4 all-gather.11
  217.1 69.0 all-gather.13
  500.3 26.5 reduce-scatter.7
  546.8 63.1 reduce-scatter.9
  629.6 70.6 reduce-scatter.5
  710.1 66.4 reduce-scatter.11
  785.0 32.8 reduce-scatter.13

commit v4 on v3

--- a/solution.py
+++ b/solution.py
@@ -912,8 +912,7 @@
 
 
 def all_tensor(value):
-    value = value + across(value, 1)
-    return value + across(value, 2)
+    return (value + across(value, 1)) + (across(value, 2) + across(value, 3))
 
 
 def cycle(value, steps):
@@ -1223,8 +1222,9 @@
     cut = lambda v: after(v, got)[:, 2 * inner : 2 * inner + w_bcdt.shape[2]]
     kept, got = owned([cut(v) for v in (w0_sum, w1_sum)])
     shard = kept.astype(F32) + got.astype(F32)
-    for bit in (1, 2):
-        shard = shard + across(shard.astype(BF16), bit).astype(F32)
+    low = shard.astype(BF16)
+    for k in (1, 2, 3):
+        shard = shard + across(low, k).astype(F32)
     grad_w_bcdt = shard[None]
     return (
         out_act,

time: 844 us -> 849 us (level)
    ppermute x40 -> x42, waiting for transfers between devices: 145 us -> 140 us  [across(): return lax.ppermute(value, 'tensor', [(i, i ^ step) for i in range(count)])]
    ppermute x40 -> x42, starting transfers between devices: 46.6 us -> 50.1 us  [across(): return lax.ppermute(value, 'tensor', [(i, i ^ step) for i in range(count)])]
    unnamed x205 -> x209, local copies, waits for them, and re-layouts: 29.6 us -> 30.3 us
  transfers between devices with their start and end apart: 96 -> 98, of which waited for: 39 -> 38; matrix products, arithmetic and copies ran while one was open for 5% -> 6% of each run, Pallas kernels for 52% -> 52%
where the time goes in v4:
time: 849 us; the launch traced here: 841 us
  Pallas kernels  446 us (53%)
  waiting for transfers between devices  216 us (25%)
  starting transfers between devices  78 us (9%)
  local copies, waits for them, and re-layouts  50.4 us (6%)
  other arithmetic  32.1 us (4%)
  between operations  18.1 us (2%)
    pallas_call x32, Pallas kernels, call(): pl.pallas_call(body, out_shape=tuple((jax.ShapeDtypeStruct(shape, kind) f...  413 us
    ppermute x42, waiting for transfers between devices, across(): return lax.ppermute(value, 'tensor', [(i, i ^ step) for i in range(count)])  140 us
    ppermute x42, starting transfers between devices, across(): return lax.ppermute(value, 'tensor', [(i, i ^ step) for i in range(count)])  50.1 us
    ppermute x3, waiting for transfers between devices, pieces_dp(): lax.ppermute(after(up[-1], *waits), 'dp', [(i, i + 1) for i in range(3)])  40 us
    pallas_call x9, Pallas kernels, run_plain(): pl.pallas_call(body, in_specs=[vmem] * count + [pl.BlockSpec(memory_space...  33.3 us
    unnamed x209, local copies, waits for them, and re-layouts  30.3 us
  transfers between devices with their start and end apart: 98, of which 38 were waited for; matrix products, arithmetic and copies ran while one was open for 6% of the time, Pallas kernels for 52%

profile of v4, /device:TPU:0, one launch (start us, length us, event | category | flops | bytes accessed | tf_op | source)
XLA Modules:
  0.0 840.9 jit_solution(5954502802751663903)
XLA Ops:
  7.2 3.7 fusion.20
  22.2 4.9 collective-permute-start.2
  28.4 17.9 %collective-permute-done.2.refs_2_.refs_1_ = bf16[384,1152]{1,0:T(8,128)(2,1)S(1)} collective-permute-done((bf16[384,1152]{1,0:T(8,128)(2,1)S(1)}, bf16[384,1152]{1,0:T(8,128)(2,1)S(1)}, u32[]{:S(2)}, u32[]{:S(2)}) %collective-permute-start.2) | collective-permute-done | bytes 884768 | tf_op jit(solution)/shard_map/ppermute | solution.py:929
  47.2 3.3 collective-permute-done.3.refs_5_.refs_4_
  56.1 4.3 collective-permute-start.4
  71.9 7.4 collective-permute-done.4.refs_3_.refs_2_
  79.4 5.0 collective-permute-done.5.refs_6_.refs_5_
  91.1 14.7 %collective-permute-done.6.refs_4_.refs_3_ = bf16[384,1152]{1,0:T(8,128)(2,1)S(1)} collective-permute-done((bf16[384,1152]{1,0:T(8,128)(2,1)}, bf16[384,1152]{1,0:T(8,128)(2,1)S(1)}, u32[]{:S(2)}, u32[]{:S(2)}) %collective-permute-start.6) | collective-permute-done | bytes 884768 | tf_op jit(solution)/shard_map/ppermute | solution.py:929
  105.8 4.1 collective-permute-done.7.refs_7_.refs_6_
  114.3 25.1 %layer_fwd.4 = (f32[1536,1152]{1,0:T(8,128)}, f32[1536,384]{1,0:T(8,128)}, bf16[12,128,384]{2,1,0:T(8,128)(2,1)}, f32[1536,384]{1,0:T(8,128)}, f32[8,1536]{1,0:T(8,128)}) custom-call(s32[5]{0:T(128)} %stack.91.sc, bf16[1536,1536]{1,0:T(8,128)(2,1)} %all-gather.6.cloned.1.call-done.refs_0_, bf16[384,1152]{1,0:T(8,128)(2,1)} %copy-done.25, ...), custom_call_target="tpu_custom_call" | custom-call | flops 25769803776 | bytes 25165824 | tf_op jit(solution)/shard_map/layer_fwd/pallas_call | solution.py:261
  143.9 25.0 %layer_fwd.5 = (f32[1536,1152]{1,0:T(8,128)}, f32[1536,384]{1,0:T(8,128)}, bf16[12,128,384]{2,1,0:T(8,128)(2,1)}, f32[1536,384]{1,0:T(8,128)}, f32[8,1536]{1,0:T(8,128)}) custom-call(s32[5]{0:T(128)} %stack.93.sc, bf16[1536,1536]{1,0:T(8,128)(2,1)} %all-gather.8.cloned.1.call-done.refs_0_, bf16[384,1152]{1,0:T(8,128)(2,1)} %copy-done.25, ...), custom_call_target="tpu_custom_call" | custom-call | flops 25769803776 | bytes 25165824 | tf_op jit(solution)/shard_map/layer_fwd/pallas_call | solution.py:261
  181.3 5.2 scale_rows.4
  194.9 6.2 half_rows.7
  201.8 5.1 scale_rows.5
  209.2 6.3 half_rows.8
  218.4 9.4 %grad_rows.3 = (f32[1536,384]{1,0:T(8,128)}, bf16[1536,1536]{1,0:T(8,128)(2,1)}) custom-call(s32[5]{0:T(128)} %stack.91.sc, bf16[2,192,1536]{2,1,0:T(8,128)(2,1)} %pad_maximum_fusion.3.refs_0_, bf16[2,192,1536]{2,1,0:T(8,128)(2,1)} %collective-permute-done.14.refs_7_.refs_1_, bf16[2,192,1536]{2,1,0:T(8,128)(2,1)} %copy-done.70, ...), custom_call_target="tpu_custom_call" | custom-call | flops 8589934592 | bytes 18874368 | tf_op jit(solution)/shard_map/grad_rows/pallas_call | solution.py:261
  227.8 33.1 %collective-permute-done.19.refs_1_ = f32[2,192,1536]{2,1,0:T(8,128)} collective-permute-done((f32[2,192,1536]{2,1,0:T(8,128)}, f32[2,192,1536]{2,1,0:T(8,128)}, u32[]{:S(2)}, u32[]{:S(2)}) %collective-permute-start.19) | collective-permute-done | bytes 2359328 | tf_op jit(solution)/shard_map/ppermute | solution.py:880
  263.6 8.9 %grad_rows.4 = (f32[1536,384]{1,0:T(8,128)}, bf16[1536,1536]{1,0:T(8,128)(2,1)}) custom-call(s32[5]{0:T(128)} %stack.93.sc, bf16[2,192,1536]{2,1,0:T(8,128)(2,1)} %copy-done.16, bf16[2,192,1536]{2,1,0:T(8,128)(2,1)} %collective-permute-done.15.refs_8_.refs_1_, bf16[2,192,1536]{2,1,0:T(8,128)(2,1)} %collective-permute-done.28.refs_2_, ...), custom_call_target="tpu_custom_call" | custom-call | flops 8589934592 | bytes 18874368 | tf_op jit(solution)/shard_map/grad_rows/pallas_call | solution.py:261
  275.7 18.7 %collective-permute-done.27.refs_2_ = f32[192,1536]{1,0:T(8,128)S(1)} collective-permute-done((f32[192,1536]{1,0:T(8,128)S(1)}, f32[192,1536]{1,0:T(8,128)S(1)}, u32[]{:S(2)}, u32[]{:S(2)}) %collective-permute-start.27) | collective-permute-done | bytes 1179680 | tf_op jit(solution)/shard_map/ppermute | solution.py:880
  295.4 4.2 owner_mid.2
  302.3 4.2 owner_mid.3
  307.7 8.3 collective-permute-done.32
  317.9 6.1 turn_weights.2
  324.0 3.0 collective-permute-done.34
  328.2 7.5 turn_weights.3
  335.6 5.3 collective-permute-done.33.refs_1_
  344.1 24.4 %layer_fwd.6 = (bf16[1536,1536]{1,0:T(8,128)(2,1)}, f32[1536,1152]{1,0:T(8,128)}, f32[1536,384]{1,0:T(8,128)}, bf16[12,128,384]{2,1,0:T(8,128)(2,1)}, f32[1536,384]{1,0:T(8,128)}, /*index=5*/f32[8,1536]{1,0:T(8,128)}) custom-call(s32[5]{0:T(128)} %stack.91.sc, bf16[2,192,1536]{2,1,0:T(8,128)(2,1)} %copy-done.18, ...), custom_call_target="tpu_custom_call" | custom-call | flops 25769803776 | bytes 25165824 | tf_op jit(solution)/shard_map/layer_fwd/pallas_call | solution.py:261
  370.5 3.3 collective-permute-done.43.refs_3_
  374.9 24.6 %layer_fwd.7 = (bf16[1536,1536]{1,0:T(8,128)(2,1)}, f32[1536,1152]{1,0:T(8,128)}, f32[1536,384]{1,0:T(8,128)}, bf16[12,128,384]{2,1,0:T(8,128)(2,1)}, f32[1536,384]{1,0:T(8,128)}, /*index=5*/f32[8,1536]{1,0:T(8,128)}) custom-call(s32[5]{0:T(128)} %stack.93.sc, bf16[2,192,1536]{2,1,0:T(8,128)(2,1)} %pad_maximum_fusion.6.refs_9_.refs_0_, ...), custom_call_target="tpu_custom_call" | custom-call | flops 25769803776 | bytes 25165824 | tf_op jit(solution)/shard_map/layer_fwd/pallas_call | solution.py:261
  408.3 5.1 scale_rows.6
  413.4 27.1 %layer_bwd.4 = (bf16[1536,1152]{1,0:T(8,128)(2,1)}, bf16[4,192,1152]{2,1,0:T(8,128)(2,1)}, f32[16,1536]{1,0:T(8,128)}) custom-call(s32[5]{0:T(128)} %stack.91.sc, f32[1536,384]{1,0:T(8,128)} %get-tuple-element.175.refs_5_.refs_9_.refs_0_, f32[1536,128]{1,0:T(8,128)} %get-tuple-element.199.refs_1_.refs_6_, f32[1536,1152]{1,0:T(8,128)} %get-tuple-element.200.refs_2_.refs_3_, ...), custom_call_target="tpu_custom_call" | custom-call | flops 30064771072 | bytes 25165824 | tf_op jit(solution)/shard_map/layer_bwd/pallas_call | solution.py:261
  442.2 5.1 scale_rows.7
  448.6 10.6 %half_rows.9 = (f32[192,1536]{1,0:T(8,128)}, f32[192,1536]{1,0:T(8,128)}, bf16[2,192,1536]{2,1,0:T(8,128)(2,1)}) custom-call(s32[5]{0:T(128)} %stack.91.sc, bf16[4,2,192,1152]{3,2,1,0:T(8,128)(2,1)} %bitcast.128, bf16[4,192,1152]{2,1,0:T(8,128)(2,1)} %copy-done.66, bf16[1152,1536]{1,0:T(8,128)(2,1)} %get-tuple-element.216.refs_2_, ...), custom_call_target="tpu_custom_call" | custom-call | flops 8589934592 | bytes 10485760 | tf_op jit(solution)/shard_map/half_rows/pallas_call | solution.py:261
  460.8 27.0 %layer_bwd.5 = (bf16[1536,1152]{1,0:T(8,128)(2,1)}, bf16[4,192,1152]{2,1,0:T(8,128)(2,1)}, f32[16,1536]{1,0:T(8,128)}) custom-call(s32[5]{0:T(128)} %stack.93.sc, f32[1536,384]{1,0:T(8,128)} %get-tuple-element.177.refs_5_.refs_9_.refs_0_, f32[1536,128]{1,0:T(8,128)} %get-tuple-element.209.refs_1_.refs_6_, f32[1536,1152]{1,0:T(8,128)} %get-tuple-element.210.refs_2_.refs_3_, ...), custom_call_target="tpu_custom_call" | custom-call | flops 30064771072 | bytes 25165824 | tf_op jit(solution)/shard_map/layer_bwd/pallas_call | solution.py:261
  490.4 9.9 %outer_rows.5.refs_4_ = bf16[1536,384]{1,0:T(8,128)(2,1)} custom-call(s32[5]{0:T(128)} %stack.91.sc, bf16[1536,1536]{1,0:T(8,128)(2,1)} %get-tuple-element.227.refs_0_, bf16[1536,384]{1,0:T(8,128)(2,1)} %get-tuple-element.195.refs_11_.refs_1_, bf16[1536,1536]{1,0:T(8,128)(2,1)} %get-tuple-element.228.refs_2_, ...), custom_call_target="tpu_custom_call" | custom-call | flops 19327352832 | bytes 16777216 | tf_op jit(solution)/shard_map/outer_rows/pallas_call | solution.py:261
  501.5 10.6 %half_rows.10 = (f32[192,1536]{1,0:T(8,128)}, f32[192,1536]{1,0:T(8,128)}, bf16[2,192,1536]{2,1,0:T(8,128)(2,1)}) custom-call(s32[5]{0:T(128)} %stack.93.sc, bf16[4,2,192,1152]{3,2,1,0:T(8,128)(2,1)} %bitcast.129, bf16[4,192,1152]{2,1,0:T(8,128)(2,1)} %copy-done.67, bf16[1152,1536]{1,0:T(8,128)(2,1)} %get-tuple-element.216.refs_2_, ...), custom_call_target="tpu_custom_call" | custom-call | flops 8589934592 | bytes 10485760 | tf_op jit(solution)/shard_map/half_rows/pallas_call | solution.py:261
  512.1 4.7 owner_back.2
  518.7 18.6 %outer_rows.6.refs_6_ = bf16[1536,1152]{1,0:T(8,128)(2,1)} custom-call(s32[5]{0:T(128)} %stack.91.sc, bf16[1536,1536]{1,0:T(8,128)(2,1)} %get-tuple-element.206.refs_0_, bf16[1536,1152]{1,0:T(8,128)(2,1)} %get-tuple-element.207.refs_1_, bf16[1536,1536]{1,0:T(8,128)(2,1)} %get-tuple-element.208.refs_2_, bf16[1536,1152]{1,0:T(8,128)(2,1)} %get-tuple-element.218.refs_3_, ...), custom_call_target="tpu_custom_call" | custom-call | flops 19327352832 | bytes 16777216 | tf_op jit(solution)/shard_map/outer_rows/pallas_call | solution.py:261
  537.3 8.3 collective-permute-done.58.refs_1_
  552.6 8.6 %half_rows.11.refs_8_ = bf16[1536,1536]{1,0:T(8,128)(2,1)} custom-call(s32[5]{0:T(128)} %stack.91.sc, bf16[4,2,192,384]{3,2,1,0:T(8,128)(2,1)} %bitcast.134, bf16[4,192,384]{2,1,0:T(8,128)(2,1)} %copy-done.83, bf16[384,1536]{1,0:T(8,128)(2,1)} %get-tuple-element.197.refs_8_.refs_2_, bf16[384,1536]{1,0:T(8,128)(2,1)} %copy-done.74, ...), custom_call_target="tpu_custom_call" | custom-call | flops 8589934592 | bytes 10485760 | tf_op jit(solution)/shard_map/half_rows/pallas_call | solution.py:261
  561.2 4.0 collective-permute-done.59.refs_2_
  566.0 4.6 owner_back.3
  570.7 7.6 collective-permute-done.60.refs_1_
  579.2 16.0 %collective-permute-done.63 = bf16[192,1664]{1,0:T(8,128)(2,1)S(1)} collective-permute-done((bf16[192,1664]{1,0:T(8,128)(2,1)}, bf16[192,1664]{1,0:T(8,128)(2,1)S(1)}, u32[]{:S(2)}, u32[]{:S(2)}) %collective-permute-start.63) | collective-permute-done | bytes 639008 | tf_op jit(solution)/shard_map/ppermute | solution.py:880
  597.5 32.0 %layer_bwd.6 = (bf16[1536,1536]{1,0:T(8,128)(2,1)}, bf16[1536,1152]{1,0:T(8,128)(2,1)}, bf16[4,192,1152]{2,1,0:T(8,128)(2,1)}, f32[16,1536]{1,0:T(8,128)}) custom-call(s32[5]{0:T(128)} %stack.91.sc, bf16[2,192,1664]{2,1,0:T(8,128)(2,1)} %copy-done.7, bf16[2,192,1664]{2,1,0:T(8,128)(2,1)} %collective-permute-done.60.refs_1_, ...), custom_call_target="tpu_custom_call" | custom-call | flops 30064771072 | bytes 25165824 | tf_op jit(solution)/shard_map/layer_bwd/pallas_call | solution.py:261
  634.7 10.5 %half_rows.12 = (f32[192,1536]{1,0:T(8,128)}, f32[192,1536]{1,0:T(8,128)}, bf16[2,192,1536]{2,1,0:T(8,128)(2,1)}) custom-call(s32[5]{0:T(128)} %stack.91.sc, bf16[4,2,192,1152]{3,2,1,0:T(8,128)(2,1)} %bitcast.131, bf16[4,192,1152]{2,1,0:T(8,128)(2,1)} %copy-done.68, bf16[1152,1536]{1,0:T(8,128)(2,1)} %get-tuple-element.187.refs_10_.refs_2_, ...), custom_call_target="tpu_custom_call" | custom-call | flops 8589934592 | bytes 10485760 | tf_op jit(solution)/shard_map/half_rows/pallas_call | solution.py:261
  645.2 11.7 %outer_rows.7.refs_5_.refs_2_ = f32[1536,1152]{1,0:T(8,128)} custom-call(s32[5]{0:T(128)} %stack.91.sc, bf16[1536,1536]{1,0:T(8,128)(2,1)} %all-gather.6.cloned.1.call-done.refs_0_, bf16[1536,1152]{1,0:T(8,128)(2,1)} %get-tuple-element.244.refs_1_, f32[192,1536]{1,0:T(8,128)} %get-tuple-element.248.refs_2_.refs_0_), custom_call_target="tpu_custom_call" | custom-call | flops 9663676416 | bytes 16777216 | tf_op jit(solution)/shard_map/outer_rows/pallas_call | solution.py:261
  660.3 9.8 %grad_rows.5 = (f32[1536,384]{1,0:T(8,128)}, bf16[1536,1536]{1,0:T(8,128)(2,1)}, f32[1536,128]{1,0:T(8,128)}) custom-call(s32[5]{0:T(128)} %stack.93.sc, bf16[2,192,1664]{2,1,0:T(8,128)(2,1)} %copy-done.8, bf16[2,192,1664]{2,1,0:T(8,128)(2,1)} %collective-permute-done.64.refs_1_, bf16[2,192,1664]{2,1,0:T(8,128)(2,1)} %copy-done.69, ...), custom_call_target="tpu_custom_call" | custom-call | flops 8589934592 | bytes 18874368 | tf_op jit(solution)/shard_map/grad_rows/pallas_call | solution.py:261
  670.0 26.2 %layer_bwd.7 = (bf16[1536,1152]{1,0:T(8,128)(2,1)}, bf16[4,192,1152]{2,1,0:T(8,128)(2,1)}, f32[16,1536]{1,0:T(8,128)}) custom-call(s32[5]{0:T(128)} %stack.93.sc, f32[1536,384]{1,0:T(8,128)} %get-tuple-element.253.refs_0_.refs_11_, f32[1536,128]{1,0:T(8,128)} %get-tuple-element.254.refs_1_, f32[1536,1152]{1,0:T(8,128)} %get-tuple-element.255.refs_2_.refs_3_, ...), custom_call_target="tpu_custom_call" | custom-call | flops 30064771072 | bytes 25165824 | tf_op jit(solution)/shard_map/layer_bwd/pallas_call | solution.py:261
  697.9 12.1 %outer_rows.8.refs_4_ = bf16[1536,1152]{1,0:T(8,128)(2,1)} custom-call(s32[5]{0:T(128)} %stack.91.sc, bf16[1536,1536]{1,0:T(8,128)(2,1)} %all-gather.8.cloned.1.call-done.refs_0_, bf16[1536,1152]{1,0:T(8,128)(2,1)} %get-tuple-element.260.refs_1_, f32[1536,1152]{1,0:T(8,128)} %outer_rows.7.refs_5_.refs_2_, f32[16,1536]{1,0:T(8,128)} %get-tuple-element.258.refs_3_, ...), custom_call_target="tpu_custom_call" | custom-call | flops 9663676416 | bytes 16777216 | tf_op jit(solution)/shard_map/outer_rows/pallas_call | solution.py:261
  713.3 11.2 %half_rows.13 = (f32[192,1536]{1,0:T(8,128)}, f32[192,1536]{1,0:T(8,128)}, bf16[2,192,1536]{2,1,0:T(8,128)(2,1)}) custom-call(s32[5]{0:T(128)} %stack.93.sc, bf16[4,2,192,1152]{3,2,1,0:T(8,128)(2,1)} %bitcast.130, bf16[4,192,1152]{2,1,0:T(8,128)(2,1)} %collective-permute-done.70.refs_1_, bf16[1152,1536]{1,0:T(8,128)(2,1)} %get-tuple-element.187.refs_10_.refs_2_, ...), custom_call_target="tpu_custom_call" | custom-call | flops 8589934592 | bytes 10485760 | tf_op jit(solution)/shard_map/half_rows/pallas_call | solution.py:261
  724.6 10.0 %outer_rows.9.refs_7_ = bf16[1536,384]{1,0:T(8,128)(2,1)} custom-call(s32[5]{0:T(128)} %stack.91.sc, bf16[1536,1536]{1,0:T(8,128)(2,1)} %get-tuple-element.263.refs_0_, bf16[1536,384]{1,0:T(8,128)(2,1)} %get-tuple-element.163.refs_1_, bf16[1536,1536]{1,0:T(8,128)(2,1)} %get-tuple-element.264.refs_2_, bf16[1536,384]{1,0:T(8,128)(2,1)} %get-tuple-element.172.refs_3_, ...), custom_call_target="tpu_custom_call" | custom-call | flops 19327352832 | bytes 16777216 | tf_op jit(solution)/shard_map/outer_rows/pallas_call | solution.py:261
  734.6 16.9 %collective-permute-done.71.refs_1_ = bf16[2,192,1536]{2,1,0:T(8,128)(2,1)S(1)} collective-permute-done((bf16[2,192,1536]{2,1,0:T(8,128)(2,1)}, bf16[2,192,1536]{2,1,0:T(8,128)(2,1)S(1)}, u32[]{:S(2)}, u32[]{:S(2)}) %collective-permute-start.71) | collective-permute-done | bytes 1179680 | tf_op jit(solution)/shard_map/ppermute | solution.py:880
  753.5 4.1 owner_last.2
  757.6 3.3 owner_out.1.refs_0_
  761.6 4.0 collective-permute-done.72.refs_1_
  767.0 4.9 join_rows.2.refs_6_
  771.9 4.7 collective-permute-done.73.refs_2_
  777.4 4.0 owner_last.3
  787.8 3.2 collective-permute-start.79
  793.3 3.5 join_rows.3
  796.9 4.7 weave_cols.1
  801.6 4.5 collective-permute-done.78
  824.3 4.0 collective-permute-done.85
  (471 shorter events, 170.5 us)
Async XLA Ops:
  7.2 105.9 %all-gather.6.cloned.1.call-start = ((), (), s32[]{:S(2)}) async-start(), calls=%async_computation.5 | async-start | bytes 5308416 | tf_op jit(solution)/shard_map/all_gather | solution.py:1007
  22.2 120.6 %all-gather.8.cloned.1.call-start = ((), (), s32[]{:S(2)}) async-start(), calls=%async_computation.6 | async-start | bytes 5308416 | tf_op jit(solution)/shard_map/all_gather | solution.py:1007
  22.2 24.1 %collective-permute-start.2 = (bf16[384,1152]{1,0:T(8,128)(2,1)S(1)}, bf16[384,1152]{1,0:T(8,128)(2,1)S(1)}, u32[]{:S(2)}, u32[]{:S(2)}) collective-permute-start(bf16[384,1152]{1,0:T(8,128)(2,1)S(1)} %get-tuple-element.146.refs_1_.refs_0_), channel_id=1, source_target_pairs={{0,4},{4,8},{8,12},{1,5},{5,9},{9,13},{2,6},{6,10},{10,14},{3,7},{... | collective-permute-start | bytes 2654216 | tf_op jit(solution)/shard_map/ppermute | solution.py:929
  27.1 23.4 %collective-permute-start.3 = (bf16[384,1152]{1,0:T(8,128)(2,1)S(1)}, bf16[384,1152]{1,0:T(8,128)(2,1)}, u32[]{:S(2)}, u32[]{:S(2)}) collective-permute-start(bf16[384,1152]{1,0:T(8,128)(2,1)S(1)} %get-tuple-element.146.refs_1_.refs_0_), channel_id=1, source_target_pairs={{4,0},{8,4},{12,8},{5,1},{9,5},{13,9},{6,2},{10,6},{14,10},{7,3},{... | collective-permute-start | bytes 2654216 | tf_op jit(solution)/shard_map/ppermute | solution.py:930
  53.6 115.3 %all-gather.10.cloned.1.call-start = ((), (), s32[]{:S(2)}) async-start(), calls=%async_computation.7 | async-start | bytes 1474560 | tf_op jit(solution)/shard_map/all_gather | solution.py:1012
  56.1 23.3 %collective-permute-start.4 = (bf16[384,1152]{1,0:T(8,128)(2,1)}, bf16[384,1152]{1,0:T(8,128)(2,1)}, u32[]{:S(2)}, u32[]{:S(2)}) collective-permute-start(bf16[384,1152]{1,0:T(8,128)(2,1)} %copy-done.79), channel_id=1, source_target_pairs={{0,4},{4,8},{8,12},{1,5},{5,9},{9,13},{2,6},{6,10},{10,14},{3,7},{... | collective-permute-start | bytes 2654216 | tf_op jit(solution)/shard_map/ppermute | solution.py:929
  60.4 24.0 %collective-permute-start.5 = (bf16[384,1152]{1,0:T(8,128)(2,1)}, bf16[384,1152]{1,0:T(8,128)(2,1)}, u32[]{:S(2)}, u32[]{:S(2)}) collective-permute-start(bf16[384,1152]{1,0:T(8,128)(2,1)} %collective-permute-done.3.refs_5_.refs_4_), channel_id=1, source_target_pairs={{4,0},{8,4},{12,8},{5,1},{9,5},{13,9},{6,2},{10,6},{14,10},{7,3},{... | collective-permute-start | bytes 2654216 | tf_op jit(solution)/shard_map/ppermute | solution.py:930
  84.4 21.4 %collective-permute-start.6 = (bf16[384,1152]{1,0:T(8,128)(2,1)}, bf16[384,1152]{1,0:T(8,128)(2,1)S(1)}, u32[]{:S(2)}, u32[]{:S(2)}) collective-permute-start(bf16[384,1152]{1,0:T(8,128)(2,1)} %collective-permute-done.4.refs_3_.refs_2_), channel_id=1, source_target_pairs={{0,4},{4,8},{8,12},{1,5},{5,9},{9,13},{2,6},{6,10},{10,14},{3,7},{... | collective-permute-start | bytes 2654216 | tf_op jit(solution)/shard_map/ppermute | solution.py:929
  87.0 22.8 %collective-permute-start.7 = (bf16[384,1152]{1,0:T(8,128)(2,1)}, bf16[384,1152]{1,0:T(8,128)(2,1)S(1)}, u32[]{:S(2)}, u32[]{:S(2)}) collective-permute-start(bf16[384,1152]{1,0:T(8,128)(2,1)} %collective-permute-done.5.refs_6_.refs_5_), channel_id=1, source_target_pairs={{4,0},{8,4},{12,8},{5,1},{9,5},{13,9},{6,2},{10,6},{14,10},{7,3},{... | collective-permute-start | bytes 2654216 | tf_op jit(solution)/shard_map/ppermute | solution.py:930
  109.8 29.6 %collective-permute-start.12 = (bf16[192,1536]{1,0:T(8,128)(2,1)S(1)}, bf16[192,1536]{1,0:T(8,128)(2,1)S(1)}, u32[]{:S(2)}, u32[]{:S(2)}) collective-permute-start(bf16[192,1536]{1,0:T(8,128)(2,1)S(1)} %copy-done.6), channel_id=1, source_target_pairs={{0,1},{1,0},{2,3},{3,2},{4,5},{5,4},{6,7},{7,6},{8,9},{9,8},{10,11... | collective-permute-start | bytes 1769480 | tf_op jit(solution)/shard_map/ppermute | solution.py:880
  111.3 29.7 %collective-permute-start.13 = (bf16[192,1536]{1,0:T(8,128)(2,1)S(1)}, bf16[192,1536]{1,0:T(8,128)(2,1)S(1)}, u32[]{:S(2)}, u32[]{:S(2)}) collective-permute-start(bf16[192,1536]{1,0:T(8,128)(2,1)S(1)} %get-tuple-element.162.refs_4_), channel_id=1, source_target_pairs={{0,2},{1,3},{2,0},{3,1},{4,6},{5,7},{6,4},{7,5},{8,10},{9,11},{10,... | collective-permute-start | bytes 1769480 | tf_op jit(solution)/shard_map/ppermute | solution.py:880
  112.9 104.4 %all-gather.12.cloned.1.call-start = ((), (), s32[]{:S(2)}) async-start(), calls=%async_computation.8 | async-start | bytes 1474560 | tf_op jit(solution)/shard_map/all_gather | solution.py:1012
  140.7 39.9 %collective-permute-start.14 = (bf16[2,192,1536]{2,1,0:T(8,128)(2,1)}, bf16[2,192,1536]{2,1,0:T(8,128)(2,1)}, u32[]{:S(2)}, u32[]{:S(2)}) collective-permute-start(bf16[2,192,1536]{2,1,0:T(8,128)(2,1)} %pad_maximum_fusion.3.refs_0_), channel_id=1, source_target_pairs={{0,2},{1,3},{2,0},{3,1},{4,6},{5,7},{6,4},{7,5},{8,10},{9,11},{10,... | collective-permute-start | bytes 3538952 | tf_op jit(solution)/shard_map/ppermute | solution.py:880
  141.9 38.8 %collective-permute-start.15 = (bf16[2,192,1536]{2,1,0:T(8,128)(2,1)S(1)}, bf16[2,192,1536]{2,1,0:T(8,128)(2,1)}, u32[]{:S(2)}, u32[]{:S(2)}) collective-permute-start(bf16[2,192,1536]{2,1,0:T(8,128)(2,1)S(1)} %pad_maximum_fusion.4.refs_0_), channel_id=1, source_target_pairs={{0,1},{1,0},{2,3},{3,2},{4,5},{5,4},{6,7},{7,6},{8,9},{9,8},{10,11... | collective-permute-start | bytes 3538952 | tf_op jit(solution)/shard_map/ppermute | solution.py:880
  168.8 24.5 %collective-permute-start.18 = (bf16[384,1536]{0,1:T(8,128)(2,1)}, bf16[384,1536]{0,1:T(8,128)(2,1)S(1)}, u32[]{:S(2)}, u32[]{:S(2)}) collective-permute-start(bf16[384,1536]{0,1:T(8,128)(2,1)} %bitcast.113), channel_id=1, source_target_pairs={{0,16},{16,0},{1,17},{17,1},{2,18},{18,2},{3,19},{19,3},{4,20},{20... | collective-permute-start | bytes 3538952 | tf_op jit(solution)/shard_map/ppermute | solution.py:884
  187.0 130.9 %all-gather.14.cloned.1.call-start = ((), (), s32[]{:S(2)}) async-start(), calls=%async_computation.9 | async-start | bytes 4423680 | tf_op jit(solution)/shard_map/all_gather | solution.py:1012
  189.8 11.3 %collective-permute-start.23 = (f32[8,1536]{1,0:T(8,128)S(1)}, f32[8,1536]{1,0:T(8,128)S(1)}, u32[]{:S(2)}, u32[]{:S(2)}) collective-permute-start(f32[8,1536]{1,0:T(8,128)S(1)} %add.129.refs_1_), channel_id=1, source_target_pairs={{0,1},{1,0},{2,3},{3,2},{4,5},{5,4},{6,7},{7,6},{8,9},{9,8},{10,11... | collective-permute-start | bytes 147464 | tf_op jit(solution)/shard_map/ppermute | solution.py:880
  206.9 54.0 %collective-permute-start.19 = (f32[2,192,1536]{2,1,0:T(8,128)}, f32[2,192,1536]{2,1,0:T(8,128)}, u32[]{:S(2)}, u32[]{:S(2)}) collective-permute-start(f32[2,192,1536]{2,1,0:T(8,128)} %get-tuple-element.168), channel_id=1, source_target_pairs={{0,2},{1,3},{2,0},{3,1},{4,6},{5,7},{6,4},{7,5},{8,10},{9,11},{10,... | collective-permute-start | bytes 7077896 | tf_op jit(solution)/shard_map/ppermute | solution.py:880
  209.1 387.9 %reduce-scatter.8.cloned.1.call-start = ((), (), s32[]{:S(2)}) async-start(), calls=%async_computation.11 | async-start | bytes 1474560 | tf_op jit(solution)/shard_map/reduce_scatter | solution.py:1165
  215.6 56.9 %collective-permute-start.30 = (f32[2,192,1536]{2,1,0:T(8,128)}, f32[2,192,1536]{2,1,0:T(8,128)}, u32[]{:S(2)}, u32[]{:S(2)}) collective-permute-start(f32[2,192,1536]{2,1,0:T(8,128)} %get-tuple-element.179), channel_id=1, source_target_pairs={{0,1},{1,0},{2,3},{3,2},{4,5},{5,4},{6,7},{7,6},{8,9},{9,8},{10,11... | collective-permute-start | bytes 7077896 | tf_op jit(solution)/shard_map/ppermute | solution.py:880
  216.8 46.8 %collective-permute-start.28 = (bf16[2,192,1536]{2,1,0:T(8,128)(2,1)S(1)}, bf16[2,192,1536]{2,1,0:T(8,128)(2,1)}, u32[]{:S(2)}, u32[]{:S(2)}) collective-permute-start(bf16[2,192,1536]{2,1,0:T(8,128)(2,1)S(1)} %pad_maximum_fusion.4.refs_0_), channel_id=1, source_target_pairs={{0,16},{16,0},{1,17},{17,1},{2,18},{18,2},{3,19},{19,3},{4,20},{20... | collective-permute-start | bytes 3538952 | tf_op jit(solution)/shard_map/ppermute | solution.py:884
  216.8 46.8 %collective-permute-start.29 = (bf16[2,192,1536]{2,1,0:T(8,128)(2,1)}, bf16[2,192,1536]{2,1,0:T(8,128)(2,1)}, u32[]{:S(2)}, u32[]{:S(2)}) collective-permute-start(bf16[2,192,1536]{2,1,0:T(8,128)(2,1)} %collective-permute-done.15.refs_8_.refs_1_), channel_id=1, source_target_pairs={{0,16},{16,0},{1,17},{17,1},{2,18},{18,2},{3,19},{19,3},{4,20},{20... | collective-permute-start | bytes 3538952 | tf_op jit(solution)/shard_map/ppermute | solution.py:884
  262.3 32.1 %collective-permute-start.27 = (f32[192,1536]{1,0:T(8,128)S(1)}, f32[192,1536]{1,0:T(8,128)S(1)}, u32[]{:S(2)}, u32[]{:S(2)}) collective-permute-start(f32[192,1536]{1,0:T(8,128)S(1)} %fusion.3.refs_6_), channel_id=1, source_target_pairs={{0,1},{1,0},{2,3},{3,2},{4,5},{5,4},{6,7},{7,6},{8,9},{9,8},{10,11... | collective-permute-start | bytes 3538952 | tf_op jit(solution)/shard_map/ppermute | solution.py:880
  273.9 27.4 %collective-permute-start.31 = (f32[192,1536]{1,0:T(8,128)S(1)}, f32[192,1536]{1,0:T(8,128)S(1)}, u32[]{:S(2)}, u32[]{:S(2)}) collective-permute-start(f32[192,1536]{1,0:T(8,128)S(1)} %fusion.2), channel_id=1, source_target_pairs={{0,2},{1,3},{2,0},{3,1},{4,6},{5,7},{6,4},{7,5},{8,10},{9,11},{10,... | collective-permute-start | bytes 3538952 | tf_op jit(solution)/shard_map/ppermute | solution.py:880
  299.6 16.5 %collective-permute-start.32 = (bf16[192,1536]{1,0:T(8,128)(2,1)}, bf16[192,1536]{1,0:T(8,128)(2,1)S(1)}, u32[]{:S(2)}, u32[]{:S(2)}) collective-permute-start(bf16[192,1536]{1,0:T(8,128)(2,1)} %get-tuple-element.183.refs_5_), channel_id=1, source_target_pairs={{0,1},{1,0},{2,3},{3,2},{4,5},{5,4},{6,7},{7,6},{8,9},{9,8},{10,11... | collective-permute-start | bytes 1769480 | tf_op jit(solution)/shard_map/ppermute | solution.py:880
  306.5 20.4 %collective-permute-start.34 = (bf16[192,1536]{1,0:T(8,128)(2,1)}, bf16[192,1536]{1,0:T(8,128)(2,1)S(1)}, u32[]{:S(2)}, u32[]{:S(2)}) collective-permute-start(bf16[192,1536]{1,0:T(8,128)(2,1)} %get-tuple-element.186), channel_id=1, source_target_pairs={{0,1},{1,0},{2,3},{3,2},{4,5},{5,4},{6,7},{7,6},{8,9},{9,8},{10,11... | collective-permute-start | bytes 1769480 | tf_op jit(solution)/shard_map/ppermute | solution.py:880
  316.2 24.7 %collective-permute-start.33 = (bf16[2,192,1536]{2,1,0:T(8,128)(2,1)S(1)}, bf16[2,192,1536]{2,1,0:T(8,128)(2,1)}, u32[]{:S(2)}, u32[]{:S(2)}) collective-permute-start(bf16[2,192,1536]{2,1,0:T(8,128)(2,1)S(1)} %pad_maximum_fusion.5.refs_2_.refs_0_), channel_id=1, source_target_pairs={{0,2},{1,3},{2,0},{3,1},{4,6},{5,7},{6,4},{7,5},{8,10},{9,11},{10,... | collective-permute-start | bytes 3538952 | tf_op jit(solution)/shard_map/ppermute | solution.py:880
  317.9 25.5 %collective-permute-start.35 = (bf16[2,192,1536]{2,1,0:T(8,128)(2,1)S(1)}, bf16[2,192,1536]{2,1,0:T(8,128)(2,1)}, u32[]{:S(2)}, u32[]{:S(2)}) collective-permute-start(bf16[2,192,1536]{2,1,0:T(8,128)(2,1)S(1)} %pad_maximum_fusion.5.refs_2_.refs_0_), channel_id=1, source_target_pairs={{0,16},{16,0},{1,17},{17,1},{2,18},{18,2},{3,19},{19,3},{4,20},{20... | collective-permute-start | bytes 3538952 | tf_op jit(solution)/shard_map/ppermute | solution.py:884
  341.5 28.4 %collective-permute-start.37 = (bf16[2,192,1536]{2,1,0:T(8,128)(2,1)S(1)}, bf16[2,192,1536]{2,1,0:T(8,128)(2,1)S(1)}, u32[]{:S(2)}, u32[]{:S(2)}) collective-permute-start(bf16[2,192,1536]{2,1,0:T(8,128)(2,1)S(1)} %copy-done.17), channel_id=1, source_target_pairs={{0,2},{1,3},{2,0},{3,1},{4,6},{5,7},{6,4},{7,5},{8,10},{9,11},{10,... | collective-permute-start | bytes 3538952 | tf_op jit(solution)/shard_map/ppermute | solution.py:880
  343.2 27.3 %collective-permute-start.42 = (bf16[2,192,1536]{2,1,0:T(8,128)(2,1)S(1)}, bf16[2,192,1536]{2,1,0:T(8,128)(2,1)S(1)}, u32[]{:S(2)}, u32[]{:S(2)}) collective-permute-start(bf16[2,192,1536]{2,1,0:T(8,128)(2,1)S(1)} %copy-done.17), channel_id=1, source_target_pairs={{0,16},{16,0},{1,17},{17,1},{2,18},{18,2},{3,19},{19,3},{4,20},{20... | collective-permute-start | bytes 3538952 | tf_op jit(solution)/shard_map/ppermute | solution.py:884
  369.9 38.4 %collective-permute-start.44 = (bf16[1152,1536]{1,0:T(8,128)(2,1)}, bf16[1152,1536]{1,0:T(8,128)(2,1)}, u32[]{:S(2)}, u32[]{:S(2)}) collective-permute-start(bf16[1152,1536]{1,0:T(8,128)(2,1)} %get-tuple-element.187.refs_10_.refs_2_), channel_id=1, source_target_pairs={{0,16},{16,0},{1,17},{17,1},{2,18},{18,2},{3,19},{19,3},{4,20},{20... | collective-permute-start | bytes 10616840 | tf_op jit(solution)/shard_map/ppermute | solution.py:884
  370.4 29.3 %collective-permute-start.38 = (f32[8,1536]{1,0:T(8,128)}, f32[8,1536]{1,0:T(8,128)S(1)}, u32[]{:S(2)}, u32[]{:S(2)}) collective-permute-start(f32[8,1536]{1,0:T(8,128)} %get-tuple-element.192.refs_10_), channel_id=1, source_target_pairs={{0,16},{16,0},{1,17},{17,1},{2,18},{18,2},{3,19},{19,3},{4,20},{20... | collective-permute-start | bytes 147464 | tf_op jit(solution)/shard_map/ppermute | solution.py:884
  403.3 44.1 %collective-permute-start.53 = (bf16[1152,1536]{1,0:T(8,128)(2,1)}, bf16[1152,1536]{1,0:T(8,128)(2,1)}, u32[]{:S(2)}, u32[]{:S(2)}) collective-permute-start(bf16[1152,1536]{1,0:T(8,128)(2,1)} %get-tuple-element.216.refs_2_), channel_id=1, source_target_pairs={{0,16},{16,0},{1,17},{17,1},{2,18},{18,2},{3,19},{19,3},{4,20},{20... | collective-permute-start | bytes 10616840 | tf_op jit(solution)/shard_map/ppermute | solution.py:884
  404.1 36.4 %collective-permute-start.48 = (f32[8,1536]{1,0:T(8,128)S(1)}, f32[8,1536]{1,0:T(8,128)S(1)}, u32[]{:S(2)}, u32[]{:S(2)}) collective-permute-start(f32[8,1536]{1,0:T(8,128)S(1)} %add.133.refs_12_.refs_1_), channel_id=1, source_target_pairs={{0,1},{1,0},{2,3},{3,2},{4,5},{5,4},{6,7},{7,6},{8,9},{9,8},{10,11... | collective-permute-start | bytes 147464 | tf_op jit(solution)/shard_map/ppermute | solution.py:880
  405.4 35.1 %collective-permute-start.49 = (f32[8,1536]{1,0:T(8,128)S(1)}, f32[8,1536]{1,0:T(8,128)S(1)}, u32[]{:S(2)}, u32[]{:S(2)}) collective-permute-start(f32[8,1536]{1,0:T(8,128)S(1)} %add.133.refs_12_.refs_1_), channel_id=1, source_target_pairs={{0,2},{1,3},{2,0},{3,1},{4,6},{5,7},{6,4},{7,5},{8,10},{9,11},{10,... | collective-permute-start | bytes 147464 | tf_op jit(solution)/shard_map/ppermute | solution.py:880
  407.6 32.9 %collective-permute-start.50 = (f32[8,1536]{1,0:T(8,128)S(1)}, f32[8,1536]{1,0:T(8,128)S(1)}, u32[]{:S(2)}, u32[]{:S(2)}) collective-permute-start(f32[8,1536]{1,0:T(8,128)S(1)} %add.133.refs_12_.refs_1_), channel_id=1, source_target_pairs={{0,3},{1,2},{2,1},{3,0},{4,7},{5,6},{6,5},{7,4},{8,11},{9,10},{10,... | collective-permute-start | bytes 147464 | tf_op jit(solution)/shard_map/ppermute | solution.py:880
  459.2 29.0 %collective-permute-start.54 = (bf16[2,192,1536]{2,1,0:T(8,128)(2,1)}, bf16[2,192,1536]{2,1,0:T(8,128)(2,1)S(1)}, u32[]{:S(2)}, u32[]{:S(2)}) collective-permute-start(bf16[2,192,1536]{2,1,0:T(8,128)(2,1)} %get-tuple-element.219), channel_id=1, source_target_pairs={{0,2},{1,3},{2,0},{3,1},{4,6},{5,7},{6,4},{7,5},{8,10},{9,11},{10,... | collective-permute-start | bytes 3538952 | tf_op jit(solution)/shard_map/ppermute | solution.py:880
  487.9 12.5 %collective-permute-start.56 = (bf16[4,192,1152]{2,1,0:T(8,128)(2,1)}, bf16[4,192,1152]{2,1,0:T(8,128)(2,1)S(1)}, u32[]{:S(2)}, u32[]{:S(2)}) collective-permute-start(bf16[4,192,1152]{2,1,0:T(8,128)(2,1)} %get-tuple-element.226), channel_id=1, source_target_pairs={{0,16},{16,0},{1,17},{17,1},{2,18},{18,2},{3,19},{19,3},{4,20},{20... | collective-permute-start | bytes 5308424 | tf_op jit(solution)/shard_map/ppermute | solution.py:884
  489.2 22.9 %collective-permute-start.55 = (bf16[192,1536]{1,0:T(8,128)(2,1)S(1)}, bf16[192,1536]{1,0:T(8,128)(2,1)}, u32[]{:S(2)}, u32[]{:S(2)}) collective-permute-start(bf16[192,1536]{1,0:T(8,128)(2,1)S(1)} %fusion.7.refs_5_), channel_id=1, source_target_pairs={{0,1},{1,0},{2,3},{3,2},{4,5},{5,4},{6,7},{7,6},{8,9},{9,8},{10,11... | collective-permute-start | bytes 1769480 | tf_op jit(solution)/shard_map/ppermute | solution.py:880
  500.3 160.0 %reduce-scatter.10.cloned.1.call-start = ((), (), s32[]{:S(2)}) async-start(), calls=%async_computation.12 | async-start | bytes 4423680 | tf_op jit(solution)/shard_map/reduce_scatter | solution.py:1165
  516.8 20.5 %collective-permute-start.57 = (bf16[192,1664]{1,0:T(8,128)(2,1)}, bf16[192,1664]{1,0:T(8,128)(2,1)S(1)}, u32[]{:S(2)}, u32[]{:S(2)}) collective-permute-start(bf16[192,1664]{1,0:T(8,128)(2,1)} %get-tuple-element.234.refs_4_), channel_id=1, source_target_pairs={{0,1},{1,0},{2,3},{3,2},{4,5},{5,4},{6,7},{7,6},{8,9},{9,8},{10,11... | collective-permute-start | bytes 1916936 | tf_op jit(solution)/shard_map/ppermute | solution.py:880
  517.6 28.0 %collective-permute-start.58 = (bf16[2,192,1536]{2,1,0:T(8,128)(2,1)S(1)}, bf16[2,192,1536]{2,1,0:T(8,128)(2,1)}, u32[]{:S(2)}, u32[]{:S(2)}) collective-permute-start(bf16[2,192,1536]{2,1,0:T(8,128)(2,1)S(1)} %copy-done.75), channel_id=1, source_target_pairs={{0,2},{1,3},{2,0},{3,1},{4,6},{5,7},{6,4},{7,5},{8,10},{9,11},{10,... | collective-permute-start | bytes 3538952 | tf_op jit(solution)/shard_map/ppermute | solution.py:880
  546.8 210.8 %reduce-scatter.6.cloned.1.call-start = ((), (), s32[]{:S(2)}) async-start(), calls=%async_computation.10 | async-start | bytes 5898240 | tf_op jit(solution)/shard_map/reduce_scatter | solution.py:1168
  548.2 30.0 %collective-permute-start.60 = (bf16[2,192,1664]{2,1,0:T(8,128)(2,1)S(1)}, bf16[2,192,1664]{2,1,0:T(8,128)(2,1)}, u32[]{:S(2)}, u32[]{:S(2)}) collective-permute-start(bf16[2,192,1664]{2,1,0:T(8,128)(2,1)S(1)} %pad_maximum_fusion.refs_8_.refs_0_), channel_id=1, source_target_pairs={{0,2},{1,3},{2,0},{3,1},{4,6},{5,7},{6,4},{7,5},{8,10},{9,11},{10,... | collective-permute-start | bytes 3833864 | tf_op jit(solution)/shard_map/ppermute | solution.py:880
  550.3 14.9 %collective-permute-start.59 = (bf16[192,1536]{1,0:T(8,128)(2,1)S(1)}, bf16[192,1536]{1,0:T(8,128)(2,1)S(1)}, u32[]{:S(2)}, u32[]{:S(2)}) collective-permute-start(bf16[192,1536]{1,0:T(8,128)(2,1)S(1)} %fusion.6.refs_7_), channel_id=1, source_target_pairs={{0,1},{1,0},{2,3},{3,2},{4,5},{5,4},{6,7},{7,6},{8,9},{9,8},{10,11... | collective-permute-start | bytes 1769480 | tf_op jit(solution)/shard_map/ppermute | solution.py:880
  551.2 45.8 %collective-permute-start.61 = (bf16[2,192,1664]{2,1,0:T(8,128)(2,1)S(1)}, bf16[2,192,1664]{2,1,0:T(8,128)(2,1)}, u32[]{:S(2)}, u32[]{:S(2)}) collective-permute-start(bf16[2,192,1664]{2,1,0:T(8,128)(2,1)S(1)} %pad_maximum_fusion.refs_8_.refs_0_), channel_id=1, source_target_pairs={{0,16},{16,0},{1,17},{17,1},{2,18},{18,2},{3,19},{19,3},{4,20},{20... | collective-permute-start | bytes 3833864 | tf_op jit(solution)/shard_map/ppermute | solution.py:884
  578.2 18.8 %collective-permute-start.62 = (bf16[2,192,1664]{2,1,0:T(8,128)(2,1)}, bf16[2,192,1664]{2,1,0:T(8,128)(2,1)}, u32[]{:S(2)}, u32[]{:S(2)}) collective-permute-start(bf16[2,192,1664]{2,1,0:T(8,128)(2,1)} %collective-permute-done.60.refs_1_), channel_id=1, source_target_pairs={{0,16},{16,0},{1,17},{17,1},{2,18},{18,2},{3,19},{19,3},{4,20},{20... | collective-permute-start | bytes 3833864 | tf_op jit(solution)/shard_map/ppermute | solution.py:884
  578.2 17.0 %collective-permute-start.63 = (bf16[192,1664]{1,0:T(8,128)(2,1)}, bf16[192,1664]{1,0:T(8,128)(2,1)S(1)}, u32[]{:S(2)}, u32[]{:S(2)}) collective-permute-start(bf16[192,1664]{1,0:T(8,128)(2,1)} %get-tuple-element.238.refs_14_.refs_4_), channel_id=1, source_target_pairs={{0,1},{1,0},{2,3},{3,2},{4,5},{5,4},{6,7},{7,6},{8,9},{9,8},{10,11... | collective-permute-start | bytes 1916936 | tf_op jit(solution)/shard_map/ppermute | solution.py:880
  596.5 33.0 %collective-permute-start.64 = (bf16[2,192,1664]{2,1,0:T(8,128)(2,1)S(1)}, bf16[2,192,1664]{2,1,0:T(8,128)(2,1)}, u32[]{:S(2)}, u32[]{:S(2)}) collective-permute-start(bf16[2,192,1664]{2,1,0:T(8,128)(2,1)S(1)} %pad_maximum_fusion.1.refs_16_.refs_5_.refs_0_), channel_id=1, source_target_pairs={{0,2},{1,3},{2,0},{3,1},{4,6},{5,7},{6,4},{7,5},{8,10},{9,11},{10,... | collective-permute-start | bytes 3833864 | tf_op jit(solution)/shard_map/ppermute | solution.py:880
  629.6 155.9 %reduce-scatter.12.cloned.1.call-start = ((), (), s32[]{:S(2)}) async-start(), calls=%async_computation.13 | async-start | bytes 4423680 | tf_op jit(solution)/shard_map/reduce_scatter | solution.py:1165
  630.8 27.3 %collective-permute-start.67 = (bf16[2,192,1664]{2,1,0:T(8,128)(2,1)S(1)}, bf16[2,192,1664]{2,1,0:T(8,128)(2,1)S(1)}, u32[]{:S(2)}, u32[]{:S(2)}) collective-permute-start(bf16[2,192,1664]{2,1,0:T(8,128)(2,1)S(1)} %copy-done.9), channel_id=1, source_target_pairs={{0,16},{16,0},{1,17},{17,1},{2,18},{18,2},{3,19},{19,3},{4,20},{20... | collective-permute-start | bytes 3833864 | tf_op jit(solution)/shard_map/ppermute | solution.py:884
  657.0 40.0 %collective-permute-start.66 = (bf16[2,192,1536]{2,1,0:T(8,128)(2,1)}, bf16[2,192,1536]{2,1,0:T(8,128)(2,1)S(1)}, u32[]{:S(2)}, u32[]{:S(2)}) collective-permute-start(bf16[2,192,1536]{2,1,0:T(8,128)(2,1)} %get-tuple-element.249), channel_id=1, source_target_pairs={{0,2},{1,3},{2,0},{3,1},{4,6},{5,7},{6,4},{7,5},{8,10},{9,11},{10,... | collective-permute-start | bytes 3538952 | tf_op jit(solution)/shard_map/ppermute | solution.py:880
  696.2 17.1 %collective-permute-start.70 = (bf16[4,192,1152]{2,1,0:T(8,128)(2,1)}, bf16[4,192,1152]{2,1,0:T(8,128)(2,1)}, u32[]{:S(2)}, u32[]{:S(2)}) collective-permute-start(bf16[4,192,1152]{2,1,0:T(8,128)(2,1)} %get-tuple-element.261), channel_id=1, source_target_pairs={{0,16},{16,0},{1,17},{17,1},{2,18},{18,2},{3,19},{19,3},{4,20},{20... | collective-permute-start | bytes 5308424 | tf_op jit(solution)/shard_map/ppermute | solution.py:884
  710.1 109.5 %reduce-scatter.14.cloned.1.call-start = ((), (), s32[]{:S(2)}) async-start(), calls=%async_computation.14 | async-start | bytes 1474560 | tf_op jit(solution)/shard_map/reduce_scatter | solution.py:1165
  711.8 40.9 %collective-permute-start.69 = (bf16[192,1536]{1,0:T(8,128)(2,1)S(1)}, bf16[192,1536]{1,0:T(8,128)(2,1)S(1)}, u32[]{:S(2)}, u32[]{:S(2)}) collective-permute-start(bf16[192,1536]{1,0:T(8,128)(2,1)S(1)} %fusion.5), channel_id=1, source_target_pairs={{0,1},{1,0},{2,3},{3,2},{4,5},{5,4},{6,7},{7,6},{8,9},{9,8},{10,11... | collective-permute-start | bytes 1769480 | tf_op jit(solution)/shard_map/ppermute | solution.py:880
  724.5 26.9 %collective-permute-start.71 = (bf16[2,192,1536]{2,1,0:T(8,128)(2,1)}, bf16[2,192,1536]{2,1,0:T(8,128)(2,1)S(1)}, u32[]{:S(2)}, u32[]{:S(2)}) collective-permute-start(bf16[2,192,1536]{2,1,0:T(8,128)(2,1)} %get-tuple-element.267), channel_id=1, source_target_pairs={{0,2},{1,3},{2,0},{3,1},{4,6},{5,7},{6,4},{7,5},{8,10},{9,11},{10,... | collective-permute-start | bytes 3538952 | tf_op jit(solution)/shard_map/ppermute | solution.py:880
  760.9 15.7 %collective-permute-start.73 = (bf16[192,1536]{1,0:T(8,128)(2,1)S(1)}, bf16[192,1536]{1,0:T(8,128)(2,1)S(1)}, u32[]{:S(2)}, u32[]{:S(2)}) collective-permute-start(bf16[192,1536]{1,0:T(8,128)(2,1)S(1)} %copy-done.31), channel_id=1, source_target_pairs={{0,1},{1,0},{2,3},{3,2},{4,5},{5,4},{6,7},{7,6},{8,9},{9,8},{10,11... | collective-permute-start | bytes 1769480 | tf_op jit(solution)/shard_map/ppermute | solution.py:880
  787.8 13.8 %collective-permute-start.79 = (f32[16,1536]{1,0:T(8,128)S(1)}, f32[16,1536]{1,0:T(8,128)S(1)}, u32[]{:S(2)}, u32[]{:S(2)}) collective-permute-start(f32[16,1536]{1,0:T(8,128)S(1)} %select_add_fusion), channel_id=1, source_target_pairs={{0,12},{4,0},{8,4},{12,8},{1,13},{5,1},{9,5},{13,9},{2,14},{6,2},{... | collective-permute-start | bytes 294920 | tf_op jit(solution)/shard_map/ppermute | solution.py:920
  791.0 10.6 %collective-permute-start.76 = (f32[16,1536]{1,0:T(8,128)S(1)}, f32[16,1536]{1,0:T(8,128)S(1)}, u32[]{:S(2)}, u32[]{:S(2)}) collective-permute-start(f32[16,1536]{1,0:T(8,128)S(1)} %select_add_fusion), channel_id=1, source_target_pairs={{0,4},{4,8},{8,12},{12,0},{1,5},{5,9},{9,13},{13,1},{2,6},{6,10},{... | collective-permute-start | bytes 294920 | tf_op jit(solution)/shard_map/ppermute | solution.py:920
  791.0 15.1 %collective-permute-start.78 = (f32[16,1536]{1,0:T(8,128)S(1)}, f32[16,1536]{1,0:T(8,128)S(1)}, u32[]{:S(2)}, u32[]{:S(2)}) collective-permute-start(f32[16,1536]{1,0:T(8,128)S(1)} %select_add_fusion), channel_id=1, source_target_pairs={{0,8},{4,12},{8,0},{12,4},{1,9},{5,13},{9,1},{13,5},{2,10},{6,14},... | collective-permute-start | bytes 294920 | tf_op jit(solution)/shard_map/ppermute | solution.py:920
  813.4 10.9 %collective-permute-start.86 = (bf16[384,304]{1,0:T(8,128)(2,1)S(1)}, bf16[384,304]{1,0:T(8,128)(2,1)S(1)}, u32[]{:S(2)}, u32[]{:S(2)}) collective-permute-start(bf16[384,304]{1,0:T(8,128)(2,1)S(1)} %fusion.8), channel_id=1, source_target_pairs={{0,3},{1,2},{2,1},{3,0},{4,7},{5,6},{6,5},{7,4},{8,11},{9,10},{10,... | collective-permute-start | bytes 700424 | tf_op jit(solution)/shard_map/ppermute | solution.py:880
  814.4 13.9 %collective-permute-start.85 = (bf16[384,304]{1,0:T(8,128)(2,1)S(1)}, bf16[384,304]{1,0:T(8,128)(2,1)S(1)}, u32[]{:S(2)}, u32[]{:S(2)}) collective-permute-start(bf16[384,304]{1,0:T(8,128)(2,1)S(1)} %fusion.8), channel_id=1, source_target_pairs={{0,2},{1,3},{2,0},{3,1},{4,6},{5,7},{6,4},{7,5},{8,10},{9,11},{10,... | collective-permute-start | bytes 700424 | tf_op jit(solution)/shard_map/ppermute | solution.py:880
  815.9 13.1 %collective-permute-start.84 = (bf16[384,304]{1,0:T(8,128)(2,1)S(1)}, bf16[384,304]{1,0:T(8,128)(2,1)}, u32[]{:S(2)}, u32[]{:S(2)}) collective-permute-start(bf16[384,304]{1,0:T(8,128)(2,1)S(1)} %fusion.8), channel_id=1, source_target_pairs={{0,1},{1,0},{2,3},{3,2},{4,5},{5,4},{6,7},{7,6},{8,9},{9,8},{10,11... | collective-permute-start | bytes 700424 | tf_op jit(solution)/shard_map/ppermute | solution.py:880
  820.3 11.0 %collective-permute-start.87 = (bf16[384,384]{1,0:T(8,128)(2,1)}, bf16[384,384]{1,0:T(8,128)(2,1)}, u32[]{:S(2)}, u32[]{:S(2)}) collective-permute-start(bf16[384,384]{1,0:T(8,128)(2,1)} %broadcast_select_fusion.13), channel_id=1, source_target_pairs={{0,16},{16,0},{1,17},{17,1},{2,18},{18,2},{3,19},{19,3},{4,20},{20... | collective-permute-start | bytes 884744 | tf_op jit(solution)/shard_map/ppermute | solution.py:884
  (133 other events, 858.7 us)
Sparse Core Ops, SparseCore 0:
  22.3 41.5 all-gather.5
  66.3 38.9 all-gather.7
  113.0 27.1 all-gather.9
  187.1 28.4 all-gather.11
  217.1 69.0 all-gather.13
  500.4 26.4 reduce-scatter.7
  546.9 63.1 reduce-scatter.9
  629.7 70.5 reduce-scatter.5
  710.2 66.4 reduce-scatter.11
  787.9 31.6 reduce-scatter.13
